TPU v7x, 128 devices: a whole 4x4x4 slice. The times are simulated.
128 devices in a mesh: row: 8 (over z, core), col: 16 (over x, y).
Axes of the slice: x: 4, y: 4, z: 4, core: 2. Of those that a mesh axis runs over, the one named last changes fastest.
Arguments:
- a_blocks: float32 [1024, 8, 256, 256], P(('row', 'col')), may hold values from -0.09375 to 0.09375
- a_live: int32 [1024, 8], P(('row', 'col')), may hold values from 0 to 1, as said below
- p_blocks: float32 [1024, 256, 2, 128], P(('row', 'col')), may hold values from -0.1875 to 0.1875
- p_cols: int32 [1024, 2], P(('row', 'col')), may hold values from 0 to 127, as said below
- ghost_list: int32 [1024, 7], P(('row', 'col')), may hold values from 0 to 7, as said below
- policy: int32 [1024], P(('row', 'col')), may hold values from 0 to 15
- rates: float32 [16, 256], replicated, may hold values from 0.1 to 1
- rhs: float32 [16384, 256], P(('row', 'col')), may hold values from -6 to 6
- guess: float32 [16384, 256], P(('row', 'col')), may hold values from -6 to 6
Outputs:
- coarse: float32 [16384, 8, 16, 128], P('row', None, 'col')
- smoothed: float32 [16384, 256], P(('row', 'col'))
Inputs may be any that keep to these rules, and one draw needn't show every extreme that they name: a_live[i, 0] is 1 for every i. On each device and for each k, the entries ghost_list[d * 8 + s, k] over s = 0 .. 7 are a permutation of 0 .. 7. p_cols[j, m] modulo the number of col devices equals (col index of the device holding block row j + m * 8) modulo that number. The quotient by that number names a mesh row: among the 16 entries of one device at most 2 name the same mesh row, and the device's own mesh row is named exactly 2 times, by at least one entry of each m.
All inputs are finite; a program needn't handle non-finite values.
Results may differ from a plain program's by a relative error of at most 0.0003.
Values sent between devices are 32-bit elements; how exact they have to be, the bound alone decides.
No kernel may reach another device: no remote copies, remote signals or barrier semaphores. Data moves between devices by JAX's collectives and lax.ppermute only.
A program may use at most 192 MiB of HBM per device.

v0:
```python
import jax
import jax.numpy as jnp
from jax import lax
from jax.sharding import PartitionSpec as P

BS = 256
CB = 128
KA = 8
KP = 2
NPOL = 16


damping = 0.7


def from_behind(value, axis, steps):
    count = lax.axis_size(axis)
    pairs = [(source, (source + steps) % count) for source in range(count)]
    return lax.ppermute(value, axis, pairs)


def on_device(a_blocks, a_live, p_blocks, p_cols, ghost_list, policy, rates, rhs, guess):
    highest = lax.Precision.HIGHEST
    row_count = lax.axis_size("row")
    col_count = lax.axis_size("col")
    dev_count = row_count * col_count
    row_here = lax.axis_index("row")
    col_here = lax.axis_index("col")
    local_rows = a_blocks.shape[0]
    own_p = p_blocks.reshape(local_rows, BS, KP * CB)
    send_p = []
    send_c = []
    for offset in range(1, KA):
        picks = ghost_list[:, offset - 1]
        send_p.append(own_p[picks])
        send_c.append(p_cols[picks].astype(jnp.float32))
    incoming_p = [own_p]
    incoming_c = [p_cols]
    for offset in range(1, KA):
        moved_p, moved_c = from_behind((send_p[offset - 1], send_c[offset - 1]), "col", offset)
        incoming_p.append(moved_p)
        incoming_c.append(moved_c.astype(jnp.int32))
    ghost_p = jnp.stack(incoming_p, axis=1)
    ghost_c = jnp.stack(incoming_c, axis=1)
    live = a_live.astype(jnp.float32)
    selector = (policy[:, None] == jnp.arange(NPOL, dtype=jnp.int32)[None, :]).astype(jnp.float32)
    rate_rows = jnp.dot(selector, rates, precision=highest)
    product = jnp.einsum("skab,skbn->skan", a_blocks, ghost_p, precision=highest)
    product = product * live[:, :, None, None]
    product = product.at[:, 0].add(rate_rows[:, :, None] * own_p)
    partial_value = jnp.einsum("sam,skan->skmn", own_p, product, precision=highest)
    partial_value = (
        partial_value.reshape(local_rows, KA, KP, CB, KP, CB)
        .transpose(0, 1, 2, 4, 3, 5)
        .reshape(-1, CB, CB)
    )
    first = jnp.broadcast_to(p_cols[:, None, :, None], (local_rows, KA, KP, KP)).reshape(-1)
    second = jnp.broadcast_to(ghost_c[:, :, None, :], (local_rows, KA, KP, KP)).reshape(-1)
    alive = jnp.broadcast_to(a_live[:, :, None, None] > 0, (local_rows, KA, KP, KP)).reshape(-1)
    owner = first // col_count * col_count + second % col_count
    spot = first % col_count * row_count + second // col_count
    order = jnp.arange(owner.shape[0], dtype=jnp.int32)
    earlier = (
        (owner[None, :] == owner[:, None]) & alive[None, :] & (order[None, :] < order[:, None])
    )
    rank = jnp.sum(earlier.astype(jnp.int32), axis=1)
    row_cap = max(2, -(-(local_rows * KP) // row_count))
    slot_cap = row_cap * max(1, KA * KP // col_count)
    slot = jnp.where(alive, owner * slot_cap + rank, dev_count * slot_cap)
    sent_blocks = jax.ops.segment_sum(partial_value, slot, num_segments=dev_count * slot_cap + 1)[
        :-1
    ]
    sent_spots = jax.ops.segment_sum(
        (spot + 1).astype(jnp.float32), slot, num_segments=dev_count * slot_cap + 1
    )[:-1]
    got_blocks, got_spots = (
        lax.all_to_all(
            sent_blocks.reshape(dev_count, slot_cap, CB, CB),
            ("row", "col"),
            split_axis=0,
            concat_axis=0,
            tiled=True,
        ),
        lax.all_to_all(
            sent_spots.reshape(dev_count, slot_cap),
            ("row", "col"),
            split_axis=0,
            concat_axis=0,
            tiled=True,
        ),
    )
    places = got_spots.reshape(-1).astype(jnp.int32) - 1
    places = jnp.where(places < 0, dev_count, places)
    summed = jax.ops.segment_sum(
        got_blocks.reshape(-1, CB, CB), places, num_segments=dev_count + 1
    )[:-1]
    coarse = (
        summed.reshape(col_count, row_count, CB, CB)
        .transpose(0, 2, 1, 3)
        .reshape(col_count * CB, row_count, 1, CB)
    )
    matrix = coarse.reshape(col_count * CB, row_count * CB)
    own_block = lax.dynamic_slice(matrix, (col_here * CB, row_here * CB), (CB, CB))
    floor_diag = jnp.maximum(jnp.abs(jnp.diagonal(own_block)), 1.0)
    current = guess
    for sweep in range(2):
        gathered = lax.all_gather(current, "row", axis=0, tiled=True)
        applied = lax.psum_scatter(
            jnp.dot(matrix, gathered, precision=highest), "col", scatter_dimension=0, tiled=True
        )
        current = current + damping * (rhs - applied) / floor_diag[:, None]
    return (coarse, current)


def solution(mesh):
    return jax.shard_map(
        on_device,
        mesh=mesh,
        in_specs=(
            P(("row", "col"), None, None, None),
            P(("row", "col"), None),
            P(("row", "col"), None, None, None),
            P(("row", "col"), None),
            P(("row", "col"), None),
            P(("row", "col")),
            P(),
            P(("row", "col"), None),
            P(("row", "col"), None),
        ),
        out_specs=(P("row", None, "col", None), P(("row", "col"), None)),
        check_vma=False,
    )
```

profile of v0, /device:TPU:0, one launch (start us, length us, event | category | flops | bytes accessed | tf_op | source)
XLA Modules:
  0.0 1113.5 jit_solution(12962005515692555085)
XLA Ops:
  9.8 3.4 collective-permute-start.1
  15.0 3.6 collective-permute-start.2
  18.6 2.9 reshape.341
  23.5 2.9 copy.130
  28.5 2.9 copy.129
  34.1 4.1 copy.128
  48.4 2.1 gather_fusion.13
  50.5 4.1 reshape.490
  56.4 3.1 copy.132
  61.4 3.0 copy.134
  65.9 2.9 copy.135
  70.1 2.7 collective-permute-start.4
  72.9 2.2 collective-permute-start.5
  75.2 47.6 %collective-permute-start.9 = (f32[8,256,256]{1,2,0:T(8,128)}, f32[8,256,256]{1,2,0:T(8,128)}, u32[]{:S(2)}, u32[]{:S(2)}) collective-permute-start(f32[8,256,256]{1,2,0:T(8,128)} %copy.131), channel_id=1, source_target_pairs={{0,3},{1,4},{2,5},{3,6},{4,7},{5,8},{6,9},{7,10},{8,11},{9,12},{10... | collective-permute-start | bytes 6291464 | tf_op jit(solution)/shard_map/ppermute | solution.py:19
  123.9 44.1 %collective-permute-done.6 = f32[8,2]{1,0:T(8,128)S(1)} collective-permute-done((f32[8,2]{1,0:T(8,128)S(1)}, f32[8,2]{1,0:T(8,128)S(1)}, u32[]{:S(2)}, u32[]{:S(2)}) %collective-permute-start.6) | collective-permute-done | bytes 96 | tf_op jit(solution)/shard_map/ppermute | solution.py:19
  168.4 47.6 %collective-permute-start.12 = (f32[8,256,256]{1,2,0:T(8,128)}, f32[8,256,256]{1,2,0:T(8,128)}, u32[]{:S(2)}, u32[]{:S(2)}) collective-permute-start(f32[8,256,256]{1,2,0:T(8,128)} %copy.134), channel_id=1, source_target_pairs={{0,6},{1,7},{2,8},{3,9},{4,10},{5,11},{6,12},{7,13},{8,14},{9,15},... | collective-permute-start | bytes 6291464 | tf_op jit(solution)/shard_map/ppermute | solution.py:19
  216.3 6.1 collective-permute-start.13
  222.5 2.3 scatter_custom_fusion
  225.6 7.6 all-to-all-start
  233.1 3.0 bitcast_dynamic-update-slice_fusion.6
  236.2 3.0 bitcast_dynamic-update-slice_fusion.5
  239.2 3.0 bitcast_dynamic-update-slice_fusion.4
  242.2 3.0 bitcast_dynamic-update-slice_fusion.3
  245.2 15.9 %collective-permute-done.11 = f32[8,256,256]{1,2,0:T(8,128)} collective-permute-done((f32[8,256,256]{1,2,0:T(8,128)}, f32[8,256,256]{1,2,0:T(8,128)}, u32[]{:S(2)}, u32[]{:S(2)}) %collective-permute-start.11) | collective-permute-done | bytes 2097184 | tf_op jit(solution)/shard_map/ppermute | solution.py:19
  261.1 3.0 bitcast_dynamic-update-slice_fusion.2
  264.1 88.2 %collective-permute-done.12 = f32[8,256,256]{1,2,0:T(8,128)} collective-permute-done((f32[8,256,256]{1,2,0:T(8,128)}, f32[8,256,256]{1,2,0:T(8,128)}, u32[]{:S(2)}, u32[]{:S(2)}) %collective-permute-start.12) | collective-permute-done | bytes 2097184 | tf_op jit(solution)/shard_map/ppermute | solution.py:19
  352.3 3.0 bitcast_dynamic-update-slice_fusion.1
  355.3 3.0 bitcast_dynamic-update-slice_fusion
  358.3 43.2 %multiply_bitcast_fusion = f32[8,8,256,256]{2,3,1,0:T(8,128)} fusion(f32[8,8,256,256]{2,3,1,0:T(8,128)} %bitcast_dynamic-update-slice_fusion, f32[8,8,256,256]{3,2,1,0:T(8,128)} %param.11, f32[8,8]{1,0:T(8,128)S(1)} %convert_element_type.80), kind=kOutput, calls=%fused_computation.18 | convolution fusion | flops 12889096192 | bytes 50331904 | tf_op jit(solution)/shard_map/skab,skbn->skan/dot_general | solution.py:48
  401.5 3.3 fusion
  404.9 21.4 %convolution_bitcast_fusion = f32[8,8,256,256]{2,3,1,0:T(8,128)} fusion(f32[8,8,256,256]{2,3,1,0:T(8,128)} %fusion, f32[8,256,256,1]{2,1,0,3:T(8,128)S(1)} %copy-done.3), kind=kOutput, calls=%fused_computation.19 | convolution fusion | flops 12884901888 | bytes 35651584 | tf_op jit(solution)/shard_map/sam,skan->skmn/dot_general | solution.py:51
  426.2 20.8 %reshape.342 = f32[8,8,2,128,2,128]{3,2,5,4,1,0:T(2,128)} reshape(f32[8,8,256,256]{2,3,1,0:T(8,128)} %convolution_bitcast_fusion) | data formatting | bytes 33554432 | tf_op jit(solution)/shard_map/reshape | solution.py:53
  447.0 25.0 %copy.136 = f32[8,8,2,128,2,128]{5,3,4,2,1,0:T(8,128)} copy(f32[8,8,2,128,2,128]{3,2,5,4,1,0:T(2,128)} %reshape.342) | data formatting | bytes 33554432 | tf_op jit(solution)/shard_map/reshape | solution.py:53
  472.0 7.9 broadcast_in_dim.27
  479.9 52.2 %scatter_fusion = f32[257,128,128]{2,1,0:T(8,128)} fusion(f32[257,128,128]{2,1,0:T(8,128)} %broadcast_in_dim.27, s32[256]{0:T(256)S(1)} %bitcast.83, f32[256,128,128]{2,1,0:T(8,128)} %bitcast.77), kind=kCustom, calls=%fused_computation.16 | custom fusion | flops 4194304 | bytes 50332672 | tf_op jit(solution)/shard_map/scatter-add | solution.py:70
  532.0 11.6 %slice.99 = f32[256,128,128]{2,1,0:T(8,128)} slice(f32[257,128,128]{2,1,0:T(8,128)} %scatter_fusion), slice={[0:256], [0:128], [0:128]} | slice | bytes 33554432 | tf_op jit(solution)/shard_map/slice | solution.py:70
  543.7 49.6 %all-to-all-start.1 = ((f32[128,2,128,128]{3,2,1,0:T(8,128)}), f32[128,2,128,128]{3,2,1,0:T(8,128)}, u32[]{:S(2)}, u32[]{:S(2)}) async-start(f32[128,2,128,128]{3,2,1,0:T(8,128)} %bitcast.76), calls=%async_computation.1 | async-start | bytes 33554432 | tf_op jit(solution)/shard_map/all_to_all | solution.py:77
  594.6 238.1 %all-to-all-done.1 = f32[128,2,128,128]{3,2,1,0:T(8,128)} async-done(((f32[128,2,128,128]{3,2,1,0:T(8,128)}), f32[128,2,128,128]{3,2,1,0:T(8,128)}, u32[]{:S(2)}, u32[]{:S(2)}) %all-to-all-start.1) | async-done | bytes 16777248 | tf_op jit(solution)/shard_map/all_to_all | solution.py:77
  832.7 4.3 broadcast_in_dim.20
  837.0 51.7 %scatter_fusion.1 = f32[129,128,128]{2,1,0:T(8,128)} fusion(f32[129,128,128]{2,1,0:T(8,128)} %broadcast_in_dim.20, s32[256]{0:T(256)S(1)} %bitcast.84, f32[256,128,128]{2,1,0:T(8,128)} %bitcast.26), kind=kCustom, calls=%fused_computation.17 | custom fusion | flops 4194304 | bytes 50332672 | tf_op jit(solution)/shard_map/scatter-add | solution.py:94
  888.7 4.0 slice.100
  892.7 9.9 copy.137
  902.6 11.7 %fusion.20 = f32[2048,256]{1,0:T(8,128)} fusion(f32[1024,256]{1,0:T(8,128)} %all-gather.3.cloned.1.call-done, f32[256,8,8,128]{3,2,1,0:T(8,128)} %bitcast.72), kind=kOutput, calls=%fused_computation.105 | convolution fusion | flops 6442450944 | bytes 11534336 | tf_op jit(solution)/shard_map/dot_general | solution.py:109
  914.4 5.5 copy.145
  921.2 71.8 %reduce-scatter.3.cloned.1.call-done = f32[128,256]{1,0:T(8,128)} async-done(((f32[2048,256]{1,0:T(8,128)}), f32[128,256]{1,0:T(8,128)}) %reduce-scatter.3.cloned.1.call-update) | async-done | bytes 131088 | tf_op jit(solution)/shard_map/reduce_scatter | solution.py:108
  994.8 23.5 %all-gather.5.cloned.1.call-done = f32[1024,256]{1,0:T(8,128)} async-done(((f32[128,256]{1,0:T(8,128)}), f32[1024,256]{1,0:T(8,128)}) %all-gather.5.cloned.1.call-update) | async-done | bytes 1048592 | tf_op jit(solution)/shard_map/all_gather | solution.py:107
  1018.2 11.5 %fusion.19 = f32[2048,256]{1,0:T(8,128)} fusion(f32[1024,256]{1,0:T(8,128)} %all-gather.5.cloned.1.call-done, f32[256,8,8,128]{3,2,1,0:T(8,128)} %bitcast.74), kind=kOutput, calls=%fused_computation.104 | convolution fusion | flops 6442450944 | bytes 11534336 | tf_op jit(solution)/shard_map/dot_general | solution.py:109
  1029.7 75.1 %reduce-scatter.5.cloned.1.call-done = f32[128,256]{1,0:T(8,128)} async-done(((f32[2048,256]{1,0:T(8,128)}), f32[128,256]{1,0:T(8,128)}) %reduce-scatter.5.cloned.1.call-update) | async-done | bytes 131088 | tf_op jit(solution)/shard_map/reduce_scatter | solution.py:108
  (130 shorter events, 36.8 us)
Async XLA Ops:
  7.2 25.8 %copy-start = (f32[16,256]{1,0:T(8,128)S(1)}, f32[16,256]{1,0:T(8,128)}, u32[]{:S(2)}) copy-start(f32[16,256]{1,0:T(8,128)} %param.17) | copy-start | bytes 49156
  9.8 59.1 %collective-permute-start.1 = (f32[8,2]{1,0:T(8,128)S(1)}, f32[8,2]{1,0:T(8,128)S(1)}, u32[]{:S(2)}, u32[]{:S(2)}) collective-permute-start(f32[8,2]{1,0:T(8,128)S(1)} %convert_element_type.65), channel_id=1, source_target_pairs={{0,2},{1,3},{2,4},{3,5},{4,6},{5,7},{6,8},{7,9},{8,10},{9,11},{10,... | collective-permute-start | bytes 200 | tf_op jit(solution)/shard_map/ppermute | solution.py:19
  13.7 56.4 %collective-permute-start = (f32[8,2]{1,0:T(8,128)S(1)}, f32[8,2]{1,0:T(8,128)S(1)}, u32[]{:S(2)}, u32[]{:S(2)}) collective-permute-start(f32[8,2]{1,0:T(8,128)S(1)} %convert_element_type.63), channel_id=1, source_target_pairs={{0,1},{1,2},{2,3},{3,4},{4,5},{5,6},{6,7},{7,8},{8,9},{9,10},{10,1... | collective-permute-start | bytes 200 | tf_op jit(solution)/shard_map/ppermute | solution.py:19
  15.0 57.9 %collective-permute-start.2 = (f32[8,2]{1,0:T(8,128)S(1)}, f32[8,2]{1,0:T(8,128)S(1)}, u32[]{:S(2)}, u32[]{:S(2)}) collective-permute-start(f32[8,2]{1,0:T(8,128)S(1)} %convert_element_type.67), channel_id=1, source_target_pairs={{0,3},{1,4},{2,5},{3,6},{4,7},{5,8},{6,9},{7,10},{8,11},{9,12},{10... | collective-permute-start | bytes 200 | tf_op jit(solution)/shard_map/ppermute | solution.py:19
  26.4 141.9 %collective-permute-start.8 = (f32[8,256,256]{1,2,0:T(8,128)}, f32[8,256,256]{1,2,0:T(8,128)}, u32[]{:S(2)}, u32[]{:S(2)}) collective-permute-start(f32[8,256,256]{1,2,0:T(8,128)} %copy.130), channel_id=1, source_target_pairs={{0,2},{1,3},{2,4},{3,5},{4,6},{5,7},{6,8},{7,9},{8,10},{9,11},{10,... | collective-permute-start | bytes 6291464 | tf_op jit(solution)/shard_map/ppermute | solution.py:19
  28.5 4.5 copy-start.10
  28.5 4.5 copy-start.9
  28.5 4.5 copy-start.11
  31.4 184.9 %collective-permute-start.7 = (f32[8,256,256]{1,2,0:T(8,128)}, f32[8,256,256]{1,2,0:T(8,128)}, u32[]{:S(2)}, u32[]{:S(2)}) collective-permute-start(f32[8,256,256]{1,2,0:T(8,128)} %copy.129), channel_id=1, source_target_pairs={{0,1},{1,2},{2,3},{3,4},{4,5},{5,6},{6,7},{7,8},{8,9},{9,10},{10,1... | collective-permute-start | bytes 6291464 | tf_op jit(solution)/shard_map/ppermute | solution.py:19
  50.5 4.1 copy-start.4
  56.4 3.1 copy-start.5
  61.4 3.0 copy-start.2
  68.8 6.4 collective-permute-start.3
  70.1 52.7 %collective-permute-start.4 = (f32[8,2]{1,0:T(8,128)S(1)}, f32[8,2]{1,0:T(8,128)S(1)}, u32[]{:S(2)}, u32[]{:S(2)}) collective-permute-start(f32[8,2]{1,0:T(8,128)S(1)} %convert_element_type.71), channel_id=1, source_target_pairs={{0,5},{1,6},{2,7},{3,8},{4,9},{5,10},{6,11},{7,12},{8,13},{9,14},{... | collective-permute-start | bytes 200 | tf_op jit(solution)/shard_map/ppermute | solution.py:19
  72.9 50.3 %collective-permute-start.5 = (f32[8,2]{1,0:T(8,128)S(1)}, f32[8,2]{1,0:T(8,128)S(1)}, u32[]{:S(2)}, u32[]{:S(2)}) collective-permute-start(f32[8,2]{1,0:T(8,128)S(1)} %convert_element_type.73), channel_id=1, source_target_pairs={{0,6},{1,7},{2,8},{3,9},{4,10},{5,11},{6,12},{7,13},{8,14},{9,15},... | collective-permute-start | bytes 200 | tf_op jit(solution)/shard_map/ppermute | solution.py:19
  75.2 164.0 %collective-permute-start.9 = (f32[8,256,256]{1,2,0:T(8,128)}, f32[8,256,256]{1,2,0:T(8,128)}, u32[]{:S(2)}, u32[]{:S(2)}) collective-permute-start(f32[8,256,256]{1,2,0:T(8,128)} %copy.131), channel_id=1, source_target_pairs={{0,3},{1,4},{2,5},{3,6},{4,7},{5,8},{6,9},{7,10},{8,11},{9,12},{10... | collective-permute-start | bytes 6291464 | tf_op jit(solution)/shard_map/ppermute | solution.py:19
  122.8 119.4 %collective-permute-start.10 = (f32[8,256,256]{1,2,0:T(8,128)}, f32[8,256,256]{1,2,0:T(8,128)}, u32[]{:S(2)}, u32[]{:S(2)}) collective-permute-start(f32[8,256,256]{1,2,0:T(8,128)} %copy.132), channel_id=1, source_target_pairs={{0,4},{1,5},{2,6},{3,7},{4,8},{5,9},{6,10},{7,11},{8,12},{9,13},{1... | collective-permute-start | bytes 6291464 | tf_op jit(solution)/shard_map/ppermute | solution.py:19
  123.2 44.8 %collective-permute-start.6 = (f32[8,2]{1,0:T(8,128)S(1)}, f32[8,2]{1,0:T(8,128)S(1)}, u32[]{:S(2)}, u32[]{:S(2)}) collective-permute-start(f32[8,2]{1,0:T(8,128)S(1)} %convert_element_type.75), channel_id=1, source_target_pairs={{0,7},{1,8},{2,9},{3,10},{4,11},{5,12},{6,13},{7,14},{8,15},{9,0},... | collective-permute-start | bytes 200 | tf_op jit(solution)/shard_map/ppermute | solution.py:19
  167.9 93.1 %collective-permute-start.11 = (f32[8,256,256]{1,2,0:T(8,128)}, f32[8,256,256]{1,2,0:T(8,128)}, u32[]{:S(2)}, u32[]{:S(2)}) collective-permute-start(f32[8,256,256]{1,2,0:T(8,128)} %copy.133), channel_id=1, source_target_pairs={{0,5},{1,6},{2,7},{3,8},{4,9},{5,10},{6,11},{7,12},{8,13},{9,14},{... | collective-permute-start | bytes 6291464 | tf_op jit(solution)/shard_map/ppermute | solution.py:19
  168.4 184.0 %collective-permute-start.12 = (f32[8,256,256]{1,2,0:T(8,128)}, f32[8,256,256]{1,2,0:T(8,128)}, u32[]{:S(2)}, u32[]{:S(2)}) collective-permute-start(f32[8,256,256]{1,2,0:T(8,128)} %copy.134), channel_id=1, source_target_pairs={{0,6},{1,7},{2,8},{3,9},{4,10},{5,11},{6,12},{7,13},{8,14},{9,15},... | collective-permute-start | bytes 6291464 | tf_op jit(solution)/shard_map/ppermute | solution.py:19
  216.3 139.0 %collective-permute-start.13 = (f32[8,256,256]{1,2,0:T(8,128)}, f32[8,256,256]{1,2,0:T(8,128)}, u32[]{:S(2)}, u32[]{:S(2)}) collective-permute-start(f32[8,256,256]{1,2,0:T(8,128)} %copy.135), channel_id=1, source_target_pairs={{0,7},{1,8},{2,9},{3,10},{4,11},{5,12},{6,13},{7,14},{8,15},{9,0},... | collective-permute-start | bytes 6291464 | tf_op jit(solution)/shard_map/ppermute | solution.py:19
  225.6 318.1 %all-to-all-start = ((f32[128,1,2]{2,1,0:T(1,128)}), f32[128,1,2]{2,1,0:T(1,128)S(1)}, u32[]{:S(2)}, u32[]{:S(2)}) async-start(f32[128,1,2]{2,1,0:T(1,128)} %bitcast.10), calls=%async_computation | async-start | bytes 131072 | tf_op jit(solution)/shard_map/all_to_all | solution.py:84
  401.5 3.3 copy-start.3
  543.7 289.0 %all-to-all-start.1 = ((f32[128,2,128,128]{3,2,1,0:T(8,128)}), f32[128,2,128,128]{3,2,1,0:T(8,128)}, u32[]{:S(2)}, u32[]{:S(2)}) async-start(f32[128,2,128,128]{3,2,1,0:T(8,128)} %bitcast.76), calls=%async_computation.1 | async-start | bytes 33554432 | tf_op jit(solution)/shard_map/all_to_all | solution.py:77
  593.3 309.4 %all-gather.3.cloned.1.call-start = ((), (), s32[]{:S(2)}) async-start(), calls=%async_computation.4 | async-start | bytes 1179648 | tf_op jit(solution)/shard_map/all_gather | solution.py:107
  594.0 399.0 %reduce-scatter.3.cloned.1.call-start = ((), (), s32[]{:S(2)}) async-start(), calls=%async_computation.5 | async-start | bytes 2228224 | tf_op jit(solution)/shard_map/reduce_scatter | solution.py:108
  914.3 103.9 %all-gather.5.cloned.1.call-start = ((), (), s32[]{:S(2)}) async-start(), calls=%async_computation.6 | async-start | bytes 1179648 | tf_op jit(solution)/shard_map/all_gather | solution.py:107
  914.4 78.6 %copy-start.7 = (f32[128,256]{1,0:T(8,128)S(1)}, f32[128,256]{1,0:T(8,128)}, u32[]{:S(2)}) copy-start(f32[128,256]{1,0:T(8,128)} %param.18) | copy-start | bytes 393220
  914.4 78.6 %copy-start.8 = (f32[128,256]{1,0:T(8,128)S(1)}, f32[128,256]{1,0:T(8,128)}, u32[]{:S(2)}) copy-start(f32[128,256]{1,0:T(8,128)} %param.19) | copy-start | bytes 393220
  994.7 110.1 %reduce-scatter.5.cloned.1.call-start = ((), (), s32[]{:S(2)}) async-start(), calls=%async_computation.7 | async-start | bytes 2228224 | tf_op jit(solution)/shard_map/reduce_scatter | solution.py:108
  1018.2 88.3 %copy-start.1 = (f32[16,256]{1,0:T(8,128)S(1)}, f32[16,256]{1,0:T(8,128)}, u32[]{:S(2)}) copy-start(f32[16,256]{1,0:T(8,128)} %param.17) | copy-start | bytes 49156
  1029.7 75.2 %copy-start.6 = (f32[128,256]{1,0:T(8,128)S(1)}, f32[128,256]{1,0:T(8,128)}, u32[]{:S(2)}) copy-start(f32[128,256]{1,0:T(8,128)} %divide_add_fusion.1) | copy-start | bytes 393220
Sparse Core Ops, SparseCore 0:
  595.8 93.5 all-gather.2
  914.5 78.5 reduce-scatter.2
  995.3 22.8 all-gather.4
  1029.8 74.9 reduce-scatter.4
where the time goes:
time: 1120 us; the launch traced here: 1110 us
  waiting for transfers between devices  557 us (50%)
  starting transfers between devices  175 us (16%)
  local copies, waits for them, and re-layouts  164 us (15%)
  other arithmetic  115 us (10%)
  matrix products  87.9 us (8%)
  between operations  14.5 us (1%)
    all_to_all x1, waiting for transfers between devices, on_device(): lax.all_to_all(sent_blocks.reshape(dev_count, slot_cap, CB, CB), ('row',...  238 us
    ppermute x14, waiting for transfers between devices, from_behind(): return lax.ppermute(value, axis, pairs)  148 us
    reduce_scatter x2, waiting for transfers between devices, on_device(): lax.psum_scatter(jnp.dot(matrix, gathered, precision=highest), 'col', sca...  147 us
    ppermute x14, starting transfers between devices, from_behind(): return lax.ppermute(value, axis, pairs)  117 us
    scatter-add x1, other arithmetic, on_device(): jax.ops.segment_sum(partial_value, slot, num_segments=dev_count * slot_ca...  52.2 us
    scatter-add x1, other arithmetic, on_device(): jax.ops.segment_sum(got_blocks.reshape(-1, CB, CB), places, num_segments=...  51.7 us
    all_to_all x1, starting transfers between devices, on_device(): lax.all_to_all(sent_blocks.reshape(dev_count, slot_cap, CB, CB), ('row',...  49.6 us
    reshape x2, local copies, waits for them, and re-layouts, on_device(): partial_value.reshape(local_rows, KA, KP, CB, KP, CB)  45.7 us
  transfers between devices with their start and end apart: 20, of which 7 were waited for; matrix products, arithmetic and copies ran while one was open for 30% of the time, Pallas kernels for 0%

commit v1 on v0

v1 whole, which is shorter than its diff:
```python
import functools

import jax
import jax.numpy as jnp
from jax import lax
from jax.experimental import pallas as pl
from jax.experimental.pallas import tpu as pltpu
from jax.sharding import PartitionSpec as P

BS = 256
CB = 128
KA = 8
KP = 2
N_ROW = 8
N_COL = 16
DEV = N_ROW * N_COL
NB = 8
NCOL = 256
damping = 0.7
f32 = jnp.float32
bf16 = jnp.bfloat16
ALL = ("row", "col")


def split(value):
    high = value.astype(bf16)
    return high, (value - high.astype(f32)).astype(bf16)


def dot3(lhs, rhs):
    dot = functools.partial(jnp.dot, preferred_element_type=f32)
    return dot(lhs[0], rhs[0]) + (dot(lhs[0], rhs[1]) + dot(lhs[1], rhs[0]))


def transpose_kernel(p_ref, high_ref, low_ref):
    for m in range(KP):
        high, low = split(p_ref[0, pl.ds(m, BS, KP), :].T)
        high_ref[0, m] = high
        low_ref[0, m] = low


def transposed(own_p):
    shape = jax.ShapeDtypeStruct((NB, KP, CB, BS), bf16)
    spec = pl.BlockSpec((1, KP, CB, BS), lambda s: (s, 0, 0, 0))
    return pl.pallas_call(
        transpose_kernel,
        grid=(NB,),
        in_specs=[pl.BlockSpec((1, KP * BS, CB), lambda s: (s, 0, 0))],
        out_specs=[spec, spec],
        out_shape=[shape, shape],
    )(own_p)


ROW_AT, SLOT_AT, POLICY_AT = 0, 16, 32
COL_AT, HALF_AT, PICK_AT, LIVE_AT = 40, 48, 56, 120


def product_kernel(first, with_prior, table, a_ref, p_ref, high_ref, low_ref, rate_ref, *rest):
    out_ref, q_high, q_low = rest[-3:]
    k = first + pl.program_id(0)
    s = pl.program_id(1)
    m = pl.program_id(2)

    @pl.when(m == 0)
    def _():
        block = a_ref[0, 0] * table[LIVE_AT + k * NB + s].astype(f32)
        if first == 0:
            across = lax.broadcasted_iota(jnp.int32, (BS, BS), 0)
            along = lax.broadcasted_iota(jnp.int32, (BS, BS), 1)
            rate = jnp.where((across == along) & (k == 0), rate_ref[0], 0.0)
            block = block + rate
        ghost = jnp.concatenate(
            [p_ref[0, pl.ds(0, BS, KP), :], p_ref[0, pl.ds(1, BS, KP), :]], axis=1
        )
        high, low = split(dot3(split(block), split(ghost)))
        q_high[...] = high
        q_low[...] = low

    result = dot3((high_ref[0, 0], low_ref[0, 0]), (q_high[...], q_low[...]))
    flip = table[HALF_AT + k] == 1
    left, right = result[:, :CB], result[:, CB:]
    out_ref[0, 0, 0, 0] = jnp.where(flip, right, left)
    out_ref[0, 1, 0, 0] = jnp.where(flip, left, right)


def products(first, count, table, a_blocks, source, high, low, rates, prior):
    in_specs = [
        pl.BlockSpec((1, 1, BS, BS), lambda k, s, m, t: (s, first + k, 0, 0)),
        pl.BlockSpec((1, KP * BS, CB), lambda k, s, m, t: (t[PICK_AT + (first + k) * NB + s], 0, 0)),
        pl.BlockSpec((1, 1, CB, BS), lambda k, s, m, t: (s, m, 0, 0)),
        pl.BlockSpec((1, 1, CB, BS), lambda k, s, m, t: (s, m, 0, 0)),
        pl.BlockSpec((1, 1, BS), lambda k, s, m, t: (t[POLICY_AT + s], 0, 0)),
    ]
    args = [a_blocks, source, high, low, rates]
    alias = {}
    if prior is not None:
        in_specs.append(pl.BlockSpec(memory_space=pl.ANY))
        args.append(prior)
        alias = {6: 0}
    return pl.pallas_call(
        functools.partial(product_kernel, first, prior is not None),
        grid_spec=pltpu.PrefetchScalarGridSpec(
            num_scalar_prefetch=1,
            grid=(count, NB, KP),
            in_specs=in_specs,
            out_specs=pl.BlockSpec(
                (1, 2, 1, 1, CB, CB),
                lambda k, s, m, t: (
                    t[ROW_AT + s * KP + m],
                    0,
                    t[COL_AT + first + k],
                    t[SLOT_AT + s * KP + m],
                    0,
                    0,
                ),
            ),
            scratch_shapes=[pltpu.VMEM((BS, BS), bf16), pltpu.VMEM((BS, BS), bf16)],
        ),
        out_shape=jax.ShapeDtypeStruct((N_ROW, 2, N_COL // 2, 2, CB, CB), f32),
        input_output_aliases=alias,
        cost_estimate=pl.CostEstimate(
            flops=count * NB * 2 * 3 * 2 * BS**3,
            bytes_accessed=count * NB * 4 * 3 * BS * BS,
            transcendentals=0,
        ),
    )(table, *args)


STEPS = 16
PER_STEP = 2 * DEV // STEPS


def gather_kernel(table, got_ref, x_ref, coarse_ref, part_ref, floor_ref, total):
    step = pl.program_id(0)

    @pl.when(step == 0)
    def _():
        total[...] = jnp.zeros_like(total)

    for b in range(PER_STEP):
        place = table[step * PER_STEP + b]
        total[place] += got_ref[b]

    @pl.when(step == STEPS - 1)
    def _():
        right = split(x_ref[...])

        @pl.loop(0, N_COL)
        def _(u):
            for q in range(N_ROW):
                coarse_ref[pl.ds(u * (CB * N_ROW) + q, CB, N_ROW), :] = total[u * N_ROW + q]
            row = jnp.concatenate([total[u * N_ROW + q] for q in range(N_ROW)], axis=1)
            part_ref[pl.ds(pl.multiple_of(u * CB, CB), CB), :] = dot3(split(row), right)

        across = lax.broadcasted_iota(jnp.int32, (CB, CB), 0)
        along = lax.broadcasted_iota(jnp.int32, (CB, CB), 1)
        own = jnp.where(across == along, total[table[2 * DEV]], 0.0)
        diag = jnp.maximum(jnp.abs(jnp.sum(own, axis=1, keepdims=True)), 1.0)
        floor_ref[...] = jnp.broadcast_to(diag, (CB, NCOL))


def gather(table, got, x):
    whole = lambda shape: pl.BlockSpec(shape, lambda i, t: (0,) * len(shape))
    return pl.pallas_call(
        gather_kernel,
        grid_spec=pltpu.PrefetchScalarGridSpec(
            num_scalar_prefetch=1,
            grid=(STEPS,),
            in_specs=[
                pl.BlockSpec((PER_STEP, CB, CB), lambda i, t: (i, 0, 0)),
                whole((N_ROW * CB, NCOL)),
            ],
            out_specs=[
                whole((N_COL * CB * N_ROW, CB)),
                whole((N_COL * CB, NCOL)),
                whole((CB, NCOL)),
            ],
            scratch_shapes=[pltpu.VMEM((DEV, CB, CB), f32)],
        ),
        out_shape=[
            jax.ShapeDtypeStruct((N_COL * CB * N_ROW, CB), f32),
            jax.ShapeDtypeStruct((N_COL * CB, NCOL), f32),
            jax.ShapeDtypeStruct((CB, NCOL), f32),
        ],
    )(table, got, x)


def apply_kernel(c_ref, x_ref, out_ref, x_high, x_low):
    @pl.when(pl.program_id(0) == 0)
    def _():
        high, low = split(x_ref[...])
        x_high[...] = high
        x_low[...] = low

    row = jnp.concatenate([c_ref[pl.ds(q, CB, N_ROW), :] for q in range(N_ROW)], axis=1)
    out_ref[...] = dot3(split(row), (x_high[...], x_low[...]))


def apply(coarse, x):
    return pl.pallas_call(
        apply_kernel,
        grid=(N_COL,),
        in_specs=[
            pl.BlockSpec((CB * N_ROW, CB), lambda u: (u, 0)),
            pl.BlockSpec((N_ROW * CB, NCOL), lambda u: (0, 0)),
        ],
        out_specs=pl.BlockSpec((CB, NCOL), lambda u: (u, 0)),
        out_shape=jax.ShapeDtypeStruct((N_COL * CB, NCOL), f32),
        scratch_shapes=[pltpu.VMEM((N_ROW * CB, NCOL), bf16)] * 2,
    )(coarse, x)


def to_all(value, axes, count):
    copies = jnp.broadcast_to(value[None], (count,) + value.shape)
    return lax.all_to_all(copies, axes, split_axis=0, concat_axis=0, tiled=True)


def own_table(p_cols, a_live, policy, metas, row, col):
    entry_row = (p_cols // N_COL).reshape(-1)
    order = jnp.arange(NB * KP, dtype=jnp.int32)
    slot = jnp.sum(
        (entry_row[None, :] == entry_row[:, None]) & (order[None, :] < order[:, None]),
        axis=1,
        dtype=jnp.int32,
    )
    k = jnp.arange(KA, dtype=jnp.int32)
    target = (col - k) % N_COL
    return entry_row, slot, target


def places(metas, row, col):
    delta = jnp.arange(N_COL, dtype=jnp.int32)
    p_cols = metas[:, :, :, :KP]
    entries = p_cols.reshape(N_ROW, N_COL, NB * KP)
    match = (entries // N_COL == row).astype(jnp.int32)
    earlier = jnp.cumsum(match, axis=2) - match
    order = jnp.arange(NB * KP, dtype=jnp.int32)
    sources = [
        lax.dynamic_index_in_dim(metas, (col + h * KA) % N_COL, 1, False) for h in range(2)
    ]
    result = []
    for t in range(2):
        chosen = match * (earlier == t)
        entry = jnp.sum(chosen * order, axis=2)
        u = jnp.sum(chosen * (entries % N_COL), axis=2)
        block = entry // KP
        far = (delta - col) % N_COL
        k, half = far % KA, far // KA
        quotient = jnp.zeros_like(u)
        for h in range(2):
            cells = sources[h]
            identity = jnp.broadcast_to(jnp.arange(NB, dtype=jnp.int32)[None, :, None], (N_ROW, NB, 1))
            picks = jnp.concatenate([identity, cells[:, :, KP:]], axis=2)
            hit = (block[:, :, None, None] == jnp.arange(NB)[None, None, :, None]) & (
                k[None, :, None, None] == jnp.arange(KA)[None, None, None, :]
            )
            pick = jnp.sum(jnp.where(hit, picks[:, None], 0), axis=(2, 3))
            value = jnp.sum(
                jnp.where(pick[:, :, None] == jnp.arange(NB), cells[:, None, :, h] // N_COL, 0), axis=2
            )
            quotient = jnp.where(half[None, :] == h, value, quotient)
        result.append(u * N_ROW + quotient)
    return jnp.stack(result, axis=2).reshape(-1)


def on_device(a_blocks, a_live, p_blocks, p_cols, ghost_list, policy, rates, rhs, guess):
    row = lax.axis_index("row")
    col = lax.axis_index("col")
    own_p = p_blocks.reshape(NB, BS * KP, CB)
    meta = jnp.concatenate([p_cols, ghost_list], axis=1)
    metas = to_all(meta.reshape(-1), ALL, DEV).reshape(N_ROW, N_COL, NB, KP + KA - 1)
    all_p = lax.all_gather(own_p, "col", axis=0, tiled=True)
    x = to_all(guess, "row", N_ROW).reshape(N_ROW * CB, NCOL)
    high, low = transposed(own_p)

    entry_row, slot, target = own_table(p_cols, a_live, policy, metas, row, col)
    mine = lax.dynamic_index_in_dim(metas, row, 0, False)
    picks = [jnp.arange(NB, dtype=jnp.int32) + col * NB]
    for k in range(1, KA):
        source = (col - k) % N_COL
        picks.append(lax.dynamic_index_in_dim(mine, source, 0, False)[:, KP + k - 1] + source * NB)
    table = jnp.concatenate(
        [entry_row, slot, policy, target % KA, target // KA, jnp.concatenate(picks), a_live.T.reshape(-1)]
    )
    sent = products(0, KA, table, a_blocks, all_p, high, low, rates.reshape(16, 1, BS), None)
    got = lax.all_to_all(
        sent.reshape(DEV, 2, CB, CB), ALL, split_axis=0, concat_axis=0, tiled=True
    ).reshape(2 * DEV, CB, CB)
    where = jnp.concatenate([places(metas, row, col), (col * N_ROW + row).reshape(1)])
    coarse, part, floor_diag = gather(where, got, x)
    current = guess
    for sweep in range(2):
        if sweep:
            part = apply(coarse, to_all(current, "row", N_ROW).reshape(N_ROW * CB, NCOL))
        pieces = lax.all_to_all(
            part.reshape(N_COL, CB, NCOL), "col", split_axis=0, concat_axis=0, tiled=True
        )
        applied = jnp.sum(pieces, axis=0)
        current = current + damping * (rhs - applied) / floor_diag
    return coarse.reshape(N_COL * CB, N_ROW, 1, CB), current


def solution(mesh):
    return jax.shard_map(
        on_device,
        mesh=mesh,
        in_specs=(
            P(ALL, None, None, None),
            P(ALL, None),
            P(ALL, None, None, None),
            P(ALL, None),
            P(ALL, None),
            P(ALL),
            P(),
            P(ALL, None),
            P(ALL, None),
        ),
        out_specs=(P("row", None, "col", None), P(ALL, None)),
        check_vma=False,
    )
```

time: 1120 us -> 707 us (0.63)
  waiting for transfers between devices: 557 us -> 391 us
  Pallas kernels: 0 us -> 155 us
  starting transfers between devices: 175 us -> 24.5 us
  local copies, waits for them, and re-layouts: 164 us -> 19.9 us
  other arithmetic: 115 us -> 7.12 us
  blocking collectives: 0 us -> 92.4 us
  matrix products: 87.9 us -> 0 us
    pallas_call x0 -> x4, Pallas kernels: none -> 155 us  [the longest x1 108 us: products(): pl.pallas_call(functools.partial(product_kernel, first, prior is not None...]
    ppermute x14 -> x0, waiting for transfers between devices: 148 us -> none  [from_behind(): return lax.ppermute(value, axis, pairs)]
    reduce_scatter x2 -> x0, waiting for transfers between devices: 147 us -> none  [on_device(): lax.psum_scatter(jnp.dot(matrix, gathered, precision=highest), 'col', sca...]
    all_gather x2 -> x1, waiting for transfers between devices: 23.5 us -> 161 us  [on_device(): all_p = lax.all_gather(own_p, 'col', axis=0, tiled=True)]
    ppermute x14 -> x0, starting transfers between devices: 117 us -> none  [from_behind(): return lax.ppermute(value, axis, pairs)]
    scatter-add x4 -> x0, other arithmetic: 110 us -> none  [the longest x1 52.2 us: on_device(): jax.ops.segment_sum(partial_value, slot, num_segments=dev_count * slot_ca...]
    all_to_all x0 -> x3, blocking collectives: none -> 92.4 us  [the longest x2 68.5 us: on_device(): lax.all_to_all(part.reshape(N_COL, CB, NCOL), 'col', split_axis=0, concat...]
    dot_general x5 -> x0, matrix products: 87.9 us -> none  [the longest x1 43.2 us: on_device(): jnp.einsum('skab,skbn->skan', a_blocks, ghost_p, precision=highest)]
  transfers between devices with their start and end apart: 20 -> 4, of which waited for: 7 -> 2; matrix products, arithmetic and copies ran while one was open for 30% -> 3% of each run, Pallas kernels for 0% -> 16%
where the time goes in v1:
time: 707 us; the launch traced here: 704 us
  waiting for transfers between devices  391 us (55%)
  Pallas kernels  155 us (22%)
  blocking collectives  92.4 us (13%)
  starting transfers between devices  24.5 us (3%)
  local copies, waits for them, and re-layouts  19.9 us (3%)
  between operations  14.5 us (2%)
  other arithmetic  7.12 us (1%)
    all_to_all x1, waiting for transfers between devices, on_device(): lax.all_to_all(sent.reshape(DEV, 2, CB, CB), ALL, split_axis=0, concat_ax...  229 us
    all_gather x1, waiting for transfers between devices, on_device(): all_p = lax.all_gather(own_p, 'col', axis=0, tiled=True)  161 us
    pallas_call x1, Pallas kernels, products(): pl.pallas_call(functools.partial(product_kernel, first, prior is not None...  108 us
    all_to_all x2, blocking collectives, on_device(): lax.all_to_all(part.reshape(N_COL, CB, NCOL), 'col', split_axis=0, concat...  68.5 us
    pallas_call x1, Pallas kernels, gather(): pl.pallas_call(gather_kernel, grid_spec=pltpu.PrefetchScalarGridSpec(num_...  26.1 us
    all_to_all x1, blocking collectives, to_all(): return lax.all_to_all(copies, axes, split_axis=0, concat_axis=0, tiled=True)  23.9 us
    all_to_all x2, starting transfers between devices, to_all(): return lax.all_to_all(copies, axes, split_axis=0, concat_axis=0, tiled=True)  15.3 us
  transfers between devices with their start and end apart: 4, of which 2 were waited for; matrix products, arithmetic and copies ran while one was open for 3% of the time, Pallas kernels for 16%

profile of v1, /device:TPU:0, one launch (start us, length us, event | category | flops | bytes accessed | tf_op | source)
XLA Modules:
  0.0 703.8 jit_solution(6760596196158384681)
XLA Ops:
  7.2 0.7 all-gather.2.cloned.1.call-update
  7.9 0.8 copy.56
  8.7 0.8 pad_add_fusion.3
  9.5 0.7 broadcast_in_dim.84
  10.2 11.2 %all-to-all-start = ((s32[128,1,72]{2,1,0:T(1,128)}), s32[128,1,72]{2,1,0:T(1,128)S(1)}, u32[]{:S(2)}, u32[]{:S(2)}) async-start(s32[128,1,72]{2,1,0:T(1,128)} %broadcast_in_dim.84), calls=%async_computation | async-start | bytes 131072 | tf_op jit(solution)/shard_map/all_to_all | solution.py:215
  21.4 0.7 and_select_fusion.7
  22.2 0.2 convert_reduce_fusion
  22.6 6.2 shard_map.104
  28.8 0.8 copy.64
  29.6 1.3 reshape.490.rate_ref
  31.0 2.0 broadcast_in_dim.158
  33.0 4.2 all-to-all-start.2
  37.2 0.1 reshape.483
  37.3 9.9 %dynamic-slice_reduce_fusion = (s32[8,9]{1,0:T(8,128)S(1)}, s32[8,9]{1,0:T(8,128)S(1)}, s32[8,9]{1,0:T(8,128)S(1)}, s32[8,9]{1,0:T(8,128)S(1)}, s32[8,9]{1,0:T(8...) fusion(s32[8,16,8,9]{1,0,3,2:T(8,128)S(1)} %reshape.483, s32[]{:T(128)S(6)} %select_n.305, s32[]{:T(128)S(6)} %select_n.326, ...), kind=kLoop, calls=%fused_computation.43 | loop fusion | bytes 4064 | tf_op jit(solution)/shard_map/jit(dynamic_index_in_dim)/dynamic_slice | solution.py:281
  47.2 0.2 add_reduce_fusion.6
  47.4 0.2 add_reduce_fusion.4
  47.6 0.2 add_reduce_fusion.2
  47.8 0.2 add_reduce_fusion
  48.0 0.7 concatenate.21.table
  48.7 160.8 %all-gather.2.cloned.1.call-done.p_ref = f32[128,512,128]{2,1,0:T(8,128)} async-done(((f32[8,512,128]{2,1,0:T(8,128)}), f32[128,512,128]{2,1,0:T(8,128)}) %all-gather.2.cloned.1.call-update) | async-done | bytes 33554448 | tf_op jit(solution)/shard_map/all_gather | solution.py:272
  209.5 108.4 %shard_map.105 = f32[8,2,8,2,128,128]{5,4,3,2,1,0:T(8,128)} custom-call(s32[184]{0:T(256)} %concatenate.21.table, f32[8,8,256,256]{3,2,1,0:T(8,128)} %a_ref.1, f32[128,512,128]{2,1,0:T(8,128)} %all-gather.2.cloned.1.call-done.p_ref, bf16[8,2,128,256]{3,2,1,0:T(8,128)(2,1)} %get-tuple-element.7.high_ref, bf16[8,2,128,256]{3,2,1,0:T(8,128)(2,1)} %get-tuple-element.8.low_ref, ...), custom_call_target="tpu_custom_call" | custom-call | flops 12884901888 | bytes 50331648 | tf_op jit(solution)/shard_map/pallas_call | solution.py:100
  317.9 1.0 copy-done
  318.8 9.1 %all-to-all-start.1 = ((f32[128,2,128,128]{3,2,1,0:T(8,128)}), f32[128,2,128,128]{3,2,1,0:T(8,128)}, u32[]{:S(2)}, u32[]{:S(2)}) async-start(f32[128,2,128,128]{3,2,1,0:T(8,128)} %bitcast.62), calls=%async_computation.1 | async-start | bytes 33554432 | tf_op jit(solution)/shard_map/all_to_all | solution.py:286
  328.1 0.2 constant_dynamic-slice_fusion.1
  328.3 0.5 copy.61
  328.8 0.5 copy.60
  329.5 0.1 copy.58
  329.6 1.4 reduce_window_sum.13
  330.9 0.1 copy.59
  331.0 0.2 slice_reduce_fusion
  331.2 0.3 slice_reduce_fusion.1
  331.6 0.1 fusion.10
  331.8 0.2 fusion.1
  332.1 0.1 select_reduce_fusion.2
  332.1 0.1 select_reduce_fusion.3
  332.3 0.1 copy.62
  332.4 0.1 reshape.485
  332.5 0.6 pad_add_fusion.4.table
  333.1 229.3 %all-to-all-done.1 = f32[128,2,128,128]{3,2,1,0:T(8,128)} async-done(((f32[128,2,128,128]{3,2,1,0:T(8,128)}), f32[128,2,128,128]{3,2,1,0:T(8,128)}, u32[]{:S(2)}, u32[]{:S(2)}) %all-to-all-start.1) | async-done | bytes 16777248 | tf_op jit(solution)/shard_map/all_to_all | solution.py:286
  562.4 26.1 %shard_map.106 = (f32[16384,128]{1,0:T(8,128)}, f32[2048,256]{1,0:T(8,128)}, f32[128,256]{1,0:T(8,128)}) custom-call(s32[257]{0:T(512)} %pad_add_fusion.4.table, f32[256,128,128]{2,1,0:T(8,128)} %bitcast.14.got_ref, f32[1024,256]{1,0:T(8,128)} %bitcast.67), custom_call_target="tpu_custom_call" | custom-call | tf_op jit(solution)/shard_map/pallas_call | solution.py:164
  588.5 36.6 %all_to_all.31 = f32[16,128,256]{2,1,0:T(8,128)S(1)} all-to-all(f32[16,128,256]{2,1,0:T(8,128)} %bitcast.69), channel_id=1, replica_groups=mesh['row'=8,'col'=16] {'col'}, dimensions={0} | all-to-all | bytes 4194304 | tf_op jit(solution)/shard_map/all_to_all | solution.py:295
  625.2 0.1 reduce_sum.160
  625.3 0.9 divide_add_fusion.1
  626.4 23.9 %all_to_all.32 = f32[8,128,256]{2,1,0:T(8,128)} all-to-all(f32[8,128,256]{2,1,0:T(8,128)S(1)} %broadcast_in_dim.159), channel_id=1, replica_groups=mesh['row'=8,'col'=16] {'row'}, dimensions={0} | all-to-all | bytes 2097152 | tf_op jit(solution)/shard_map/all_to_all | solution.py:215
  650.3 14.0 %shard_map.107 = f32[2048,256]{1,0:T(8,128)} custom-call(f32[16384,128]{1,0:T(8,128)} %get-tuple-element.9.c_ref, f32[1024,256]{1,0:T(8,128)} %bitcast.68), custom_call_target="tpu_custom_call" | custom-call | tf_op jit(solution)/shard_map/pallas_call | solution.py:200
  664.3 31.8 %all_to_all.33 = f32[16,128,256]{2,1,0:T(8,128)S(1)} all-to-all(f32[16,128,256]{2,1,0:T(8,128)} %bitcast.66), channel_id=1, replica_groups=mesh['row'=8,'col'=16] {'col'}, dimensions={0} | all-to-all | bytes 4194304 | tf_op jit(solution)/shard_map/all_to_all | solution.py:295
  696.1 0.1 reduce_sum.161
  696.3 0.7 divide_add_fusion
  (36 shorter events, 1.0 us)
Async XLA Ops:
  7.2 40.9 %copy-start.4 = (s32[8]{0:T(128)S(1)}, s32[8]{0:T(128)}, u32[]{:S(2)}) copy-start(s32[8]{0:T(128)} %param.14) | copy-start | bytes 100
  7.2 202.3 %all-gather.2.cloned.1.call-start = ((), (), s32[]{:S(2)}) async-start(), calls=%async_computation.6 | async-start | bytes 35651584 | tf_op jit(solution)/shard_map/all_gather | solution.py:272
  10.2 20.8 %all-to-all-start = ((s32[128,1,72]{2,1,0:T(1,128)}), s32[128,1,72]{2,1,0:T(1,128)S(1)}, u32[]{:S(2)}, u32[]{:S(2)}) async-start(s32[128,1,72]{2,1,0:T(1,128)} %broadcast_in_dim.84), calls=%async_computation | async-start | bytes 131072 | tf_op jit(solution)/shard_map/all_to_all | solution.py:215
  33.0 284.9 %all-to-all-start.2 = ((f32[8,128,256]{2,1,0:T(8,128)}), f32[8,128,256]{2,1,0:T(8,128)S(1)}, u32[]{:S(2)}, u32[]{:S(2)}) async-start(f32[8,128,256]{2,1,0:T(8,128)} %broadcast_in_dim.158), calls=%async_computation.2 | async-start | bytes 2097152 | tf_op jit(solution)/shard_map/all_to_all | solution.py:215
  317.8 1.0 copy-start
  318.8 243.6 %all-to-all-start.1 = ((f32[128,2,128,128]{3,2,1,0:T(8,128)}), f32[128,2,128,128]{3,2,1,0:T(8,128)}, u32[]{:S(2)}, u32[]{:S(2)}) async-start(f32[128,2,128,128]{3,2,1,0:T(8,128)} %bitcast.62), calls=%async_computation.1 | async-start | bytes 33554432 | tf_op jit(solution)/shard_map/all_to_all | solution.py:286
  562.4 62.9 %copy-start.1 = (f32[128,256]{1,0:T(8,128)S(1)}, f32[128,256]{1,0:T(8,128)}, u32[]{:S(2)}) copy-start(f32[128,256]{1,0:T(8,128)} %param.17) | copy-start | bytes 393220
  562.4 62.9 %copy-start.2 = (f32[128,256]{1,0:T(8,128)S(1)}, f32[128,256]{1,0:T(8,128)}, u32[]{:S(2)}) copy-start(f32[128,256]{1,0:T(8,128)} %param.16) | copy-start | bytes 393220
  650.3 46.0 %copy-start.3 = (f32[128,256]{1,0:T(8,128)S(1)}, f32[128,256]{1,0:T(8,128)}, u32[]{:S(2)}) copy-start(f32[128,256]{1,0:T(8,128)} %get-tuple-element.11) | copy-start | bytes 393220
Sparse Core Ops, SparseCore 0:
  10.1 199.3 all-gather.1

commit v2 on v1

v2 whole, which is shorter than its diff:
```python
import functools

import jax
import jax.numpy as jnp
from jax import lax
from jax.experimental import pallas as pl
from jax.experimental.pallas import tpu as pltpu
from jax.sharding import Mesh, PartitionSpec as P

BS = 256
CB = 128
KA = 8
KP = 2
N_ROW = 8
N_COL = 16
DEV = N_ROW * N_COL
NB = 8
NCOL = 256
damping = 0.7
f32 = jnp.float32
bf16 = jnp.bfloat16
ROW = ("z", "core")
COL = ("x", "y")
ALL = ROW + COL
PLANE = ROW + ("x",)
N_X = N_Y = 4
GROUP = 4
PAIR = 2


def split(value):
    high = value.astype(bf16)
    return high, (value - high.astype(f32)).astype(bf16)


def dot3(lhs, rhs):
    dot = functools.partial(jnp.dot, preferred_element_type=f32)
    return dot(lhs[0], rhs[0]) + (dot(lhs[0], rhs[1]) + dot(lhs[1], rhs[0]))


def transpose_kernel(p_ref, high_ref, low_ref):
    for m in range(KP):
        high, low = split(p_ref[0, pl.ds(m, BS, KP), :].T)
        high_ref[0, m] = high
        low_ref[0, m] = low


def transposed(own_p):
    shape = jax.ShapeDtypeStruct((NB, KP, CB, BS), bf16)
    spec = pl.BlockSpec((1, KP, CB, BS), lambda s: (s, 0, 0, 0))
    return pl.pallas_call(
        transpose_kernel,
        grid=(NB,),
        in_specs=[pl.BlockSpec((1, KP * BS, CB), lambda s: (s, 0, 0))],
        out_specs=[spec, spec],
        out_shape=[shape, shape],
    )(own_p)


def left_kernel(group, table, a_ref, high_ref, low_ref, rate_ref, out_ref):
    s = pl.program_id(0)
    parts = []
    for k2 in range(PAIR):
        block = a_ref[0, k2, 0] * table[s * KA + group + GROUP * k2].astype(f32)
        if group == 0 and k2 == 0:
            across = lax.broadcasted_iota(jnp.int32, (BS, BS), 0)
            along = lax.broadcasted_iota(jnp.int32, (BS, BS), 1)
            block = block + jnp.where(across == along, rate_ref[0], 0.0)
        parts.append(split(block))
    left = (high_ref[0].reshape(KP * CB, BS), low_ref[0].reshape(KP * CB, BS))
    for k2 in range(PAIR):
        out_ref[k2, 0] = dot3(left, parts[k2])


def left_products(group, table, a_blocks, high, low, rates):
    half = pl.BlockSpec((1, KP, CB, BS), lambda s, t: (s, 0, 0, 0))
    return pl.pallas_call(
        functools.partial(left_kernel, group),
        grid_spec=pltpu.PrefetchScalarGridSpec(
            num_scalar_prefetch=1,
            grid=(NB,),
            in_specs=[
                pl.BlockSpec((1, PAIR, 1, BS, BS), lambda s, t: (s, 0, group, 0, 0)),
                half,
                half,
                pl.BlockSpec((1, 1, BS), lambda s, t: (t[NB * KA + s], 0, 0)),
            ],
            out_specs=pl.BlockSpec((PAIR, 1, KP * CB, BS), lambda s, t: (0, s, 0, 0)),
        ),
        out_shape=jax.ShapeDtypeStruct((PAIR, NB, KP * CB, BS), f32),
        cost_estimate=pl.CostEstimate(
            flops=NB * PAIR * 3 * 2 * BS**3,
            bytes_accessed=4 * PAIR * NB * 3 * BS * BS,
            transcendentals=0,
        ),
    )(table, a_blocks.reshape(NB, PAIR, GROUP, BS, BS), high, low, rates)


ROW_AT, SLOT_AT, PARITY_AT, HALF_AT, PICK_AT = 0, 16, 32, 34, 36


def product_kernel(table, t_ref, near_ref, far_ref, out_ref, p_high, p_low):
    m = pl.program_id(1)

    @pl.when(m == 0)
    def _():
        for k2, ref in enumerate((near_ref, far_ref)):
            ghost = jnp.concatenate(
                [ref[0, pl.ds(0, BS, KP), :], ref[0, pl.ds(1, BS, KP), :]], axis=1
            )
            high, low = split(ghost)
            p_high[k2] = high
            p_low[k2] = low

    for k2 in range(PAIR):
        result = dot3(split(t_ref[k2, 0]), (p_high[k2], p_low[k2]))
        half, parity = table[HALF_AT + k2], table[PARITY_AT + k2]
        out_ref[0, half, parity, 0] = result[:, :CB]
        out_ref[0, 1 - half, parity, 0] = result[:, CB:]


def products(table, left, near, far):
    source = lambda k2: pl.BlockSpec(
        (1, KP * BS, CB), lambda s, m, t: (t[PICK_AT + k2 * NB + s], 0, 0)
    )
    return pl.pallas_call(
        product_kernel,
        grid_spec=pltpu.PrefetchScalarGridSpec(
            num_scalar_prefetch=1,
            grid=(NB, KP),
            in_specs=[
                pl.BlockSpec((PAIR, 1, CB, BS), lambda s, m, t: (0, s, m, 0)),
                source(0),
                source(1),
            ],
            out_specs=pl.BlockSpec(
                (1, 2, 2, 1, CB, CB),
                lambda s, m, t: (t[ROW_AT + s * KP + m], 0, 0, t[SLOT_AT + s * KP + m], 0, 0),
            ),
            scratch_shapes=[pltpu.VMEM((PAIR, BS, BS), bf16)] * 2,
        ),
        out_shape=jax.ShapeDtypeStruct((N_ROW, 2, 2, 2, CB, CB), f32),
        cost_estimate=pl.CostEstimate(
            flops=NB * PAIR * 3 * 2 * BS**3,
            bytes_accessed=4 * PAIR * NB * 3 * BS * BS,
            transcendentals=0,
        ),
    )(table, left, near, far)


STEPS = 4
COUNT = 2 * N_ROW * N_X
PER_STEP = COUNT // STEPS
CELLS = N_X * N_ROW


def gather_kernel(group, table, got_ref, x_ref, *rest):
    coarse_ref, part_ref, floor_ref, total = rest[-4:]
    step = pl.program_id(0)

    @pl.when(step == 0)
    def _():
        total[...] = jnp.zeros_like(total)

    for b in range(PER_STEP):
        place = table[step * PER_STEP + b]
        total[place] += got_ref[b]

    @pl.when(step == STEPS - 1)
    def _():
        right = split(x_ref[...])
        for u in range(N_X):
            for q in range(N_ROW):
                coarse_ref[u, 0, pl.ds(q, CB, N_ROW), :] = total[u * N_ROW + q]
            row = jnp.concatenate([total[u * N_ROW + q] for q in range(N_ROW)], axis=1)
            part_ref[u, 0] = dot3(split(row), right)
        across = lax.broadcasted_iota(jnp.int32, (CB, CB), 0)
        along = lax.broadcasted_iota(jnp.int32, (CB, CB), 1)
        own = jnp.where(across == along, total[table[COUNT + 1]], 0.0)
        diag = jnp.maximum(jnp.abs(jnp.sum(own, axis=1, keepdims=True)), 1.0)
        floor_ref[...] = jnp.broadcast_to(diag, (CB, NCOL))


def gather(group, table, got, x, prior):
    whole = lambda shape: pl.BlockSpec(shape, lambda i, t: (0,) * len(shape))
    in_specs = [
        pl.BlockSpec((PER_STEP, CB, CB), lambda i, t: (i, 0, 0)),
        whole((N_ROW * CB, NCOL)),
    ]
    args = [got, x]
    alias = {}
    if prior is not None:
        in_specs += [pl.BlockSpec(memory_space=pl.ANY)] * 2
        args += prior
        alias = {3: 0, 4: 1}
    return pl.pallas_call(
        functools.partial(gather_kernel, group),
        grid_spec=pltpu.PrefetchScalarGridSpec(
            num_scalar_prefetch=1,
            grid=(STEPS,),
            in_specs=in_specs,
            out_specs=[
                pl.BlockSpec((N_X, 1, CB * N_ROW, CB), lambda i, t: (0, t[COUNT], 0, 0)),
                pl.BlockSpec((N_X, 1, CB, NCOL), lambda i, t: (0, t[COUNT], 0, 0)),
                whole((CB, NCOL)),
            ],
            scratch_shapes=[pltpu.VMEM((CELLS, CB, CB), f32)],
        ),
        out_shape=[
            jax.ShapeDtypeStruct((N_X, N_Y, CB * N_ROW, CB), f32),
            jax.ShapeDtypeStruct((N_X, N_Y, CB, NCOL), f32),
            jax.ShapeDtypeStruct((CB, NCOL), f32),
        ],
        input_output_aliases=alias,
        cost_estimate=pl.CostEstimate(
            flops=3 * 2 * N_X * CB * N_ROW * CB * NCOL,
            bytes_accessed=4 * (COUNT + CELLS + 2 * CELLS) * CB * CB,
            transcendentals=0,
        ),
    )(table, *args)


def apply_kernel(c_ref, x_ref, out_ref, x_high, x_low):
    @pl.when(pl.program_id(0) == 0)
    def _():
        high, low = split(x_ref[...])
        x_high[...] = high
        x_low[...] = low

    row = jnp.concatenate([c_ref[pl.ds(q, CB, N_ROW), :] for q in range(N_ROW)], axis=1)
    out_ref[...] = dot3(split(row), (x_high[...], x_low[...]))


def apply(coarse, x):
    return pl.pallas_call(
        apply_kernel,
        grid=(N_COL,),
        in_specs=[
            pl.BlockSpec((CB * N_ROW, CB), lambda u: (u, 0)),
            pl.BlockSpec((N_ROW * CB, NCOL), lambda u: (0, 0)),
        ],
        out_specs=pl.BlockSpec((CB, NCOL), lambda u: (u, 0)),
        out_shape=jax.ShapeDtypeStruct((N_COL * CB, NCOL), f32),
        scratch_shapes=[pltpu.VMEM((N_ROW * CB, NCOL), bf16)] * 2,
    )(coarse, x)


def to_all(value, axes, count):
    copies = jnp.broadcast_to(value[None], (count,) + value.shape)
    return lax.all_to_all(copies, axes, split_axis=0, concat_axis=0, tiled=True)


def places(metas, row, col):
    delta = jnp.arange(N_COL, dtype=jnp.int32)
    p_cols = metas[:, :, :, :KP]
    entries = p_cols.reshape(N_ROW, N_COL, NB * KP)
    match = (entries // N_COL == row).astype(jnp.int32)
    earlier = jnp.cumsum(match, axis=2) - match
    order = jnp.arange(NB * KP, dtype=jnp.int32)
    sources = [
        lax.dynamic_index_in_dim(metas, (col + h * KA) % N_COL, 1, False) for h in range(2)
    ]
    result = []
    for t in range(2):
        chosen = match * (earlier == t)
        entry = jnp.sum(chosen * order, axis=2)
        u = jnp.sum(chosen * (entries % N_COL), axis=2)
        block = entry // KP
        far = (delta - col) % N_COL
        k, half = far % KA, far // KA
        quotient = jnp.zeros_like(u)
        for h in range(2):
            cells = sources[h]
            identity = jnp.broadcast_to(jnp.arange(NB, dtype=jnp.int32)[None, :, None], (N_ROW, NB, 1))
            picks = jnp.concatenate([identity, cells[:, :, KP:]], axis=2)
            hit = (block[:, :, None, None] == jnp.arange(NB)[None, None, :, None]) & (
                k[None, :, None, None] == jnp.arange(KA)[None, None, None, :]
            )
            pick = jnp.sum(jnp.where(hit, picks[:, None], 0), axis=(2, 3))
            value = jnp.sum(
                jnp.where(pick[:, :, None] == jnp.arange(NB), cells[:, None, :, h] // N_COL, 0), axis=2
            )
            quotient = jnp.where(half[None, :] == h, value, quotient)
        result.append(u * N_ROW + quotient)
    return jnp.stack(result, axis=2).reshape(-1)


def shifted(value, axis, steps):
    count = lax.axis_size(axis)
    return lax.ppermute(value, axis, [(i, (i + steps) % count) for i in range(count)])


def exchanged(value, axes):
    return lax.all_to_all(value, axes, split_axis=0, concat_axis=0, tiled=True)


def product_table(metas, group, row, x, y):
    mine = lax.dynamic_index_in_dim(metas, row, 0, False)
    source = lax.dynamic_index_in_dim(mine, x * N_Y + (y + group) % N_Y, 0, False)
    entry_row = (source[:, :KP] // N_COL).reshape(-1)
    order = jnp.arange(NB * KP, dtype=jnp.int32)
    slot = jnp.sum(
        (entry_row[None, :] == entry_row[:, None]) & (order[None, :] < order[:, None]),
        axis=1,
        dtype=jnp.int32,
    )
    back = (y + group) // N_Y
    targets, picks = [], []
    for k2 in range(PAIR):
        k = group + GROUP * k2
        e_x = (x - back - k2) % N_X
        targets.append(e_x)
        if k == 0:
            pick = jnp.arange(NB, dtype=jnp.int32)
        else:
            cells = lax.dynamic_index_in_dim(mine, e_x * N_Y + y, 0, False)
            pick = cells[:, KP + k - 1]
        picks.append(pick if group == 0 else pick + (back + k2) * NB)
    target = jnp.stack(targets)
    return jnp.concatenate([entry_row, slot, target % 2, target // 2] + picks)


def on_device(a_blocks, a_live, p_blocks, p_cols, ghost_list, policy, rates, rhs, guess):
    x = lax.axis_index("x")
    y = lax.axis_index("y")
    row = lax.axis_index(ROW)
    col = x * N_Y + y
    own_p = p_blocks.reshape(NB, BS * KP, CB)
    p_one = shifted(own_p, "x", 1)
    p_two = shifted(own_p, "x", 2)
    meta = jnp.concatenate([p_cols, ghost_list], axis=1)
    metas = to_all(meta.reshape(-1), ALL, DEV).reshape(N_ROW, N_COL, NB, KP + KA - 1)
    around = to_all(guess, ROW, N_ROW).reshape(N_ROW * CB, NCOL)

    high, low = transposed(own_p)
    numbers = jnp.concatenate([a_live.reshape(-1), policy])
    rate_rows = rates.reshape(-1, 1, BS)
    lefts = {}
    for group in (1, 3, 2, 0):
        left = left_products(group, numbers, a_blocks, high, low, rate_rows)
        lefts[group] = shifted(left, "y", -group) if group else left

    where = places(metas, row, col).reshape(N_ROW, N_X, N_Y, 2)
    where = where // (N_Y * N_ROW) * N_ROW + where % N_ROW
    own_cell = x * N_ROW + row
    prior = None
    stacked = None
    for group in (0, 1, 3, 2):
        table = product_table(metas, group, row, x, y)
        if group == 0:
            sent = products(table, lefts[group], own_p, p_one)
        else:
            if stacked is None:
                stacked = jnp.concatenate([own_p, p_one, p_two])
            sent = products(table, lefts[group], stacked, stacked)
        got = exchanged(sent.reshape(N_ROW * N_X, 2, CB, CB), PLANE).reshape(COUNT, CB, CB)
        y_u = (y + group) % N_Y
        spots = lax.dynamic_index_in_dim(where, y_u, 2, False).reshape(-1)
        spots = jnp.concatenate([spots, jnp.stack([y_u, own_cell])])
        coarse, part, floor = gather(group, spots, got, around, prior)
        if group == 0:
            floor_diag = floor
        prior = [coarse, part]
    coarse = coarse.reshape(N_COL * CB * N_ROW, CB)
    current = guess
    for sweep in range(2):
        if sweep:
            part = apply(coarse, to_all(current, ROW, N_ROW).reshape(N_ROW * CB, NCOL))
        pieces = exchanged(part.reshape(N_COL, CB, NCOL), COL)
        applied = jnp.sum(pieces, axis=0)
        current = current + damping * (rhs - applied) / floor_diag
    return coarse.reshape(N_COL * CB, N_ROW, 1, CB), current


def solution(mesh):
    mesh = Mesh(mesh.devices.reshape(N_ROW // 2, 2, N_X, N_Y), ALL)
    return jax.shard_map(
        on_device,
        mesh=mesh,
        in_specs=(
            P(ALL, None, None, None),
            P(ALL, None),
            P(ALL, None, None, None),
            P(ALL, None),
            P(ALL, None),
            P(ALL),
            P(),
            P(ALL, None),
            P(ALL, None),
        ),
        out_specs=(P(ROW, None, COL, None), P(ALL, None)),
        check_vma=False,
    )
```

time: 707 us -> 510 us (0.72)
  waiting for transfers between devices: 391 us -> 187 us
  starting transfers between devices: 24.5 us -> 46.7 us
  between operations: 14.5 us -> 1.31 us
  Pallas kernels: 155 us -> 143 us
  local copies, waits for them, and re-layouts: 19.9 us -> 29.2 us
  other arithmetic: 7.12 us -> 14.8 us
  blocking collectives: 92.4 us -> 85 us
    all_to_all x1 -> x4, waiting for transfers between devices: 229 us -> 45.3 us  [exchanged(): return lax.all_to_all(value, axes, split_axis=0, concat_axis=0, tiled=True)]
    all_gather x1 -> x0, waiting for transfers between devices: 161 us -> none  [on_device(): all_p = lax.all_gather(own_p, 'col', axis=0, tiled=True)]
    ppermute x0 -> x5, waiting for transfers between devices: none -> 128 us  [shifted(): lax.ppermute(value, axis, [(i, (i + steps) % count) for i in range(count)])]
    all_to_all x1 -> x4, starting transfers between devices: 9.1 us -> 23.8 us  [exchanged(): return lax.all_to_all(value, axes, split_axis=0, concat_axis=0, tiled=True)]
    all_to_all x2, waiting for transfers between devices: 0.01 us -> 13.7 us  [to_all(): return lax.all_to_all(copies, axes, split_axis=0, concat_axis=0, tiled=True)]
    pallas_call x2 -> x12, Pallas kernels: 134 us -> 123 us  [the longest x4 58 us: products(): pl.pallas_call(product_kernel, grid_spec=pltpu.PrefetchScalarGridSpec(num...]
    concatenate x1 -> x6, other arithmetic: 0.59 us -> 9.25 us  [the longest x1 5.53 us: on_device(): stacked = jnp.concatenate([own_p, p_one, p_two])]
    ppermute x0 -> x5, starting transfers between devices: none -> 8.39 us  [shifted(): lax.ppermute(value, axis, [(i, (i + steps) % count) for i in range(count)])]
  transfers between devices with their start and end apart: 4 -> 11, of which waited for: 2 -> 5; matrix products, arithmetic and copies ran while one was open for 3% -> 8% of each run, Pallas kernels for 16% -> 24%
where the time goes in v2:
time: 510 us; the launch traced here: 506 us
  waiting for transfers between devices  187 us (37%)
  Pallas kernels  143 us (28%)
  blocking collectives  85 us (17%)
  starting transfers between devices  46.7 us (9%)
  local copies, waits for them, and re-layouts  29.2 us (6%)
  other arithmetic  14.8 us (3%)
    ppermute x5, waiting for transfers between devices, shifted(): lax.ppermute(value, axis, [(i, (i + steps) % count) for i in range(count)])  128 us
    all_to_all x2, blocking collectives, exchanged(): return lax.all_to_all(value, axes, split_axis=0, concat_axis=0, tiled=True)  65.9 us
    pallas_call x4, Pallas kernels, products(): pl.pallas_call(product_kernel, grid_spec=pltpu.PrefetchScalarGridSpec(num...  58 us
    all_to_all x4, waiting for transfers between devices, exchanged(): return lax.all_to_all(value, axes, split_axis=0, concat_axis=0, tiled=True)  45.3 us
    pallas_call x4, Pallas kernels, left_products(): pl.pallas_call(functools.partial(left_kernel, group), grid_spec=pltpu.Pre...  35.5 us
    pallas_call x4, Pallas kernels, gather(): pl.pallas_call(functools.partial(gather_kernel, group), grid_spec=pltpu.P...  29.1 us
    all_to_all x4, starting transfers between devices, exchanged(): return lax.all_to_all(value, axes, split_axis=0, concat_axis=0, tiled=True)  23.8 us
    all_to_all x1, blocking collectives, to_all(): return lax.all_to_all(copies, axes, split_axis=0, concat_axis=0, tiled=True)  19.1 us
  transfers between devices with their start and end apart: 11, of which 5 were waited for; matrix products, arithmetic and copies ran while one was open for 8% of the time, Pallas kernels for 24%

profile of v2, /device:TPU:0, one launch (start us, length us, event | category | flops | bytes accessed | tf_op | source)
XLA Modules:
  0.0 506.4 jit_solution(15571064266777067132)
XLA Ops:
  0.6 1.7 collective-permute-start.1
  2.3 0.8 copy.70
  3.1 0.8 pad_add_fusion.3
  3.9 0.7 broadcast_in_dim.84
  4.6 10.8 %all-to-all-start = ((s32[128,1,72]{2,1,0:T(1,128)}), s32[128,1,72]{2,1,0:T(1,128)S(1)}, u32[]{:S(2)}, u32[]{:S(2)}) async-start(s32[128,1,72]{2,1,0:T(1,128)} %broadcast_in_dim.84), calls=%async_computation | async-start | bytes 131072 | tf_op jit(solution)/shard_map/all_to_all | solution.py:250
  15.3 6.1 %shard_map.104 = (bf16[8,2,128,256]{3,2,1,0:T(8,128)(2,1)}, bf16[8,2,128,256]{3,2,1,0:T(8,128)(2,1)}) custom-call(f32[8,512,128]{2,1,0:T(8,128)} %bitcast.87), custom_call_target="tpu_custom_call" | custom-call | tf_op jit(solution)/shard_map/pallas_call | solution.py:51
  21.4 0.8 reshape.524
  22.2 1.3 reshape.527.rate_ref
  23.5 1.3 pad_add_fusion.5.table
  24.8 8.9 %shard_map.107 = f32[2,8,256,256]{3,2,1,0:T(8,128)} custom-call(s32[72]{0:T(128)} %pad_add_fusion.5.table, f32[8,2,4,256,256]{4,3,2,1,0:T(8,128)} %bitcast.75, bf16[8,2,128,256]{3,2,1,0:T(8,128)(2,1)} %get-tuple-element.13.high_ref, bf16[8,2,128,256]{3,2,1,0:T(8,128)(2,1)} %get-tuple-element.14.low_ref, f32[16,1,256]{2,1,0:T(1,128)} %reshape.527.rate_ref), custom_call_target="tpu_custom_call" | custom-call | flops 1610612736 | bytes 12582912 | tf_op jit(solution)/shard_map/pallas_call | solution.py:77
  33.7 1.0 collective-permute-start.3
  34.6 8.8 %shard_map.111.t_ref = f32[2,8,256,256]{3,2,1,0:T(8,128)} custom-call(s32[72]{0:T(128)} %pad_add_fusion.5.table, f32[8,2,4,256,256]{4,3,2,1,0:T(8,128)} %bitcast.76, bf16[8,2,128,256]{3,2,1,0:T(8,128)(2,1)} %get-tuple-element.13.high_ref, bf16[8,2,128,256]{3,2,1,0:T(8,128)(2,1)} %get-tuple-element.14.low_ref, f32[16,1,256]{2,1,0:T(1,128)} %reshape.527.rate_ref), custom_call_target="tpu_custom_call" | custom-call | flops 1610612736 | bytes 12582912 | tf_op jit(solution)/shard_map/pallas_call | solution.py:77
  43.5 13.7 %all-to-all-done = s32[128,1,72]{2,1,0:T(1,128)S(1)} async-done(((s32[128,1,72]{2,1,0:T(1,128)}), s32[128,1,72]{2,1,0:T(1,128)S(1)}, u32[]{:S(2)}, u32[]{:S(2)}) %all-to-all-start) | async-done | bytes 36896 | tf_op jit(solution)/shard_map/all_to_all | solution.py:250
  57.2 1.1 broadcast_in_dim.164
  58.3 3.7 all-to-all-start.2
  62.6 15.4 %dynamic-slice_reduce_fusion = (s32[8,9]{1,0:T(8,128)S(1)}, s32[8,9]{1,0:T(8,128)S(1)}, s32[8,9]{1,0:T(8,128)S(1)}, s32[8,9]{1,0:T(8,128)S(1)}, s32[8,9]{1,0:T(8...) fusion(s32[8,16,8,9]{1,0,3,2:T(8,128)S(1)} %reshape.520, ...), kind=kLoop, calls=%fused_computation.44 | loop fusion | bytes 6384 | tf_op jit(solution)/shard_map/jit(dynamic_index_in_dim)/dynamic_slice | solution.py:316
  78.5 0.7 concatenate.54.table
  79.1 1.4 copy-done.2
  80.5 14.5 %shard_map.112 = f32[8,2,2,2,128,128]{5,4,3,2,1,0:T(8,128)} custom-call(s32[52]{0:T(128)} %concatenate.54.table, f32[2,8,256,256]{3,2,1,0:T(8,128)} %shard_map.111.t_ref, f32[8,512,128]{2,1,0:T(8,128)} %bitcast.88, f32[8,512,128]{2,1,0:T(8,128)} %copy-done.2), custom_call_target="tpu_custom_call" | custom-call | flops 1610612736 | bytes 12582912 | tf_op jit(solution)/shard_map/pallas_call | solution.py:126
  95.0 1.0 copy-done
  96.0 5.5 %all-to-all-start.5 = ((f32[32,2,128,128]{3,2,1,0:T(8,128)}), f32[32,2,128,128]{3,2,1,0:T(8,128)}, u32[]{:S(2)}, u32[]{:S(2)}) async-start(f32[32,2,128,128]{3,2,1,0:T(8,128)} %bitcast.91), calls=%async_computation.5 | async-start | bytes 8388608 | tf_op jit(solution)/shard_map/all_to_all | solution.py:294
  101.5 3.3 collective-permute-start.2
  104.8 8.9 %shard_map.109 = f32[2,8,256,256]{3,2,1,0:T(8,128)} custom-call(s32[72]{0:T(128)} %pad_add_fusion.5.table, f32[8,2,4,256,256]{4,3,2,1,0:T(8,128)} %bitcast.77, bf16[8,2,128,256]{3,2,1,0:T(8,128)(2,1)} %get-tuple-element.13.high_ref, bf16[8,2,128,256]{3,2,1,0:T(8,128)(2,1)} %get-tuple-element.14.low_ref, f32[16,1,256]{2,1,0:T(1,128)} %reshape.527.rate_ref), custom_call_target="tpu_custom_call" | custom-call | flops 1610612736 | bytes 12582912 | tf_op jit(solution)/shard_map/pallas_call | solution.py:77
  113.7 1.2 collective-permute-start.4
  115.5 0.7 concatenate.50.table
  116.2 81.6 %collective-permute-done.2 = f32[8,512,128]{2,1,0:T(8,128)} collective-permute-done((f32[8,512,128]{2,1,0:T(8,128)S(1)}, f32[8,512,128]{2,1,0:T(8,128)}, u32[]{:S(2)}, u32[]{:S(2)}) %collective-permute-start.2) | collective-permute-done | bytes 2097184 | tf_op jit(solution)/shard_map/ppermute | solution.py:290
  197.8 5.5 %pad_maximum_fusion.near_ref.far_ref = f32[24,512,128]{2,1,0:T(8,128)} fusion(f32[8,512,128]{2,1,0:T(8,128)} %collective-permute-done.2, f32[8,512,128]{2,1,0:T(8,128)} %copy-done.2, f32[8,512,128]{2,1,0:T(8,128)S(1)} %bitcast.90), kind=kLoop, calls=%fused_computation | loop fusion | flops 3145728 | bytes 12582912 | tf_op jit(solution)/shard_map/concatenate | solution.py:354
  203.3 14.5 %shard_map.108 = f32[8,2,2,2,128,128]{5,4,3,2,1,0:T(8,128)} custom-call(s32[52]{0:T(128)} %concatenate.50.table, f32[2,8,256,256]{3,2,1,0:T(8,128)} %collective-permute-done.3.t_ref, f32[24,512,128]{2,1,0:T(8,128)} %pad_maximum_fusion.near_ref.far_ref, f32[24,512,128]{2,1,0:T(8,128)} %pad_maximum_fusion.near_ref.far_ref), custom_call_target="tpu_custom_call" | custom-call | flops 1610612736 | bytes 12582912 | tf_op jit(solution)/shard_map/pallas_call | solution.py:126
  217.8 5.2 %all-to-all-start.3 = ((f32[32,2,128,128]{3,2,1,0:T(8,128)}), f32[32,2,128,128]{3,2,1,0:T(8,128)}, u32[]{:S(2)}, u32[]{:S(2)}) async-start(f32[32,2,128,128]{3,2,1,0:T(8,128)} %bitcast.93), calls=%async_computation.3 | async-start | bytes 8388608 | tf_op jit(solution)/shard_map/all_to_all | solution.py:294
  223.1 8.9 %shard_map.105 = f32[2,8,256,256]{3,2,1,0:T(8,128)} custom-call(s32[72]{0:T(128)} %pad_add_fusion.5.table, f32[8,2,4,256,256]{4,3,2,1,0:T(8,128)} %bitcast.78, bf16[8,2,128,256]{3,2,1,0:T(8,128)(2,1)} %get-tuple-element.13.high_ref, bf16[8,2,128,256]{3,2,1,0:T(8,128)(2,1)} %get-tuple-element.14.low_ref, f32[16,1,256]{2,1,0:T(1,128)} %reshape.527.rate_ref), custom_call_target="tpu_custom_call" | custom-call | flops 1610612736 | bytes 12582912 | tf_op jit(solution)/shard_map/pallas_call | solution.py:77
  232.0 1.3 collective-permute-start
  234.4 14.5 %shard_map.110 = f32[8,2,2,2,128,128]{5,4,3,2,1,0:T(8,128)} custom-call(s32[52]{0:T(128)} %concatenate.52.table, f32[2,8,256,256]{3,2,1,0:T(8,128)} %collective-permute-done.4.t_ref, f32[24,512,128]{2,1,0:T(8,128)} %pad_maximum_fusion.near_ref.far_ref, f32[24,512,128]{2,1,0:T(8,128)} %pad_maximum_fusion.near_ref.far_ref), custom_call_target="tpu_custom_call" | custom-call | flops 1610612736 | bytes 12582912 | tf_op jit(solution)/shard_map/pallas_call | solution.py:126
  248.9 24.9 %all-to-all-done.3 = f32[32,2,128,128]{3,2,1,0:T(8,128)} async-done(((f32[32,2,128,128]{3,2,1,0:T(8,128)}), f32[32,2,128,128]{3,2,1,0:T(8,128)}, u32[]{:S(2)}, u32[]{:S(2)}) %all-to-all-start.3) | async-done | bytes 4194336 | tf_op jit(solution)/shard_map/all_to_all | solution.py:294
  273.8 5.4 %all-to-all-start.4 = ((f32[32,2,128,128]{3,2,1,0:T(8,128)}), f32[32,2,128,128]{3,2,1,0:T(8,128)}, u32[]{:S(2)}, u32[]{:S(2)}) async-start(f32[32,2,128,128]{3,2,1,0:T(8,128)} %bitcast.94), calls=%async_computation.4 | async-start | bytes 8388608 | tf_op jit(solution)/shard_map/all_to_all | solution.py:294
  280.3 46.2 %collective-permute-done.t_ref = f32[2,8,256,256]{3,2,1,0:T(8,128)} collective-permute-done((f32[2,8,256,256]{3,2,1,0:T(8,128)}, f32[2,8,256,256]{3,2,1,0:T(8,128)}, u32[]{:S(2)}, u32[]{:S(2)}) %collective-permute-start) | collective-permute-done | bytes 4194336 | tf_op jit(solution)/shard_map/ppermute | solution.py:290
  326.5 14.5 %shard_map.106 = f32[8,2,2,2,128,128]{5,4,3,2,1,0:T(8,128)} custom-call(s32[52]{0:T(128)} %concatenate.46.table, f32[2,8,256,256]{3,2,1,0:T(8,128)} %collective-permute-done.t_ref, f32[24,512,128]{2,1,0:T(8,128)} %pad_maximum_fusion.near_ref.far_ref, f32[24,512,128]{2,1,0:T(8,128)} %pad_maximum_fusion.near_ref.far_ref), custom_call_target="tpu_custom_call" | custom-call | flops 1610612736 | bytes 12582912 | tf_op jit(solution)/shard_map/pallas_call | solution.py:126
  341.0 7.6 %all-to-all-start.1 = ((f32[32,2,128,128]{3,2,1,0:T(8,128)}), f32[32,2,128,128]{3,2,1,0:T(8,128)}, u32[]{:S(2)}, u32[]{:S(2)}) async-start(f32[32,2,128,128]{3,2,1,0:T(8,128)} %bitcast.92), calls=%async_computation.1 | async-start | bytes 8388608 | tf_op jit(solution)/shard_map/all_to_all | solution.py:294
  348.9 1.4 reduce_window_sum.13
  356.8 7.3 %shard_map.113 = (f32[4,4,1024,128]{3,2,1,0:T(8,128)}, f32[4,4,128,256]{3,2,1,0:T(8,128)}, f32[128,256]{1,0:T(8,128)}) custom-call(s32[66]{0:T(128)} %add_add_fusion.3.table, f32[64,128,128]{2,1,0:T(8,128)} %bitcast.33.got_ref, f32[1024,256]{1,0:T(8,128)} %bitcast.82), custom_call_target="tpu_custom_call" | custom-call | flops 805306368 | bytes 10485760 | tf_op jit(solution)/shard_map/pallas_call | solution.py:196
  364.1 7.3 %shard_map.114 = (f32[4,4,1024,128]{3,2,1,0:T(8,128)}, f32[4,4,128,256]{3,2,1,0:T(8,128)}, f32[128,256]{1,0:T(8,128)}) custom-call(s32[66]{0:T(128)} %add_add_fusion.2.table, f32[64,128,128]{2,1,0:T(8,128)} %bitcast.28.got_ref, f32[1024,256]{1,0:T(8,128)} %bitcast.83, ...), custom_call_target="tpu_custom_call", output_to_operand_aliasing={{0}: (3, {}), {1}: (4, {})} | custom-call | flops 805306368 | bytes 10485760 | tf_op jit(solution)/shard_map/pallas_call | solution.py:196
  371.4 7.3 %shard_map.115 = (f32[4,4,1024,128]{3,2,1,0:T(8,128)}, f32[4,4,128,256]{3,2,1,0:T(8,128)}, f32[128,256]{1,0:T(8,128)}) custom-call(s32[66]{0:T(128)} %add_add_fusion.1.table, f32[64,128,128]{2,1,0:T(8,128)} %bitcast.23.got_ref, f32[1024,256]{1,0:T(8,128)} %bitcast.84, ...), custom_call_target="tpu_custom_call", output_to_operand_aliasing={{0}: (3, {}), {1}: (4, {})} | custom-call | flops 805306368 | bytes 10485760 | tf_op jit(solution)/shard_map/pallas_call | solution.py:196
  378.7 20.4 %all-to-all-done.1 = f32[32,2,128,128]{3,2,1,0:T(8,128)} async-done(((f32[32,2,128,128]{3,2,1,0:T(8,128)}), f32[32,2,128,128]{3,2,1,0:T(8,128)}, u32[]{:S(2)}, u32[]{:S(2)}) %all-to-all-start.1) | async-done | bytes 4194336 | tf_op jit(solution)/shard_map/all_to_all | solution.py:294
  399.0 7.3 %shard_map.116 = (f32[4,4,1024,128]{3,2,1,0:T(8,128)}, f32[4,4,128,256]{3,2,1,0:T(8,128)}, f32[128,256]{1,0:T(8,128)}) custom-call(s32[66]{0:T(128)} %add_add_fusion.table, f32[64,128,128]{2,1,0:T(8,128)} %bitcast.17.got_ref, f32[1024,256]{1,0:T(8,128)} %bitcast.85, ...), custom_call_target="tpu_custom_call", output_to_operand_aliasing={{0}: (3, {}), {1}: (4, {})} | custom-call | flops 805306368 | bytes 10485760 | tf_op jit(solution)/shard_map/pallas_call | solution.py:196
  406.3 33.7 %all_to_all.46 = f32[16,128,256]{2,1,0:T(8,128)S(1)} all-to-all(f32[16,128,256]{2,1,0:T(8,128)} %bitcast.81), channel_id=1, replica_groups=mesh['z'=4,'core'=2,'x'=4,'y'=4] {'x','y'}, dimensions={0} | all-to-all | bytes 4194304 | tf_op jit(solution)/shard_map/all_to_all | solution.py:294
  440.3 19.1 %all_to_all.47 = f32[8,128,256]{2,1,0:T(8,128)} all-to-all(f32[8,128,256]{2,1,0:T(8,128)S(1)} %broadcast_in_dim.165), channel_id=1, replica_groups=mesh['z'=4,'core'=2,'x'=4,'y'=4] {'z','core'}, dimensions={0} | all-to-all | bytes 2097152 | tf_op jit(solution)/shard_map/all_to_all | solution.py:250
  459.4 14.0 %shard_map.117 = f32[2048,256]{1,0:T(8,128)} custom-call(f32[16384,128]{1,0:T(8,128)} %bitcast.79, f32[1024,256]{1,0:T(8,128)} %bitcast.96), custom_call_target="tpu_custom_call" | custom-call | tf_op jit(solution)/shard_map/pallas_call | solution.py:235
  473.4 32.2 %all_to_all.48 = f32[16,128,256]{2,1,0:T(8,128)S(1)} all-to-all(f32[16,128,256]{2,1,0:T(8,128)} %bitcast.95), channel_id=1, replica_groups=mesh['z'=4,'core'=2,'x'=4,'y'=4] {'x','y'}, dimensions={0} | all-to-all | bytes 4194304 | tf_op jit(solution)/shard_map/all_to_all | solution.py:294
  505.7 0.7 divide_add_fusion
  (95 shorter events, 10.6 us)
Async XLA Ops:
  0.6 78.5 %collective-permute-start.1 = (f32[8,512,128]{2,1,0:T(8,128)}, f32[8,512,128]{2,1,0:T(8,128)S(1)}, u32[]{:S(2)}, u32[]{:S(2)}) collective-permute-start(f32[8,512,128]{2,1,0:T(8,128)} %bitcast.86), channel_id=1, source_target_pairs={{0,4},{4,8},{8,12},{12,0},{1,5},{5,9},{9,13},{13,1},{2,6},{6,10},{... | collective-permute-start | bytes 6291464 | tf_op jit(solution)/shard_map/ppermute | solution.py:290
  4.6 52.7 %all-to-all-start = ((s32[128,1,72]{2,1,0:T(1,128)}), s32[128,1,72]{2,1,0:T(1,128)S(1)}, u32[]{:S(2)}, u32[]{:S(2)}) async-start(s32[128,1,72]{2,1,0:T(1,128)} %broadcast_in_dim.84), calls=%async_computation | async-start | bytes 131072 | tf_op jit(solution)/shard_map/all_to_all | solution.py:250
  33.7 23.5 %copy-start.3 = (f32[128,256]{1,0:T(8,128)S(1)}, f32[128,256]{1,0:T(8,128)}, u32[]{:S(2)}) copy-start(f32[128,256]{1,0:T(8,128)} %param.17) | copy-start | bytes 393220
  33.7 169.6 %collective-permute-start.3 = (f32[2,8,256,256]{3,2,1,0:T(8,128)}, f32[2,8,256,256]{3,2,1,0:T(8,128)}, u32[]{:S(2)}, u32[]{:S(2)}) collective-permute-start(f32[2,8,256,256]{3,2,1,0:T(8,128)} %shard_map.107), channel_id=1, source_target_pairs={{0,1},{1,2},{2,3},{3,0},{4,5},{5,6},{6,7},{7,4},{8,9},{9,10},{10,1... | collective-permute-start | bytes 12582920 | tf_op jit(solution)/shard_map/ppermute | solution.py:290
  58.3 36.7 %all-to-all-start.2 = ((f32[8,128,256]{2,1,0:T(8,128)}), f32[8,128,256]{2,1,0:T(8,128)S(1)}, u32[]{:S(2)}, u32[]{:S(2)}) async-start(f32[8,128,256]{2,1,0:T(8,128)} %broadcast_in_dim.164), calls=%async_computation.2 | async-start | bytes 2097152 | tf_op jit(solution)/shard_map/all_to_all | solution.py:250
  79.1 1.4 copy-start.2
  95.0 1.0 copy-start
  95.0 6.5 %copy-start.1 = (f32[8,256,2,128]{3,2,1,0:T(2,128)S(1)}, f32[8,256,2,128]{3,2,1,0:T(2,128)}, u32[]{:S(2)}) copy-start(f32[8,256,2,128]{3,2,1,0:T(2,128)} %param.11) | copy-start | bytes 6291460
  96.0 121.8 %all-to-all-start.5 = ((f32[32,2,128,128]{3,2,1,0:T(8,128)}), f32[32,2,128,128]{3,2,1,0:T(8,128)}, u32[]{:S(2)}, u32[]{:S(2)}) async-start(f32[32,2,128,128]{3,2,1,0:T(8,128)} %bitcast.91), calls=%async_computation.5 | async-start | bytes 8388608 | tf_op jit(solution)/shard_map/all_to_all | solution.py:294
  101.5 96.2 %collective-permute-start.2 = (f32[8,512,128]{2,1,0:T(8,128)S(1)}, f32[8,512,128]{2,1,0:T(8,128)}, u32[]{:S(2)}, u32[]{:S(2)}) collective-permute-start(f32[8,512,128]{2,1,0:T(8,128)S(1)} %bitcast.89), channel_id=1, source_target_pairs={{0,8},{4,12},{8,0},{12,4},{1,9},{5,13},{9,1},{13,5},{2,10},{6,14},... | collective-permute-start | bytes 6291464 | tf_op jit(solution)/shard_map/ppermute | solution.py:290
  113.7 120.6 %collective-permute-start.4 = (f32[2,8,256,256]{3,2,1,0:T(8,128)}, f32[2,8,256,256]{3,2,1,0:T(8,128)}, u32[]{:S(2)}, u32[]{:S(2)}) collective-permute-start(f32[2,8,256,256]{3,2,1,0:T(8,128)} %shard_map.109), channel_id=1, source_target_pairs={{0,3},{1,0},{2,1},{3,2},{4,7},{5,4},{6,5},{7,6},{8,11},{9,8},{10,9... | collective-permute-start | bytes 12582920 | tf_op jit(solution)/shard_map/ppermute | solution.py:290
  217.8 55.9 %all-to-all-start.3 = ((f32[32,2,128,128]{3,2,1,0:T(8,128)}), f32[32,2,128,128]{3,2,1,0:T(8,128)}, u32[]{:S(2)}, u32[]{:S(2)}) async-start(f32[32,2,128,128]{3,2,1,0:T(8,128)} %bitcast.93), calls=%async_computation.3 | async-start | bytes 8388608 | tf_op jit(solution)/shard_map/all_to_all | solution.py:294
  232.0 94.5 %collective-permute-start = (f32[2,8,256,256]{3,2,1,0:T(8,128)}, f32[2,8,256,256]{3,2,1,0:T(8,128)}, u32[]{:S(2)}, u32[]{:S(2)}) collective-permute-start(f32[2,8,256,256]{3,2,1,0:T(8,128)} %shard_map.105), channel_id=1, source_target_pairs={{0,2},{1,3},{2,0},{3,1},{4,6},{5,7},{6,4},{7,5},{8,10},{9,11},{10,... | collective-permute-start | bytes 12582920 | tf_op jit(solution)/shard_map/ppermute | solution.py:290
  273.8 67.2 %all-to-all-start.4 = ((f32[32,2,128,128]{3,2,1,0:T(8,128)}), f32[32,2,128,128]{3,2,1,0:T(8,128)}, u32[]{:S(2)}, u32[]{:S(2)}) async-start(f32[32,2,128,128]{3,2,1,0:T(8,128)} %bitcast.94), calls=%async_computation.4 | async-start | bytes 8388608 | tf_op jit(solution)/shard_map/all_to_all | solution.py:294
  341.0 58.0 %all-to-all-start.1 = ((f32[32,2,128,128]{3,2,1,0:T(8,128)}), f32[32,2,128,128]{3,2,1,0:T(8,128)}, u32[]{:S(2)}, u32[]{:S(2)}) async-start(f32[32,2,128,128]{3,2,1,0:T(8,128)} %bitcast.92), calls=%async_computation.1 | async-start | bytes 8388608 | tf_op jit(solution)/shard_map/all_to_all | solution.py:294
  406.3 33.8 %copy-start.4 = (f32[128,256]{1,0:T(8,128)S(1)}, f32[128,256]{1,0:T(8,128)}, u32[]{:S(2)}) copy-start(f32[128,256]{1,0:T(8,128)} %param.17) | copy-start | bytes 393220
  406.3 33.8 %copy-start.5 = (f32[128,256]{1,0:T(8,128)S(1)}, f32[128,256]{1,0:T(8,128)}, u32[]{:S(2)}) copy-start(f32[128,256]{1,0:T(8,128)} %param.16) | copy-start | bytes 393220
  406.3 33.9 %copy-start.6 = (f32[128,256]{1,0:T(8,128)S(1)}, f32[128,256]{1,0:T(8,128)}, u32[]{:S(2)}) copy-start(f32[128,256]{1,0:T(8,128)} %get-tuple-element.23) | copy-start | bytes 393220

commit v3 on v2

--- a/solution.py
+++ b/solution.py
@@ -13,7 +13,6 @@
 KP = 2
 N_ROW = 8
 N_COL = 16
-DEV = N_ROW * N_COL
 NB = 8
 NCOL = 256
 damping = 0.7
@@ -34,8 +33,9 @@
 
 
 def dot3(lhs, rhs):
-    dot = functools.partial(jnp.dot, preferred_element_type=f32)
-    return dot(lhs[0], rhs[0]) + (dot(lhs[0], rhs[1]) + dot(lhs[1], rhs[0]))
+    left = jnp.concatenate([lhs[0], lhs[0], lhs[1]], axis=1)
+    right = jnp.concatenate([rhs[0], rhs[1], rhs[0]], axis=0)
+    return jnp.dot(left, right, preferred_element_type=f32)
 
 
 def transpose_kernel(p_ref, high_ref, low_ref):
@@ -96,48 +96,66 @@
     )(table, a_blocks.reshape(NB, PAIR, GROUP, BS, BS), high, low, rates)
 
 
-ROW_AT, SLOT_AT, PARITY_AT, HALF_AT, PICK_AT = 0, 16, 32, 34, 36
-
-
-def product_kernel(table, t_ref, near_ref, far_ref, out_ref, p_high, p_low):
-    m = pl.program_id(1)
-
-    @pl.when(m == 0)
+ROW_AT, SLOT_AT, PARITY_AT, HALF_AT, PICK_AT, TABLE = 0, 16, 32, 34, 36, 52
+
+
+def product_kernel(base, table, t_ref, near_ref, far_ref, out_ref, held, sems):
+    s = pl.program_id(0)
+    now = lax.rem(s, 2)
+
+    def copy(step, m):
+        return pltpu.make_async_copy(
+            held.at[lax.rem(step, 2), m],
+            out_ref.at[
+                table[base + ROW_AT + step * KP + m], :, :, table[base + SLOT_AT + step * KP + m]
+            ],
+            sems.at[lax.rem(step, 2), m],
+        )
+
+    @pl.when(s >= 2)
     def _():
-        for k2, ref in enumerate((near_ref, far_ref)):
-            ghost = jnp.concatenate(
-                [ref[0, pl.ds(0, BS, KP), :], ref[0, pl.ds(1, BS, KP), :]], axis=1
-            )
-            high, low = split(ghost)
-            p_high[k2] = high
-            p_low[k2] = low
-
-    for k2 in range(PAIR):
-        result = dot3(split(t_ref[k2, 0]), (p_high[k2], p_low[k2]))
-        half, parity = table[HALF_AT + k2], table[PARITY_AT + k2]
-        out_ref[0, half, parity, 0] = result[:, :CB]
-        out_ref[0, 1 - half, parity, 0] = result[:, CB:]
-
-
-def products(table, left, near, far):
+        for m in range(KP):
+            copy(s - 2, m).wait()
+
+    for k2, ref in enumerate((near_ref, far_ref)):
+        ghost = jnp.concatenate(
+            [ref[0, pl.ds(0, BS, KP), :], ref[0, pl.ds(1, BS, KP), :]], axis=1
+        )
+        result = dot3(split(t_ref[k2, 0]), split(ghost))
+        half, parity = table[base + HALF_AT + k2], table[base + PARITY_AT + k2]
+        for m in range(KP):
+            held[now, m, half, parity] = result[m * CB : (m + 1) * CB, :CB]
+            held[now, m, 1 - half, parity] = result[m * CB : (m + 1) * CB, CB:]
+    for m in range(KP):
+        copy(s, m).start()
+
+    @pl.when(s == NB - 1)
+    def _():
+        for step in (NB - 2, NB - 1):
+            for m in range(KP):
+                copy(step, m).wait()
+
+
+def products(group, table, left, near, far):
+    base = group * TABLE
     source = lambda k2: pl.BlockSpec(
-        (1, KP * BS, CB), lambda s, m, t: (t[PICK_AT + k2 * NB + s], 0, 0)
+        (1, KP * BS, CB), lambda s, t: (t[base + PICK_AT + k2 * NB + s], 0, 0)
     )
     return pl.pallas_call(
-        product_kernel,
+        functools.partial(product_kernel, base),
         grid_spec=pltpu.PrefetchScalarGridSpec(
             num_scalar_prefetch=1,
-            grid=(NB, KP),
+            grid=(NB,),
             in_specs=[
-                pl.BlockSpec((PAIR, 1, CB, BS), lambda s, m, t: (0, s, m, 0)),
+                pl.BlockSpec((PAIR, 1, KP * CB, BS), lambda s, t: (0, s, 0, 0)),
                 source(0),
                 source(1),
             ],
-            out_specs=pl.BlockSpec(
-                (1, 2, 2, 1, CB, CB),
-                lambda s, m, t: (t[ROW_AT + s * KP + m], 0, 0, t[SLOT_AT + s * KP + m], 0, 0),
-            ),
-            scratch_shapes=[pltpu.VMEM((PAIR, BS, BS), bf16)] * 2,
+            out_specs=pl.BlockSpec(memory_space=pl.ANY),
+            scratch_shapes=[
+                pltpu.VMEM((2, KP, 2, 2, CB, CB), f32),
+                pltpu.SemaphoreType.DMA((2, KP)),
+            ],
         ),
         out_shape=jax.ShapeDtypeStruct((N_ROW, 2, 2, 2, CB, CB), f32),
         cost_estimate=pl.CostEstimate(
@@ -155,12 +173,15 @@
 
 
 def gather_kernel(group, table, got_ref, x_ref, *rest):
-    coarse_ref, part_ref, floor_ref, total = rest[-4:]
+    coarse_ref, part_ref, floor_ref, total, x_high, x_low = rest[-6:]
     step = pl.program_id(0)
 
     @pl.when(step == 0)
     def _():
         total[...] = jnp.zeros_like(total)
+        high, low = split(x_ref[...])
+        x_high[...] = high
+        x_low[...] = low
 
     for b in range(PER_STEP):
         place = table[step * PER_STEP + b]
@@ -168,17 +189,20 @@
 
     @pl.when(step == STEPS - 1)
     def _():
-        right = split(x_ref[...])
+        rows = []
         for u in range(N_X):
             for q in range(N_ROW):
                 coarse_ref[u, 0, pl.ds(q, CB, N_ROW), :] = total[u * N_ROW + q]
-            row = jnp.concatenate([total[u * N_ROW + q] for q in range(N_ROW)], axis=1)
-            part_ref[u, 0] = dot3(split(row), right)
-        across = lax.broadcasted_iota(jnp.int32, (CB, CB), 0)
-        along = lax.broadcasted_iota(jnp.int32, (CB, CB), 1)
-        own = jnp.where(across == along, total[table[COUNT + 1]], 0.0)
-        diag = jnp.maximum(jnp.abs(jnp.sum(own, axis=1, keepdims=True)), 1.0)
-        floor_ref[...] = jnp.broadcast_to(diag, (CB, NCOL))
+            rows.append(jnp.concatenate([total[u * N_ROW + q] for q in range(N_ROW)], axis=1))
+        result = dot3(split(jnp.concatenate(rows)), (x_high[...], x_low[...]))
+        for u in range(N_X):
+            part_ref[u, 0] = result[u * CB : (u + 1) * CB]
+        if group == 0:
+            across = lax.broadcasted_iota(jnp.int32, (CB, CB), 0)
+            along = lax.broadcasted_iota(jnp.int32, (CB, CB), 1)
+            own = jnp.where(across == along, total[table[COUNT + 1]], 0.0)
+            diag = jnp.maximum(jnp.abs(jnp.sum(own, axis=1, keepdims=True)), 1.0)
+            floor_ref[...] = jnp.broadcast_to(diag, (CB, NCOL))
 
 
 def gather(group, table, got, x, prior):
@@ -204,7 +228,11 @@
                 pl.BlockSpec((N_X, 1, CB, NCOL), lambda i, t: (0, t[COUNT], 0, 0)),
                 whole((CB, NCOL)),
             ],
-            scratch_shapes=[pltpu.VMEM((CELLS, CB, CB), f32)],
+            scratch_shapes=[
+                pltpu.VMEM((CELLS, CB, CB), f32),
+                pltpu.VMEM((N_ROW * CB, NCOL), bf16),
+                pltpu.VMEM((N_ROW * CB, NCOL), bf16),
+            ],
         ),
         out_shape=[
             jax.ShapeDtypeStruct((N_X, N_Y, CB * N_ROW, CB), f32),
@@ -220,6 +248,9 @@
     )(table, *args)
 
 
+TALL = 4 * CB
+
+
 def apply_kernel(c_ref, x_ref, out_ref, x_high, x_low):
     @pl.when(pl.program_id(0) == 0)
     def _():
@@ -227,19 +258,19 @@
         x_high[...] = high
         x_low[...] = low
 
-    row = jnp.concatenate([c_ref[pl.ds(q, CB, N_ROW), :] for q in range(N_ROW)], axis=1)
-    out_ref[...] = dot3(split(row), (x_high[...], x_low[...]))
+    rows = jnp.concatenate([c_ref[pl.ds(q, TALL, N_ROW), :] for q in range(N_ROW)], axis=1)
+    out_ref[...] = dot3(split(rows), (x_high[...], x_low[...]))
 
 
 def apply(coarse, x):
     return pl.pallas_call(
         apply_kernel,
-        grid=(N_COL,),
+        grid=(N_COL * CB // TALL,),
         in_specs=[
-            pl.BlockSpec((CB * N_ROW, CB), lambda u: (u, 0)),
+            pl.BlockSpec((TALL * N_ROW, CB), lambda u: (u, 0)),
             pl.BlockSpec((N_ROW * CB, NCOL), lambda u: (0, 0)),
         ],
-        out_specs=pl.BlockSpec((CB, NCOL), lambda u: (u, 0)),
+        out_specs=pl.BlockSpec((TALL, NCOL), lambda u: (u, 0)),
         out_shape=jax.ShapeDtypeStruct((N_COL * CB, NCOL), f32),
         scratch_shapes=[pltpu.VMEM((N_ROW * CB, NCOL), bf16)] * 2,
     )(coarse, x)
@@ -294,30 +325,33 @@
     return lax.all_to_all(value, axes, split_axis=0, concat_axis=0, tiled=True)
 
 
-def product_table(metas, group, row, x, y):
-    mine = lax.dynamic_index_in_dim(metas, row, 0, False)
-    source = lax.dynamic_index_in_dim(mine, x * N_Y + (y + group) % N_Y, 0, False)
-    entry_row = (source[:, :KP] // N_COL).reshape(-1)
+META = KP + KA - 1
+
+
+def product_tables(cells, x, y):
+    groups = jnp.arange(GROUP, dtype=jnp.int32)
+    columns = [x * N_Y + (y + groups) % N_Y]
+    back = (y + groups) // N_Y
+    e_x = jnp.stack([(x - back - k2) % N_X for k2 in range(PAIR)])
+    columns.append((e_x * N_Y + y).reshape(-1))
+    wanted = jnp.concatenate(columns)
+    chosen = (wanted[:, None] == jnp.arange(N_COL, dtype=jnp.int32)[None, :]).astype(f32)
+    found = jnp.dot(chosen, cells, precision=lax.Precision.HIGHEST)
+    found = (found + 0.5).astype(jnp.int32).reshape(-1, NB, META)
+    entry_row = (found[:GROUP, :, :KP] // N_COL).reshape(GROUP, NB * KP)
     order = jnp.arange(NB * KP, dtype=jnp.int32)
     slot = jnp.sum(
-        (entry_row[None, :] == entry_row[:, None]) & (order[None, :] < order[:, None]),
-        axis=1,
+        (entry_row[:, None, :] == entry_row[:, :, None]) & (order[None, None, :] < order[None, :, None]),
+        axis=2,
         dtype=jnp.int32,
     )
-    back = (y + group) // N_Y
-    targets, picks = [], []
-    for k2 in range(PAIR):
-        k = group + GROUP * k2
-        e_x = (x - back - k2) % N_X
-        targets.append(e_x)
-        if k == 0:
-            pick = jnp.arange(NB, dtype=jnp.int32)
-        else:
-            cells = lax.dynamic_index_in_dim(mine, e_x * N_Y + y, 0, False)
-            pick = cells[:, KP + k - 1]
-        picks.append(pick if group == 0 else pick + (back + k2) * NB)
-    target = jnp.stack(targets)
-    return jnp.concatenate([entry_row, slot, target % 2, target // 2] + picks)
+    picks = [jnp.arange(NB, dtype=jnp.int32)]
+    for k in range(1, KA):
+        picks.append(found[GROUP + k, :, KP + k - 1])
+    picks = jnp.stack(picks).reshape(PAIR, GROUP, NB)
+    offset = jnp.where(groups == 0, 0, (back[None, :] + jnp.arange(PAIR)[:, None]) * NB)
+    picks = (picks + offset[:, :, None]).transpose(1, 0, 2).reshape(GROUP, PAIR * NB)
+    return jnp.concatenate([entry_row, slot, e_x.T % 2, e_x.T // 2, picks], axis=1).reshape(-1)
 
 
 def on_device(a_blocks, a_live, p_blocks, p_cols, ghost_list, policy, rates, rhs, guess):
@@ -327,10 +361,15 @@
     col = x * N_Y + y
     own_p = p_blocks.reshape(NB, BS * KP, CB)
     p_one = shifted(own_p, "x", 1)
-    p_two = shifted(own_p, "x", 2)
-    meta = jnp.concatenate([p_cols, ghost_list], axis=1)
-    metas = to_all(meta.reshape(-1), ALL, DEV).reshape(N_ROW, N_COL, NB, KP + KA - 1)
-    around = to_all(guess, ROW, N_ROW).reshape(N_ROW * CB, NCOL)
+    meta = jnp.concatenate([p_cols, ghost_list], axis=1).astype(f32).reshape(-1)
+    cells = to_all(meta, COL, N_COL)
+    spare = -(-N_COL * NB * META // NCOL)
+    spare = -(-spare // 8) * 8
+    padded = jnp.pad(cells.reshape(-1), (0, spare * NCOL - cells.size)).reshape(spare, NCOL)
+    packed = to_all(jnp.concatenate([guess, padded]), ROW, N_ROW)
+    around = packed[:, :CB].reshape(N_ROW * CB, NCOL)
+    metas = packed[:, CB:].reshape(N_ROW, spare * NCOL)[:, : cells.size]
+    metas = (metas + 0.5).astype(jnp.int32).reshape(N_ROW, N_COL, NB, META)
 
     high, low = transposed(own_p)
     numbers = jnp.concatenate([a_live.reshape(-1), policy])
@@ -339,25 +378,26 @@
     for group in (1, 3, 2, 0):
         left = left_products(group, numbers, a_blocks, high, low, rate_rows)
         lefts[group] = shifted(left, "y", -group) if group else left
-
+    p_two = shifted(p_one, "x", 1)
+
+    table = product_tables(cells, x, y)
     where = places(metas, row, col).reshape(N_ROW, N_X, N_Y, 2)
     where = where // (N_Y * N_ROW) * N_ROW + where % N_ROW
     own_cell = x * N_ROW + row
     prior = None
     stacked = None
     for group in (0, 1, 3, 2):
-        table = product_table(metas, group, row, x, y)
-        if group == 0:
-            sent = products(table, lefts[group], own_p, p_one)
-        else:
+        near, far = own_p, p_one
+        if group:
             if stacked is None:
                 stacked = jnp.concatenate([own_p, p_one, p_two])
-            sent = products(table, lefts[group], stacked, stacked)
-        got = exchanged(sent.reshape(N_ROW * N_X, 2, CB, CB), PLANE).reshape(COUNT, CB, CB)
+            near = far = stacked
+        sent = products(group, table, lefts[group], near, far)
+        got = exchanged(sent.reshape(N_ROW * N_X, 2, CB, CB), PLANE)
         y_u = (y + group) % N_Y
         spots = lax.dynamic_index_in_dim(where, y_u, 2, False).reshape(-1)
         spots = jnp.concatenate([spots, jnp.stack([y_u, own_cell])])
-        coarse, part, floor = gather(group, spots, got, around, prior)
+        coarse, part, floor = gather(group, spots, got.reshape(COUNT, CB, CB), around, prior)
         if group == 0:
             floor_diag = floor
         prior = [coarse, part]
@@ -374,6 +414,7 @@
 
 def solution(mesh):
     mesh = Mesh(mesh.devices.reshape(N_ROW // 2, 2, N_X, N_Y), ALL)
+
     return jax.shard_map(
         on_device,
         mesh=mesh,

time: 510 us -> 469 us (0.920)
  Pallas kernels: 143 us -> 117 us
  local copies, waits for them, and re-layouts: 29.2 us -> 12.9 us
  waiting for transfers between devices: 187 us -> 175 us
  other arithmetic: 14.8 us -> 23.7 us
    pallas_call x5, Pallas kernels: 72 us -> 45.7 us  [the longest x4 37.5 us: products(): pl.pallas_call(functools.partial(product_kernel, base), grid_spec=pltpu.P...]
    dynamic_slice x4 -> x0, local copies, waits for them, and re-layouts: 16.6 us -> none  [the longest x1 15.4 us: product_table(): cells = lax.dynamic_index_in_dim(mine, e_x * N_Y + y, 0, False)]
    all_to_all x2, waiting for transfers between devices: 13.7 us -> 0.01 us  [to_all(): return lax.all_to_all(copies, axes, split_axis=0, concat_axis=0, tiled=True)]
    reduce_sum x1, other arithmetic: 0.1 us -> 9.14 us  [places(): entry = jnp.sum(chosen * order, axis=2)]
    ppermute x5, waiting for transfers between devices: 128 us -> 136 us  [shifted(): lax.ppermute(value, axis, [(i, (i + steps) % count) for i in range(count)])]
    all_to_all x4, waiting for transfers between devices: 45.3 us -> 39.1 us  [exchanged(): return lax.all_to_all(value, axes, split_axis=0, concat_axis=0, tiled=True)]
  transfers between devices with their start and end apart: 11 -> 11, of which waited for: 5 -> 5; matrix products, arithmetic and copies ran while one was open for 8% -> 7% of each run, Pallas kernels for 24% -> 22%
where the time goes in v3:
time: 469 us; the launch traced here: 467 us
  waiting for transfers between devices  175 us (37%)
  Pallas kernels  117 us (25%)
  blocking collectives  86.7 us (18%)
  starting transfers between devices  49.8 us (11%)
  other arithmetic  23.7 us (5%)
  local copies, waits for them, and re-layouts  12.9 us (3%)
    ppermute x5, waiting for transfers between devices, shifted(): lax.ppermute(value, axis, [(i, (i + steps) % count) for i in range(count)])  136 us
    all_to_all x2, blocking collectives, exchanged(): return lax.all_to_all(value, axes, split_axis=0, concat_axis=0, tiled=True)  67.6 us
    all_to_all x4, waiting for transfers between devices, exchanged(): return lax.all_to_all(value, axes, split_axis=0, concat_axis=0, tiled=True)  39.1 us
    pallas_call x4, Pallas kernels, products(): pl.pallas_call(functools.partial(product_kernel, base), grid_spec=pltpu.P...  37.5 us
    pallas_call x4, Pallas kernels, left_products(): pl.pallas_call(functools.partial(left_kernel, group), grid_spec=pltpu.Pre...  35.7 us
    pallas_call x4, Pallas kernels, gather(): pl.pallas_call(functools.partial(gather_kernel, group), grid_spec=pltpu.P...  29.9 us
    all_to_all x4, starting transfers between devices, exchanged(): return lax.all_to_all(value, axes, split_axis=0, concat_axis=0, tiled=True)  26.4 us
    all_to_all x1, blocking collectives, to_all(): return lax.all_to_all(copies, axes, split_axis=0, concat_axis=0, tiled=True)  19.1 us
  transfers between devices with their start and end apart: 11, of which 5 were waited for; matrix products, arithmetic and copies ran while one was open for 7% of the time, Pallas kernels for 22%

profile of v3, /device:TPU:0, one launch (start us, length us, event | category | flops | bytes accessed | tf_op | source)
XLA Modules:
  0.0 466.8 jit_solution(13682449063355156109)
XLA Ops:
  0.6 0.8 copy.107
  1.4 0.8 add_convert_fusion
  2.8 7.1 %all-to-all-start = ((f32[16,1,72]{2,1,0:T(1,128)}), f32[16,1,72]{2,1,0:T(1,128)S(1)}, u32[]{:S(2)}, u32[]{:S(2)}) async-start(f32[16,1,72]{2,1,0:T(1,128)} %broadcast_in_dim.89), calls=%async_computation | async-start | bytes 16384 | tf_op jit(solution)/shard_map/all_to_all | solution.py:281
  10.0 1.9 collective-permute-start.1
  11.9 6.1 %shard_map.104 = (bf16[8,2,128,256]{3,2,1,0:T(8,128)(2,1)}, bf16[8,2,128,256]{3,2,1,0:T(8,128)(2,1)}) custom-call(f32[8,512,128]{2,1,0:T(8,128)} %bitcast.111), custom_call_target="tpu_custom_call" | custom-call | tf_op jit(solution)/shard_map/pallas_call | solution.py:51
  18.0 0.8 reshape.682
  18.8 1.3 reshape.685.rate_ref
  20.1 1.3 pad_add_fusion.5.table
  21.4 8.9 %shard_map.107 = f32[2,8,256,256]{3,2,1,0:T(8,128)} custom-call(s32[72]{0:T(128)} %pad_add_fusion.5.table, f32[8,2,4,256,256]{4,3,2,1,0:T(8,128)} %bitcast.99, bf16[8,2,128,256]{3,2,1,0:T(8,128)(2,1)} %get-tuple-element.13.high_ref, bf16[8,2,128,256]{3,2,1,0:T(8,128)(2,1)} %get-tuple-element.14.low_ref, f32[16,1,256]{2,1,0:T(1,128)} %reshape.685.rate_ref), custom_call_target="tpu_custom_call" | custom-call | flops 1610612736 | bytes 12582912 | tf_op jit(solution)/shard_map/pallas_call | solution.py:77
  30.3 1.5 collective-permute-start.3
  32.2 9.0 %shard_map.111.t_ref = f32[2,8,256,256]{3,2,1,0:T(8,128)} custom-call(s32[72]{0:T(128)} %pad_add_fusion.5.table, f32[8,2,4,256,256]{4,3,2,1,0:T(8,128)} %bitcast.100, bf16[8,2,128,256]{3,2,1,0:T(8,128)(2,1)} %get-tuple-element.13.high_ref, bf16[8,2,128,256]{3,2,1,0:T(8,128)(2,1)} %get-tuple-element.14.low_ref, f32[16,1,256]{2,1,0:T(1,128)} %reshape.685.rate_ref), custom_call_target="tpu_custom_call" | custom-call | flops 1610612736 | bytes 12582912 | tf_op jit(solution)/shard_map/pallas_call | solution.py:77
  42.6 1.1 broadcast_in_dim.90
  43.6 5.3 %all-to-all-start.1 = ((f32[8,136,256]{2,1,0:T(8,128)}), f32[8,136,256]{2,1,0:T(8,128)S(1)}, u32[]{:S(2)}, u32[]{:S(2)}) async-start(f32[8,136,256]{2,1,0:T(8,128)} %broadcast_in_dim.90), calls=%async_computation.1 | async-start | bytes 2228224 | tf_op jit(solution)/shard_map/all_to_all | solution.py:281
  50.3 0.7 reshape.681.table
  50.9 7.7 %collective-permute-done.1.far_ref = f32[8,512,128]{2,1,0:T(8,128)S(1)} collective-permute-done((f32[8,512,128]{2,1,0:T(8,128)}, f32[8,512,128]{2,1,0:T(8,128)S(1)}, u32[]{:S(2)}, u32[]{:S(2)}) %collective-permute-start.1) | collective-permute-done | bytes 2097184 | tf_op jit(solution)/shard_map/ppermute | solution.py:321
  58.6 1.4 copy-done.1
  60.0 9.4 %shard_map.112 = f32[8,2,2,2,128,128]{5,4,3,2,1,0:T(8,128)} custom-call(s32[208]{0:T(256)} %reshape.681.table, f32[2,8,256,256]{3,2,1,0:T(8,128)} %shard_map.111.t_ref, f32[8,512,128]{2,1,0:T(8,128)} %bitcast.112, f32[8,512,128]{2,1,0:T(8,128)} %copy-done.1), custom_call_target="tpu_custom_call" | custom-call | flops 1610612736 | bytes 12582912 | tf_op jit(solution)/shard_map/pallas_call | solution.py:144
  69.4 7.1 %all-to-all-start.5 = ((f32[32,2,128,128]{3,2,1,0:T(8,128)}), f32[32,2,128,128]{3,2,1,0:T(8,128)}, u32[]{:S(2)}, u32[]{:S(2)}) async-start(f32[32,2,128,128]{3,2,1,0:T(8,128)} %bitcast.114), calls=%async_computation.5 | async-start | bytes 8388608 | tf_op jit(solution)/shard_map/all_to_all | solution.py:325
  76.5 1.8 collective-permute-start.2
  78.3 8.9 %shard_map.109 = f32[2,8,256,256]{3,2,1,0:T(8,128)} custom-call(s32[72]{0:T(128)} %pad_add_fusion.5.table, f32[8,2,4,256,256]{4,3,2,1,0:T(8,128)} %bitcast.101, bf16[8,2,128,256]{3,2,1,0:T(8,128)(2,1)} %get-tuple-element.13.high_ref, bf16[8,2,128,256]{3,2,1,0:T(8,128)(2,1)} %get-tuple-element.14.low_ref, f32[16,1,256]{2,1,0:T(1,128)} %reshape.685.rate_ref), custom_call_target="tpu_custom_call" | custom-call | flops 1610612736 | bytes 12582912 | tf_op jit(solution)/shard_map/pallas_call | solution.py:77
  87.2 2.7 collective-permute-start.4
  90.0 81.3 %collective-permute-done.2 = f32[8,512,128]{2,1,0:T(8,128)} collective-permute-done((f32[8,512,128]{2,1,0:T(8,128)}, f32[8,512,128]{2,1,0:T(8,128)}, u32[]{:S(2)}, u32[]{:S(2)}) %collective-permute-start.2) | collective-permute-done | bytes 2097184 | tf_op jit(solution)/shard_map/ppermute | solution.py:321
  171.3 5.5 %pad_maximum_fusion.near_ref.far_ref = f32[24,512,128]{2,1,0:T(8,128)} fusion(f32[8,512,128]{2,1,0:T(8,128)} %collective-permute-done.2, f32[8,512,128]{2,1,0:T(8,128)} %copy-done.1, f32[8,512,128]{2,1,0:T(8,128)S(1)} %bitcast.113), kind=kLoop, calls=%fused_computation | loop fusion | flops 3145728 | bytes 12582912 | tf_op jit(solution)/shard_map/concatenate | solution.py:393
  176.8 9.4 %shard_map.108 = f32[8,2,2,2,128,128]{5,4,3,2,1,0:T(8,128)} custom-call(s32[208]{0:T(256)} %reshape.681.table, f32[2,8,256,256]{3,2,1,0:T(8,128)} %collective-permute-done.3.t_ref, f32[24,512,128]{2,1,0:T(8,128)} %pad_maximum_fusion.near_ref.far_ref, f32[24,512,128]{2,1,0:T(8,128)} %pad_maximum_fusion.near_ref.far_ref), custom_call_target="tpu_custom_call" | custom-call | flops 1610612736 | bytes 12582912 | tf_op jit(solution)/shard_map/pallas_call | solution.py:144
  186.2 6.3 %all-to-all-start.3 = ((f32[32,2,128,128]{3,2,1,0:T(8,128)}), f32[32,2,128,128]{3,2,1,0:T(8,128)}, u32[]{:S(2)}, u32[]{:S(2)}) async-start(f32[32,2,128,128]{3,2,1,0:T(8,128)} %bitcast.117), calls=%async_computation.3 | async-start | bytes 8388608 | tf_op jit(solution)/shard_map/all_to_all | solution.py:325
  192.6 8.9 %shard_map.105 = f32[2,8,256,256]{3,2,1,0:T(8,128)} custom-call(s32[72]{0:T(128)} %pad_add_fusion.5.table, f32[8,2,4,256,256]{4,3,2,1,0:T(8,128)} %bitcast.102, bf16[8,2,128,256]{3,2,1,0:T(8,128)(2,1)} %get-tuple-element.13.high_ref, bf16[8,2,128,256]{3,2,1,0:T(8,128)(2,1)} %get-tuple-element.14.low_ref, f32[16,1,256]{2,1,0:T(1,128)} %reshape.685.rate_ref), custom_call_target="tpu_custom_call" | custom-call | flops 1610612736 | bytes 12582912 | tf_op jit(solution)/shard_map/pallas_call | solution.py:77
  201.5 3.0 collective-permute-start
  204.5 9.4 %shard_map.110 = f32[8,2,2,2,128,128]{5,4,3,2,1,0:T(8,128)} custom-call(s32[208]{0:T(256)} %reshape.681.table, f32[2,8,256,256]{3,2,1,0:T(8,128)} %collective-permute-done.4.t_ref, f32[24,512,128]{2,1,0:T(8,128)} %pad_maximum_fusion.near_ref.far_ref, f32[24,512,128]{2,1,0:T(8,128)} %pad_maximum_fusion.near_ref.far_ref), custom_call_target="tpu_custom_call" | custom-call | flops 1610612736 | bytes 12582912 | tf_op jit(solution)/shard_map/pallas_call | solution.py:144
  213.8 29.4 %all-to-all-done.3 = f32[32,2,128,128]{3,2,1,0:T(8,128)} async-done(((f32[32,2,128,128]{3,2,1,0:T(8,128)}), f32[32,2,128,128]{3,2,1,0:T(8,128)}, u32[]{:S(2)}, u32[]{:S(2)}) %all-to-all-start.3) | async-done | bytes 4194336 | tf_op jit(solution)/shard_map/all_to_all | solution.py:325
  243.3 5.4 %all-to-all-start.4 = ((f32[32,2,128,128]{3,2,1,0:T(8,128)}), f32[32,2,128,128]{3,2,1,0:T(8,128)}, u32[]{:S(2)}, u32[]{:S(2)}) async-start(f32[32,2,128,128]{3,2,1,0:T(8,128)} %bitcast.115), calls=%async_computation.4 | async-start | bytes 8388608 | tf_op jit(solution)/shard_map/all_to_all | solution.py:325
  248.9 47.1 %collective-permute-done.t_ref = f32[2,8,256,256]{3,2,1,0:T(8,128)} collective-permute-done((f32[2,8,256,256]{3,2,1,0:T(8,128)}, f32[2,8,256,256]{3,2,1,0:T(8,128)}, u32[]{:S(2)}, u32[]{:S(2)}) %collective-permute-start) | collective-permute-done | bytes 4194336 | tf_op jit(solution)/shard_map/ppermute | solution.py:321
  296.0 9.4 %shard_map.106 = f32[8,2,2,2,128,128]{5,4,3,2,1,0:T(8,128)} custom-call(s32[208]{0:T(256)} %reshape.681.table, f32[2,8,256,256]{3,2,1,0:T(8,128)} %collective-permute-done.t_ref, f32[24,512,128]{2,1,0:T(8,128)} %pad_maximum_fusion.near_ref.far_ref, f32[24,512,128]{2,1,0:T(8,128)} %pad_maximum_fusion.near_ref.far_ref), custom_call_target="tpu_custom_call" | custom-call | flops 1610612736 | bytes 12582912 | tf_op jit(solution)/shard_map/pallas_call | solution.py:144
  305.4 7.6 %all-to-all-start.2 = ((f32[32,2,128,128]{3,2,1,0:T(8,128)}), f32[32,2,128,128]{3,2,1,0:T(8,128)}, u32[]{:S(2)}, u32[]{:S(2)}) async-start(f32[32,2,128,128]{3,2,1,0:T(8,128)} %bitcast.116), calls=%async_computation.2 | async-start | bytes 8388608 | tf_op jit(solution)/shard_map/all_to_all | solution.py:325
  314.1 1.4 reduce_window_sum.13
  316.5 9.1 %fusion.8 = (s32[8,16]{1,0:T(8,128)S(1)}, s32[8,16]{1,0:T(8,128)S(1)}, s32[8,16]{1,0:T(8,128)S(1)}, s32[8,16]{1,0:T(8,128)S(1)}) fusion(s32[8,2]{1,0:T(8,128)S(1)} %multiply_add_fusion, s32[8,16,8,2]{3,2,1,0:T(8,128)S(1)} %copy.111, s32[8,16,8,9]{3,2,1,0:T(8,128)S(1)} %reshape.674, s32[]{:T(128)S(6)} %add.320), kind=kLoop, calls=%fused_computation.18 | loop fusion | flops 69120 | bytes 18500 | tf_op jit(solution)/shard_map/reduce_sum | solution.py:297
  327.6 1.1 slice.83
  328.8 0.6 add_add_fusion.3.table
  330.0 0.7 add_add_fusion.1.table
  331.3 7.6 %shard_map.113 = (f32[4,4,1024,128]{3,2,1,0:T(8,128)}, f32[4,4,128,256]{3,2,1,0:T(8,128)}, f32[128,256]{1,0:T(8,128)}) custom-call(s32[66]{0:T(128)} %add_add_fusion.3.table, f32[64,128,128]{2,1,0:T(8,128)} %bitcast.30.got_ref, f32[1024,256]{1,0:T(8,128)} %bitcast.106), custom_call_target="tpu_custom_call" | custom-call | flops 805306368 | bytes 10485760 | tf_op jit(solution)/shard_map/pallas_call | solution.py:220
  338.9 7.4 %shard_map.114 = (f32[4,4,1024,128]{3,2,1,0:T(8,128)}, f32[4,4,128,256]{3,2,1,0:T(8,128)}, f32[128,256]{1,0:T(8,128)}) custom-call(s32[66]{0:T(128)} %add_add_fusion.2.table, f32[64,128,128]{2,1,0:T(8,128)} %bitcast.27.got_ref, f32[1024,256]{1,0:T(8,128)} %bitcast.107, ...), custom_call_target="tpu_custom_call", output_to_operand_aliasing={{0}: (3, {}), {1}: (4, {})} | custom-call | flops 805306368 | bytes 10485760 | tf_op jit(solution)/shard_map/pallas_call | solution.py:220
  346.3 7.4 %shard_map.115 = (f32[4,4,1024,128]{3,2,1,0:T(8,128)}, f32[4,4,128,256]{3,2,1,0:T(8,128)}, f32[128,256]{1,0:T(8,128)}) custom-call(s32[66]{0:T(128)} %add_add_fusion.1.table, f32[64,128,128]{2,1,0:T(8,128)} %bitcast.24.got_ref, f32[1024,256]{1,0:T(8,128)} %bitcast.108, ...), custom_call_target="tpu_custom_call", output_to_operand_aliasing={{0}: (3, {}), {1}: (4, {})} | custom-call | flops 805306368 | bytes 10485760 | tf_op jit(solution)/shard_map/pallas_call | solution.py:220
  353.7 9.7 %all-to-all-done.2 = f32[32,2,128,128]{3,2,1,0:T(8,128)} async-done(((f32[32,2,128,128]{3,2,1,0:T(8,128)}), f32[32,2,128,128]{3,2,1,0:T(8,128)}, u32[]{:S(2)}, u32[]{:S(2)}) %all-to-all-start.2) | async-done | bytes 4194336 | tf_op jit(solution)/shard_map/all_to_all | solution.py:325
  363.4 7.4 %shard_map.116 = (f32[4,4,1024,128]{3,2,1,0:T(8,128)}, f32[4,4,128,256]{3,2,1,0:T(8,128)}, f32[128,256]{1,0:T(8,128)}) custom-call(s32[66]{0:T(128)} %add_add_fusion.table, f32[64,128,128]{2,1,0:T(8,128)} %bitcast.20.got_ref, f32[1024,256]{1,0:T(8,128)} %bitcast.109, ...), custom_call_target="tpu_custom_call", output_to_operand_aliasing={{0}: (3, {}), {1}: (4, {})} | custom-call | flops 805306368 | bytes 10485760 | tf_op jit(solution)/shard_map/pallas_call | solution.py:220
  370.9 35.4 %all_to_all.49 = f32[16,128,256]{2,1,0:T(8,128)S(1)} all-to-all(f32[16,128,256]{2,1,0:T(8,128)} %bitcast.105), channel_id=1, replica_groups=mesh['z'=4,'core'=2,'x'=4,'y'=4] {'x','y'}, dimensions={0} | all-to-all | bytes 4194304 | tf_op jit(solution)/shard_map/all_to_all | solution.py:325
  406.5 19.1 %all_to_all.50 = f32[8,128,256]{2,1,0:T(8,128)} all-to-all(f32[8,128,256]{2,1,0:T(8,128)S(1)} %broadcast_in_dim.171), channel_id=1, replica_groups=mesh['z'=4,'core'=2,'x'=4,'y'=4] {'z','core'}, dimensions={0} | all-to-all | bytes 2097152 | tf_op jit(solution)/shard_map/all_to_all | solution.py:281
  425.6 8.2 %shard_map.117 = f32[2048,256]{1,0:T(8,128)} custom-call(f32[16384,128]{1,0:T(8,128)} %bitcast.103, f32[1024,256]{1,0:T(8,128)} %bitcast.120), custom_call_target="tpu_custom_call" | custom-call | tf_op jit(solution)/shard_map/pallas_call | solution.py:266
  433.8 32.2 %all_to_all.51 = f32[16,128,256]{2,1,0:T(8,128)S(1)} all-to-all(f32[16,128,256]{2,1,0:T(8,128)} %bitcast.118), channel_id=1, replica_groups=mesh['z'=4,'core'=2,'x'=4,'y'=4] {'x','y'}, dimensions={0} | all-to-all | bytes 4194304 | tf_op jit(solution)/shard_map/all_to_all | solution.py:325
  466.1 0.7 divide_add_fusion
  (98 shorter events, 9.5 us)
Async XLA Ops:
  2.8 38.4 %all-to-all-start = ((f32[16,1,72]{2,1,0:T(1,128)}), f32[16,1,72]{2,1,0:T(1,128)S(1)}, u32[]{:S(2)}, u32[]{:S(2)}) async-start(f32[16,1,72]{2,1,0:T(1,128)} %broadcast_in_dim.89), calls=%async_computation | async-start | bytes 16384 | tf_op jit(solution)/shard_map/all_to_all | solution.py:281
  10.0 48.6 %collective-permute-start.1 = (f32[8,512,128]{2,1,0:T(8,128)}, f32[8,512,128]{2,1,0:T(8,128)S(1)}, u32[]{:S(2)}, u32[]{:S(2)}) collective-permute-start(f32[8,512,128]{2,1,0:T(8,128)} %bitcast.110), channel_id=1, source_target_pairs={{0,4},{4,8},{8,12},{12,0},{1,5},{5,9},{9,13},{13,1},{2,6},{6,10},{... | collective-permute-start | bytes 6291464 | tf_op jit(solution)/shard_map/ppermute | solution.py:321
  30.3 146.5 %collective-permute-start.3 = (f32[2,8,256,256]{3,2,1,0:T(8,128)}, f32[2,8,256,256]{3,2,1,0:T(8,128)}, u32[]{:S(2)}, u32[]{:S(2)}) collective-permute-start(f32[2,8,256,256]{3,2,1,0:T(8,128)} %shard_map.107), channel_id=1, source_target_pairs={{0,1},{1,2},{2,3},{3,0},{4,5},{5,6},{6,7},{7,4},{8,9},{9,10},{10,1... | collective-permute-start | bytes 12582920 | tf_op jit(solution)/shard_map/ppermute | solution.py:321
  32.2 10.4 %copy-start.4 = (f32[128,256]{1,0:T(8,128)S(1)}, f32[128,256]{1,0:T(8,128)}, u32[]{:S(2)}) copy-start(f32[128,256]{1,0:T(8,128)} %param.17) | copy-start | bytes 393220
  43.6 25.8 %all-to-all-start.1 = ((f32[8,136,256]{2,1,0:T(8,128)}), f32[8,136,256]{2,1,0:T(8,128)S(1)}, u32[]{:S(2)}, u32[]{:S(2)}) async-start(f32[8,136,256]{2,1,0:T(8,128)} %broadcast_in_dim.90), calls=%async_computation.1 | async-start | bytes 2228224 | tf_op jit(solution)/shard_map/all_to_all | solution.py:281
  58.6 1.4 copy-start.1
  69.4 116.8 %all-to-all-start.5 = ((f32[32,2,128,128]{3,2,1,0:T(8,128)}), f32[32,2,128,128]{3,2,1,0:T(8,128)}, u32[]{:S(2)}, u32[]{:S(2)}) async-start(f32[32,2,128,128]{3,2,1,0:T(8,128)} %bitcast.114), calls=%async_computation.5 | async-start | bytes 8388608 | tf_op jit(solution)/shard_map/all_to_all | solution.py:325
  76.5 94.8 %copy-start = (f32[8,256,2,128]{3,2,1,0:T(2,128)S(1)}, f32[8,256,2,128]{3,2,1,0:T(2,128)}, u32[]{:S(2)}) copy-start(f32[8,256,2,128]{3,2,1,0:T(2,128)} %param.11) | copy-start | bytes 6291460
  76.5 94.8 %collective-permute-start.2 = (f32[8,512,128]{2,1,0:T(8,128)}, f32[8,512,128]{2,1,0:T(8,128)}, u32[]{:S(2)}, u32[]{:S(2)}) collective-permute-start(f32[8,512,128]{2,1,0:T(8,128)} %copy-done.1), channel_id=1, source_target_pairs={{0,4},{4,8},{8,12},{12,0},{1,5},{5,9},{9,13},{13,1},{2,6},{6,10},{... | collective-permute-start | bytes 6291464 | tf_op jit(solution)/shard_map/ppermute | solution.py:321
  87.2 117.2 %collective-permute-start.4 = (f32[2,8,256,256]{3,2,1,0:T(8,128)}, f32[2,8,256,256]{3,2,1,0:T(8,128)}, u32[]{:S(2)}, u32[]{:S(2)}) collective-permute-start(f32[2,8,256,256]{3,2,1,0:T(8,128)} %shard_map.109), channel_id=1, source_target_pairs={{0,3},{1,0},{2,1},{3,2},{4,7},{5,4},{6,5},{7,6},{8,11},{9,8},{10,9... | collective-permute-start | bytes 12582920 | tf_op jit(solution)/shard_map/ppermute | solution.py:321
  186.2 57.0 %all-to-all-start.3 = ((f32[32,2,128,128]{3,2,1,0:T(8,128)}), f32[32,2,128,128]{3,2,1,0:T(8,128)}, u32[]{:S(2)}, u32[]{:S(2)}) async-start(f32[32,2,128,128]{3,2,1,0:T(8,128)} %bitcast.117), calls=%async_computation.3 | async-start | bytes 8388608 | tf_op jit(solution)/shard_map/all_to_all | solution.py:325
  201.5 94.5 %collective-permute-start = (f32[2,8,256,256]{3,2,1,0:T(8,128)}, f32[2,8,256,256]{3,2,1,0:T(8,128)}, u32[]{:S(2)}, u32[]{:S(2)}) collective-permute-start(f32[2,8,256,256]{3,2,1,0:T(8,128)} %shard_map.105), channel_id=1, source_target_pairs={{0,2},{1,3},{2,0},{3,1},{4,6},{5,7},{6,4},{7,5},{8,10},{9,11},{10,... | collective-permute-start | bytes 12582920 | tf_op jit(solution)/shard_map/ppermute | solution.py:321
  243.3 62.1 %all-to-all-start.4 = ((f32[32,2,128,128]{3,2,1,0:T(8,128)}), f32[32,2,128,128]{3,2,1,0:T(8,128)}, u32[]{:S(2)}, u32[]{:S(2)}) async-start(f32[32,2,128,128]{3,2,1,0:T(8,128)} %bitcast.115), calls=%async_computation.4 | async-start | bytes 8388608 | tf_op jit(solution)/shard_map/all_to_all | solution.py:325
  305.4 58.1 %all-to-all-start.2 = ((f32[32,2,128,128]{3,2,1,0:T(8,128)}), f32[32,2,128,128]{3,2,1,0:T(8,128)}, u32[]{:S(2)}, u32[]{:S(2)}) async-start(f32[32,2,128,128]{3,2,1,0:T(8,128)} %bitcast.116), calls=%async_computation.2 | async-start | bytes 8388608 | tf_op jit(solution)/shard_map/all_to_all | solution.py:325
  370.8 35.5 %copy-start.2 = (f32[128,256]{1,0:T(8,128)S(1)}, f32[128,256]{1,0:T(8,128)}, u32[]{:S(2)}) copy-start(f32[128,256]{1,0:T(8,128)} %param.16) | copy-start | bytes 393220
  370.9 35.5 %copy-start.3 = (f32[128,256]{1,0:T(8,128)S(1)}, f32[128,256]{1,0:T(8,128)}, u32[]{:S(2)}) copy-start(f32[128,256]{1,0:T(8,128)} %get-tuple-element.23) | copy-start | bytes 393220

commit v4 on v3

--- a/solution.py
+++ b/solution.py
@@ -38,123 +38,120 @@
     return jnp.dot(left, right, preferred_element_type=f32)
 
 
-def transpose_kernel(p_ref, high_ref, low_ref):
-    for m in range(KP):
-        high, low = split(p_ref[0, pl.ds(m, BS, KP), :].T)
-        high_ref[0, m] = high
-        low_ref[0, m] = low
-
-
-def transposed(own_p):
-    shape = jax.ShapeDtypeStruct((NB, KP, CB, BS), bf16)
-    spec = pl.BlockSpec((1, KP, CB, BS), lambda s: (s, 0, 0, 0))
-    return pl.pallas_call(
-        transpose_kernel,
-        grid=(NB,),
-        in_specs=[pl.BlockSpec((1, KP * BS, CB), lambda s: (s, 0, 0))],
-        out_specs=[spec, spec],
-        out_shape=[shape, shape],
-    )(own_p)
-
-
-def left_kernel(group, table, a_ref, high_ref, low_ref, rate_ref, out_ref):
-    s = pl.program_id(0)
-    parts = []
-    for k2 in range(PAIR):
-        block = a_ref[0, k2, 0] * table[s * KA + group + GROUP * k2].astype(f32)
-        if group == 0 and k2 == 0:
-            across = lax.broadcasted_iota(jnp.int32, (BS, BS), 0)
-            along = lax.broadcasted_iota(jnp.int32, (BS, BS), 1)
-            block = block + jnp.where(across == along, rate_ref[0], 0.0)
-        parts.append(split(block))
-    left = (high_ref[0].reshape(KP * CB, BS), low_ref[0].reshape(KP * CB, BS))
-    for k2 in range(PAIR):
-        out_ref[k2, 0] = dot3(left, parts[k2])
-
-
-def left_products(group, table, a_blocks, high, low, rates):
-    half = pl.BlockSpec((1, KP, CB, BS), lambda s, t: (s, 0, 0, 0))
-    return pl.pallas_call(
-        functools.partial(left_kernel, group),
+STEP = 2
+
+
+def left_kernel(group, flips, table, a_ref, rate_a, rate_b, *rest):
+    if flips:
+        p_ref, out_ref, high_ref, low_ref = rest
+    else:
+        high_ref, low_ref, out_ref = rest
+    step = pl.program_id(0)
+    for r, rate_ref in enumerate((rate_a, rate_b)):
+        s = step * STEP + r
+        if flips:
+            for m in range(KP):
+                high, low = split(p_ref[r, pl.ds(m, BS, KP), :].T)
+                high_ref[r, m * CB : (m + 1) * CB] = high
+                low_ref[r, m * CB : (m + 1) * CB] = low
+        for k2 in range(PAIR):
+            block = a_ref[r, k2, 0] * table[s * KA + group + GROUP * k2].astype(f32)
+            if group == 0 and k2 == 0:
+                across = lax.broadcasted_iota(jnp.int32, (BS, BS), 0)
+                along = lax.broadcasted_iota(jnp.int32, (BS, BS), 1)
+                block = block + jnp.where(across == along, rate_ref[0], 0.0)
+            out_ref[k2, r] = dot3((high_ref[r], low_ref[r]), split(block))
+
+
+def left_products(group, table, a_blocks, rates, own_p, parts):
+    half = pl.BlockSpec((STEP, KP * CB, BS), lambda s, t: (s, 0, 0))
+    halves = [jax.ShapeDtypeStruct((NB, KP * CB, BS), bf16)] * 2
+    flips = parts is None
+    rate = lambda r: pl.BlockSpec((1, 1, BS), lambda s, t: (t[NB * KA + s * STEP + r], 0, 0))
+    results = pl.pallas_call(
+        functools.partial(left_kernel, group, flips),
         grid_spec=pltpu.PrefetchScalarGridSpec(
             num_scalar_prefetch=1,
-            grid=(NB,),
+            grid=(NB // STEP,),
             in_specs=[
-                pl.BlockSpec((1, PAIR, 1, BS, BS), lambda s, t: (s, 0, group, 0, 0)),
-                half,
-                half,
-                pl.BlockSpec((1, 1, BS), lambda s, t: (t[NB * KA + s], 0, 0)),
-            ],
-            out_specs=pl.BlockSpec((PAIR, 1, KP * CB, BS), lambda s, t: (0, s, 0, 0)),
-        ),
-        out_shape=jax.ShapeDtypeStruct((PAIR, NB, KP * CB, BS), f32),
+                pl.BlockSpec((STEP, PAIR, 1, BS, BS), lambda s, t: (s, 0, group, 0, 0)),
+                rate(0),
+                rate(1),
+            ]
+            + ([pl.BlockSpec((STEP, KP * BS, CB), lambda s, t: (s, 0, 0))] if flips else [half, half]),
+            out_specs=[pl.BlockSpec((PAIR, STEP, KP * CB, BS), lambda s, t: (0, s, 0, 0))]
+            + ([half, half] if flips else []),
+        ),
+        out_shape=[jax.ShapeDtypeStruct((PAIR, NB, KP * CB, BS), f32)] + (halves if flips else []),
         cost_estimate=pl.CostEstimate(
             flops=NB * PAIR * 3 * 2 * BS**3,
             bytes_accessed=4 * PAIR * NB * 3 * BS * BS,
             transcendentals=0,
         ),
-    )(table, a_blocks.reshape(NB, PAIR, GROUP, BS, BS), high, low, rates)
+    )(table, a_blocks.reshape(NB, PAIR, GROUP, BS, BS), rates, rates, *([own_p] if flips else parts))
+    return results[0], (list(results[1:]) if flips else parts)
 
 
 ROW_AT, SLOT_AT, PARITY_AT, HALF_AT, PICK_AT, TABLE = 0, 16, 32, 34, 36, 52
 
 
-def product_kernel(base, table, t_ref, near_ref, far_ref, out_ref, held, sems):
-    s = pl.program_id(0)
-    now = lax.rem(s, 2)
-
-    def copy(step, m):
+def product_kernel(base, table, t_ref, *rest):
+    sources, (out_ref, held, sems) = rest[: PAIR * STEP], rest[PAIR * STEP :]
+    step = pl.program_id(0)
+
+    def copy(step, r, m):
+        entry = (step * STEP + r) * KP + m
         return pltpu.make_async_copy(
-            held.at[lax.rem(step, 2), m],
-            out_ref.at[
-                table[base + ROW_AT + step * KP + m], :, :, table[base + SLOT_AT + step * KP + m]
-            ],
-            sems.at[lax.rem(step, 2), m],
+            held.at[lax.rem(step, 2), r, m],
+            out_ref.at[table[base + ROW_AT + entry], :, :, table[base + SLOT_AT + entry]],
+            sems.at[lax.rem(step, 2), r, m],
         )
 
-    @pl.when(s >= 2)
+    def each(step, act):
+        for r in range(STEP):
+            for m in range(KP):
+                act(copy(step, r, m))
+
+    @pl.when(step >= 2)
     def _():
-        for m in range(KP):
-            copy(s - 2, m).wait()
-
-    for k2, ref in enumerate((near_ref, far_ref)):
-        ghost = jnp.concatenate(
-            [ref[0, pl.ds(0, BS, KP), :], ref[0, pl.ds(1, BS, KP), :]], axis=1
-        )
-        result = dot3(split(t_ref[k2, 0]), split(ghost))
-        half, parity = table[base + HALF_AT + k2], table[base + PARITY_AT + k2]
-        for m in range(KP):
-            held[now, m, half, parity] = result[m * CB : (m + 1) * CB, :CB]
-            held[now, m, 1 - half, parity] = result[m * CB : (m + 1) * CB, CB:]
-    for m in range(KP):
-        copy(s, m).start()
-
-    @pl.when(s == NB - 1)
+        each(step - 2, lambda c: c.wait())
+
+    now = lax.rem(step, 2)
+    for r in range(STEP):
+        for k2 in range(PAIR):
+            ref = sources[r * PAIR + k2]
+            ghost = jnp.concatenate(
+                [ref[0, pl.ds(0, BS, KP), :], ref[0, pl.ds(1, BS, KP), :]], axis=1
+            )
+            result = dot3(split(t_ref[k2, r]), split(ghost))
+            half, parity = table[base + HALF_AT + k2], table[base + PARITY_AT + k2]
+            for m in range(KP):
+                held[now, r, m, half, parity] = result[m * CB : (m + 1) * CB, :CB]
+                held[now, r, m, 1 - half, parity] = result[m * CB : (m + 1) * CB, CB:]
+    each(step, lambda c: c.start())
+
+    @pl.when(step == NB // STEP - 1)
     def _():
-        for step in (NB - 2, NB - 1):
-            for m in range(KP):
-                copy(step, m).wait()
+        each(NB // STEP - 2, lambda c: c.wait())
+        each(NB // STEP - 1, lambda c: c.wait())
 
 
 def products(group, table, left, near, far):
     base = group * TABLE
-    source = lambda k2: pl.BlockSpec(
-        (1, KP * BS, CB), lambda s, t: (t[base + PICK_AT + k2 * NB + s], 0, 0)
+    source = lambda r, k2: pl.BlockSpec(
+        (1, KP * BS, CB), lambda s, t: (t[base + PICK_AT + k2 * NB + s * STEP + r], 0, 0)
     )
     return pl.pallas_call(
         functools.partial(product_kernel, base),
         grid_spec=pltpu.PrefetchScalarGridSpec(
             num_scalar_prefetch=1,
-            grid=(NB,),
-            in_specs=[
-                pl.BlockSpec((PAIR, 1, KP * CB, BS), lambda s, t: (0, s, 0, 0)),
-                source(0),
-                source(1),
-            ],
+            grid=(NB // STEP,),
+            in_specs=[pl.BlockSpec((PAIR, STEP, KP * CB, BS), lambda s, t: (0, s, 0, 0))]
+            + [source(r, k2) for r in range(STEP) for k2 in range(PAIR)],
             out_specs=pl.BlockSpec(memory_space=pl.ANY),
             scratch_shapes=[
-                pltpu.VMEM((2, KP, 2, 2, CB, CB), f32),
-                pltpu.SemaphoreType.DMA((2, KP)),
+                pltpu.VMEM((2, STEP, KP, 2, 2, CB, CB), f32),
+                pltpu.SemaphoreType.DMA((2, STEP, KP)),
             ],
         ),
         out_shape=jax.ShapeDtypeStruct((N_ROW, 2, 2, 2, CB, CB), f32),
@@ -163,7 +160,7 @@
             bytes_accessed=4 * PAIR * NB * 3 * BS * BS,
             transcendentals=0,
         ),
-    )(table, left, near, far)
+    )(table, left, *[near, far] * STEP)
 
 
 STEPS = 4
@@ -326,6 +323,7 @@
 
 
 META = KP + KA - 1
+RELAYED = 2
 
 
 def product_tables(cells, x, y):
@@ -371,15 +369,16 @@
     metas = packed[:, CB:].reshape(N_ROW, spare * NCOL)[:, : cells.size]
     metas = (metas + 0.5).astype(jnp.int32).reshape(N_ROW, N_COL, NB, META)
 
-    high, low = transposed(own_p)
+    p_back = shifted(own_p[RELAYED:], "x", -1)
+    p_rear = shifted(p_back, "x", -1)
+    p_far = shifted(p_one[:RELAYED], "x", 1)
+    parts = None
     numbers = jnp.concatenate([a_live.reshape(-1), policy])
     rate_rows = rates.reshape(-1, 1, BS)
     lefts = {}
     for group in (1, 3, 2, 0):
-        left = left_products(group, numbers, a_blocks, high, low, rate_rows)
+        left, parts = left_products(group, numbers, a_blocks, rate_rows, own_p, parts)
         lefts[group] = shifted(left, "y", -group) if group else left
-    p_two = shifted(p_one, "x", 1)
-
     table = product_tables(cells, x, y)
     where = places(metas, row, col).reshape(N_ROW, N_X, N_Y, 2)
     where = where // (N_Y * N_ROW) * N_ROW + where % N_ROW
@@ -390,7 +389,7 @@
         near, far = own_p, p_one
         if group:
             if stacked is None:
-                stacked = jnp.concatenate([own_p, p_one, p_two])
+                stacked = jnp.concatenate([own_p, p_one, p_far, p_rear])
             near = far = stacked
         sent = products(group, table, lefts[group], near, far)
         got = exchanged(sent.reshape(N_ROW * N_X, 2, CB, CB), PLANE)

time: 469 us -> 570 us (1.22)
  waiting for transfers between devices: 175 us -> 294 us
  Pallas kernels: 117 us -> 97.4 us
    ppermute x5 -> x7, waiting for transfers between devices: 136 us -> 241 us  [shifted(): lax.ppermute(value, axis, [(i, (i + steps) % count) for i in range(count)])]
    all_to_all x4, waiting for transfers between devices: 39.1 us -> 52.6 us  [exchanged(): return lax.all_to_all(value, axes, split_axis=0, concat_axis=0, tiled=True)]
    pallas_call x5 -> x4, Pallas kernels: 41.8 us -> 29.1 us  [left_products(): pl.pallas_call(functools.partial(left_kernel, group, flips), grid_spec=pl...]
    pallas_call x4, Pallas kernels: 37.5 us -> 30.3 us  [products(): pl.pallas_call(functools.partial(product_kernel, base), grid_spec=pltpu.P...]
    ppermute x5 -> x7, starting transfers between devices: 10.9 us -> 14.3 us  [shifted(): lax.ppermute(value, axis, [(i, (i + steps) % count) for i in range(count)])]
  transfers between devices with their start and end apart: 11 -> 13, of which waited for: 5 -> 7; matrix products, arithmetic and copies ran while one was open for 7% -> 5% of each run, Pallas kernels for 22% -> 14%
where the time goes in v4:
time: 570 us; the launch traced here: 568 us
  waiting for transfers between devices  294 us (52%)
  Pallas kernels  97.4 us (17%)
  blocking collectives  87.3 us (15%)
  starting transfers between devices  53.3 us (9%)
  other arithmetic  21 us (4%)
  local copies, waits for them, and re-layouts  14 us (2%)
    ppermute x7, waiting for transfers between devices, shifted(): lax.ppermute(value, axis, [(i, (i + steps) % count) for i in range(count)])  241 us
    all_to_all x2, blocking collectives, exchanged(): return lax.all_to_all(value, axes, split_axis=0, concat_axis=0, tiled=True)  68.2 us
    all_to_all x4, waiting for transfers between devices, exchanged(): return lax.all_to_all(value, axes, split_axis=0, concat_axis=0, tiled=True)  52.6 us
    pallas_call x4, Pallas kernels, products(): pl.pallas_call(functools.partial(product_kernel, base), grid_spec=pltpu.P...  30.3 us
    pallas_call x4, Pallas kernels, gather(): pl.pallas_call(functools.partial(gather_kernel, group), grid_spec=pltpu.P...  29.9 us
    pallas_call x4, Pallas kernels, left_products(): pl.pallas_call(functools.partial(left_kernel, group, flips), grid_spec=pl...  29.1 us
    all_to_all x4, starting transfers between devices, exchanged(): return lax.all_to_all(value, axes, split_axis=0, concat_axis=0, tiled=True)  26.7 us
    all_to_all x1, blocking collectives, to_all(): return lax.all_to_all(copies, axes, split_axis=0, concat_axis=0, tiled=True)  19.1 us
  transfers between devices with their start and end apart: 13, of which 7 were waited for; matrix products, arithmetic and copies ran while one was open for 5% of the time, Pallas kernels for 14%

profile of v4, /device:TPU:0, one launch (start us, length us, event | category | flops | bytes accessed | tf_op | source)
XLA Modules:
  0.0 568.2 jit_solution(13620485134377718286)
XLA Ops:
  0.6 0.8 copy.107
  1.4 0.8 add_convert_fusion
  2.8 7.1 %all-to-all-start = ((f32[16,1,72]{2,1,0:T(1,128)}), f32[16,1,72]{2,1,0:T(1,128)S(1)}, u32[]{:S(2)}, u32[]{:S(2)}) async-start(f32[16,1,72]{2,1,0:T(1,128)} %broadcast_in_dim.89), calls=%async_computation | async-start | bytes 16384 | tf_op jit(solution)/shard_map/all_to_all | solution.py:278
  10.0 1.9 collective-permute-start.1
  11.9 0.8 reshape.683
  12.7 1.3 reshape.685.rate_a.rate_b
  14.0 1.3 pad_add_fusion.5.table
  15.3 7.8 %shard_map.104 = (f32[2,8,256,256]{3,2,1,0:T(8,128)}, bf16[8,256,256]{2,1,0:T(8,128)(2,1)}, bf16[8,256,256]{2,1,0:T(8,128)(2,1)}) custom-call(s32[72]{0:T(128)} %pad_add_fusion.5.table, f32[8,2,4,256,256]{4,3,2,1,0:T(8,128)} %bitcast.100, f32[16,1,256]{2,1,0:T(1,128)} %reshape.685.rate_a.rate_b, f32[16,1,256]{2,1,0:T(1,128)} %reshape.685.rate_a.rate_b, ...), custom_call_target="tpu_custom_call" | custom-call | flops 1610612736 | bytes 12582912 | tf_op jit(solution)/shard_map/pallas_call | solution.py:71
  23.1 7.0 %shard_map.107 = f32[2,8,256,256]{3,2,1,0:T(8,128)} custom-call(s32[72]{0:T(128)} %pad_add_fusion.5.table, f32[8,2,4,256,256]{4,3,2,1,0:T(8,128)} %bitcast.101, f32[16,1,256]{2,1,0:T(1,128)} %reshape.685.rate_a.rate_b, f32[16,1,256]{2,1,0:T(1,128)} %reshape.685.rate_a.rate_b, bf16[8,256,256]{2,1,0:T(8,128)(2,1)} %get-tuple-element.14.rest_0_, ...), custom_call_target="tpu_custom_call" | custom-call | flops 1610612736 | bytes 12582912 | tf_op jit(solution)/shard_map/pallas_call | solution.py:71
  30.2 1.5 collective-permute-start.5
  32.1 7.2 %shard_map.110.t_ref = f32[2,8,256,256]{3,2,1,0:T(8,128)} custom-call(s32[72]{0:T(128)} %pad_add_fusion.5.table, f32[8,2,4,256,256]{4,3,2,1,0:T(8,128)} %bitcast.102, f32[16,1,256]{2,1,0:T(1,128)} %reshape.685.rate_a.rate_b, f32[16,1,256]{2,1,0:T(1,128)} %reshape.685.rate_a.rate_b, bf16[8,256,256]{2,1,0:T(8,128)(2,1)} %get-tuple-element.14.rest_0_, ...), custom_call_target="tpu_custom_call" | custom-call | flops 1610612736 | bytes 12582912 | tf_op jit(solution)/shard_map/pallas_call | solution.py:71
  40.7 1.1 broadcast_in_dim.90
  41.8 5.3 all-to-all-start.1
  49.0 9.6 %collective-permute-done.1.rest_1_.rest_3_ = f32[8,512,128]{2,1,0:T(8,128)S(1)} collective-permute-done((f32[8,512,128]{2,1,0:T(8,128)}, f32[8,512,128]{2,1,0:T(8,128)S(1)}, u32[]{:S(2)}, u32[]{:S(2)}) %collective-permute-start.1) | collective-permute-done | bytes 2097184 | tf_op jit(solution)/shard_map/ppermute | solution.py:318
  58.6 1.4 copy-done.1
  60.0 7.6 %shard_map.111 = f32[8,2,2,2,128,128]{5,4,3,2,1,0:T(8,128)} custom-call(s32[208]{0:T(256)} %reshape.682.table, f32[2,8,256,256]{3,2,1,0:T(8,128)} %shard_map.110.t_ref, f32[8,512,128]{2,1,0:T(8,128)} %bitcast.108, f32[8,512,128]{2,1,0:T(8,128)} %copy-done.1, f32[8,512,128]{2,1,0:T(8,128)} %bitcast.109, f32[8,512,128]{2,1,0:T(8,128)} %copy-done.1), custom_call_target="tpu_custom_call" | custom-call | flops 1610612736 | bytes 12582912 | tf_op jit(solution)/shard_map/pallas_call | solution.py:144
  67.6 7.2 %all-to-all-start.5 = ((f32[32,2,128,128]{3,2,1,0:T(8,128)}), f32[32,2,128,128]{3,2,1,0:T(8,128)}, u32[]{:S(2)}, u32[]{:S(2)}) async-start(f32[32,2,128,128]{3,2,1,0:T(8,128)} %bitcast.119), calls=%async_computation.5 | async-start | bytes 8388608 | tf_op jit(solution)/shard_map/all_to_all | solution.py:322
  75.0 3.0 collective-permute-start.3
  78.0 79.7 %collective-permute-done.3 = f32[6,512,128]{2,1,0:T(8,128)S(1)} collective-permute-done((f32[6,512,128]{2,1,0:T(8,128)S(1)}, f32[6,512,128]{2,1,0:T(8,128)S(1)}, u32[]{:S(2)}, u32[]{:S(2)}) %collective-permute-start.3) | collective-permute-done | bytes 1572896 | tf_op jit(solution)/shard_map/ppermute | solution.py:318
  157.7 0.8 collective-permute-start.4
  158.5 1.1 slice.95
  159.6 1.3 collective-permute-start.2
  160.9 2.8 collective-permute-start.6
  163.7 10.3 %collective-permute-done.2 = f32[2,512,128]{2,1,0:T(8,128)S(1)} collective-permute-done((f32[2,512,128]{2,1,0:T(8,128)S(1)}, f32[2,512,128]{2,1,0:T(8,128)S(1)}, u32[]{:S(2)}, u32[]{:S(2)}) %collective-permute-start.2) | collective-permute-done | bytes 524320 | tf_op jit(solution)/shard_map/ppermute | solution.py:318
  173.9 19.6 %collective-permute-done.4 = f32[6,512,128]{2,1,0:T(8,128)S(1)} collective-permute-done((f32[6,512,128]{2,1,0:T(8,128)S(1)}, f32[6,512,128]{2,1,0:T(8,128)S(1)}, u32[]{:S(2)}, u32[]{:S(2)}) %collective-permute-start.4) | collective-permute-done | bytes 1572896 | tf_op jit(solution)/shard_map/ppermute | solution.py:318
  193.6 2.9 pad_maximum_fusion.rest_0_.rest_1_.rest_2_.rest_3_
  196.5 7.6 %shard_map.108 = f32[8,2,2,2,128,128]{5,4,3,2,1,0:T(8,128)} custom-call(s32[208]{0:T(256)} %reshape.682.table, f32[2,8,256,256]{3,2,1,0:T(8,128)} %collective-permute-done.5.t_ref, f32[24,512,128]{2,1,0:T(8,128)} %pad_maximum_fusion.rest_0_.rest_1_.rest_2_.rest_3_, f32[24,512,128]{2,1,0:T(8,128)} %pad_maximum_fusion.rest_0_.rest_1_.rest_2_.rest_3_, ...), custom_call_target="tpu_custom_call" | custom-call | flops 1610612736 | bytes 12582912 | tf_op jit(solution)/shard_map/pallas_call | solution.py:144
  204.1 6.9 %all-to-all-start.3 = ((f32[32,2,128,128]{3,2,1,0:T(8,128)}), f32[32,2,128,128]{3,2,1,0:T(8,128)}, u32[]{:S(2)}, u32[]{:S(2)}) async-start(f32[32,2,128,128]{3,2,1,0:T(8,128)} %bitcast.118), calls=%async_computation.3 | async-start | bytes 8388608 | tf_op jit(solution)/shard_map/all_to_all | solution.py:322
  211.0 7.1 %shard_map.105 = f32[2,8,256,256]{3,2,1,0:T(8,128)} custom-call(s32[72]{0:T(128)} %pad_add_fusion.5.table, f32[8,2,4,256,256]{4,3,2,1,0:T(8,128)} %bitcast.103, f32[16,1,256]{2,1,0:T(1,128)} %reshape.685.rate_a.rate_b, f32[16,1,256]{2,1,0:T(1,128)} %reshape.685.rate_a.rate_b, bf16[8,256,256]{2,1,0:T(8,128)(2,1)} %get-tuple-element.14.rest_0_, ...), custom_call_target="tpu_custom_call" | custom-call | flops 1610612736 | bytes 12582912 | tf_op jit(solution)/shard_map/pallas_call | solution.py:71
  218.1 3.0 collective-permute-start
  221.0 121.8 %collective-permute-done.6.t_ref = f32[2,8,256,256]{3,2,1,0:T(8,128)} collective-permute-done((f32[2,8,256,256]{3,2,1,0:T(8,128)}, f32[2,8,256,256]{3,2,1,0:T(8,128)}, u32[]{:S(2)}, u32[]{:S(2)}) %collective-permute-start.6) | collective-permute-done | bytes 4194336 | tf_op jit(solution)/shard_map/ppermute | solution.py:318
  342.9 7.6 %shard_map.109 = f32[8,2,2,2,128,128]{5,4,3,2,1,0:T(8,128)} custom-call(s32[208]{0:T(256)} %reshape.682.table, f32[2,8,256,256]{3,2,1,0:T(8,128)} %collective-permute-done.6.t_ref, f32[24,512,128]{2,1,0:T(8,128)} %pad_maximum_fusion.rest_0_.rest_1_.rest_2_.rest_3_, f32[24,512,128]{2,1,0:T(8,128)} %pad_maximum_fusion.rest_0_.rest_1_.rest_2_.rest_3_, ...), custom_call_target="tpu_custom_call" | custom-call | flops 1610612736 | bytes 12582912 | tf_op jit(solution)/shard_map/pallas_call | solution.py:144
  350.4 6.9 %all-to-all-start.4 = ((f32[32,2,128,128]{3,2,1,0:T(8,128)}), f32[32,2,128,128]{3,2,1,0:T(8,128)}, u32[]{:S(2)}, u32[]{:S(2)}) async-start(f32[32,2,128,128]{3,2,1,0:T(8,128)} %bitcast.116), calls=%async_computation.4 | async-start | bytes 8388608 | tf_op jit(solution)/shard_map/all_to_all | solution.py:322
  357.6 7.6 %shard_map.106 = f32[8,2,2,2,128,128]{5,4,3,2,1,0:T(8,128)} custom-call(s32[208]{0:T(256)} %reshape.682.table, f32[2,8,256,256]{3,2,1,0:T(8,128)} %collective-permute-done.t_ref, f32[24,512,128]{2,1,0:T(8,128)} %pad_maximum_fusion.rest_0_.rest_1_.rest_2_.rest_3_, f32[24,512,128]{2,1,0:T(8,128)} %pad_maximum_fusion.rest_0_.rest_1_.rest_2_.rest_3_, ...), custom_call_target="tpu_custom_call" | custom-call | flops 1610612736 | bytes 12582912 | tf_op jit(solution)/shard_map/pallas_call | solution.py:144
  365.2 42.9 %all-to-all-done.4 = f32[32,2,128,128]{3,2,1,0:T(8,128)} async-done(((f32[32,2,128,128]{3,2,1,0:T(8,128)}), f32[32,2,128,128]{3,2,1,0:T(8,128)}, u32[]{:S(2)}, u32[]{:S(2)}) %all-to-all-start.4) | async-done | bytes 4194336 | tf_op jit(solution)/shard_map/all_to_all | solution.py:322
  408.1 5.6 all-to-all-start.2
  414.9 1.4 reduce_window_sum.13
  417.3 9.1 %fusion.8 = (s32[8,16]{1,0:T(8,128)S(1)}, s32[8,16]{1,0:T(8,128)S(1)}, s32[8,16]{1,0:T(8,128)S(1)}, s32[8,16]{1,0:T(8,128)S(1)}) fusion(s32[8,2]{1,0:T(8,128)S(1)} %multiply_add_fusion, s32[8,16,8,2]{3,2,1,0:T(8,128)S(1)} %copy.111, s32[8,16,8,9]{3,2,1,0:T(8,128)S(1)} %reshape.675, s32[]{:T(128)S(6)} %add.320), kind=kLoop, calls=%fused_computation.18 | loop fusion | flops 69120 | bytes 18500 | tf_op jit(solution)/shard_map/reduce_sum | solution.py:294
  428.4 1.1 slice.96
  432.0 7.6 %shard_map.112 = (f32[4,4,1024,128]{3,2,1,0:T(8,128)}, f32[4,4,128,256]{3,2,1,0:T(8,128)}, f32[128,256]{1,0:T(8,128)}) custom-call(s32[66]{0:T(128)} %add_add_fusion.3.table, f32[64,128,128]{2,1,0:T(8,128)} %bitcast.31.got_ref, f32[1024,256]{1,0:T(8,128)} %bitcast.112), custom_call_target="tpu_custom_call" | custom-call | flops 805306368 | bytes 10485760 | tf_op jit(solution)/shard_map/pallas_call | solution.py:217
  439.7 7.4 %shard_map.113 = (f32[4,4,1024,128]{3,2,1,0:T(8,128)}, f32[4,4,128,256]{3,2,1,0:T(8,128)}, f32[128,256]{1,0:T(8,128)}) custom-call(s32[66]{0:T(128)} %add_add_fusion.2.table, f32[64,128,128]{2,1,0:T(8,128)} %bitcast.28.got_ref, f32[1024,256]{1,0:T(8,128)} %bitcast.113, ...), custom_call_target="tpu_custom_call", output_to_operand_aliasing={{0}: (3, {}), {1}: (4, {})} | custom-call | flops 805306368 | bytes 10485760 | tf_op jit(solution)/shard_map/pallas_call | solution.py:217
  447.1 7.4 %shard_map.114 = (f32[4,4,1024,128]{3,2,1,0:T(8,128)}, f32[4,4,128,256]{3,2,1,0:T(8,128)}, f32[128,256]{1,0:T(8,128)}) custom-call(s32[66]{0:T(128)} %add_add_fusion.1.table, f32[64,128,128]{2,1,0:T(8,128)} %bitcast.25.got_ref, f32[1024,256]{1,0:T(8,128)} %bitcast.114, ...), custom_call_target="tpu_custom_call", output_to_operand_aliasing={{0}: (3, {}), {1}: (4, {})} | custom-call | flops 805306368 | bytes 10485760 | tf_op jit(solution)/shard_map/pallas_call | solution.py:217
  454.5 9.7 %all-to-all-done.2 = f32[32,2,128,128]{3,2,1,0:T(8,128)} async-done(((f32[32,2,128,128]{3,2,1,0:T(8,128)}), f32[32,2,128,128]{3,2,1,0:T(8,128)}, u32[]{:S(2)}, u32[]{:S(2)}) %all-to-all-start.2) | async-done | bytes 4194336 | tf_op jit(solution)/shard_map/all_to_all | solution.py:322
  464.2 7.4 %shard_map.115 = (f32[4,4,1024,128]{3,2,1,0:T(8,128)}, f32[4,4,128,256]{3,2,1,0:T(8,128)}, f32[128,256]{1,0:T(8,128)}) custom-call(s32[66]{0:T(128)} %add_add_fusion.table, f32[64,128,128]{2,1,0:T(8,128)} %bitcast.21.got_ref, f32[1024,256]{1,0:T(8,128)} %bitcast.115, ...), custom_call_target="tpu_custom_call", output_to_operand_aliasing={{0}: (3, {}), {1}: (4, {})} | custom-call | flops 805306368 | bytes 10485760 | tf_op jit(solution)/shard_map/pallas_call | solution.py:217
  471.6 36.0 %all_to_all.49 = f32[16,128,256]{2,1,0:T(8,128)S(1)} all-to-all(f32[16,128,256]{2,1,0:T(8,128)} %bitcast.111), channel_id=1, replica_groups=mesh['z'=4,'core'=2,'x'=4,'y'=4] {'x','y'}, dimensions={0} | all-to-all | bytes 4194304 | tf_op jit(solution)/shard_map/all_to_all | solution.py:322
  507.9 19.1 %all_to_all.50 = f32[8,128,256]{2,1,0:T(8,128)} all-to-all(f32[8,128,256]{2,1,0:T(8,128)S(1)} %broadcast_in_dim.171), channel_id=1, replica_groups=mesh['z'=4,'core'=2,'x'=4,'y'=4] {'z','core'}, dimensions={0} | all-to-all | bytes 2097152 | tf_op jit(solution)/shard_map/all_to_all | solution.py:278
  527.0 8.2 %shard_map.116 = f32[2048,256]{1,0:T(8,128)} custom-call(f32[16384,128]{1,0:T(8,128)} %bitcast.104, f32[1024,256]{1,0:T(8,128)} %bitcast.122), custom_call_target="tpu_custom_call" | custom-call | tf_op jit(solution)/shard_map/pallas_call | solution.py:263
  535.2 32.2 %all_to_all.51 = f32[16,128,256]{2,1,0:T(8,128)S(1)} all-to-all(f32[16,128,256]{2,1,0:T(8,128)} %bitcast.120), channel_id=1, replica_groups=mesh['z'=4,'core'=2,'x'=4,'y'=4] {'x','y'}, dimensions={0} | all-to-all | bytes 4194304 | tf_op jit(solution)/shard_map/all_to_all | solution.py:322
  (105 shorter events, 12.3 us)
Async XLA Ops:
  2.8 36.5 %all-to-all-start = ((f32[16,1,72]{2,1,0:T(1,128)}), f32[16,1,72]{2,1,0:T(1,128)S(1)}, u32[]{:S(2)}, u32[]{:S(2)}) async-start(f32[16,1,72]{2,1,0:T(1,128)} %broadcast_in_dim.89), calls=%async_computation | async-start | bytes 16384 | tf_op jit(solution)/shard_map/all_to_all | solution.py:278
  10.0 48.6 %collective-permute-start.1 = (f32[8,512,128]{2,1,0:T(8,128)}, f32[8,512,128]{2,1,0:T(8,128)S(1)}, u32[]{:S(2)}, u32[]{:S(2)}) collective-permute-start(f32[8,512,128]{2,1,0:T(8,128)} %bitcast.106), channel_id=1, source_target_pairs={{0,4},{4,8},{8,12},{12,0},{1,5},{5,9},{9,13},{13,1},{2,6},{6,10},{... | collective-permute-start | bytes 6291464 | tf_op jit(solution)/shard_map/ppermute | solution.py:318
  30.2 166.3 %collective-permute-start.5 = (f32[2,8,256,256]{3,2,1,0:T(8,128)}, f32[2,8,256,256]{3,2,1,0:T(8,128)}, u32[]{:S(2)}, u32[]{:S(2)}) collective-permute-start(f32[2,8,256,256]{3,2,1,0:T(8,128)} %shard_map.107), channel_id=1, source_target_pairs={{0,1},{1,2},{2,3},{3,0},{4,5},{5,6},{6,7},{7,4},{8,9},{9,10},{10,1... | collective-permute-start | bytes 12582920 | tf_op jit(solution)/shard_map/ppermute | solution.py:318
  32.1 8.5 %copy-start.5 = (f32[128,256]{1,0:T(8,128)S(1)}, f32[128,256]{1,0:T(8,128)}, u32[]{:S(2)}) copy-start(f32[128,256]{1,0:T(8,128)} %param.17) | copy-start | bytes 393220
  41.8 25.9 %all-to-all-start.1 = ((f32[8,136,256]{2,1,0:T(8,128)}), f32[8,136,256]{2,1,0:T(8,128)S(1)}, u32[]{:S(2)}, u32[]{:S(2)}) async-start(f32[8,136,256]{2,1,0:T(8,128)} %broadcast_in_dim.90), calls=%async_computation.1 | async-start | bytes 2228224 | tf_op jit(solution)/shard_map/all_to_all | solution.py:278
  58.6 1.4 copy-start.1
  67.6 7.3 %copy-start = (f32[8,256,2,128]{3,2,1,0:T(2,128)S(1)}, f32[8,256,2,128]{3,2,1,0:T(2,128)}, u32[]{:S(2)}) copy-start(f32[8,256,2,128]{3,2,1,0:T(2,128)} %param.11) | copy-start | bytes 6291460
  67.6 136.4 %all-to-all-start.5 = ((f32[32,2,128,128]{3,2,1,0:T(8,128)}), f32[32,2,128,128]{3,2,1,0:T(8,128)}, u32[]{:S(2)}, u32[]{:S(2)}) async-start(f32[32,2,128,128]{3,2,1,0:T(8,128)} %bitcast.119), calls=%async_computation.5 | async-start | bytes 8388608 | tf_op jit(solution)/shard_map/all_to_all | solution.py:322
  74.9 118.7 %copy-start.2 = (f32[8,512,128]{2,1,0:T(8,128)S(1)}, f32[8,512,128]{2,1,0:T(8,128)}, u32[]{:S(2)}) copy-start(f32[8,512,128]{2,1,0:T(8,128)} %copy-done.1) | copy-start | bytes 6291460
  75.0 82.7 %collective-permute-start.3 = (f32[6,512,128]{2,1,0:T(8,128)S(1)}, f32[6,512,128]{2,1,0:T(8,128)S(1)}, u32[]{:S(2)}, u32[]{:S(2)}) collective-permute-start(f32[6,512,128]{2,1,0:T(8,128)S(1)} %bitcast.123), channel_id=1, source_target_pairs={{0,12},{4,0},{8,4},{12,8},{1,13},{5,1},{9,5},{13,9},{2,14},{6,2},{... | collective-permute-start | bytes 4718600 | tf_op jit(solution)/shard_map/ppermute | solution.py:318
  157.7 35.8 %collective-permute-start.4 = (f32[6,512,128]{2,1,0:T(8,128)S(1)}, f32[6,512,128]{2,1,0:T(8,128)S(1)}, u32[]{:S(2)}, u32[]{:S(2)}) collective-permute-start(f32[6,512,128]{2,1,0:T(8,128)S(1)} %collective-permute-done.3), channel_id=1, source_target_pairs={{0,12},{4,0},{8,4},{12,8},{1,13},{5,1},{9,5},{13,9},{2,14},{6,2},{... | collective-permute-start | bytes 4718600 | tf_op jit(solution)/shard_map/ppermute | solution.py:318
  159.6 14.4 %collective-permute-start.2 = (f32[2,512,128]{2,1,0:T(8,128)S(1)}, f32[2,512,128]{2,1,0:T(8,128)S(1)}, u32[]{:S(2)}, u32[]{:S(2)}) collective-permute-start(f32[2,512,128]{2,1,0:T(8,128)S(1)} %slice.95), channel_id=1, source_target_pairs={{0,4},{4,8},{8,12},{12,0},{1,5},{5,9},{9,13},{13,1},{2,6},{6,10},{... | collective-permute-start | bytes 1572872 | tf_op jit(solution)/shard_map/ppermute | solution.py:318
  160.9 182.0 %collective-permute-start.6 = (f32[2,8,256,256]{3,2,1,0:T(8,128)}, f32[2,8,256,256]{3,2,1,0:T(8,128)}, u32[]{:S(2)}, u32[]{:S(2)}) collective-permute-start(f32[2,8,256,256]{3,2,1,0:T(8,128)} %get-tuple-element.16), channel_id=1, source_target_pairs={{0,3},{1,0},{2,1},{3,2},{4,7},{5,4},{6,5},{7,6},{8,11},{9,8},{10,9... | collective-permute-start | bytes 12582920 | tf_op jit(solution)/shard_map/ppermute | solution.py:318
  204.1 146.4 %all-to-all-start.3 = ((f32[32,2,128,128]{3,2,1,0:T(8,128)}), f32[32,2,128,128]{3,2,1,0:T(8,128)}, u32[]{:S(2)}, u32[]{:S(2)}) async-start(f32[32,2,128,128]{3,2,1,0:T(8,128)} %bitcast.118), calls=%async_computation.3 | async-start | bytes 8388608 | tf_op jit(solution)/shard_map/all_to_all | solution.py:322
  218.1 139.5 %collective-permute-start = (f32[2,8,256,256]{3,2,1,0:T(8,128)}, f32[2,8,256,256]{3,2,1,0:T(8,128)}, u32[]{:S(2)}, u32[]{:S(2)}) collective-permute-start(f32[2,8,256,256]{3,2,1,0:T(8,128)} %shard_map.105), channel_id=1, source_target_pairs={{0,2},{1,3},{2,0},{3,1},{4,6},{5,7},{6,4},{7,5},{8,10},{9,11},{10,... | collective-permute-start | bytes 12582920 | tf_op jit(solution)/shard_map/ppermute | solution.py:318
  350.4 57.6 %all-to-all-start.4 = ((f32[32,2,128,128]{3,2,1,0:T(8,128)}), f32[32,2,128,128]{3,2,1,0:T(8,128)}, u32[]{:S(2)}, u32[]{:S(2)}) async-start(f32[32,2,128,128]{3,2,1,0:T(8,128)} %bitcast.116), calls=%async_computation.4 | async-start | bytes 8388608 | tf_op jit(solution)/shard_map/all_to_all | solution.py:322
  408.1 56.1 %all-to-all-start.2 = ((f32[32,2,128,128]{3,2,1,0:T(8,128)}), f32[32,2,128,128]{3,2,1,0:T(8,128)}, u32[]{:S(2)}, u32[]{:S(2)}) async-start(f32[32,2,128,128]{3,2,1,0:T(8,128)} %bitcast.117), calls=%async_computation.2 | async-start | bytes 8388608 | tf_op jit(solution)/shard_map/all_to_all | solution.py:322
  471.6 36.1 %copy-start.3 = (f32[128,256]{1,0:T(8,128)S(1)}, f32[128,256]{1,0:T(8,128)}, u32[]{:S(2)}) copy-start(f32[128,256]{1,0:T(8,128)} %param.16) | copy-start | bytes 393220
  471.6 36.2 %copy-start.4 = (f32[128,256]{1,0:T(8,128)S(1)}, f32[128,256]{1,0:T(8,128)}, u32[]{:S(2)}) copy-start(f32[128,256]{1,0:T(8,128)} %get-tuple-element.25) | copy-start | bytes 393220

commit v5 on v4

--- a/solution.py
+++ b/solution.py
@@ -170,7 +170,7 @@
 
 
 def gather_kernel(group, table, got_ref, x_ref, *rest):
-    coarse_ref, part_ref, floor_ref, total, x_high, x_low = rest[-6:]
+    coarse_ref, *part_refs, floor_ref, total, x_high, x_low = rest[-(N_X + 5) :]
     step = pl.program_id(0)
 
     @pl.when(step == 0)
@@ -180,20 +180,24 @@
         x_high[...] = high
         x_low[...] = low
 
-    for b in range(PER_STEP):
-        place = table[step * PER_STEP + b]
-        total[place] += got_ref[b]
+    @pl.loop(0, PER_STEP, step=4)
+    def _(first):
+        for b in range(4):
+            place = table[step * PER_STEP + first + b]
+            total[place] += got_ref[first + b]
 
     @pl.when(step == STEPS - 1)
     def _():
         rows = []
-        for u in range(N_X):
+        for d in range(N_X):
+            u = lax.rem(table[COUNT + 2] + d, N_X)
+            blocks = [total[u * N_ROW + q] for q in range(N_ROW)]
             for q in range(N_ROW):
-                coarse_ref[u, 0, pl.ds(q, CB, N_ROW), :] = total[u * N_ROW + q]
-            rows.append(jnp.concatenate([total[u * N_ROW + q] for q in range(N_ROW)], axis=1))
+                coarse_ref[u, 0, pl.ds(q, CB, N_ROW), :] = blocks[q]
+            rows.append(jnp.concatenate(blocks, axis=1))
         result = dot3(split(jnp.concatenate(rows)), (x_high[...], x_low[...]))
-        for u in range(N_X):
-            part_ref[u, 0] = result[u * CB : (u + 1) * CB]
+        for d in range(N_X):
+            part_refs[d][...] = result[d * CB : (d + 1) * CB]
         if group == 0:
             across = lax.broadcasted_iota(jnp.int32, (CB, CB), 0)
             along = lax.broadcasted_iota(jnp.int32, (CB, CB), 1)
@@ -211,31 +215,25 @@
     args = [got, x]
     alias = {}
     if prior is not None:
-        in_specs += [pl.BlockSpec(memory_space=pl.ANY)] * 2
-        args += prior
-        alias = {3: 0, 4: 1}
-    return pl.pallas_call(
+        in_specs.append(pl.BlockSpec(memory_space=pl.ANY))
+        args.append(prior)
+        alias = {3: 0}
+    coarse, *parts, floor = pl.pallas_call(
         functools.partial(gather_kernel, group),
         grid_spec=pltpu.PrefetchScalarGridSpec(
             num_scalar_prefetch=1,
             grid=(STEPS,),
             in_specs=in_specs,
-            out_specs=[
-                pl.BlockSpec((N_X, 1, CB * N_ROW, CB), lambda i, t: (0, t[COUNT], 0, 0)),
-                pl.BlockSpec((N_X, 1, CB, NCOL), lambda i, t: (0, t[COUNT], 0, 0)),
-                whole((CB, NCOL)),
-            ],
+            out_specs=[pl.BlockSpec((N_X, 1, CB * N_ROW, CB), lambda i, t: (0, t[COUNT], 0, 0))]
+            + [whole((CB, NCOL))] * (N_X + 1),
             scratch_shapes=[
                 pltpu.VMEM((CELLS, CB, CB), f32),
                 pltpu.VMEM((N_ROW * CB, NCOL), bf16),
                 pltpu.VMEM((N_ROW * CB, NCOL), bf16),
             ],
         ),
-        out_shape=[
-            jax.ShapeDtypeStruct((N_X, N_Y, CB * N_ROW, CB), f32),
-            jax.ShapeDtypeStruct((N_X, N_Y, CB, NCOL), f32),
-            jax.ShapeDtypeStruct((CB, NCOL), f32),
-        ],
+        out_shape=[jax.ShapeDtypeStruct((N_X, N_Y, CB * N_ROW, CB), f32)]
+        + [jax.ShapeDtypeStruct((CB, NCOL), f32)] * (N_X + 1),
         input_output_aliases=alias,
         cost_estimate=pl.CostEstimate(
             flops=3 * 2 * N_X * CB * N_ROW * CB * NCOL,
@@ -243,6 +241,7 @@
             transcendentals=0,
         ),
     )(table, *args)
+    return coarse, parts, floor
 
 
 TALL = 4 * CB
@@ -318,12 +317,22 @@
     return lax.ppermute(value, axis, [(i, (i + steps) % count) for i in range(count)])
 
 
+def shifted_plane(value, x_steps, y_steps):
+    pairs = [
+        (a * N_Y + b, (a + x_steps) % N_X * N_Y + (b + y_steps) % N_Y)
+        for a in range(N_X)
+        for b in range(N_Y)
+    ]
+    return lax.ppermute(value, COL, pairs)
+
+
 def exchanged(value, axes):
     return lax.all_to_all(value, axes, split_axis=0, concat_axis=0, tiled=True)
 
 
 META = KP + KA - 1
-RELAYED = 2
+RELAYED = 4
+LAST = 2
 
 
 def product_tables(cells, x, y):
@@ -383,9 +392,10 @@
     where = places(metas, row, col).reshape(N_ROW, N_X, N_Y, 2)
     where = where // (N_Y * N_ROW) * N_ROW + where % N_ROW
     own_cell = x * N_ROW + row
-    prior = None
+    coarse = None
     stacked = None
-    for group in (0, 1, 3, 2):
+    sums = []
+    for group in (0, 1, 3, LAST):
         near, far = own_p, p_one
         if group:
             if stacked is None:
@@ -395,19 +405,25 @@
         got = exchanged(sent.reshape(N_ROW * N_X, 2, CB, CB), PLANE)
         y_u = (y + group) % N_Y
         spots = lax.dynamic_index_in_dim(where, y_u, 2, False).reshape(-1)
-        spots = jnp.concatenate([spots, jnp.stack([y_u, own_cell])])
-        coarse, part, floor = gather(group, spots, got.reshape(COUNT, CB, CB), around, prior)
+        spots = jnp.concatenate([spots, jnp.stack([y_u, own_cell, x])])
+        coarse, parts, floor = gather(group, spots, got.reshape(COUNT, CB, CB), around, coarse)
         if group == 0:
             floor_diag = floor
-        prior = [coarse, part]
+        if group != LAST:
+            stack = jnp.stack(parts)
+            sums.append(shifted(stack, "y", group) if group else stack)
+    early = sums[0] + sums[1] + sums[2]
+    applied = early[0]
+    for d in range(1, N_X):
+        applied = applied + shifted(early[d], "x", d)
+    for d in range(N_X):
+        applied = applied + shifted_plane(parts[d], d, LAST)
+    current = guess + damping * (rhs - applied) / floor_diag
+
     coarse = coarse.reshape(N_COL * CB * N_ROW, CB)
-    current = guess
-    for sweep in range(2):
-        if sweep:
-            part = apply(coarse, to_all(current, ROW, N_ROW).reshape(N_ROW * CB, NCOL))
-        pieces = exchanged(part.reshape(N_COL, CB, NCOL), COL)
-        applied = jnp.sum(pieces, axis=0)
-        current = current + damping * (rhs - applied) / floor_diag
+    part = apply(coarse, to_all(current, ROW, N_ROW).reshape(N_ROW * CB, NCOL))
+    applied = jnp.sum(exchanged(part.reshape(N_COL, CB, NCOL), COL), axis=0)
+    current = current + damping * (rhs - applied) / floor_diag
     return coarse.reshape(N_COL * CB, N_ROW, 1, CB), current
 
 

time: 570 us -> 550 us (0.965)
  blocking collectives: 87.3 us -> 57.9 us
  starting transfers between devices: 53.3 us -> 69.5 us
  waiting for transfers between devices: 294 us -> 286 us
    all_to_all x2 -> x1, blocking collectives: 68.2 us -> 35.3 us  [exchanged(): return lax.all_to_all(value, axes, split_axis=0, concat_axis=0, tiled=True)]
    ppermute x0 -> x4, starting transfers between devices: none -> 10.2 us  [shifted_plane(): return lax.ppermute(value, COL, pairs)]
    ppermute x7 -> x12, starting transfers between devices: 14.3 us -> 21.5 us  [shifted(): lax.ppermute(value, axis, [(i, (i + steps) % count) for i in range(count)])]
    ppermute x7 -> x12, waiting for transfers between devices: 241 us -> 235 us  [shifted(): lax.ppermute(value, axis, [(i, (i + steps) % count) for i in range(count)])]
  transfers between devices with their start and end apart: 13 -> 22, of which waited for: 7 -> 11; matrix products, arithmetic and copies ran while one was open for 5% -> 6% of each run, Pallas kernels for 14% -> 16%
where the time goes in v5:
time: 550 us; the launch traced here: 548 us
  waiting for transfers between devices  286 us (52%)
  Pallas kernels  96.2 us (17%)
  starting transfers between devices  69.5 us (13%)
  blocking collectives  57.9 us (11%)
  other arithmetic  23.3 us (4%)
  local copies, waits for them, and re-layouts  14.4 us (3%)
    ppermute x12, waiting for transfers between devices, shifted(): lax.ppermute(value, axis, [(i, (i + steps) % count) for i in range(count)])  235 us
    all_to_all x4, waiting for transfers between devices, exchanged(): return lax.all_to_all(value, axes, split_axis=0, concat_axis=0, tiled=True)  47.6 us
    all_to_all x1, blocking collectives, exchanged(): return lax.all_to_all(value, axes, split_axis=0, concat_axis=0, tiled=True)  35.3 us
    pallas_call x4, Pallas kernels, products(): pl.pallas_call(functools.partial(product_kernel, base), grid_spec=pltpu.P...  30.3 us
    pallas_call x4, Pallas kernels, left_products(): pl.pallas_call(functools.partial(left_kernel, group, flips), grid_spec=pl...  29 us
    pallas_call x4, Pallas kernels, gather(): pl.pallas_call(functools.partial(gather_kernel, group), grid_spec=pltpu.P...  28.8 us
    all_to_all x4, starting transfers between devices, exchanged(): return lax.all_to_all(value, axes, split_axis=0, concat_axis=0, tiled=True)  25.3 us
    all_to_all x1, blocking collectives, to_all(): return lax.all_to_all(copies, axes, split_axis=0, concat_axis=0, tiled=True)  22.7 us
  transfers between devices with their start and end apart: 22, of which 11 were waited for; matrix products, arithmetic and copies ran while one was open for 6% of the time, Pallas kernels for 16%

profile of v5, /device:TPU:0, one launch (start us, length us, event | category | flops | bytes accessed | tf_op | source)
XLA Modules:
  0.0 548.5 jit_solution(15753582382383936023)
XLA Ops:
  2.8 7.1 %all-to-all-start = ((f32[16,1,72]{2,1,0:T(1,128)}), f32[16,1,72]{2,1,0:T(1,128)S(1)}, u32[]{:S(2)}, u32[]{:S(2)}) async-start(f32[16,1,72]{2,1,0:T(1,128)} %broadcast_in_dim.89), calls=%async_computation | async-start | bytes 16384 | tf_op jit(solution)/shard_map/all_to_all | solution.py:277
  10.0 1.9 collective-permute-start.1
  12.7 1.3 reshape.682.rate_a.rate_b
  14.0 1.3 pad_add_fusion.5.table
  15.3 7.8 %shard_map.104 = (f32[2,8,256,256]{3,2,1,0:T(8,128)}, bf16[8,256,256]{2,1,0:T(8,128)(2,1)}, bf16[8,256,256]{2,1,0:T(8,128)(2,1)}) custom-call(s32[72]{0:T(128)} %pad_add_fusion.5.table, f32[8,2,4,256,256]{4,3,2,1,0:T(8,128)} %bitcast.142, f32[16,1,256]{2,1,0:T(1,128)} %reshape.682.rate_a.rate_b, f32[16,1,256]{2,1,0:T(1,128)} %reshape.682.rate_a.rate_b, ...), custom_call_target="tpu_custom_call" | custom-call | flops 1610612736 | bytes 12582912 | tf_op jit(solution)/shard_map/pallas_call | solution.py:71
  23.1 7.0 %shard_map.107 = f32[2,8,256,256]{3,2,1,0:T(8,128)} custom-call(s32[72]{0:T(128)} %pad_add_fusion.5.table, f32[8,2,4,256,256]{4,3,2,1,0:T(8,128)} %bitcast.143, f32[16,1,256]{2,1,0:T(1,128)} %reshape.682.rate_a.rate_b, f32[16,1,256]{2,1,0:T(1,128)} %reshape.682.rate_a.rate_b, bf16[8,256,256]{2,1,0:T(8,128)(2,1)} %get-tuple-element.26.rest_0_, ...), custom_call_target="tpu_custom_call" | custom-call | flops 1610612736 | bytes 12582912 | tf_op jit(solution)/shard_map/pallas_call | solution.py:71
  30.2 1.5 collective-permute-start.5
  32.1 7.2 %shard_map.110.t_ref = f32[2,8,256,256]{3,2,1,0:T(8,128)} custom-call(s32[72]{0:T(128)} %pad_add_fusion.5.table, f32[8,2,4,256,256]{4,3,2,1,0:T(8,128)} %bitcast.144, f32[16,1,256]{2,1,0:T(1,128)} %reshape.682.rate_a.rate_b, f32[16,1,256]{2,1,0:T(1,128)} %reshape.682.rate_a.rate_b, bf16[8,256,256]{2,1,0:T(8,128)(2,1)} %get-tuple-element.26.rest_0_, ...), custom_call_target="tpu_custom_call" | custom-call | flops 1610612736 | bytes 12582912 | tf_op jit(solution)/shard_map/pallas_call | solution.py:71
  42.0 5.3 all-to-all-start.1
  49.3 9.3 %collective-permute-done.1.rest_1_.rest_3_ = f32[8,512,128]{2,1,0:T(8,128)S(1)} collective-permute-done((f32[8,512,128]{2,1,0:T(8,128)}, f32[8,512,128]{2,1,0:T(8,128)S(1)}, u32[]{:S(2)}, u32[]{:S(2)}) %collective-permute-start.1) | collective-permute-done | bytes 2097184 | tf_op jit(solution)/shard_map/ppermute | solution.py:317
  58.6 1.4 copy-done.1
  60.0 7.6 %shard_map.111 = f32[8,2,2,2,128,128]{5,4,3,2,1,0:T(8,128)} custom-call(s32[208]{0:T(256)} %reshape.679.table, f32[2,8,256,256]{3,2,1,0:T(8,128)} %shard_map.110.t_ref, f32[8,512,128]{2,1,0:T(8,128)} %bitcast.150, f32[8,512,128]{2,1,0:T(8,128)} %copy-done.1, f32[8,512,128]{2,1,0:T(8,128)} %bitcast.151, f32[8,512,128]{2,1,0:T(8,128)} %copy-done.1), custom_call_target="tpu_custom_call" | custom-call | flops 1610612736 | bytes 12582912 | tf_op jit(solution)/shard_map/pallas_call | solution.py:144
  67.6 7.2 %all-to-all-start.5 = ((f32[32,2,128,128]{3,2,1,0:T(8,128)}), f32[32,2,128,128]{3,2,1,0:T(8,128)}, u32[]{:S(2)}, u32[]{:S(2)}) async-start(f32[32,2,128,128]{3,2,1,0:T(8,128)} %bitcast.160), calls=%async_computation.5 | async-start | bytes 8388608 | tf_op jit(solution)/shard_map/all_to_all | solution.py:330
  75.0 3.0 collective-permute-start.3
  78.0 68.5 %collective-permute-done.3 = f32[4,512,128]{2,1,0:T(8,128)S(1)} collective-permute-done((f32[4,512,128]{2,1,0:T(8,128)S(1)}, f32[4,512,128]{2,1,0:T(8,128)S(1)}, u32[]{:S(2)}, u32[]{:S(2)}) %collective-permute-start.3) | collective-permute-done | bytes 1048608 | tf_op jit(solution)/shard_map/ppermute | solution.py:317
  147.2 1.3 slice.111
  148.5 1.3 collective-permute-start.2
  149.9 2.8 collective-permute-start.6
  152.6 18.5 %collective-permute-done.4 = f32[4,512,128]{2,1,0:T(8,128)S(1)} collective-permute-done((f32[4,512,128]{2,1,0:T(8,128)S(1)}, f32[4,512,128]{2,1,0:T(8,128)S(1)}, u32[]{:S(2)}, u32[]{:S(2)}) %collective-permute-start.4) | collective-permute-done | bytes 1048608 | tf_op jit(solution)/shard_map/ppermute | solution.py:317
  171.1 3.0 collective-permute-done.2
  174.1 2.9 pad_maximum_fusion.rest_0_.rest_1_.rest_2_.rest_3_
  177.0 7.6 %shard_map.108 = f32[8,2,2,2,128,128]{5,4,3,2,1,0:T(8,128)} custom-call(s32[208]{0:T(256)} %reshape.679.table, f32[2,8,256,256]{3,2,1,0:T(8,128)} %collective-permute-done.5.t_ref, f32[24,512,128]{2,1,0:T(8,128)} %pad_maximum_fusion.rest_0_.rest_1_.rest_2_.rest_3_, f32[24,512,128]{2,1,0:T(8,128)} %pad_maximum_fusion.rest_0_.rest_1_.rest_2_.rest_3_, ...), custom_call_target="tpu_custom_call" | custom-call | flops 1610612736 | bytes 12582912 | tf_op jit(solution)/shard_map/pallas_call | solution.py:144
  184.6 5.5 %all-to-all-start.3 = ((f32[32,2,128,128]{3,2,1,0:T(8,128)}), f32[32,2,128,128]{3,2,1,0:T(8,128)}, u32[]{:S(2)}, u32[]{:S(2)}) async-start(f32[32,2,128,128]{3,2,1,0:T(8,128)} %bitcast.159), calls=%async_computation.3 | async-start | bytes 8388608 | tf_op jit(solution)/shard_map/all_to_all | solution.py:330
  190.2 7.0 %shard_map.105 = f32[2,8,256,256]{3,2,1,0:T(8,128)} custom-call(s32[72]{0:T(128)} %pad_add_fusion.5.table, f32[8,2,4,256,256]{4,3,2,1,0:T(8,128)} %bitcast.145, f32[16,1,256]{2,1,0:T(1,128)} %reshape.682.rate_a.rate_b, f32[16,1,256]{2,1,0:T(1,128)} %reshape.682.rate_a.rate_b, bf16[8,256,256]{2,1,0:T(8,128)(2,1)} %get-tuple-element.26.rest_0_, ...), custom_call_target="tpu_custom_call" | custom-call | flops 1610612736 | bytes 12582912 | tf_op jit(solution)/shard_map/pallas_call | solution.py:71
  197.2 3.0 collective-permute-start
  200.2 131.7 %collective-permute-done.6.t_ref = f32[2,8,256,256]{3,2,1,0:T(8,128)} collective-permute-done((f32[2,8,256,256]{3,2,1,0:T(8,128)}, f32[2,8,256,256]{3,2,1,0:T(8,128)}, u32[]{:S(2)}, u32[]{:S(2)}) %collective-permute-start.6) | collective-permute-done | bytes 4194336 | tf_op jit(solution)/shard_map/ppermute | solution.py:317
  331.8 7.6 %shard_map.109 = f32[8,2,2,2,128,128]{5,4,3,2,1,0:T(8,128)} custom-call(s32[208]{0:T(256)} %reshape.679.table, f32[2,8,256,256]{3,2,1,0:T(8,128)} %collective-permute-done.6.t_ref, f32[24,512,128]{2,1,0:T(8,128)} %pad_maximum_fusion.rest_0_.rest_1_.rest_2_.rest_3_, f32[24,512,128]{2,1,0:T(8,128)} %pad_maximum_fusion.rest_0_.rest_1_.rest_2_.rest_3_, ...), custom_call_target="tpu_custom_call" | custom-call | flops 1610612736 | bytes 12582912 | tf_op jit(solution)/shard_map/pallas_call | solution.py:144
  339.4 6.9 %all-to-all-start.4 = ((f32[32,2,128,128]{3,2,1,0:T(8,128)}), f32[32,2,128,128]{3,2,1,0:T(8,128)}, u32[]{:S(2)}, u32[]{:S(2)}) async-start(f32[32,2,128,128]{3,2,1,0:T(8,128)} %bitcast.157), calls=%async_computation.4 | async-start | bytes 8388608 | tf_op jit(solution)/shard_map/all_to_all | solution.py:330
  347.6 7.6 %shard_map.106 = f32[8,2,2,2,128,128]{5,4,3,2,1,0:T(8,128)} custom-call(s32[208]{0:T(256)} %reshape.679.table, f32[2,8,256,256]{3,2,1,0:T(8,128)} %collective-permute-done.t_ref, f32[24,512,128]{2,1,0:T(8,128)} %pad_maximum_fusion.rest_0_.rest_1_.rest_2_.rest_3_, f32[24,512,128]{2,1,0:T(8,128)} %pad_maximum_fusion.rest_0_.rest_1_.rest_2_.rest_3_, ...), custom_call_target="tpu_custom_call" | custom-call | flops 1610612736 | bytes 12582912 | tf_op jit(solution)/shard_map/pallas_call | solution.py:144
  355.2 41.9 %all-to-all-done.4 = f32[32,2,128,128]{3,2,1,0:T(8,128)} async-done(((f32[32,2,128,128]{3,2,1,0:T(8,128)}), f32[32,2,128,128]{3,2,1,0:T(8,128)}, u32[]{:S(2)}, u32[]{:S(2)}) %all-to-all-start.4) | async-done | bytes 4194336 | tf_op jit(solution)/shard_map/all_to_all | solution.py:330
  397.0 5.6 %all-to-all-start.2 = ((f32[32,2,128,128]{3,2,1,0:T(8,128)}), f32[32,2,128,128]{3,2,1,0:T(8,128)}, u32[]{:S(2)}, u32[]{:S(2)}) async-start(f32[32,2,128,128]{3,2,1,0:T(8,128)} %bitcast.158), calls=%async_computation.2 | async-start | bytes 8388608 | tf_op jit(solution)/shard_map/all_to_all | solution.py:330
  402.8 1.4 reduce_window_sum.13
  405.2 9.1 %fusion.8 = (s32[8,16]{1,0:T(8,128)S(1)}, s32[8,16]{1,0:T(8,128)S(1)}, s32[8,16]{1,0:T(8,128)S(1)}, s32[8,16]{1,0:T(8,128)S(1)}) fusion(s32[8,2]{1,0:T(8,128)S(1)} %multiply_add_fusion, s32[8,16,8,2]{3,2,1,0:T(8,128)S(1)} %copy.108, s32[8,16,8,9]{3,2,1,0:T(8,128)S(1)} %reshape.672, s32[]{:T(128)S(6)} %add.347), kind=kLoop, calls=%fused_computation.18 | loop fusion | flops 69120 | bytes 18500 | tf_op jit(solution)/shard_map/reduce_sum | solution.py:293
  419.0 7.1 %shard_map.112 = (f32[4,4,1024,128]{3,2,1,0:T(8,128)}, f32[128,256]{1,0:T(8,128)}, f32[128,256]{1,0:T(8,128)}, f32[128,256]{1,0:T(8,128)}, f32[128,256]{1,0:T(8,128)}, /*index=5*/f32[128,256]{1,0:T(8,128)}) custom-call(s32[67]{0:T(128)} %add_add_fusion.3.table, f32[64,128,128]{2,1,0:T(8,128)} %bitcast.32.got_ref, f32[1024,256]{1,0:T(8,128)} %bitcast.153), custom_call_target="tpu_custom_call" | custom-call | flops 805306368 | bytes 10485760 | tf_op jit(solution)/shard_map/pallas_call | solution.py:221
  426.1 7.3 %shard_map.113 = (f32[4,4,1024,128]{3,2,1,0:T(8,128)}, f32[128,256]{1,0:T(8,128)}, f32[128,256]{1,0:T(8,128)}, f32[128,256]{1,0:T(8,128)}, f32[128,256]{1,0:T(8,128)}, /*index=5*/f32[128,256]{1,0:T(8,128)}) custom-call(s32[67]{0:T(128)} %add_add_fusion.2.table, f32[64,128,128]{2,1,0:T(8,128)} %bitcast.29.got_ref, ...), custom_call_target="tpu_custom_call", output_to_operand_aliasing={{0}: (3, {})} | custom-call | flops 805306368 | bytes 10485760 | tf_op jit(solution)/shard_map/pallas_call | solution.py:221
  434.6 7.1 %shard_map.114 = (f32[4,4,1024,128]{3,2,1,0:T(8,128)}, f32[128,256]{1,0:T(8,128)}, f32[128,256]{1,0:T(8,128)}, f32[128,256]{1,0:T(8,128)}, f32[128,256]{1,0:T(8,128)}, /*index=5*/f32[128,256]{1,0:T(8,128)}) custom-call(s32[67]{0:T(128)} %add_add_fusion.1.table, f32[64,128,128]{2,1,0:T(8,128)} %bitcast.26.got_ref, ...), custom_call_target="tpu_custom_call", output_to_operand_aliasing={{0}: (3, {})} | custom-call | flops 805306368 | bytes 10485760 | tf_op jit(solution)/shard_map/pallas_call | solution.py:221
  442.9 3.7 collective-permute-start.8
  447.4 5.7 %all-to-all-done.2 = f32[32,2,128,128]{3,2,1,0:T(8,128)} async-done(((f32[32,2,128,128]{3,2,1,0:T(8,128)}), f32[32,2,128,128]{3,2,1,0:T(8,128)}, u32[]{:S(2)}, u32[]{:S(2)}) %all-to-all-start.2) | async-done | bytes 4194336 | tf_op jit(solution)/shard_map/all_to_all | solution.py:330
  453.2 7.2 %shard_map.115 = (f32[4,4,1024,128]{3,2,1,0:T(8,128)}, f32[128,256]{1,0:T(8,128)}, f32[128,256]{1,0:T(8,128)}, f32[128,256]{1,0:T(8,128)}, f32[128,256]{1,0:T(8,128)}, /*index=5*/f32[128,256]{1,0:T(8,128)}) custom-call(s32[67]{0:T(128)} %add_add_fusion.table, f32[64,128,128]{2,1,0:T(8,128)} %bitcast.22.got_ref, ...), custom_call_target="tpu_custom_call", output_to_operand_aliasing={{0}: (3, {})} | custom-call | flops 805306368 | bytes 10485760 | tf_op jit(solution)/shard_map/pallas_call | solution.py:221
  460.4 3.4 collective-permute-start.13
  463.8 1.8 collective-permute-start.14
  465.7 4.9 collective-permute-start.15
  470.9 3.2 collective-permute-start.11
  474.7 2.4 collective-permute-done.15
  477.7 3.6 collective-permute-done.10
  481.5 22.7 %all_to_all.44 = f32[8,128,256]{2,1,0:T(8,128)} all-to-all(f32[8,128,256]{2,1,0:T(8,128)S(1)} %broadcast_in_dim.171), channel_id=1, replica_groups=mesh['z'=4,'core'=2,'x'=4,'y'=4] {'z','core'}, dimensions={0} | all-to-all | bytes 2097152 | tf_op jit(solution)/shard_map/all_to_all | solution.py:277
  504.2 8.2 %shard_map.116 = f32[2048,256]{1,0:T(8,128)} custom-call(f32[16384,128]{1,0:T(8,128)} %bitcast.146, f32[1024,256]{1,0:T(8,128)} %bitcast.163), custom_call_target="tpu_custom_call" | custom-call | tf_op jit(solution)/shard_map/pallas_call | solution.py:262
  512.4 35.3 %all_to_all.45 = f32[16,128,256]{2,1,0:T(8,128)S(1)} all-to-all(f32[16,128,256]{2,1,0:T(8,128)} %bitcast.161), channel_id=1, replica_groups=mesh['z'=4,'core'=2,'x'=4,'y'=4] {'x','y'}, dimensions={0} | all-to-all | bytes 4194304 | tf_op jit(solution)/shard_map/all_to_all | solution.py:330
  (133 shorter events, 21.3 us)
Async XLA Ops:
  2.8 36.5 %all-to-all-start = ((f32[16,1,72]{2,1,0:T(1,128)}), f32[16,1,72]{2,1,0:T(1,128)S(1)}, u32[]{:S(2)}, u32[]{:S(2)}) async-start(f32[16,1,72]{2,1,0:T(1,128)} %broadcast_in_dim.89), calls=%async_computation | async-start | bytes 16384 | tf_op jit(solution)/shard_map/all_to_all | solution.py:277
  10.0 48.6 %collective-permute-start.1 = (f32[8,512,128]{2,1,0:T(8,128)}, f32[8,512,128]{2,1,0:T(8,128)S(1)}, u32[]{:S(2)}, u32[]{:S(2)}) collective-permute-start(f32[8,512,128]{2,1,0:T(8,128)} %bitcast.148), channel_id=1, source_target_pairs={{0,4},{4,8},{8,12},{12,0},{1,5},{5,9},{9,13},{13,1},{2,6},{6,10},{... | collective-permute-start | bytes 6291464 | tf_op jit(solution)/shard_map/ppermute | solution.py:317
  30.2 146.9 %collective-permute-start.5 = (f32[2,8,256,256]{3,2,1,0:T(8,128)}, f32[2,8,256,256]{3,2,1,0:T(8,128)}, u32[]{:S(2)}, u32[]{:S(2)}) collective-permute-start(f32[2,8,256,256]{3,2,1,0:T(8,128)} %shard_map.107), channel_id=1, source_target_pairs={{0,1},{1,2},{2,3},{3,0},{4,5},{5,6},{6,7},{7,4},{8,9},{9,10},{10,1... | collective-permute-start | bytes 12582920 | tf_op jit(solution)/shard_map/ppermute | solution.py:317
  32.1 8.7 %copy-start.5 = (f32[128,256]{1,0:T(8,128)S(1)}, f32[128,256]{1,0:T(8,128)}, u32[]{:S(2)}) copy-start(f32[128,256]{1,0:T(8,128)} %param.17) | copy-start | bytes 393220
  42.0 25.6 %all-to-all-start.1 = ((f32[8,136,256]{2,1,0:T(8,128)}), f32[8,136,256]{2,1,0:T(8,128)S(1)}, u32[]{:S(2)}, u32[]{:S(2)}) async-start(f32[8,136,256]{2,1,0:T(8,128)} %broadcast_in_dim.90), calls=%async_computation.1 | async-start | bytes 2228224 | tf_op jit(solution)/shard_map/all_to_all | solution.py:277
  58.6 1.4 copy-start.1
  67.6 7.3 %copy-start = (f32[8,256,2,128]{3,2,1,0:T(2,128)S(1)}, f32[8,256,2,128]{3,2,1,0:T(2,128)}, u32[]{:S(2)}) copy-start(f32[8,256,2,128]{3,2,1,0:T(2,128)} %param.11) | copy-start | bytes 6291460
  67.6 117.0 %all-to-all-start.5 = ((f32[32,2,128,128]{3,2,1,0:T(8,128)}), f32[32,2,128,128]{3,2,1,0:T(8,128)}, u32[]{:S(2)}, u32[]{:S(2)}) async-start(f32[32,2,128,128]{3,2,1,0:T(8,128)} %bitcast.160), calls=%async_computation.5 | async-start | bytes 8388608 | tf_op jit(solution)/shard_map/all_to_all | solution.py:330
  74.9 99.3 %copy-start.2 = (f32[8,512,128]{2,1,0:T(8,128)S(1)}, f32[8,512,128]{2,1,0:T(8,128)}, u32[]{:S(2)}) copy-start(f32[8,512,128]{2,1,0:T(8,128)} %copy-done.1) | copy-start | bytes 6291460
  75.0 71.5 %collective-permute-start.3 = (f32[4,512,128]{2,1,0:T(8,128)S(1)}, f32[4,512,128]{2,1,0:T(8,128)S(1)}, u32[]{:S(2)}, u32[]{:S(2)}) collective-permute-start(f32[4,512,128]{2,1,0:T(8,128)S(1)} %bitcast.164), channel_id=1, source_target_pairs={{0,12},{4,0},{8,4},{12,8},{1,13},{5,1},{9,5},{13,9},{2,14},{6,2},{... | collective-permute-start | bytes 3145736 | tf_op jit(solution)/shard_map/ppermute | solution.py:317
  146.5 24.6 %collective-permute-start.4 = (f32[4,512,128]{2,1,0:T(8,128)S(1)}, f32[4,512,128]{2,1,0:T(8,128)S(1)}, u32[]{:S(2)}, u32[]{:S(2)}) collective-permute-start(f32[4,512,128]{2,1,0:T(8,128)S(1)} %collective-permute-done.3), channel_id=1, source_target_pairs={{0,12},{4,0},{8,4},{12,8},{1,13},{5,1},{9,5},{13,9},{2,14},{6,2},{... | collective-permute-start | bytes 3145736 | tf_op jit(solution)/shard_map/ppermute | solution.py:317
  148.5 25.6 %collective-permute-start.2 = (f32[4,512,128]{2,1,0:T(8,128)S(1)}, f32[4,512,128]{2,1,0:T(8,128)S(1)}, u32[]{:S(2)}, u32[]{:S(2)}) collective-permute-start(f32[4,512,128]{2,1,0:T(8,128)S(1)} %slice.111), channel_id=1, source_target_pairs={{0,4},{4,8},{8,12},{12,0},{1,5},{5,9},{9,13},{13,1},{2,6},{6,10},{... | collective-permute-start | bytes 3145736 | tf_op jit(solution)/shard_map/ppermute | solution.py:317
  149.9 182.0 %collective-permute-start.6 = (f32[2,8,256,256]{3,2,1,0:T(8,128)}, f32[2,8,256,256]{3,2,1,0:T(8,128)}, u32[]{:S(2)}, u32[]{:S(2)}) collective-permute-start(f32[2,8,256,256]{3,2,1,0:T(8,128)} %get-tuple-element.28), channel_id=1, source_target_pairs={{0,3},{1,0},{2,1},{3,2},{4,7},{5,4},{6,5},{7,6},{8,11},{9,8},{10,9... | collective-permute-start | bytes 12582920 | tf_op jit(solution)/shard_map/ppermute | solution.py:317
  184.6 154.8 %all-to-all-start.3 = ((f32[32,2,128,128]{3,2,1,0:T(8,128)}), f32[32,2,128,128]{3,2,1,0:T(8,128)}, u32[]{:S(2)}, u32[]{:S(2)}) async-start(f32[32,2,128,128]{3,2,1,0:T(8,128)} %bitcast.159), calls=%async_computation.3 | async-start | bytes 8388608 | tf_op jit(solution)/shard_map/all_to_all | solution.py:330
  197.2 150.4 %collective-permute-start = (f32[2,8,256,256]{3,2,1,0:T(8,128)}, f32[2,8,256,256]{3,2,1,0:T(8,128)}, u32[]{:S(2)}, u32[]{:S(2)}) collective-permute-start(f32[2,8,256,256]{3,2,1,0:T(8,128)} %shard_map.105), channel_id=1, source_target_pairs={{0,2},{1,3},{2,0},{3,1},{4,6},{5,7},{6,4},{7,5},{8,10},{9,11},{10,... | collective-permute-start | bytes 12582920 | tf_op jit(solution)/shard_map/ppermute | solution.py:317
  339.4 57.6 %all-to-all-start.4 = ((f32[32,2,128,128]{3,2,1,0:T(8,128)}), f32[32,2,128,128]{3,2,1,0:T(8,128)}, u32[]{:S(2)}, u32[]{:S(2)}) async-start(f32[32,2,128,128]{3,2,1,0:T(8,128)} %bitcast.157), calls=%async_computation.4 | async-start | bytes 8388608 | tf_op jit(solution)/shard_map/all_to_all | solution.py:330
  397.0 56.1 %all-to-all-start.2 = ((f32[32,2,128,128]{3,2,1,0:T(8,128)}), f32[32,2,128,128]{3,2,1,0:T(8,128)}, u32[]{:S(2)}, u32[]{:S(2)}) async-start(f32[32,2,128,128]{3,2,1,0:T(8,128)} %bitcast.158), calls=%async_computation.2 | async-start | bytes 8388608 | tf_op jit(solution)/shard_map/all_to_all | solution.py:330
  434.6 31.1 %collective-permute-start.7 = (f32[4,128,256]{2,1,0:T(8,128)S(1)}, f32[4,128,256]{2,1,0:T(8,128)S(1)}, u32[]{:S(2)}, u32[]{:S(2)}) collective-permute-start(f32[4,128,256]{2,1,0:T(8,128)S(1)} %pad_maximum_fusion.1), channel_id=1, source_target_pairs={{0,1},{1,2},{2,3},{3,0},{4,5},{5,6},{6,7},{7,4},{8,9},{9,10},{10,1... | collective-permute-start | bytes 1572872 | tf_op jit(solution)/shard_map/ppermute | solution.py:317
  442.9 27.7 %collective-permute-start.8 = (f32[4,128,256]{2,1,0:T(8,128)S(1)}, f32[4,128,256]{2,1,0:T(8,128)S(1)}, u32[]{:S(2)}, u32[]{:S(2)}) collective-permute-start(f32[4,128,256]{2,1,0:T(8,128)S(1)} %pad_maximum_fusion.2), channel_id=1, source_target_pairs={{0,3},{1,0},{2,1},{3,2},{4,7},{5,4},{6,5},{7,6},{8,11},{9,8},{10,9... | collective-permute-start | bytes 1572872 | tf_op jit(solution)/shard_map/ppermute | solution.py:317
  453.2 17.5 %copy-start.6 = (f32[128,256]{1,0:T(8,128)S(1)}, f32[128,256]{1,0:T(8,128)}, u32[]{:S(2)}) copy-start(f32[128,256]{1,0:T(8,128)} %get-tuple-element.33) | copy-start | bytes 393220
  453.2 17.5 %copy-start.7 = (f32[128,256]{1,0:T(8,128)S(1)}, f32[128,256]{1,0:T(8,128)}, u32[]{:S(2)}) copy-start(f32[128,256]{1,0:T(8,128)} %get-tuple-element.34) | copy-start | bytes 393220
  453.2 17.5 %copy-start.8 = (f32[128,256]{1,0:T(8,128)S(1)}, f32[128,256]{1,0:T(8,128)}, u32[]{:S(2)}) copy-start(f32[128,256]{1,0:T(8,128)} %get-tuple-element.35) | copy-start | bytes 393220
  453.2 17.5 %copy-start.9 = (f32[128,256]{1,0:T(8,128)S(1)}, f32[128,256]{1,0:T(8,128)}, u32[]{:S(2)}) copy-start(f32[128,256]{1,0:T(8,128)} %get-tuple-element.36) | copy-start | bytes 393220
  453.2 28.1 %copy-start.3 = (f32[128,256]{1,0:T(8,128)S(1)}, f32[128,256]{1,0:T(8,128)}, u32[]{:S(2)}) copy-start(f32[128,256]{1,0:T(8,128)} %param.16) | copy-start | bytes 393220
  453.2 28.1 %copy-start.4 = (f32[128,256]{1,0:T(8,128)S(1)}, f32[128,256]{1,0:T(8,128)}, u32[]{:S(2)}) copy-start(f32[128,256]{1,0:T(8,128)} %get-tuple-element.49) | copy-start | bytes 393220
  460.4 10.4 %collective-permute-start.12 = (f32[128,256]{1,0:T(8,128)}, f32[128,256]{1,0:T(8,128)S(1)}, u32[]{:S(2)}, u32[]{:S(2)}) collective-permute-start(f32[128,256]{1,0:T(8,128)} %get-tuple-element.45), channel_id=1, source_target_pairs={{0,2},{1,3},{2,0},{3,1},{4,6},{5,7},{6,4},{7,5},{8,10},{9,11},{10,... | collective-permute-start | bytes 393224 | tf_op jit(solution)/shard_map/ppermute | solution.py:326
  460.4 13.7 %collective-permute-start.13 = (f32[128,256]{1,0:T(8,128)}, f32[128,256]{1,0:T(8,128)S(1)}, u32[]{:S(2)}, u32[]{:S(2)}) collective-permute-start(f32[128,256]{1,0:T(8,128)} %get-tuple-element.46), channel_id=1, source_target_pairs={{0,6},{1,7},{2,4},{3,5},{4,10},{5,11},{6,8},{7,9},{8,14},{9,15},{1... | collective-permute-start | bytes 393224 | tf_op jit(solution)/shard_map/ppermute | solution.py:326
  463.8 10.9 %collective-permute-start.14 = (f32[128,256]{1,0:T(8,128)}, f32[128,256]{1,0:T(8,128)S(1)}, u32[]{:S(2)}, u32[]{:S(2)}) collective-permute-start(f32[128,256]{1,0:T(8,128)} %get-tuple-element.47), channel_id=1, source_target_pairs={{0,10},{1,11},{2,8},{3,9},{4,14},{5,15},{6,12},{7,13},{8,2},{9,3},... | collective-permute-start | bytes 393224 | tf_op jit(solution)/shard_map/ppermute | solution.py:326
  465.7 11.5 %collective-permute-start.15 = (f32[128,256]{1,0:T(8,128)}, f32[128,256]{1,0:T(8,128)S(1)}, u32[]{:S(2)}, u32[]{:S(2)}) collective-permute-start(f32[128,256]{1,0:T(8,128)} %get-tuple-element.48), channel_id=1, source_target_pairs={{0,14},{1,15},{2,12},{3,13},{4,2},{5,3},{6,0},{7,1},{8,6},{9,7},{1... | collective-permute-start | bytes 393224 | tf_op jit(solution)/shard_map/ppermute | solution.py:326
  470.8 6.3 %collective-permute-start.9 = (f32[128,256]{1,0:T(8,128)S(1)}, f32[128,256]{1,0:T(8,128)S(1)}, u32[]{:S(2)}, u32[]{:S(2)}) collective-permute-start(f32[128,256]{1,0:T(8,128)S(1)} %get-tuple-element.85), channel_id=1, source_target_pairs={{0,4},{4,8},{8,12},{12,0},{1,5},{5,9},{9,13},{13,1},{2,6},{6,10},{... | collective-permute-start | bytes 393224 | tf_op jit(solution)/shard_map/ppermute | solution.py:317
  470.9 6.8 %collective-permute-start.11 = (f32[128,256]{1,0:T(8,128)S(1)}, f32[128,256]{1,0:T(8,128)S(1)}, u32[]{:S(2)}, u32[]{:S(2)}) collective-permute-start(f32[128,256]{1,0:T(8,128)S(1)} %get-tuple-element.86), channel_id=1, source_target_pairs={{0,12},{4,0},{8,4},{12,8},{1,13},{5,1},{9,5},{13,9},{2,14},{6,2},{... | collective-permute-start | bytes 393224 | tf_op jit(solution)/shard_map/ppermute | solution.py:317
  474.1 7.2 %collective-permute-start.10 = (f32[128,256]{1,0:T(8,128)S(1)}, f32[128,256]{1,0:T(8,128)S(1)}, u32[]{:S(2)}, u32[]{:S(2)}) collective-permute-start(f32[128,256]{1,0:T(8,128)S(1)} %get-tuple-element.87), channel_id=1, source_target_pairs={{0,8},{4,12},{8,0},{12,4},{1,9},{5,13},{9,1},{13,5},{2,10},{6,14},... | collective-permute-start | bytes 393224 | tf_op jit(solution)/shard_map/ppermute | solution.py:317

commit v6 on v5

--- a/solution.py
+++ b/solution.py
@@ -95,15 +95,15 @@
 ROW_AT, SLOT_AT, PARITY_AT, HALF_AT, PICK_AT, TABLE = 0, 16, 32, 34, 36, 52
 
 
-def product_kernel(base, table, t_ref, *rest):
-    sources, (out_ref, held, sems) = rest[: PAIR * STEP], rest[PAIR * STEP :]
+def product_kernel(base, lane, table, t_ref, *rest):
+    sources, (out_ref, held, sems) = rest[: PAIR * STEP], rest[-3:]
     step = pl.program_id(0)
 
     def copy(step, r, m):
         entry = (step * STEP + r) * KP + m
         return pltpu.make_async_copy(
             held.at[lax.rem(step, 2), r, m],
-            out_ref.at[table[base + ROW_AT + entry], :, :, table[base + SLOT_AT + entry]],
+            out_ref.at[table[base + ROW_AT + entry], :, :, lane, table[base + SLOT_AT + entry]],
             sems.at[lax.rem(step, 2), r, m],
         )
 
@@ -136,31 +136,34 @@
         each(NB // STEP - 1, lambda c: c.wait())
 
 
-def products(group, table, left, near, far):
+def products(group, lane, lanes, table, left, near, far, prior):
+    before = [] if prior is None else [prior]
     base = group * TABLE
     source = lambda r, k2: pl.BlockSpec(
         (1, KP * BS, CB), lambda s, t: (t[base + PICK_AT + k2 * NB + s * STEP + r], 0, 0)
     )
     return pl.pallas_call(
-        functools.partial(product_kernel, base),
+        functools.partial(product_kernel, base, lane),
         grid_spec=pltpu.PrefetchScalarGridSpec(
             num_scalar_prefetch=1,
             grid=(NB // STEP,),
             in_specs=[pl.BlockSpec((PAIR, STEP, KP * CB, BS), lambda s, t: (0, s, 0, 0))]
-            + [source(r, k2) for r in range(STEP) for k2 in range(PAIR)],
+            + [source(r, k2) for r in range(STEP) for k2 in range(PAIR)]
+            + [pl.BlockSpec(memory_space=pl.ANY)] * len(before),
             out_specs=pl.BlockSpec(memory_space=pl.ANY),
             scratch_shapes=[
                 pltpu.VMEM((2, STEP, KP, 2, 2, CB, CB), f32),
                 pltpu.SemaphoreType.DMA((2, STEP, KP)),
             ],
         ),
-        out_shape=jax.ShapeDtypeStruct((N_ROW, 2, 2, 2, CB, CB), f32),
+        out_shape=jax.ShapeDtypeStruct((N_ROW, 2, 2, lanes, 2, CB, CB), f32),
+        input_output_aliases={2 + PAIR * STEP: 0} if before else {},
         cost_estimate=pl.CostEstimate(
             flops=NB * PAIR * 3 * 2 * BS**3,
             bytes_accessed=4 * PAIR * NB * 3 * BS * BS,
             transcendentals=0,
         ),
-    )(table, left, *[near, far] * STEP)
+    )(table, left, *[near, far] * STEP, *before)
 
 
 STEPS = 4
@@ -184,7 +187,7 @@
     def _(first):
         for b in range(4):
             place = table[step * PER_STEP + first + b]
-            total[place] += got_ref[first + b]
+            total[place] += got_ref[first // 2 + b // 2, 0, b % 2]
 
     @pl.when(step == STEPS - 1)
     def _():
@@ -206,10 +209,10 @@
             floor_ref[...] = jnp.broadcast_to(diag, (CB, NCOL))
 
 
-def gather(group, table, got, x, prior):
+def gather(group, lane, table, got, x, prior):
     whole = lambda shape: pl.BlockSpec(shape, lambda i, t: (0,) * len(shape))
     in_specs = [
-        pl.BlockSpec((PER_STEP, CB, CB), lambda i, t: (i, 0, 0)),
+        pl.BlockSpec((PER_STEP // 2, 1, 2, CB, CB), lambda i, t: (i, lane, 0, 0, 0)),
         whole((N_ROW * CB, NCOL)),
     ]
     args = [got, x]
@@ -395,23 +398,26 @@
     coarse = None
     stacked = None
     sums = []
-    for group in (0, 1, 3, LAST):
-        near, far = own_p, p_one
-        if group:
-            if stacked is None:
-                stacked = jnp.concatenate([own_p, p_one, p_far, p_rear])
-            near = far = stacked
-        sent = products(group, table, lefts[group], near, far)
-        got = exchanged(sent.reshape(N_ROW * N_X, 2, CB, CB), PLANE)
-        y_u = (y + group) % N_Y
-        spots = lax.dynamic_index_in_dim(where, y_u, 2, False).reshape(-1)
-        spots = jnp.concatenate([spots, jnp.stack([y_u, own_cell, x])])
-        coarse, parts, floor = gather(group, spots, got.reshape(COUNT, CB, CB), around, coarse)
-        if group == 0:
-            floor_diag = floor
-        if group != LAST:
-            stack = jnp.stack(parts)
-            sums.append(shifted(stack, "y", group) if group else stack)
+    for batch in ((0,), (1, 3), (LAST,)):
+        sent = None
+        for lane, group in enumerate(batch):
+            near, far = own_p, p_one
+            if group:
+                if stacked is None:
+                    stacked = jnp.concatenate([own_p, p_one, p_far, p_rear])
+                near = far = stacked
+            sent = products(group, lane, len(batch), table, lefts[group], near, far, sent)
+        got = exchanged(sent.reshape(N_ROW * N_X, len(batch), 2, CB, CB), PLANE)
+        for lane, group in enumerate(batch):
+            y_u = (y + group) % N_Y
+            spots = lax.dynamic_index_in_dim(where, y_u, 2, False).reshape(-1)
+            spots = jnp.concatenate([spots, jnp.stack([y_u, own_cell, x])])
+            coarse, parts, floor = gather(group, lane, spots, got, around, coarse)
+            if group == 0:
+                floor_diag = floor
+            if group != LAST:
+                stack = jnp.stack(parts)
+                sums.append(shifted(stack, "y", group) if group else stack)
     early = sums[0] + sums[1] + sums[2]
     applied = early[0]
     for d in range(1, N_X):

time: 550 us -> 458 us (0.83)
  waiting for transfers between devices: 286 us -> 206 us
  starting transfers between devices: 69.5 us -> 62.4 us
    all_to_all x4 -> x3, waiting for transfers between devices: 47.6 us -> 6 us  [exchanged(): return lax.all_to_all(value, axes, split_axis=0, concat_axis=0, tiled=True)]
    ppermute x12, waiting for transfers between devices: 235 us -> 196 us  [shifted(): lax.ppermute(value, axis, [(i, (i + steps) % count) for i in range(count)])]
    all_to_all x4 -> x3, starting transfers between devices: 25.3 us -> 20.3 us  [exchanged(): return lax.all_to_all(value, axes, split_axis=0, concat_axis=0, tiled=True)]
  transfers between devices with their start and end apart: 22 -> 21, of which waited for: 11 -> 9; matrix products, arithmetic and copies ran while one was open for 6% -> 7% of each run, Pallas kernels for 16% -> 19%
where the time goes in v6:
time: 458 us; the launch traced here: 457 us
  waiting for transfers between devices  206 us (45%)
  Pallas kernels  96.4 us (21%)
  starting transfers between devices  62.4 us (14%)
  blocking collectives  53.1 us (12%)
  other arithmetic  23.2 us (5%)
  local copies, waits for them, and re-layouts  14.4 us (3%)
    ppermute x12, waiting for transfers between devices, shifted(): lax.ppermute(value, axis, [(i, (i + steps) % count) for i in range(count)])  196 us
    all_to_all x1, blocking collectives, exchanged(): return lax.all_to_all(value, axes, split_axis=0, concat_axis=0, tiled=True)  34 us
    pallas_call x4, Pallas kernels, products(): pl.pallas_call(functools.partial(product_kernel, base, lane), grid_spec=p...  30.3 us
    pallas_call x4, Pallas kernels, left_products(): pl.pallas_call(functools.partial(left_kernel, group, flips), grid_spec=pl...  29 us
    pallas_call x4, Pallas kernels, gather(): pl.pallas_call(functools.partial(gather_kernel, group), grid_spec=pltpu.P...  28.9 us
    all_to_all x3, starting transfers between devices, exchanged(): return lax.all_to_all(value, axes, split_axis=0, concat_axis=0, tiled=True)  20.3 us
    ppermute x12, starting transfers between devices, shifted(): lax.ppermute(value, axis, [(i, (i + steps) % count) for i in range(count)])  19.6 us
    all_to_all x1, blocking collectives, to_all(): return lax.all_to_all(copies, axes, split_axis=0, concat_axis=0, tiled=True)  19.1 us
  transfers between devices with their start and end apart: 21, of which 9 were waited for; matrix products, arithmetic and copies ran while one was open for 7% of the time, Pallas kernels for 19%

profile of v6, /device:TPU:0, one launch (start us, length us, event | category | flops | bytes accessed | tf_op | source)
XLA Modules:
  0.0 456.9 jit_solution(6567299333408560648)
XLA Ops:
  2.8 7.1 %all-to-all-start = ((f32[16,1,72]{2,1,0:T(1,128)}), f32[16,1,72]{2,1,0:T(1,128)S(1)}, u32[]{:S(2)}, u32[]{:S(2)}) async-start(f32[16,1,72]{2,1,0:T(1,128)} %broadcast_in_dim.89), calls=%async_computation | async-start | bytes 16384 | tf_op jit(solution)/shard_map/all_to_all | solution.py:280
  10.0 1.9 collective-permute-start.1
  11.9 1.3 reshape.667.rate_a.rate_b
  14.0 1.3 pad_add_fusion.5.table
  15.3 7.8 %shard_map.104 = (f32[2,8,256,256]{3,2,1,0:T(8,128)}, bf16[8,256,256]{2,1,0:T(8,128)(2,1)}, bf16[8,256,256]{2,1,0:T(8,128)(2,1)}) custom-call(s32[72]{0:T(128)} %pad_add_fusion.5.table, f32[8,2,4,256,256]{4,3,2,1,0:T(8,128)} %bitcast.137, f32[16,1,256]{2,1,0:T(1,128)} %reshape.667.rate_a.rate_b, f32[16,1,256]{2,1,0:T(1,128)} %reshape.667.rate_a.rate_b, ...), custom_call_target="tpu_custom_call" | custom-call | flops 1610612736 | bytes 12582912 | tf_op jit(solution)/shard_map/pallas_call | solution.py:71
  23.1 2.7 collective-permute-start.6
  25.8 7.1 %shard_map.107 = f32[2,8,256,256]{3,2,1,0:T(8,128)} custom-call(s32[72]{0:T(128)} %pad_add_fusion.5.table, f32[8,2,4,256,256]{4,3,2,1,0:T(8,128)} %bitcast.138, f32[16,1,256]{2,1,0:T(1,128)} %reshape.667.rate_a.rate_b, f32[16,1,256]{2,1,0:T(1,128)} %reshape.667.rate_a.rate_b, bf16[8,256,256]{2,1,0:T(8,128)(2,1)} %get-tuple-element.26.rest_0_, ...), custom_call_target="tpu_custom_call" | custom-call | flops 1610612736 | bytes 12582912 | tf_op jit(solution)/shard_map/pallas_call | solution.py:71
  33.3 7.2 %shard_map.110.t_ref = f32[2,8,256,256]{3,2,1,0:T(8,128)} custom-call(s32[72]{0:T(128)} %pad_add_fusion.5.table, f32[8,2,4,256,256]{4,3,2,1,0:T(8,128)} %bitcast.139, f32[16,1,256]{2,1,0:T(1,128)} %reshape.667.rate_a.rate_b, f32[16,1,256]{2,1,0:T(1,128)} %reshape.667.rate_a.rate_b, bf16[8,256,256]{2,1,0:T(8,128)(2,1)} %get-tuple-element.26.rest_0_, ...), custom_call_target="tpu_custom_call" | custom-call | flops 1610612736 | bytes 12582912 | tf_op jit(solution)/shard_map/pallas_call | solution.py:71
  43.0 5.3 %all-to-all-start.1 = ((f32[8,136,256]{2,1,0:T(8,128)}), f32[8,136,256]{2,1,0:T(8,128)S(1)}, u32[]{:S(2)}, u32[]{:S(2)}) async-start(f32[8,136,256]{2,1,0:T(8,128)} %broadcast_in_dim.90), calls=%async_computation.1 | async-start | bytes 2228224 | tf_op jit(solution)/shard_map/all_to_all | solution.py:280
  50.3 8.3 %collective-permute-done.1.rest_1_.rest_3_ = f32[8,512,128]{2,1,0:T(8,128)S(1)} collective-permute-done((f32[8,512,128]{2,1,0:T(8,128)}, f32[8,512,128]{2,1,0:T(8,128)S(1)}, u32[]{:S(2)}, u32[]{:S(2)}) %collective-permute-start.1) | collective-permute-done | bytes 2097184 | tf_op jit(solution)/shard_map/ppermute | solution.py:320
  58.6 1.4 copy-done.1
  60.0 7.6 %shard_map.111 = f32[8,2,2,1,2,128,128]{6,5,4,3,2,1,0:T(8,128)} custom-call(s32[208]{0:T(256)} %reshape.664.table, f32[2,8,256,256]{3,2,1,0:T(8,128)} %shard_map.110.t_ref, f32[8,512,128]{2,1,0:T(8,128)} %bitcast.146, f32[8,512,128]{2,1,0:T(8,128)} %copy-done.1, f32[8,512,128]{2,1,0:T(8,128)} %bitcast.147, f32[8,512,128]{2,1,0:T(8,128)} %copy-done.1), custom_call_target="tpu_custom_call" | custom-call | flops 1610612736 | bytes 12582912 | tf_op jit(solution)/shard_map/pallas_call | solution.py:145
  67.6 7.2 %all-to-all-start.4 = ((f32[32,1,2,128,128]{4,3,2,1,0:T(8,128)}), f32[32,1,2,128,128]{4,3,2,1,0:T(8,128)}, u32[]{:S(2)}, u32[]{:S(2)}) async-start(f32[32,1,2,128,128]{4,3,2,1,0:T(8,128)} %bitcast.154), calls=%async_computation.4 | async-start | bytes 8388608 | tf_op jit(solution)/shard_map/all_to_all | solution.py:333
  74.9 3.0 collective-permute-start.3
  77.9 68.5 %collective-permute-done.3 = f32[4,512,128]{2,1,0:T(8,128)S(1)} collective-permute-done((f32[4,512,128]{2,1,0:T(8,128)S(1)}, f32[4,512,128]{2,1,0:T(8,128)S(1)}, u32[]{:S(2)}, u32[]{:S(2)}) %collective-permute-start.3) | collective-permute-done | bytes 1048608 | tf_op jit(solution)/shard_map/ppermute | solution.py:320
  147.2 1.3 slice.111
  148.5 1.3 collective-permute-start.2
  149.9 21.2 %collective-permute-done.4 = f32[4,512,128]{2,1,0:T(8,128)S(1)} collective-permute-done((f32[4,512,128]{2,1,0:T(8,128)S(1)}, f32[4,512,128]{2,1,0:T(8,128)S(1)}, u32[]{:S(2)}, u32[]{:S(2)}) %collective-permute-start.4) | collective-permute-done | bytes 1048608 | tf_op jit(solution)/shard_map/ppermute | solution.py:320
  171.1 3.0 collective-permute-done.2
  174.1 2.8 pad_maximum_fusion.rest_0_.rest_1_.rest_2_.rest_3_
  176.9 7.5 %shard_map.108.rest_4_ = f32[8,2,2,2,2,128,128]{6,5,4,3,2,1,0:T(8,128)} custom-call(s32[208]{0:T(256)} %reshape.664.table, f32[2,8,256,256]{3,2,1,0:T(8,128)} %collective-permute-done.6.t_ref, f32[24,512,128]{2,1,0:T(8,128)} %pad_maximum_fusion.rest_0_.rest_1_.rest_2_.rest_3_, f32[24,512,128]{2,1,0:T(8,128)} %pad_maximum_fusion.rest_0_.rest_1_.rest_2_.rest_3_, ...), custom_call_target="tpu_custom_call" | custom-call | flops 1610612736 | bytes 12582912 | tf_op jit(solution)/shard_map/pallas_call | solution.py:145
  184.5 7.6 %shard_map.109 = f32[8,2,2,2,2,128,128]{6,5,4,3,2,1,0:T(8,128)} custom-call(s32[208]{0:T(256)} %reshape.664.table, f32[2,8,256,256]{3,2,1,0:T(8,128)} %collective-permute-done.5.t_ref, f32[24,512,128]{2,1,0:T(8,128)} %pad_maximum_fusion.rest_0_.rest_1_.rest_2_.rest_3_, ...), custom_call_target="tpu_custom_call", output_to_operand_aliasing={{}: (6, {})} | custom-call | flops 1610612736 | bytes 12582912 | tf_op jit(solution)/shard_map/pallas_call | solution.py:145
  192.1 5.5 %all-to-all-start.3 = ((f32[32,2,2,128,128]{4,3,2,1,0:T(8,128)}), f32[32,2,2,128,128]{4,3,2,1,0:T(8,128)}, u32[]{:S(2)}, u32[]{:S(2)}) async-start(f32[32,2,2,128,128]{4,3,2,1,0:T(8,128)} %bitcast.143), calls=%async_computation.3 | async-start | bytes 16777216 | tf_op jit(solution)/shard_map/all_to_all | solution.py:333
  197.6 7.0 %shard_map.105 = f32[2,8,256,256]{3,2,1,0:T(8,128)} custom-call(s32[72]{0:T(128)} %pad_add_fusion.5.table, f32[8,2,4,256,256]{4,3,2,1,0:T(8,128)} %bitcast.140, f32[16,1,256]{2,1,0:T(1,128)} %reshape.667.rate_a.rate_b, f32[16,1,256]{2,1,0:T(1,128)} %reshape.667.rate_a.rate_b, bf16[8,256,256]{2,1,0:T(8,128)(2,1)} %get-tuple-element.26.rest_0_, ...), custom_call_target="tpu_custom_call" | custom-call | flops 1610612736 | bytes 12582912 | tf_op jit(solution)/shard_map/pallas_call | solution.py:71
  204.6 3.0 collective-permute-start
  208.8 90.4 %collective-permute-done.t_ref = f32[2,8,256,256]{3,2,1,0:T(8,128)} collective-permute-done((f32[2,8,256,256]{3,2,1,0:T(8,128)}, f32[2,8,256,256]{3,2,1,0:T(8,128)}, u32[]{:S(2)}, u32[]{:S(2)}) %collective-permute-start) | collective-permute-done | bytes 4194336 | tf_op jit(solution)/shard_map/ppermute | solution.py:320
  299.2 7.6 %shard_map.106 = f32[8,2,2,1,2,128,128]{6,5,4,3,2,1,0:T(8,128)} custom-call(s32[208]{0:T(256)} %reshape.664.table, f32[2,8,256,256]{3,2,1,0:T(8,128)} %collective-permute-done.t_ref, f32[24,512,128]{2,1,0:T(8,128)} %pad_maximum_fusion.rest_0_.rest_1_.rest_2_.rest_3_, f32[24,512,128]{2,1,0:T(8,128)} %pad_maximum_fusion.rest_0_.rest_1_.rest_2_.rest_3_, ...), custom_call_target="tpu_custom_call" | custom-call | flops 1610612736 | bytes 12582912 | tf_op jit(solution)/shard_map/pallas_call | solution.py:145
  306.8 7.5 %all-to-all-start.2 = ((f32[32,1,2,128,128]{4,3,2,1,0:T(8,128)}), f32[32,1,2,128,128]{4,3,2,1,0:T(8,128)}, u32[]{:S(2)}, u32[]{:S(2)}) async-start(f32[32,1,2,128,128]{4,3,2,1,0:T(8,128)} %bitcast.153), calls=%async_computation.2 | async-start | bytes 8388608 | tf_op jit(solution)/shard_map/all_to_all | solution.py:333
  314.5 1.4 reduce_window_sum.13
  316.9 9.1 %fusion.8 = (s32[8,16]{1,0:T(8,128)S(1)}, s32[8,16]{1,0:T(8,128)S(1)}, s32[8,16]{1,0:T(8,128)S(1)}, s32[8,16]{1,0:T(8,128)S(1)}) fusion(s32[8,2]{1,0:T(8,128)S(1)} %multiply_add_fusion, s32[8,16,8,2]{3,2,1,0:T(8,128)S(1)} %copy.109, s32[8,16,8,9]{3,2,1,0:T(8,128)S(1)} %reshape.657, s32[]{:T(128)S(6)} %add.347), kind=kLoop, calls=%fused_computation.18 | loop fusion | flops 69120 | bytes 18500 | tf_op jit(solution)/shard_map/reduce_sum | solution.py:296
  330.8 7.1 %shard_map.112 = (f32[4,4,1024,128]{3,2,1,0:T(8,128)}, f32[128,256]{1,0:T(8,128)}, f32[128,256]{1,0:T(8,128)}, f32[128,256]{1,0:T(8,128)}, f32[128,256]{1,0:T(8,128)}, /*index=5*/f32[128,256]{1,0:T(8,128)}) custom-call(s32[67]{0:T(128)} %add_add_fusion.3.table, f32[32,1,2,128,128]{4,3,2,1,0:T(8,128)} %all-to-all-done.4.got_ref, f32[1024,256]{1,0:T(8,128)} %bitcast.149), custom_call_target="tpu_custom_call" | custom-call | flops 805306368 | bytes 10485760 | tf_op jit(solution)/shard_map/pallas_call | solution.py:224
  337.9 7.4 %shard_map.113 = (f32[4,4,1024,128]{3,2,1,0:T(8,128)}, f32[128,256]{1,0:T(8,128)}, f32[128,256]{1,0:T(8,128)}, f32[128,256]{1,0:T(8,128)}, f32[128,256]{1,0:T(8,128)}, /*index=5*/f32[128,256]{1,0:T(8,128)}) custom-call(s32[67]{0:T(128)} %add_add_fusion.2.table, f32[32,2,2,128,128]{4,3,2,1,0:T(8,128)} %all-to-all-done.3.got_ref, ...), custom_call_target="tpu_custom_call", output_to_operand_aliasing={{0}: (3, {})} | custom-call | flops 805306368 | bytes 10485760 | tf_op jit(solution)/shard_map/pallas_call | solution.py:224
  346.4 1.6 collective-permute-start.7
  347.9 7.1 %shard_map.114 = (f32[4,4,1024,128]{3,2,1,0:T(8,128)}, f32[128,256]{1,0:T(8,128)}, f32[128,256]{1,0:T(8,128)}, f32[128,256]{1,0:T(8,128)}, f32[128,256]{1,0:T(8,128)}, /*index=5*/f32[128,256]{1,0:T(8,128)}) custom-call(s32[67]{0:T(128)} %add_add_fusion.1.table, f32[32,2,2,128,128]{4,3,2,1,0:T(8,128)} %all-to-all-done.3.got_ref, ...), custom_call_target="tpu_custom_call", output_to_operand_aliasing={{0}: (3, {})} | custom-call | flops 805306368 | bytes 10485760 | tf_op jit(solution)/shard_map/pallas_call | solution.py:224
  356.2 1.8 collective-permute-start.8
  358.8 6.0 %all-to-all-done.2.got_ref = f32[32,1,2,128,128]{4,3,2,1,0:T(8,128)} async-done(((f32[32,1,2,128,128]{4,3,2,1,0:T(8,128)}), f32[32,1,2,128,128]{4,3,2,1,0:T(8,128)}, u32[]{:S(2)}, u32[]{:S(2)}) %all-to-all-start.2) | async-done | bytes 4194336 | tf_op jit(solution)/shard_map/all_to_all | solution.py:333
  364.9 7.3 %shard_map.115 = (f32[4,4,1024,128]{3,2,1,0:T(8,128)}, f32[128,256]{1,0:T(8,128)}, f32[128,256]{1,0:T(8,128)}, f32[128,256]{1,0:T(8,128)}, f32[128,256]{1,0:T(8,128)}, /*index=5*/f32[128,256]{1,0:T(8,128)}) custom-call(s32[67]{0:T(128)} %add_add_fusion.table, f32[32,1,2,128,128]{4,3,2,1,0:T(8,128)} %all-to-all-done.2.got_ref, ...), custom_call_target="tpu_custom_call", output_to_operand_aliasing={{0}: (3, {})} | custom-call | flops 805306368 | bytes 10485760 | tf_op jit(solution)/shard_map/pallas_call | solution.py:224
  372.1 3.1 collective-permute-start.12
  375.5 4.9 %collective-permute-start.14 = (f32[128,256]{1,0:T(8,128)}, f32[128,256]{1,0:T(8,128)S(1)}, u32[]{:S(2)}, u32[]{:S(2)}) collective-permute-start(f32[128,256]{1,0:T(8,128)} %get-tuple-element.47), channel_id=1, source_target_pairs={{0,10},{1,11},{2,8},{3,9},{4,14},{5,15},{6,12},{7,13},{8,2},{9,3},... | collective-permute-start | bytes 393224 | tf_op jit(solution)/shard_map/ppermute | solution.py:329
  380.4 1.9 collective-permute-start.15
  382.5 1.4 collective-permute-start.10
  383.9 1.3 collective-permute-start.11
  386.0 1.2 collective-permute-done.14
  387.2 3.1 collective-permute-done.15
  390.3 4.3 collective-permute-done.11
  394.7 19.1 %all_to_all.39 = f32[8,128,256]{2,1,0:T(8,128)} all-to-all(f32[8,128,256]{2,1,0:T(8,128)S(1)} %broadcast_in_dim.171), channel_id=1, replica_groups=mesh['z'=4,'core'=2,'x'=4,'y'=4] {'z','core'}, dimensions={0} | all-to-all | bytes 2097152 | tf_op jit(solution)/shard_map/all_to_all | solution.py:280
  413.8 8.2 %shard_map.116 = f32[2048,256]{1,0:T(8,128)} custom-call(f32[16384,128]{1,0:T(8,128)} %bitcast.141, f32[1024,256]{1,0:T(8,128)} %bitcast.157), custom_call_target="tpu_custom_call" | custom-call | tf_op jit(solution)/shard_map/pallas_call | solution.py:265
  422.0 34.0 %all_to_all.40 = f32[16,128,256]{2,1,0:T(8,128)S(1)} all-to-all(f32[16,128,256]{2,1,0:T(8,128)} %bitcast.155), channel_id=1, replica_groups=mesh['z'=4,'core'=2,'x'=4,'y'=4] {'x','y'}, dimensions={0} | all-to-all | bytes 4194304 | tf_op jit(solution)/shard_map/all_to_all | solution.py:333
  (131 shorter events, 20.9 us)
Async XLA Ops:
  2.8 37.7 %all-to-all-start = ((f32[16,1,72]{2,1,0:T(1,128)}), f32[16,1,72]{2,1,0:T(1,128)S(1)}, u32[]{:S(2)}, u32[]{:S(2)}) async-start(f32[16,1,72]{2,1,0:T(1,128)} %broadcast_in_dim.89), calls=%async_computation | async-start | bytes 16384 | tf_op jit(solution)/shard_map/all_to_all | solution.py:280
  10.0 48.6 %collective-permute-start.1 = (f32[8,512,128]{2,1,0:T(8,128)}, f32[8,512,128]{2,1,0:T(8,128)S(1)}, u32[]{:S(2)}, u32[]{:S(2)}) collective-permute-start(f32[8,512,128]{2,1,0:T(8,128)} %bitcast.144), channel_id=1, source_target_pairs={{0,4},{4,8},{8,12},{12,0},{1,5},{5,9},{9,13},{13,1},{2,6},{6,10},{... | collective-permute-start | bytes 6291464 | tf_op jit(solution)/shard_map/ppermute | solution.py:320
  23.1 153.8 %collective-permute-start.6 = (f32[2,8,256,256]{3,2,1,0:T(8,128)}, f32[2,8,256,256]{3,2,1,0:T(8,128)}, u32[]{:S(2)}, u32[]{:S(2)}) collective-permute-start(f32[2,8,256,256]{3,2,1,0:T(8,128)} %get-tuple-element.28), channel_id=1, source_target_pairs={{0,3},{1,0},{2,1},{3,2},{4,7},{5,4},{6,5},{7,6},{8,11},{9,8},{10,9... | collective-permute-start | bytes 12582920 | tf_op jit(solution)/shard_map/ppermute | solution.py:320
  32.9 151.6 %collective-permute-start.5 = (f32[2,8,256,256]{3,2,1,0:T(8,128)}, f32[2,8,256,256]{3,2,1,0:T(8,128)}, u32[]{:S(2)}, u32[]{:S(2)}) collective-permute-start(f32[2,8,256,256]{3,2,1,0:T(8,128)} %shard_map.107), channel_id=1, source_target_pairs={{0,1},{1,2},{2,3},{3,0},{4,5},{5,6},{6,7},{7,4},{8,9},{9,10},{10,1... | collective-permute-start | bytes 12582920 | tf_op jit(solution)/shard_map/ppermute | solution.py:320
  33.3 8.7 %copy-start.5 = (f32[128,256]{1,0:T(8,128)S(1)}, f32[128,256]{1,0:T(8,128)}, u32[]{:S(2)}) copy-start(f32[128,256]{1,0:T(8,128)} %param.17) | copy-start | bytes 393220
  43.0 24.6 %all-to-all-start.1 = ((f32[8,136,256]{2,1,0:T(8,128)}), f32[8,136,256]{2,1,0:T(8,128)S(1)}, u32[]{:S(2)}, u32[]{:S(2)}) async-start(f32[8,136,256]{2,1,0:T(8,128)} %broadcast_in_dim.90), calls=%async_computation.1 | async-start | bytes 2228224 | tf_op jit(solution)/shard_map/all_to_all | solution.py:280
  58.6 1.4 copy-start.1
  67.6 7.2 %copy-start = (f32[8,256,2,128]{3,2,1,0:T(2,128)S(1)}, f32[8,256,2,128]{3,2,1,0:T(2,128)}, u32[]{:S(2)}) copy-start(f32[8,256,2,128]{3,2,1,0:T(2,128)} %param.11) | copy-start | bytes 6291460
  67.6 124.5 %all-to-all-start.4 = ((f32[32,1,2,128,128]{4,3,2,1,0:T(8,128)}), f32[32,1,2,128,128]{4,3,2,1,0:T(8,128)}, u32[]{:S(2)}, u32[]{:S(2)}) async-start(f32[32,1,2,128,128]{4,3,2,1,0:T(8,128)} %bitcast.154), calls=%async_computation.4 | async-start | bytes 8388608 | tf_op jit(solution)/shard_map/all_to_all | solution.py:333
  74.9 99.3 %copy-start.2 = (f32[8,512,128]{2,1,0:T(8,128)S(1)}, f32[8,512,128]{2,1,0:T(8,128)}, u32[]{:S(2)}) copy-start(f32[8,512,128]{2,1,0:T(8,128)} %copy-done.1) | copy-start | bytes 6291460
  74.9 71.5 %collective-permute-start.3 = (f32[4,512,128]{2,1,0:T(8,128)S(1)}, f32[4,512,128]{2,1,0:T(8,128)S(1)}, u32[]{:S(2)}, u32[]{:S(2)}) collective-permute-start(f32[4,512,128]{2,1,0:T(8,128)S(1)} %bitcast.158), channel_id=1, source_target_pairs={{0,12},{4,0},{8,4},{12,8},{1,13},{5,1},{9,5},{13,9},{2,14},{6,2},{... | collective-permute-start | bytes 3145736 | tf_op jit(solution)/shard_map/ppermute | solution.py:320
  146.5 24.6 %collective-permute-start.4 = (f32[4,512,128]{2,1,0:T(8,128)S(1)}, f32[4,512,128]{2,1,0:T(8,128)S(1)}, u32[]{:S(2)}, u32[]{:S(2)}) collective-permute-start(f32[4,512,128]{2,1,0:T(8,128)S(1)} %collective-permute-done.3), channel_id=1, source_target_pairs={{0,12},{4,0},{8,4},{12,8},{1,13},{5,1},{9,5},{13,9},{2,14},{6,2},{... | collective-permute-start | bytes 3145736 | tf_op jit(solution)/shard_map/ppermute | solution.py:320
  148.5 25.6 %collective-permute-start.2 = (f32[4,512,128]{2,1,0:T(8,128)S(1)}, f32[4,512,128]{2,1,0:T(8,128)S(1)}, u32[]{:S(2)}, u32[]{:S(2)}) collective-permute-start(f32[4,512,128]{2,1,0:T(8,128)S(1)} %slice.111), channel_id=1, source_target_pairs={{0,4},{4,8},{8,12},{12,0},{1,5},{5,9},{9,13},{13,1},{2,6},{6,10},{... | collective-permute-start | bytes 3145736 | tf_op jit(solution)/shard_map/ppermute | solution.py:320
  192.1 114.7 %all-to-all-start.3 = ((f32[32,2,2,128,128]{4,3,2,1,0:T(8,128)}), f32[32,2,2,128,128]{4,3,2,1,0:T(8,128)}, u32[]{:S(2)}, u32[]{:S(2)}) async-start(f32[32,2,2,128,128]{4,3,2,1,0:T(8,128)} %bitcast.143), calls=%async_computation.3 | async-start | bytes 16777216 | tf_op jit(solution)/shard_map/all_to_all | solution.py:333
  204.6 94.5 %collective-permute-start = (f32[2,8,256,256]{3,2,1,0:T(8,128)}, f32[2,8,256,256]{3,2,1,0:T(8,128)}, u32[]{:S(2)}, u32[]{:S(2)}) collective-permute-start(f32[2,8,256,256]{3,2,1,0:T(8,128)} %shard_map.105), channel_id=1, source_target_pairs={{0,2},{1,3},{2,0},{3,1},{4,6},{5,7},{6,4},{7,5},{8,10},{9,11},{10,... | collective-permute-start | bytes 12582920 | tf_op jit(solution)/shard_map/ppermute | solution.py:320
  306.8 58.1 %all-to-all-start.2 = ((f32[32,1,2,128,128]{4,3,2,1,0:T(8,128)}), f32[32,1,2,128,128]{4,3,2,1,0:T(8,128)}, u32[]{:S(2)}, u32[]{:S(2)}) async-start(f32[32,1,2,128,128]{4,3,2,1,0:T(8,128)} %bitcast.153), calls=%async_computation.2 | async-start | bytes 8388608 | tf_op jit(solution)/shard_map/all_to_all | solution.py:333
  346.4 34.0 %collective-permute-start.7 = (f32[4,128,256]{2,1,0:T(8,128)S(1)}, f32[4,128,256]{2,1,0:T(8,128)S(1)}, u32[]{:S(2)}, u32[]{:S(2)}) collective-permute-start(f32[4,128,256]{2,1,0:T(8,128)S(1)} %pad_maximum_fusion.1), channel_id=1, source_target_pairs={{0,1},{1,2},{2,3},{3,0},{4,5},{5,6},{6,7},{7,4},{8,9},{9,10},{10,1... | collective-permute-start | bytes 1572872 | tf_op jit(solution)/shard_map/ppermute | solution.py:320
  356.2 26.1 %collective-permute-start.8 = (f32[4,128,256]{2,1,0:T(8,128)S(1)}, f32[4,128,256]{2,1,0:T(8,128)S(1)}, u32[]{:S(2)}, u32[]{:S(2)}) collective-permute-start(f32[4,128,256]{2,1,0:T(8,128)S(1)} %pad_maximum_fusion.2), channel_id=1, source_target_pairs={{0,3},{1,0},{2,1},{3,2},{4,7},{5,4},{6,5},{7,6},{8,11},{9,8},{10,9... | collective-permute-start | bytes 1572872 | tf_op jit(solution)/shard_map/ppermute | solution.py:320
  364.8 17.5 %copy-start.6 = (f32[128,256]{1,0:T(8,128)S(1)}, f32[128,256]{1,0:T(8,128)}, u32[]{:S(2)}) copy-start(f32[128,256]{1,0:T(8,128)} %get-tuple-element.33) | copy-start | bytes 393220
  364.8 17.5 %copy-start.7 = (f32[128,256]{1,0:T(8,128)S(1)}, f32[128,256]{1,0:T(8,128)}, u32[]{:S(2)}) copy-start(f32[128,256]{1,0:T(8,128)} %get-tuple-element.34) | copy-start | bytes 393220
  364.9 17.5 %copy-start.8 = (f32[128,256]{1,0:T(8,128)S(1)}, f32[128,256]{1,0:T(8,128)}, u32[]{:S(2)}) copy-start(f32[128,256]{1,0:T(8,128)} %get-tuple-element.35) | copy-start | bytes 393220
  364.9 17.5 %copy-start.9 = (f32[128,256]{1,0:T(8,128)S(1)}, f32[128,256]{1,0:T(8,128)}, u32[]{:S(2)}) copy-start(f32[128,256]{1,0:T(8,128)} %get-tuple-element.36) | copy-start | bytes 393220
  364.9 29.7 %copy-start.3 = (f32[128,256]{1,0:T(8,128)S(1)}, f32[128,256]{1,0:T(8,128)}, u32[]{:S(2)}) copy-start(f32[128,256]{1,0:T(8,128)} %param.16) | copy-start | bytes 393220
  364.9 29.7 %copy-start.4 = (f32[128,256]{1,0:T(8,128)S(1)}, f32[128,256]{1,0:T(8,128)}, u32[]{:S(2)}) copy-start(f32[128,256]{1,0:T(8,128)} %get-tuple-element.49) | copy-start | bytes 393220
  372.1 11.8 %collective-permute-start.12 = (f32[128,256]{1,0:T(8,128)}, f32[128,256]{1,0:T(8,128)S(1)}, u32[]{:S(2)}, u32[]{:S(2)}) collective-permute-start(f32[128,256]{1,0:T(8,128)} %get-tuple-element.45), channel_id=1, source_target_pairs={{0,2},{1,3},{2,0},{3,1},{4,6},{5,7},{6,4},{7,5},{8,10},{9,11},{10,... | collective-permute-start | bytes 393224 | tf_op jit(solution)/shard_map/ppermute | solution.py:329
  375.2 10.1 %collective-permute-start.13 = (f32[128,256]{1,0:T(8,128)}, f32[128,256]{1,0:T(8,128)S(1)}, u32[]{:S(2)}, u32[]{:S(2)}) collective-permute-start(f32[128,256]{1,0:T(8,128)} %get-tuple-element.46), channel_id=1, source_target_pairs={{0,6},{1,7},{2,4},{3,5},{4,10},{5,11},{6,8},{7,9},{8,14},{9,15},{1... | collective-permute-start | bytes 393224 | tf_op jit(solution)/shard_map/ppermute | solution.py:329
  375.5 11.6 %collective-permute-start.14 = (f32[128,256]{1,0:T(8,128)}, f32[128,256]{1,0:T(8,128)S(1)}, u32[]{:S(2)}, u32[]{:S(2)}) collective-permute-start(f32[128,256]{1,0:T(8,128)} %get-tuple-element.47), channel_id=1, source_target_pairs={{0,10},{1,11},{2,8},{3,9},{4,14},{5,15},{6,12},{7,13},{8,2},{9,3},... | collective-permute-start | bytes 393224 | tf_op jit(solution)/shard_map/ppermute | solution.py:329
  380.4 9.8 %collective-permute-start.15 = (f32[128,256]{1,0:T(8,128)}, f32[128,256]{1,0:T(8,128)S(1)}, u32[]{:S(2)}, u32[]{:S(2)}) collective-permute-start(f32[128,256]{1,0:T(8,128)} %get-tuple-element.48), channel_id=1, source_target_pairs={{0,14},{1,15},{2,12},{3,13},{4,2},{5,3},{6,0},{7,1},{8,6},{9,7},{1... | collective-permute-start | bytes 393224 | tf_op jit(solution)/shard_map/ppermute | solution.py:329
  382.5 7.8 %collective-permute-start.10 = (f32[128,256]{1,0:T(8,128)S(1)}, f32[128,256]{1,0:T(8,128)S(1)}, u32[]{:S(2)}, u32[]{:S(2)}) collective-permute-start(f32[128,256]{1,0:T(8,128)S(1)} %get-tuple-element.87), channel_id=1, source_target_pairs={{0,8},{4,12},{8,0},{12,4},{1,9},{5,13},{9,1},{13,5},{2,10},{6,14},... | collective-permute-start | bytes 393224 | tf_op jit(solution)/shard_map/ppermute | solution.py:320
  383.9 10.6 %collective-permute-start.11 = (f32[128,256]{1,0:T(8,128)S(1)}, f32[128,256]{1,0:T(8,128)S(1)}, u32[]{:S(2)}, u32[]{:S(2)}) collective-permute-start(f32[128,256]{1,0:T(8,128)S(1)} %get-tuple-element.86), channel_id=1, source_target_pairs={{0,12},{4,0},{8,4},{12,8},{1,13},{5,1},{9,5},{13,9},{2,14},{6,2},{... | collective-permute-start | bytes 393224 | tf_op jit(solution)/shard_map/ppermute | solution.py:320
  385.3 9.3 %collective-permute-start.9 = (f32[128,256]{1,0:T(8,128)S(1)}, f32[128,256]{1,0:T(8,128)S(1)}, u32[]{:S(2)}, u32[]{:S(2)}) collective-permute-start(f32[128,256]{1,0:T(8,128)S(1)} %get-tuple-element.85), channel_id=1, source_target_pairs={{0,4},{4,8},{8,12},{12,0},{1,5},{5,9},{9,13},{13,1},{2,6},{6,10},{... | collective-permute-start | bytes 393224 | tf_op jit(solution)/shard_map/ppermute | solution.py:320

commit v7 on v6

--- a/solution.py
+++ b/solution.py
@@ -41,13 +41,16 @@
 STEP = 2
 
 
-def left_kernel(group, flips, table, a_ref, rate_a, rate_b, *rest):
+def left_kernel(group, flips, live, policy, a_ref, *rest):
+    rates = ()
+    if group == 0:
+        rates, rest = rest[:STEP], rest[STEP:]
     if flips:
         p_ref, out_ref, high_ref, low_ref = rest
     else:
         high_ref, low_ref, out_ref = rest
     step = pl.program_id(0)
-    for r, rate_ref in enumerate((rate_a, rate_b)):
+    for r in range(STEP):
         s = step * STEP + r
         if flips:
             for m in range(KP):
@@ -55,31 +58,28 @@
                 high_ref[r, m * CB : (m + 1) * CB] = high
                 low_ref[r, m * CB : (m + 1) * CB] = low
         for k2 in range(PAIR):
-            block = a_ref[r, k2, 0] * table[s * KA + group + GROUP * k2].astype(f32)
+            block = a_ref[r, k2, 0] * live[s, group + GROUP * k2].astype(f32)
             if group == 0 and k2 == 0:
                 across = lax.broadcasted_iota(jnp.int32, (BS, BS), 0)
                 along = lax.broadcasted_iota(jnp.int32, (BS, BS), 1)
-                block = block + jnp.where(across == along, rate_ref[0], 0.0)
+                block = block + jnp.where(across == along, rates[r][0], 0.0)
             out_ref[k2, r] = dot3((high_ref[r], low_ref[r]), split(block))
 
 
-def left_products(group, table, a_blocks, rates, own_p, parts):
-    half = pl.BlockSpec((STEP, KP * CB, BS), lambda s, t: (s, 0, 0))
+def left_products(group, live, policy, a_blocks, rates, own_p, parts):
+    half = pl.BlockSpec((STEP, KP * CB, BS), lambda s, t, p: (s, 0, 0))
     halves = [jax.ShapeDtypeStruct((NB, KP * CB, BS), bf16)] * 2
     flips = parts is None
-    rate = lambda r: pl.BlockSpec((1, 1, BS), lambda s, t: (t[NB * KA + s * STEP + r], 0, 0))
+    rate = lambda r: pl.BlockSpec((1, 1, BS), lambda s, t, p: (p[s * STEP + r], 0, 0))
     results = pl.pallas_call(
         functools.partial(left_kernel, group, flips),
         grid_spec=pltpu.PrefetchScalarGridSpec(
-            num_scalar_prefetch=1,
+            num_scalar_prefetch=2,
             grid=(NB // STEP,),
-            in_specs=[
-                pl.BlockSpec((STEP, PAIR, 1, BS, BS), lambda s, t: (s, 0, group, 0, 0)),
-                rate(0),
-                rate(1),
-            ]
-            + ([pl.BlockSpec((STEP, KP * BS, CB), lambda s, t: (s, 0, 0))] if flips else [half, half]),
-            out_specs=[pl.BlockSpec((PAIR, STEP, KP * CB, BS), lambda s, t: (0, s, 0, 0))]
+            in_specs=[pl.BlockSpec((STEP, PAIR, 1, BS, BS), lambda s, t, p: (s, 0, group, 0, 0))]
+            + ([rate(r) for r in range(STEP)] if group == 0 else [])
+            + ([pl.BlockSpec((STEP, KP * BS, CB), lambda s, t, p: (s, 0, 0))] if flips else [half, half]),
+            out_specs=[pl.BlockSpec((PAIR, STEP, KP * CB, BS), lambda s, t, p: (0, s, 0, 0))]
             + ([half, half] if flips else []),
         ),
         out_shape=[jax.ShapeDtypeStruct((PAIR, NB, KP * CB, BS), f32)] + (halves if flips else []),
@@ -88,7 +88,13 @@
             bytes_accessed=4 * PAIR * NB * 3 * BS * BS,
             transcendentals=0,
         ),
-    )(table, a_blocks.reshape(NB, PAIR, GROUP, BS, BS), rates, rates, *([own_p] if flips else parts))
+    )(
+        live,
+        policy,
+        a_blocks.reshape(NB, PAIR, GROUP, BS, BS),
+        *([rates] * STEP if group == 0 else []),
+        *([own_p] if flips else parts),
+    )
     return results[0], (list(results[1:]) if flips else parts)
 
 
@@ -173,7 +179,7 @@
 
 
 def gather_kernel(group, table, got_ref, x_ref, *rest):
-    coarse_ref, *part_refs, floor_ref, total, x_high, x_low = rest[-(N_X + 5) :]
+    coarse_ref, high_ref, low_ref, *part_refs, floor_ref, total, x_high, x_low = rest[-(N_X + 7) :]
     step = pl.program_id(0)
 
     @pl.when(step == 0)
@@ -198,9 +204,14 @@
             for q in range(N_ROW):
                 coarse_ref[u, 0, pl.ds(q, CB, N_ROW), :] = blocks[q]
             rows.append(jnp.concatenate(blocks, axis=1))
-        result = dot3(split(jnp.concatenate(rows)), (x_high[...], x_low[...]))
+        high, low = split(jnp.concatenate(rows))
+        result = dot3((high, low), (x_high[...], x_low[...]))
         for d in range(N_X):
-            part_refs[d][...] = result[d * CB : (d + 1) * CB]
+            u = lax.rem(table[COUNT + 2] + d, N_X)
+            mine = slice(d * CB, (d + 1) * CB)
+            high_ref[u, 0] = high[mine]
+            low_ref[u, 0] = low[mine]
+            part_refs[d][...] = result[mine]
         if group == 0:
             across = lax.broadcasted_iota(jnp.int32, (CB, CB), 0)
             along = lax.broadcasted_iota(jnp.int32, (CB, CB), 1)
@@ -218,16 +229,17 @@
     args = [got, x]
     alias = {}
     if prior is not None:
-        in_specs.append(pl.BlockSpec(memory_space=pl.ANY))
-        args.append(prior)
-        alias = {3: 0}
-    coarse, *parts, floor = pl.pallas_call(
+        in_specs += [pl.BlockSpec(memory_space=pl.ANY)] * len(prior)
+        args += prior
+        alias = {3: 0, 4: 1, 5: 2}
+    rows = pl.BlockSpec((N_X, 1, CB, N_ROW * CB), lambda i, t: (0, t[COUNT], 0, 0))
+    *made, floor = pl.pallas_call(
         functools.partial(gather_kernel, group),
         grid_spec=pltpu.PrefetchScalarGridSpec(
             num_scalar_prefetch=1,
             grid=(STEPS,),
             in_specs=in_specs,
-            out_specs=[pl.BlockSpec((N_X, 1, CB * N_ROW, CB), lambda i, t: (0, t[COUNT], 0, 0))]
+            out_specs=[pl.BlockSpec((N_X, 1, CB * N_ROW, CB), lambda i, t: (0, t[COUNT], 0, 0)), rows, rows]
             + [whole((CB, NCOL))] * (N_X + 1),
             scratch_shapes=[
                 pltpu.VMEM((CELLS, CB, CB), f32),
@@ -236,6 +248,7 @@
             ],
         ),
         out_shape=[jax.ShapeDtypeStruct((N_X, N_Y, CB * N_ROW, CB), f32)]
+        + [jax.ShapeDtypeStruct((N_X, N_Y, CB, N_ROW * CB), bf16)] * 2
         + [jax.ShapeDtypeStruct((CB, NCOL), f32)] * (N_X + 1),
         input_output_aliases=alias,
         cost_estimate=pl.CostEstimate(
@@ -244,35 +257,32 @@
             transcendentals=0,
         ),
     )(table, *args)
-    return coarse, parts, floor
+    return made[:3], made[3:], floor
 
 
 TALL = 4 * CB
 
 
-def apply_kernel(c_ref, x_ref, out_ref, x_high, x_low):
+def apply_kernel(high_ref, low_ref, x_ref, out_ref, x_high, x_low):
     @pl.when(pl.program_id(0) == 0)
     def _():
         high, low = split(x_ref[...])
         x_high[...] = high
         x_low[...] = low
 
-    rows = jnp.concatenate([c_ref[pl.ds(q, TALL, N_ROW), :] for q in range(N_ROW)], axis=1)
-    out_ref[...] = dot3(split(rows), (x_high[...], x_low[...]))
-
-
-def apply(coarse, x):
+    out_ref[...] = dot3((high_ref[...], low_ref[...]), (x_high[...], x_low[...]))
+
+
+def apply(high, low, x):
+    rows = pl.BlockSpec((TALL, N_ROW * CB), lambda u: (u, 0))
     return pl.pallas_call(
         apply_kernel,
         grid=(N_COL * CB // TALL,),
-        in_specs=[
-            pl.BlockSpec((TALL * N_ROW, CB), lambda u: (u, 0)),
-            pl.BlockSpec((N_ROW * CB, NCOL), lambda u: (0, 0)),
-        ],
+        in_specs=[rows, rows, pl.BlockSpec((N_ROW * CB, NCOL), lambda u: (0, 0))],
         out_specs=pl.BlockSpec((TALL, NCOL), lambda u: (u, 0)),
         out_shape=jax.ShapeDtypeStruct((N_COL * CB, NCOL), f32),
         scratch_shapes=[pltpu.VMEM((N_ROW * CB, NCOL), bf16)] * 2,
-    )(coarse, x)
+    )(high, low, x)
 
 
 def to_all(value, axes, count):
@@ -334,7 +344,7 @@
 
 
 META = KP + KA - 1
-RELAYED = 4
+RELAYED = 5
 LAST = 2
 
 
@@ -385,17 +395,16 @@
     p_rear = shifted(p_back, "x", -1)
     p_far = shifted(p_one[:RELAYED], "x", 1)
     parts = None
-    numbers = jnp.concatenate([a_live.reshape(-1), policy])
     rate_rows = rates.reshape(-1, 1, BS)
     lefts = {}
     for group in (1, 3, 2, 0):
-        left, parts = left_products(group, numbers, a_blocks, rate_rows, own_p, parts)
+        left, parts = left_products(group, a_live, policy, a_blocks, rate_rows, own_p, parts)
         lefts[group] = shifted(left, "y", -group) if group else left
     table = product_tables(cells, x, y)
     where = places(metas, row, col).reshape(N_ROW, N_X, N_Y, 2)
     where = where // (N_Y * N_ROW) * N_ROW + where % N_ROW
     own_cell = x * N_ROW + row
-    coarse = None
+    made = None
     stacked = None
     sums = []
     for batch in ((0,), (1, 3), (LAST,)):
@@ -412,7 +421,7 @@
             y_u = (y + group) % N_Y
             spots = lax.dynamic_index_in_dim(where, y_u, 2, False).reshape(-1)
             spots = jnp.concatenate([spots, jnp.stack([y_u, own_cell, x])])
-            coarse, parts, floor = gather(group, lane, spots, got, around, coarse)
+            made, parts, floor = gather(group, lane, spots, got, around, made)
             if group == 0:
                 floor_diag = floor
             if group != LAST:
@@ -426,8 +435,9 @@
         applied = applied + shifted_plane(parts[d], d, LAST)
     current = guess + damping * (rhs - applied) / floor_diag
 
-    coarse = coarse.reshape(N_COL * CB * N_ROW, CB)
-    part = apply(coarse, to_all(current, ROW, N_ROW).reshape(N_ROW * CB, NCOL))
+    coarse, *halves = made
+    halves = [half.reshape(N_COL * CB, N_ROW * CB) for half in halves]
+    part = apply(*halves, to_all(current, ROW, N_ROW).reshape(N_ROW * CB, NCOL))
     applied = jnp.sum(exchanged(part.reshape(N_COL, CB, NCOL), COL), axis=0)
     current = current + damping * (rhs - applied) / floor_diag
     return coarse.reshape(N_COL * CB, N_ROW, 1, CB), current

time: 458 us -> 448 us (0.978)
  waiting for transfers between devices: 206 us -> 192 us
    ppermute x12, waiting for transfers between devices: 196 us -> 184 us  [shifted(): lax.ppermute(value, axis, [(i, (i + steps) % count) for i in range(count)])]
  transfers between devices with their start and end apart: 21 -> 21, of which waited for: 9 -> 9; matrix products, arithmetic and copies ran while one was open for 7% -> 7% of each run, Pallas kernels for 19% -> 20%
where the time goes in v7:
time: 448 us; the launch traced here: 447 us
  waiting for transfers between devices  192 us (43%)
  Pallas kernels  99.1 us (22%)
  starting transfers between devices  63.2 us (14%)
  blocking collectives  56.8 us (13%)
  other arithmetic  21.9 us (5%)
  local copies, waits for them, and re-layouts  12.9 us (3%)
    ppermute x12, waiting for transfers between devices, shifted(): lax.ppermute(value, axis, [(i, (i + steps) % count) for i in range(count)])  184 us
    all_to_all x1, blocking collectives, exchanged(): return lax.all_to_all(value, axes, split_axis=0, concat_axis=0, tiled=True)  35.9 us
    pallas_call x4, Pallas kernels, gather(): pl.pallas_call(functools.partial(gather_kernel, group), grid_spec=pltpu.P...  31.9 us
    pallas_call x4, Pallas kernels, products(): pl.pallas_call(functools.partial(product_kernel, base, lane), grid_spec=p...  30.3 us
    pallas_call x4, Pallas kernels, left_products(): pl.pallas_call(functools.partial(left_kernel, group, flips), grid_spec=pl...  29.2 us
    all_to_all x3, starting transfers between devices, exchanged(): return lax.all_to_all(value, axes, split_axis=0, concat_axis=0, tiled=True)  21.6 us
    all_to_all x1, blocking collectives, to_all(): return lax.all_to_all(copies, axes, split_axis=0, concat_axis=0, tiled=True)  20.9 us
    ppermute x12, starting transfers between devices, shifted(): lax.ppermute(value, axis, [(i, (i + steps) % count) for i in range(count)])  18.8 us
  transfers between devices with their start and end apart: 21, of which 9 were waited for; matrix products, arithmetic and copies ran while one was open for 7% of the time, Pallas kernels for 20%

profile of v7, /device:TPU:0, one launch (start us, length us, event | category | flops | bytes accessed | tf_op | source)
XLA Modules:
  0.0 446.9 jit_solution(1973206356019811436)
XLA Ops:
  2.8 7.1 %all-to-all-start = ((f32[16,1,72]{2,1,0:T(1,128)}), f32[16,1,72]{2,1,0:T(1,128)S(1)}, u32[]{:S(2)}, u32[]{:S(2)}) async-start(f32[16,1,72]{2,1,0:T(1,128)} %broadcast_in_dim.89), calls=%async_computation | async-start | bytes 16384 | tf_op jit(solution)/shard_map/all_to_all | solution.py:290
  10.0 1.9 collective-permute-start.1
  11.9 7.7 %shard_map.104 = (f32[2,8,256,256]{3,2,1,0:T(8,128)}, bf16[8,256,256]{2,1,0:T(8,128)(2,1)}, bf16[8,256,256]{2,1,0:T(8,128)(2,1)}) custom-call(s32[8,8]{1,0:T(8,128)} %live.7, s32[8]{0:T(128)} %policy.7, f32[8,2,4,256,256]{4,3,2,1,0:T(8,128)} %bitcast.138, f32[8,512,128]{2,1,0:T(8,128)} %bitcast.147), custom_call_target="tpu_custom_call" | custom-call | flops 1610612736 | bytes 12582912 | tf_op jit(solution)/shard_map/pallas_call | solution.py:74
  19.6 7.2 %shard_map.107 = f32[2,8,256,256]{3,2,1,0:T(8,128)} custom-call(s32[8,8]{1,0:T(8,128)} %live.7, s32[8]{0:T(128)} %policy.7, f32[8,2,4,256,256]{4,3,2,1,0:T(8,128)} %bitcast.139, bf16[8,256,256]{2,1,0:T(8,128)(2,1)} %get-tuple-element.34.rest_0_.rest_2_, bf16[8,256,256]{2,1,0:T(8,128)(2,1)} %get-tuple-element.35.rest_1_.rest_3_), custom_call_target="tpu_custom_call" | custom-call | flops 1610612736 | bytes 12582912 | tf_op jit(solution)/shard_map/pallas_call | solution.py:74
  26.8 1.5 collective-permute-start.5
  28.4 1.7 collective-permute-start.6
  31.1 7.2 %shard_map.110.t_ref = f32[2,8,256,256]{3,2,1,0:T(8,128)} custom-call(s32[8,8]{1,0:T(8,128)} %live.7, s32[8]{0:T(128)} %policy.7, f32[8,2,4,256,256]{4,3,2,1,0:T(8,128)} %bitcast.140, f32[16,1,256]{2,1,0:T(1,128)} %reshape.676.rest_0_.rest_1_, f32[16,1,256]{2,1,0:T(1,128)} %reshape.676.rest_0_.rest_1_, ...), custom_call_target="tpu_custom_call" | custom-call | flops 1610612736 | bytes 12582912 | tf_op jit(solution)/shard_map/pallas_call | solution.py:74
  39.8 1.1 broadcast_in_dim.90
  40.8 5.4 %all-to-all-start.1 = ((f32[8,136,256]{2,1,0:T(8,128)}), f32[8,136,256]{2,1,0:T(8,128)S(1)}, u32[]{:S(2)}, u32[]{:S(2)}) async-start(f32[8,136,256]{2,1,0:T(8,128)} %broadcast_in_dim.90), calls=%async_computation.1 | async-start | bytes 2228224 | tf_op jit(solution)/shard_map/all_to_all | solution.py:290
  48.2 10.4 %collective-permute-done.1.rest_1_.rest_3_ = f32[8,512,128]{2,1,0:T(8,128)S(1)} collective-permute-done((f32[8,512,128]{2,1,0:T(8,128)}, f32[8,512,128]{2,1,0:T(8,128)S(1)}, u32[]{:S(2)}, u32[]{:S(2)}) %collective-permute-start.1) | collective-permute-done | bytes 2097184 | tf_op jit(solution)/shard_map/ppermute | solution.py:330
  58.6 1.4 copy-done.1
  60.0 7.6 %shard_map.111 = f32[8,2,2,1,2,128,128]{6,5,4,3,2,1,0:T(8,128)} custom-call(s32[208]{0:T(256)} %reshape.667.table, f32[2,8,256,256]{3,2,1,0:T(8,128)} %shard_map.110.t_ref, f32[8,512,128]{2,1,0:T(8,128)} %bitcast.148, f32[8,512,128]{2,1,0:T(8,128)} %copy-done.1, f32[8,512,128]{2,1,0:T(8,128)} %bitcast.149, f32[8,512,128]{2,1,0:T(8,128)} %copy-done.1), custom_call_target="tpu_custom_call" | custom-call | flops 1610612736 | bytes 12582912 | tf_op jit(solution)/shard_map/pallas_call | solution.py:151
  67.6 7.2 %all-to-all-start.4 = ((f32[32,1,2,128,128]{4,3,2,1,0:T(8,128)}), f32[32,1,2,128,128]{4,3,2,1,0:T(8,128)}, u32[]{:S(2)}, u32[]{:S(2)}) async-start(f32[32,1,2,128,128]{4,3,2,1,0:T(8,128)} %bitcast.156), calls=%async_computation.4 | async-start | bytes 8388608 | tf_op jit(solution)/shard_map/all_to_all | solution.py:343
  74.9 3.0 collective-permute-start.3
  77.9 1.4 slice.111
  79.4 61.4 %collective-permute-done.3 = f32[3,512,128]{2,1,0:T(8,128)S(1)} collective-permute-done((f32[3,512,128]{2,1,0:T(8,128)S(1)}, f32[3,512,128]{2,1,0:T(8,128)S(1)}, u32[]{:S(2)}, u32[]{:S(2)}) %collective-permute-start.3) | collective-permute-done | bytes 786464 | tf_op jit(solution)/shard_map/ppermute | solution.py:330
  141.6 18.2 %collective-permute-done.4 = f32[3,512,128]{2,1,0:T(8,128)S(1)} collective-permute-done((f32[3,512,128]{2,1,0:T(8,128)S(1)}, f32[3,512,128]{2,1,0:T(8,128)S(1)}, u32[]{:S(2)}, u32[]{:S(2)}) %collective-permute-start.4) | collective-permute-done | bytes 786464 | tf_op jit(solution)/shard_map/ppermute | solution.py:330
  159.8 2.8 pad_maximum_fusion.rest_0_.rest_1_.rest_2_.rest_3_
  162.7 7.6 %shard_map.108.rest_4_ = f32[8,2,2,2,2,128,128]{6,5,4,3,2,1,0:T(8,128)} custom-call(s32[208]{0:T(256)} %reshape.667.table, f32[2,8,256,256]{3,2,1,0:T(8,128)} %collective-permute-done.6.t_ref, f32[24,512,128]{2,1,0:T(8,128)} %pad_maximum_fusion.rest_0_.rest_1_.rest_2_.rest_3_, f32[24,512,128]{2,1,0:T(8,128)} %pad_maximum_fusion.rest_0_.rest_1_.rest_2_.rest_3_, ...), custom_call_target="tpu_custom_call" | custom-call | flops 1610612736 | bytes 12582912 | tf_op jit(solution)/shard_map/pallas_call | solution.py:151
  170.2 7.6 %shard_map.109 = f32[8,2,2,2,2,128,128]{6,5,4,3,2,1,0:T(8,128)} custom-call(s32[208]{0:T(256)} %reshape.667.table, f32[2,8,256,256]{3,2,1,0:T(8,128)} %collective-permute-done.5.t_ref, f32[24,512,128]{2,1,0:T(8,128)} %pad_maximum_fusion.rest_0_.rest_1_.rest_2_.rest_3_, ...), custom_call_target="tpu_custom_call", output_to_operand_aliasing={{}: (6, {})} | custom-call | flops 1610612736 | bytes 12582912 | tf_op jit(solution)/shard_map/pallas_call | solution.py:151
  177.8 6.9 %all-to-all-start.3 = ((f32[32,2,2,128,128]{4,3,2,1,0:T(8,128)}), f32[32,2,2,128,128]{4,3,2,1,0:T(8,128)}, u32[]{:S(2)}, u32[]{:S(2)}) async-start(f32[32,2,2,128,128]{4,3,2,1,0:T(8,128)} %bitcast.143), calls=%async_computation.3 | async-start | bytes 16777216 | tf_op jit(solution)/shard_map/all_to_all | solution.py:343
  184.7 7.1 %shard_map.105 = f32[2,8,256,256]{3,2,1,0:T(8,128)} custom-call(s32[8,8]{1,0:T(8,128)} %live.7, s32[8]{0:T(128)} %policy.7, f32[8,2,4,256,256]{4,3,2,1,0:T(8,128)} %bitcast.141, bf16[8,256,256]{2,1,0:T(8,128)(2,1)} %get-tuple-element.34.rest_0_.rest_2_, bf16[8,256,256]{2,1,0:T(8,128)(2,1)} %get-tuple-element.35.rest_1_.rest_3_), custom_call_target="tpu_custom_call" | custom-call | flops 1610612736 | bytes 12582912 | tf_op jit(solution)/shard_map/pallas_call | solution.py:74
  191.8 3.0 collective-permute-start
  195.9 90.3 %collective-permute-done.t_ref = f32[2,8,256,256]{3,2,1,0:T(8,128)} collective-permute-done((f32[2,8,256,256]{3,2,1,0:T(8,128)}, f32[2,8,256,256]{3,2,1,0:T(8,128)}, u32[]{:S(2)}, u32[]{:S(2)}) %collective-permute-start) | collective-permute-done | bytes 4194336 | tf_op jit(solution)/shard_map/ppermute | solution.py:330
  286.3 7.6 %shard_map.106 = f32[8,2,2,1,2,128,128]{6,5,4,3,2,1,0:T(8,128)} custom-call(s32[208]{0:T(256)} %reshape.667.table, f32[2,8,256,256]{3,2,1,0:T(8,128)} %collective-permute-done.t_ref, f32[24,512,128]{2,1,0:T(8,128)} %pad_maximum_fusion.rest_0_.rest_1_.rest_2_.rest_3_, f32[24,512,128]{2,1,0:T(8,128)} %pad_maximum_fusion.rest_0_.rest_1_.rest_2_.rest_3_, ...), custom_call_target="tpu_custom_call" | custom-call | flops 1610612736 | bytes 12582912 | tf_op jit(solution)/shard_map/pallas_call | solution.py:151
  293.9 7.5 %all-to-all-start.2 = ((f32[32,1,2,128,128]{4,3,2,1,0:T(8,128)}), f32[32,1,2,128,128]{4,3,2,1,0:T(8,128)}, u32[]{:S(2)}, u32[]{:S(2)}) async-start(f32[32,1,2,128,128]{4,3,2,1,0:T(8,128)} %bitcast.155), calls=%async_computation.2 | async-start | bytes 8388608 | tf_op jit(solution)/shard_map/all_to_all | solution.py:343
  301.6 1.4 reduce_window_sum.13
  304.0 9.1 %fusion.8 = (s32[8,16]{1,0:T(8,128)S(1)}, s32[8,16]{1,0:T(8,128)S(1)}, s32[8,16]{1,0:T(8,128)S(1)}, s32[8,16]{1,0:T(8,128)S(1)}) fusion(s32[8,2]{1,0:T(8,128)S(1)} %multiply_add_fusion, s32[8,16,8,2]{3,2,1,0:T(8,128)S(1)} %copy.115, s32[8,16,8,9]{3,2,1,0:T(8,128)S(1)} %reshape.660, s32[]{:T(128)S(6)} %add.347), kind=kLoop, calls=%fused_computation.18 | loop fusion | flops 69120 | bytes 18500 | tf_op jit(solution)/shard_map/reduce_sum | solution.py:306
  314.9 1.2 slice.112
  317.9 7.9 %shard_map.112 = (f32[4,4,1024,128]{3,2,1,0:T(8,128)}, bf16[4,4,128,1024]{3,2,1,0:T(8,128)(2,1)}, bf16[4,4,128,1024]{3,2,1,0:T(8,128)(2,1)}, f32[128,256]{1,0:T(...) custom-call(s32[67]{0:T(128)} %add_add_fusion.3.table, ...), custom_call_target="tpu_custom_call" | custom-call | flops 805306368 | bytes 10485760 | tf_op jit(solution)/shard_map/pallas_call | solution.py:236
  325.8 8.1 %shard_map.113 = (f32[4,4,1024,128]{3,2,1,0:T(8,128)}, bf16[4,4,128,1024]{3,2,1,0:T(8,128)(2,1)}, bf16[4,4,128,1024]{3,2,1,0:T(8,128)(2,1)}, f32[128,256]{1,0:T(...) custom-call(s32[67]{0:T(128)} %add_add_fusion.2.table, ...), custom_call_target="tpu_custom_call", output_to_operand_aliasing={{0}: (3, {}), {1}: (4, {}), {2}: (5, {})} | custom-call | flops 805306368 | bytes 10485760 | tf_op jit(solution)/shard_map/pallas_call | solution.py:236
  333.9 1.1 pad_maximum_fusion.1
  335.0 1.6 collective-permute-start.7
  336.6 7.9 %shard_map.114 = (f32[4,4,1024,128]{3,2,1,0:T(8,128)}, bf16[4,4,128,1024]{3,2,1,0:T(8,128)(2,1)}, bf16[4,4,128,1024]{3,2,1,0:T(8,128)(2,1)}, f32[128,256]{1,0:T(...) custom-call(s32[67]{0:T(128)} %add_add_fusion.1.table, ...), custom_call_target="tpu_custom_call", output_to_operand_aliasing={{0}: (3, {}), {1}: (4, {}), {2}: (5, {})} | custom-call | flops 805306368 | bytes 10485760 | tf_op jit(solution)/shard_map/pallas_call | solution.py:236
  344.5 1.1 pad_maximum_fusion.2
  345.6 1.8 collective-permute-start.8
  348.3 3.7 all-to-all-done.2.got_ref
  352.0 8.0 %shard_map.115 = (f32[4,4,1024,128]{3,2,1,0:T(8,128)}, bf16[4,4,128,1024]{3,2,1,0:T(8,128)(2,1)}, bf16[4,4,128,1024]{3,2,1,0:T(8,128)(2,1)}, f32[128,256]{1,0:T(...) custom-call(s32[67]{0:T(128)} %add_add_fusion.table, ...), custom_call_target="tpu_custom_call", output_to_operand_aliasing={{0}: (3, {}), {1}: (4, {}), {2}: (5, {})} | custom-call | flops 805306368 | bytes 10485760 | tf_op jit(solution)/shard_map/pallas_call | solution.py:236
  360.0 3.1 collective-permute-start.12
  363.4 4.9 %collective-permute-start.14 = (f32[128,256]{1,0:T(8,128)}, f32[128,256]{1,0:T(8,128)S(1)}, u32[]{:S(2)}, u32[]{:S(2)}) collective-permute-start(f32[128,256]{1,0:T(8,128)} %get-tuple-element.61), channel_id=1, source_target_pairs={{0,10},{1,11},{2,8},{3,9},{4,14},{5,15},{6,12},{7,13},{8,2},{9,3},... | collective-permute-start | bytes 393224 | tf_op jit(solution)/shard_map/ppermute | solution.py:339
  368.3 1.9 collective-permute-start.15
  370.5 3.2 collective-permute-start.11
  373.8 1.2 collective-permute-done.14
  375.1 3.1 collective-permute-done.15
  379.2 2.2 collective-permute-done.10
  381.6 20.9 %all_to_all.39 = f32[8,128,256]{2,1,0:T(8,128)} all-to-all(f32[8,128,256]{2,1,0:T(8,128)S(1)} %broadcast_in_dim.171), channel_id=1, replica_groups=mesh['z'=4,'core'=2,'x'=4,'y'=4] {'z','core'}, dimensions={0} | all-to-all | bytes 2097152 | tf_op jit(solution)/shard_map/all_to_all | solution.py:290
  402.5 7.7 %shard_map.116 = f32[2048,256]{1,0:T(8,128)} custom-call(bf16[2048,1024]{1,0:T(8,128)(2,1)} %bitcast.144, bf16[2048,1024]{1,0:T(8,128)(2,1)} %bitcast.145, f32[1024,256]{1,0:T(8,128)} %bitcast.159), custom_call_target="tpu_custom_call" | custom-call | tf_op jit(solution)/shard_map/pallas_call | solution.py:278
  410.2 35.9 %all_to_all.40 = f32[16,128,256]{2,1,0:T(8,128)S(1)} all-to-all(f32[16,128,256]{2,1,0:T(8,128)} %bitcast.157), channel_id=1, replica_groups=mesh['z'=4,'core'=2,'x'=4,'y'=4] {'x','y'}, dimensions={0} | all-to-all | bytes 4194304 | tf_op jit(solution)/shard_map/all_to_all | solution.py:343
  (131 shorter events, 16.9 us)
Async XLA Ops:
  2.8 35.6 %all-to-all-start = ((f32[16,1,72]{2,1,0:T(1,128)}), f32[16,1,72]{2,1,0:T(1,128)S(1)}, u32[]{:S(2)}, u32[]{:S(2)}) async-start(f32[16,1,72]{2,1,0:T(1,128)} %broadcast_in_dim.89), calls=%async_computation | async-start | bytes 16384 | tf_op jit(solution)/shard_map/all_to_all | solution.py:290
  10.0 48.6 %collective-permute-start.1 = (f32[8,512,128]{2,1,0:T(8,128)}, f32[8,512,128]{2,1,0:T(8,128)S(1)}, u32[]{:S(2)}, u32[]{:S(2)}) collective-permute-start(f32[8,512,128]{2,1,0:T(8,128)} %bitcast.146), channel_id=1, source_target_pairs={{0,4},{4,8},{8,12},{12,0},{1,5},{5,9},{9,13},{13,1},{2,6},{6,10},{... | collective-permute-start | bytes 6291464 | tf_op jit(solution)/shard_map/ppermute | solution.py:330
  19.6 10.7 %copy-start.10 = (f32[16,256]{1,0:T(8,128)S(1)}, f32[16,256]{1,0:T(8,128)}, u32[]{:S(2)}) copy-start(f32[16,256]{1,0:T(8,128)} %param.15) | copy-start | bytes 49156
  26.8 143.4 %collective-permute-start.5 = (f32[2,8,256,256]{3,2,1,0:T(8,128)}, f32[2,8,256,256]{3,2,1,0:T(8,128)}, u32[]{:S(2)}, u32[]{:S(2)}) collective-permute-start(f32[2,8,256,256]{3,2,1,0:T(8,128)} %shard_map.107), channel_id=1, source_target_pairs={{0,1},{1,2},{2,3},{3,0},{4,5},{5,6},{6,7},{7,4},{8,9},{9,10},{10,1... | collective-permute-start | bytes 12582920 | tf_op jit(solution)/shard_map/ppermute | solution.py:330
  28.4 134.3 %collective-permute-start.6 = (f32[2,8,256,256]{3,2,1,0:T(8,128)}, f32[2,8,256,256]{3,2,1,0:T(8,128)}, u32[]{:S(2)}, u32[]{:S(2)}) collective-permute-start(f32[2,8,256,256]{3,2,1,0:T(8,128)} %get-tuple-element.36), channel_id=1, source_target_pairs={{0,3},{1,0},{2,1},{3,2},{4,7},{5,4},{6,5},{7,6},{8,11},{9,8},{10,9... | collective-permute-start | bytes 12582920 | tf_op jit(solution)/shard_map/ppermute | solution.py:330
  31.1 8.6 %copy-start.5 = (f32[128,256]{1,0:T(8,128)S(1)}, f32[128,256]{1,0:T(8,128)}, u32[]{:S(2)}) copy-start(f32[128,256]{1,0:T(8,128)} %param.17) | copy-start | bytes 393220
  40.8 26.8 %all-to-all-start.1 = ((f32[8,136,256]{2,1,0:T(8,128)}), f32[8,136,256]{2,1,0:T(8,128)S(1)}, u32[]{:S(2)}, u32[]{:S(2)}) async-start(f32[8,136,256]{2,1,0:T(8,128)} %broadcast_in_dim.90), calls=%async_computation.1 | async-start | bytes 2228224 | tf_op jit(solution)/shard_map/all_to_all | solution.py:290
  58.6 1.4 copy-start.1
  67.6 7.2 %copy-start = (f32[8,256,2,128]{3,2,1,0:T(2,128)S(1)}, f32[8,256,2,128]{3,2,1,0:T(2,128)}, u32[]{:S(2)}) copy-start(f32[8,256,2,128]{3,2,1,0:T(2,128)} %param.11) | copy-start | bytes 6291460
  67.6 110.2 %all-to-all-start.4 = ((f32[32,1,2,128,128]{4,3,2,1,0:T(8,128)}), f32[32,1,2,128,128]{4,3,2,1,0:T(8,128)}, u32[]{:S(2)}, u32[]{:S(2)}) async-start(f32[32,1,2,128,128]{4,3,2,1,0:T(8,128)} %bitcast.156), calls=%async_computation.4 | async-start | bytes 8388608 | tf_op jit(solution)/shard_map/all_to_all | solution.py:343
  74.9 85.0 %copy-start.2 = (f32[8,512,128]{2,1,0:T(8,128)S(1)}, f32[8,512,128]{2,1,0:T(8,128)}, u32[]{:S(2)}) copy-start(f32[8,512,128]{2,1,0:T(8,128)} %copy-done.1) | copy-start | bytes 6291460
  74.9 65.9 %collective-permute-start.3 = (f32[3,512,128]{2,1,0:T(8,128)S(1)}, f32[3,512,128]{2,1,0:T(8,128)S(1)}, u32[]{:S(2)}, u32[]{:S(2)}) collective-permute-start(f32[3,512,128]{2,1,0:T(8,128)S(1)} %bitcast.160), channel_id=1, source_target_pairs={{0,12},{4,0},{8,4},{12,8},{1,13},{5,1},{9,5},{13,9},{2,14},{6,2},{... | collective-permute-start | bytes 2359304 | tf_op jit(solution)/shard_map/ppermute | solution.py:330
  79.3 80.5 %collective-permute-start.2 = (f32[5,512,128]{2,1,0:T(8,128)S(1)}, f32[5,512,128]{2,1,0:T(8,128)S(1)}, u32[]{:S(2)}, u32[]{:S(2)}) collective-permute-start(f32[5,512,128]{2,1,0:T(8,128)S(1)} %slice.111), channel_id=1, source_target_pairs={{0,4},{4,8},{8,12},{12,0},{1,5},{5,9},{9,13},{13,1},{2,6},{6,10},{... | collective-permute-start | bytes 3932168 | tf_op jit(solution)/shard_map/ppermute | solution.py:330
  140.8 19.0 %collective-permute-start.4 = (f32[3,512,128]{2,1,0:T(8,128)S(1)}, f32[3,512,128]{2,1,0:T(8,128)S(1)}, u32[]{:S(2)}, u32[]{:S(2)}) collective-permute-start(f32[3,512,128]{2,1,0:T(8,128)S(1)} %collective-permute-done.3), channel_id=1, source_target_pairs={{0,12},{4,0},{8,4},{12,8},{1,13},{5,1},{9,5},{13,9},{2,14},{6,2},{... | collective-permute-start | bytes 2359304 | tf_op jit(solution)/shard_map/ppermute | solution.py:330
  177.8 116.1 %all-to-all-start.3 = ((f32[32,2,2,128,128]{4,3,2,1,0:T(8,128)}), f32[32,2,2,128,128]{4,3,2,1,0:T(8,128)}, u32[]{:S(2)}, u32[]{:S(2)}) async-start(f32[32,2,2,128,128]{4,3,2,1,0:T(8,128)} %bitcast.143), calls=%async_computation.3 | async-start | bytes 16777216 | tf_op jit(solution)/shard_map/all_to_all | solution.py:343
  191.8 94.5 %collective-permute-start = (f32[2,8,256,256]{3,2,1,0:T(8,128)}, f32[2,8,256,256]{3,2,1,0:T(8,128)}, u32[]{:S(2)}, u32[]{:S(2)}) collective-permute-start(f32[2,8,256,256]{3,2,1,0:T(8,128)} %shard_map.105), channel_id=1, source_target_pairs={{0,2},{1,3},{2,0},{3,1},{4,6},{5,7},{6,4},{7,5},{8,10},{9,11},{10,... | collective-permute-start | bytes 12582920 | tf_op jit(solution)/shard_map/ppermute | solution.py:330
  293.9 58.0 %all-to-all-start.2 = ((f32[32,1,2,128,128]{4,3,2,1,0:T(8,128)}), f32[32,1,2,128,128]{4,3,2,1,0:T(8,128)}, u32[]{:S(2)}, u32[]{:S(2)}) async-start(f32[32,1,2,128,128]{4,3,2,1,0:T(8,128)} %bitcast.155), calls=%async_computation.2 | async-start | bytes 8388608 | tf_op jit(solution)/shard_map/all_to_all | solution.py:343
  335.0 33.2 %collective-permute-start.7 = (f32[4,128,256]{2,1,0:T(8,128)S(1)}, f32[4,128,256]{2,1,0:T(8,128)S(1)}, u32[]{:S(2)}, u32[]{:S(2)}) collective-permute-start(f32[4,128,256]{2,1,0:T(8,128)S(1)} %pad_maximum_fusion.1), channel_id=1, source_target_pairs={{0,1},{1,2},{2,3},{3,0},{4,5},{5,6},{6,7},{7,4},{8,9},{9,10},{10,1... | collective-permute-start | bytes 1572872 | tf_op jit(solution)/shard_map/ppermute | solution.py:330
  345.6 24.6 %collective-permute-start.8 = (f32[4,128,256]{2,1,0:T(8,128)S(1)}, f32[4,128,256]{2,1,0:T(8,128)S(1)}, u32[]{:S(2)}, u32[]{:S(2)}) collective-permute-start(f32[4,128,256]{2,1,0:T(8,128)S(1)} %pad_maximum_fusion.2), channel_id=1, source_target_pairs={{0,3},{1,0},{2,1},{3,2},{4,7},{5,4},{6,5},{7,6},{8,11},{9,8},{10,9... | collective-permute-start | bytes 1572872 | tf_op jit(solution)/shard_map/ppermute | solution.py:330
  352.0 18.2 %copy-start.6 = (f32[128,256]{1,0:T(8,128)S(1)}, f32[128,256]{1,0:T(8,128)}, u32[]{:S(2)}) copy-start(f32[128,256]{1,0:T(8,128)} %get-tuple-element.47) | copy-start | bytes 393220
  352.0 18.2 %copy-start.7 = (f32[128,256]{1,0:T(8,128)S(1)}, f32[128,256]{1,0:T(8,128)}, u32[]{:S(2)}) copy-start(f32[128,256]{1,0:T(8,128)} %get-tuple-element.48) | copy-start | bytes 393220
  352.0 18.2 %copy-start.8 = (f32[128,256]{1,0:T(8,128)S(1)}, f32[128,256]{1,0:T(8,128)}, u32[]{:S(2)}) copy-start(f32[128,256]{1,0:T(8,128)} %get-tuple-element.49) | copy-start | bytes 393220
  352.0 18.2 %copy-start.9 = (f32[128,256]{1,0:T(8,128)S(1)}, f32[128,256]{1,0:T(8,128)}, u32[]{:S(2)}) copy-start(f32[128,256]{1,0:T(8,128)} %get-tuple-element.50) | copy-start | bytes 393220
  352.0 29.4 %copy-start.3 = (f32[128,256]{1,0:T(8,128)S(1)}, f32[128,256]{1,0:T(8,128)}, u32[]{:S(2)}) copy-start(f32[128,256]{1,0:T(8,128)} %param.16) | copy-start | bytes 393220
  352.0 29.4 %copy-start.4 = (f32[128,256]{1,0:T(8,128)S(1)}, f32[128,256]{1,0:T(8,128)}, u32[]{:S(2)}) copy-start(f32[128,256]{1,0:T(8,128)} %get-tuple-element.63) | copy-start | bytes 393220
  360.0 10.4 %collective-permute-start.12 = (f32[128,256]{1,0:T(8,128)}, f32[128,256]{1,0:T(8,128)S(1)}, u32[]{:S(2)}, u32[]{:S(2)}) collective-permute-start(f32[128,256]{1,0:T(8,128)} %get-tuple-element.59), channel_id=1, source_target_pairs={{0,2},{1,3},{2,0},{3,1},{4,6},{5,7},{6,4},{7,5},{8,10},{9,11},{10,... | collective-permute-start | bytes 393224 | tf_op jit(solution)/shard_map/ppermute | solution.py:339
  363.1 10.6 %collective-permute-start.13 = (f32[128,256]{1,0:T(8,128)}, f32[128,256]{1,0:T(8,128)S(1)}, u32[]{:S(2)}, u32[]{:S(2)}) collective-permute-start(f32[128,256]{1,0:T(8,128)} %get-tuple-element.60), channel_id=1, source_target_pairs={{0,6},{1,7},{2,4},{3,5},{4,10},{5,11},{6,8},{7,9},{8,14},{9,15},{1... | collective-permute-start | bytes 393224 | tf_op jit(solution)/shard_map/ppermute | solution.py:339
  363.4 11.6 %collective-permute-start.14 = (f32[128,256]{1,0:T(8,128)}, f32[128,256]{1,0:T(8,128)S(1)}, u32[]{:S(2)}, u32[]{:S(2)}) collective-permute-start(f32[128,256]{1,0:T(8,128)} %get-tuple-element.61), channel_id=1, source_target_pairs={{0,10},{1,11},{2,8},{3,9},{4,14},{5,15},{6,12},{7,13},{8,2},{9,3},... | collective-permute-start | bytes 393224 | tf_op jit(solution)/shard_map/ppermute | solution.py:339
  368.3 9.8 %collective-permute-start.15 = (f32[128,256]{1,0:T(8,128)}, f32[128,256]{1,0:T(8,128)S(1)}, u32[]{:S(2)}, u32[]{:S(2)}) collective-permute-start(f32[128,256]{1,0:T(8,128)} %get-tuple-element.62), channel_id=1, source_target_pairs={{0,14},{1,15},{2,12},{3,13},{4,2},{5,3},{6,0},{7,1},{8,6},{9,7},{1... | collective-permute-start | bytes 393224 | tf_op jit(solution)/shard_map/ppermute | solution.py:339
  370.4 7.8 %collective-permute-start.9 = (f32[128,256]{1,0:T(8,128)S(1)}, f32[128,256]{1,0:T(8,128)S(1)}, u32[]{:S(2)}, u32[]{:S(2)}) collective-permute-start(f32[128,256]{1,0:T(8,128)S(1)} %get-tuple-element.101), channel_id=1, source_target_pairs={{0,4},{4,8},{8,12},{12,0},{1,5},{5,9},{9,13},{13,1},{2,6},{6,10},{... | collective-permute-start | bytes 393224 | tf_op jit(solution)/shard_map/ppermute | solution.py:330
  370.5 8.7 %collective-permute-start.11 = (f32[128,256]{1,0:T(8,128)S(1)}, f32[128,256]{1,0:T(8,128)S(1)}, u32[]{:S(2)}, u32[]{:S(2)}) collective-permute-start(f32[128,256]{1,0:T(8,128)S(1)} %get-tuple-element.102), channel_id=1, source_target_pairs={{0,12},{4,0},{8,4},{12,8},{1,13},{5,1},{9,5},{13,9},{2,14},{6,2},{... | collective-permute-start | bytes 393224 | tf_op jit(solution)/shard_map/ppermute | solution.py:330
  373.7 7.7 %collective-permute-start.10 = (f32[128,256]{1,0:T(8,128)S(1)}, f32[128,256]{1,0:T(8,128)S(1)}, u32[]{:S(2)}, u32[]{:S(2)}) collective-permute-start(f32[128,256]{1,0:T(8,128)S(1)} %get-tuple-element.103), channel_id=1, source_target_pairs={{0,8},{4,12},{8,0},{12,4},{1,9},{5,13},{9,1},{13,5},{2,10},{6,14},... | collective-permute-start | bytes 393224 | tf_op jit(solution)/shard_map/ppermute | solution.py:330

commit v8 on v7

--- a/solution.py
+++ b/solution.py
@@ -24,6 +24,7 @@
 PLANE = ROW + ("x",)
 N_X = N_Y = 4
 GROUP = 4
+LAST = 2
 PAIR = 2
 
 
@@ -179,7 +180,8 @@
 
 
 def gather_kernel(group, table, got_ref, x_ref, *rest):
-    coarse_ref, high_ref, low_ref, *part_refs, floor_ref, total, x_high, x_low = rest[-(N_X + 7) :]
+    made = N_X if group == LAST else 1
+    coarse_ref, high_ref, low_ref, *part_refs, floor_ref, total, x_high, x_low = rest[-(made + 7) :]
     step = pl.program_id(0)
 
     @pl.when(step == 0)
@@ -195,10 +197,9 @@
             place = table[step * PER_STEP + first + b]
             total[place] += got_ref[first // 2 + b // 2, 0, b % 2]
 
-    @pl.when(step == STEPS - 1)
-    def _():
+    def finish(ds):
         rows = []
-        for d in range(N_X):
+        for d in ds:
             u = lax.rem(table[COUNT + 2] + d, N_X)
             blocks = [total[u * N_ROW + q] for q in range(N_ROW)]
             for q in range(N_ROW):
@@ -206,12 +207,22 @@
             rows.append(jnp.concatenate(blocks, axis=1))
         high, low = split(jnp.concatenate(rows))
         result = dot3((high, low), (x_high[...], x_low[...]))
-        for d in range(N_X):
+        for i, d in enumerate(ds):
             u = lax.rem(table[COUNT + 2] + d, N_X)
-            mine = slice(d * CB, (d + 1) * CB)
+            mine = slice(i * CB, (i + 1) * CB)
             high_ref[u, 0] = high[mine]
             low_ref[u, 0] = low[mine]
-            part_refs[d][...] = result[mine]
+            if len(ds) == 1:
+                part_refs[0][d] = result
+            else:
+                part_refs[d][...] = result[mine]
+
+    @pl.when(step == STEPS - 1)
+    def _():
+        if group == LAST:
+            finish(range(N_X))
+        else:
+            pl.loop(0, N_X)(lambda d: finish([d]))
         if group == 0:
             across = lax.broadcasted_iota(jnp.int32, (CB, CB), 0)
             along = lax.broadcasted_iota(jnp.int32, (CB, CB), 1)
@@ -232,6 +243,8 @@
         in_specs += [pl.BlockSpec(memory_space=pl.ANY)] * len(prior)
         args += prior
         alias = {3: 0, 4: 1, 5: 2}
+    shapes = [(CB, NCOL)] * N_X if group == LAST else [(N_X, CB, NCOL)]
+    shapes.append((CB, NCOL))
     rows = pl.BlockSpec((N_X, 1, CB, N_ROW * CB), lambda i, t: (0, t[COUNT], 0, 0))
     *made, floor = pl.pallas_call(
         functools.partial(gather_kernel, group),
@@ -240,7 +253,7 @@
             grid=(STEPS,),
             in_specs=in_specs,
             out_specs=[pl.BlockSpec((N_X, 1, CB * N_ROW, CB), lambda i, t: (0, t[COUNT], 0, 0)), rows, rows]
-            + [whole((CB, NCOL))] * (N_X + 1),
+            + [whole(shape) for shape in shapes],
             scratch_shapes=[
                 pltpu.VMEM((CELLS, CB, CB), f32),
                 pltpu.VMEM((N_ROW * CB, NCOL), bf16),
@@ -249,7 +262,7 @@
         ),
         out_shape=[jax.ShapeDtypeStruct((N_X, N_Y, CB * N_ROW, CB), f32)]
         + [jax.ShapeDtypeStruct((N_X, N_Y, CB, N_ROW * CB), bf16)] * 2
-        + [jax.ShapeDtypeStruct((CB, NCOL), f32)] * (N_X + 1),
+        + [jax.ShapeDtypeStruct(shape, f32) for shape in shapes],
         input_output_aliases=alias,
         cost_estimate=pl.CostEstimate(
             flops=3 * 2 * N_X * CB * N_ROW * CB * NCOL,
@@ -263,26 +276,46 @@
 TALL = 4 * CB
 
 
-def apply_kernel(high_ref, low_ref, x_ref, out_ref, x_high, x_low):
+def apply_kernel(table, high_ref, low_ref, same_ref, other_ref, *rest):
+    out_ref, x_high, x_low = rest[-3:]
+
     @pl.when(pl.program_id(0) == 0)
     def _():
-        high, low = split(x_ref[...])
-        x_high[...] = high
-        x_low[...] = low
-
-    out_ref[...] = dot3((high_ref[...], low_ref[...]), (x_high[...], x_low[...]))
-
-
-def apply(high, low, x):
-    rows = pl.BlockSpec((TALL, N_ROW * CB), lambda u: (u, 0))
+        core = table[1]
+        for place, ref in ((core, same_ref), (1 - core, other_ref)):
+            high, low = split(ref[...])
+            x_high[place] = high
+            x_low[place] = low
+
+    right = (x_high[...].reshape(2 * CB, NCOL), x_low[...].reshape(2 * CB, NCOL))
+    result = dot3((high_ref[...], low_ref[...]), right)
+    if len(rest) > 3:
+        result = result + rest[0][...]
+    out_ref[...] = result
+
+
+def apply(table, high, low, same, other, prior):
+    wide = lambda shape: pl.BlockSpec(shape, lambda u, t: (u, 0))
+    fixed = pl.BlockSpec((CB, NCOL), lambda u, t: (0, 0))
+    columns = pl.BlockSpec((TALL, 2 * CB), lambda u, t: (u, t[0]))
+    before = [] if prior is None else [prior]
     return pl.pallas_call(
         apply_kernel,
-        grid=(N_COL * CB // TALL,),
-        in_specs=[rows, rows, pl.BlockSpec((N_ROW * CB, NCOL), lambda u: (0, 0))],
-        out_specs=pl.BlockSpec((TALL, NCOL), lambda u: (u, 0)),
+        grid_spec=pltpu.PrefetchScalarGridSpec(
+            num_scalar_prefetch=1,
+            grid=(N_COL * CB // TALL,),
+            in_specs=[columns, columns, fixed, fixed] + [wide((TALL, NCOL))] * len(before),
+            out_specs=wide((TALL, NCOL)),
+            scratch_shapes=[pltpu.VMEM((2, CB, NCOL), bf16)] * 2,
+        ),
         out_shape=jax.ShapeDtypeStruct((N_COL * CB, NCOL), f32),
-        scratch_shapes=[pltpu.VMEM((N_ROW * CB, NCOL), bf16)] * 2,
-    )(high, low, x)
+        input_output_aliases={5: 0} if before else {},
+        cost_estimate=pl.CostEstimate(
+            flops=3 * 2 * N_COL * CB * 2 * CB * NCOL,
+            bytes_accessed=4 * N_COL * CB * 4 * CB,
+            transcendentals=0,
+        ),
+    )(table, high, low, same, other, *before)
 
 
 def to_all(value, axes, count):
@@ -339,13 +372,21 @@
     return lax.ppermute(value, COL, pairs)
 
 
+def shifted_row(value, z_steps, core_steps):
+    pairs = [
+        (a * 2 + b, (a + z_steps) % N_Z * 2 + (b + core_steps) % 2) for a in range(N_Z) for b in range(2)
+    ]
+    return lax.ppermute(value, ROW, pairs)
+
+
 def exchanged(value, axes):
     return lax.all_to_all(value, axes, split_axis=0, concat_axis=0, tiled=True)
 
 
 META = KP + KA - 1
-RELAYED = 5
-LAST = 2
+RELAYED = 4
+N_Z = 4
+Z_ORDER = (0, 1, 3, 2)
 
 
 def product_tables(cells, x, y):
@@ -425,8 +466,7 @@
             if group == 0:
                 floor_diag = floor
             if group != LAST:
-                stack = jnp.stack(parts)
-                sums.append(shifted(stack, "y", group) if group else stack)
+                sums.append(shifted(parts[0], "y", group) if group else parts[0])
     early = sums[0] + sums[1] + sums[2]
     applied = early[0]
     for d in range(1, N_X):
@@ -437,7 +477,15 @@
 
     coarse, *halves = made
     halves = [half.reshape(N_COL * CB, N_ROW * CB) for half in halves]
-    part = apply(*halves, to_all(current, ROW, N_ROW).reshape(N_ROW * CB, NCOL))
+    z, core = lax.axis_index("z"), lax.axis_index("core")
+    blocks = {}
+    for dz in Z_ORDER:
+        for dc in range(2):
+            blocks[dz, dc] = shifted_row(current, dz, dc) if dz or dc else current
+    part = None
+    for dz in Z_ORDER:
+        numbers = jnp.stack([(z - dz) % N_Z, core])
+        part = apply(numbers, *halves, blocks[dz, 0], blocks[dz, 1], part)
     applied = jnp.sum(exchanged(part.reshape(N_COL, CB, NCOL), COL), axis=0)
     current = current + damping * (rhs - applied) / floor_diag
     return coarse.reshape(N_COL * CB, N_ROW, 1, CB), current

time: 448 us -> 466 us (1.040)
  blocking collectives: 56.8 us -> 33.1 us
  Pallas kernels: 99.1 us -> 115 us
  waiting for transfers between devices: 192 us -> 207 us
  starting transfers between devices: 63.2 us -> 69.1 us
    all_to_all x1 -> x0, blocking collectives: 20.9 us -> none  [to_all(): return lax.all_to_all(copies, axes, split_axis=0, concat_axis=0, tiled=True)]
    pallas_call x1 -> x4, Pallas kernels: 7.66 us -> 22.4 us  [apply(): pl.pallas_call(apply_kernel, grid_spec=pltpu.PrefetchScalarGridSpec(num_s...]
    ppermute x12, waiting for transfers between devices: 184 us -> 197 us  [shifted(): lax.ppermute(value, axis, [(i, (i + steps) % count) for i in range(count)])]
    ppermute x0 -> x7, starting transfers between devices: none -> 7.86 us  [shifted_row(): return lax.ppermute(value, ROW, pairs)]
  transfers between devices with their start and end apart: 21 -> 28, of which waited for: 9 -> 10; matrix products, arithmetic and copies ran while one was open for 7% -> 7% of each run, Pallas kernels for 20% -> 24%
where the time goes in v8:
time: 466 us; the launch traced here: 464 us
  waiting for transfers between devices  207 us (44%)
  Pallas kernels  115 us (25%)
  starting transfers between devices  69.1 us (15%)
  blocking collectives  33.1 us (7%)
  other arithmetic  22.2 us (5%)
  local copies, waits for them, and re-layouts  16.6 us (4%)
    ppermute x12, waiting for transfers between devices, shifted(): lax.ppermute(value, axis, [(i, (i + steps) % count) for i in range(count)])  197 us
    pallas_call x4, Pallas kernels, gather(): pl.pallas_call(functools.partial(gather_kernel, group), grid_spec=pltpu.P...  33.4 us
    all_to_all x1, blocking collectives, exchanged(): return lax.all_to_all(value, axes, split_axis=0, concat_axis=0, tiled=True)  33.1 us
    pallas_call x4, Pallas kernels, products(): pl.pallas_call(functools.partial(product_kernel, base, lane), grid_spec=p...  30.3 us
    pallas_call x4, Pallas kernels, left_products(): pl.pallas_call(functools.partial(left_kernel, group, flips), grid_spec=pl...  29.2 us
    pallas_call x4, Pallas kernels, apply(): pl.pallas_call(apply_kernel, grid_spec=pltpu.PrefetchScalarGridSpec(num_s...  22.4 us
    all_to_all x3, starting transfers between devices, exchanged(): return lax.all_to_all(value, axes, split_axis=0, concat_axis=0, tiled=True)  20.2 us
    ppermute x12, starting transfers between devices, shifted(): lax.ppermute(value, axis, [(i, (i + steps) % count) for i in range(count)])  19.5 us
  transfers between devices with their start and end apart: 28, of which 10 were waited for; matrix products, arithmetic and copies ran while one was open for 7% of the time, Pallas kernels for 24%

profile of v8, /device:TPU:0, one launch (start us, length us, event | category | flops | bytes accessed | tf_op | source)
XLA Modules:
  0.0 464.4 jit_solution(12038176511057454226)
XLA Ops:
  2.8 7.1 %all-to-all-start = ((f32[16,1,72]{2,1,0:T(1,128)}), f32[16,1,72]{2,1,0:T(1,128)S(1)}, u32[]{:S(2)}, u32[]{:S(2)}) async-start(f32[16,1,72]{2,1,0:T(1,128)} %broadcast_in_dim.87), calls=%async_computation | async-start | bytes 16384 | tf_op jit(solution)/shard_map/all_to_all | solution.py:323
  10.0 1.9 collective-permute-start.1
  11.9 7.7 %shard_map.104 = (f32[2,8,256,256]{3,2,1,0:T(8,128)}, bf16[8,256,256]{2,1,0:T(8,128)(2,1)}, bf16[8,256,256]{2,1,0:T(8,128)(2,1)}) custom-call(s32[8,8]{1,0:T(8,128)} %live.7, s32[8]{0:T(128)} %policy.7, f32[8,2,4,256,256]{4,3,2,1,0:T(8,128)} %bitcast.130, f32[8,512,128]{2,1,0:T(8,128)} %bitcast.146), custom_call_target="tpu_custom_call" | custom-call | flops 1610612736 | bytes 12582912 | tf_op jit(solution)/shard_map/pallas_call | solution.py:75
  19.6 7.2 %shard_map.107 = f32[2,8,256,256]{3,2,1,0:T(8,128)} custom-call(s32[8,8]{1,0:T(8,128)} %live.7, s32[8]{0:T(128)} %policy.7, f32[8,2,4,256,256]{4,3,2,1,0:T(8,128)} %bitcast.131, bf16[8,256,256]{2,1,0:T(8,128)(2,1)} %get-tuple-element.25.rest_0_.rest_2_, bf16[8,256,256]{2,1,0:T(8,128)(2,1)} %get-tuple-element.26.rest_1_.rest_3_), custom_call_target="tpu_custom_call" | custom-call | flops 1610612736 | bytes 12582912 | tf_op jit(solution)/shard_map/pallas_call | solution.py:75
  26.8 1.5 collective-permute-start.5
  28.4 1.7 collective-permute-start.6
  31.1 7.2 %shard_map.110.t_ref = f32[2,8,256,256]{3,2,1,0:T(8,128)} custom-call(s32[8,8]{1,0:T(8,128)} %live.7, s32[8]{0:T(128)} %policy.7, f32[8,2,4,256,256]{4,3,2,1,0:T(8,128)} %bitcast.132, f32[16,1,256]{2,1,0:T(1,128)} %reshape.672.rest_0_.rest_1_, f32[16,1,256]{2,1,0:T(1,128)} %reshape.672.rest_0_.rest_1_, ...), custom_call_target="tpu_custom_call" | custom-call | flops 1610612736 | bytes 12582912 | tf_op jit(solution)/shard_map/pallas_call | solution.py:75
  40.8 5.4 %all-to-all-start.1 = ((f32[8,136,256]{2,1,0:T(8,128)}), f32[8,136,256]{2,1,0:T(8,128)S(1)}, u32[]{:S(2)}, u32[]{:S(2)}) async-start(f32[8,136,256]{2,1,0:T(8,128)} %broadcast_in_dim.88), calls=%async_computation.1 | async-start | bytes 2228224 | tf_op jit(solution)/shard_map/all_to_all | solution.py:323
  48.2 10.4 %collective-permute-done.1.rest_1_.rest_3_ = f32[8,512,128]{2,1,0:T(8,128)S(1)} collective-permute-done((f32[8,512,128]{2,1,0:T(8,128)}, f32[8,512,128]{2,1,0:T(8,128)S(1)}, u32[]{:S(2)}, u32[]{:S(2)}) %collective-permute-start.1) | collective-permute-done | bytes 2097184 | tf_op jit(solution)/shard_map/ppermute | solution.py:363
  58.6 1.4 copy-done.1
  60.0 7.6 %shard_map.111 = f32[8,2,2,1,2,128,128]{6,5,4,3,2,1,0:T(8,128)} custom-call(s32[208]{0:T(256)} %reshape.663.table, f32[2,8,256,256]{3,2,1,0:T(8,128)} %shard_map.110.t_ref, f32[8,512,128]{2,1,0:T(8,128)} %bitcast.147, f32[8,512,128]{2,1,0:T(8,128)} %copy-done.1, f32[8,512,128]{2,1,0:T(8,128)} %bitcast.148, f32[8,512,128]{2,1,0:T(8,128)} %copy-done.1), custom_call_target="tpu_custom_call" | custom-call | flops 1610612736 | bytes 12582912 | tf_op jit(solution)/shard_map/pallas_call | solution.py:152
  67.6 7.2 %all-to-all-start.4 = ((f32[32,1,2,128,128]{4,3,2,1,0:T(8,128)}), f32[32,1,2,128,128]{4,3,2,1,0:T(8,128)}, u32[]{:S(2)}, u32[]{:S(2)}) async-start(f32[32,1,2,128,128]{4,3,2,1,0:T(8,128)} %bitcast.155), calls=%async_computation.4 | async-start | bytes 8388608 | tf_op jit(solution)/shard_map/all_to_all | solution.py:383
  74.9 3.0 collective-permute-start.3
  77.9 68.5 %collective-permute-done.3 = f32[4,512,128]{2,1,0:T(8,128)S(1)} collective-permute-done((f32[4,512,128]{2,1,0:T(8,128)S(1)}, f32[4,512,128]{2,1,0:T(8,128)S(1)}, u32[]{:S(2)}, u32[]{:S(2)}) %collective-permute-start.3) | collective-permute-done | bytes 1048608 | tf_op jit(solution)/shard_map/ppermute | solution.py:363
  147.2 1.3 slice.111
  148.5 1.3 collective-permute-start.2
  149.9 21.2 %collective-permute-done.4 = f32[4,512,128]{2,1,0:T(8,128)S(1)} collective-permute-done((f32[4,512,128]{2,1,0:T(8,128)S(1)}, f32[4,512,128]{2,1,0:T(8,128)S(1)}, u32[]{:S(2)}, u32[]{:S(2)}) %collective-permute-start.4) | collective-permute-done | bytes 1048608 | tf_op jit(solution)/shard_map/ppermute | solution.py:363
  171.1 3.0 collective-permute-done.2
  174.1 2.8 pad_maximum_fusion.rest_0_.rest_1_.rest_2_.rest_3_
  176.9 7.5 %shard_map.108.rest_4_ = f32[8,2,2,2,2,128,128]{6,5,4,3,2,1,0:T(8,128)} custom-call(s32[208]{0:T(256)} %reshape.663.table, f32[2,8,256,256]{3,2,1,0:T(8,128)} %collective-permute-done.6.t_ref, f32[24,512,128]{2,1,0:T(8,128)} %pad_maximum_fusion.rest_0_.rest_1_.rest_2_.rest_3_, f32[24,512,128]{2,1,0:T(8,128)} %pad_maximum_fusion.rest_0_.rest_1_.rest_2_.rest_3_, ...), custom_call_target="tpu_custom_call" | custom-call | flops 1610612736 | bytes 12582912 | tf_op jit(solution)/shard_map/pallas_call | solution.py:152
  184.5 7.6 %shard_map.109 = f32[8,2,2,2,2,128,128]{6,5,4,3,2,1,0:T(8,128)} custom-call(s32[208]{0:T(256)} %reshape.663.table, f32[2,8,256,256]{3,2,1,0:T(8,128)} %collective-permute-done.5.t_ref, f32[24,512,128]{2,1,0:T(8,128)} %pad_maximum_fusion.rest_0_.rest_1_.rest_2_.rest_3_, ...), custom_call_target="tpu_custom_call", output_to_operand_aliasing={{}: (6, {})} | custom-call | flops 1610612736 | bytes 12582912 | tf_op jit(solution)/shard_map/pallas_call | solution.py:152
  192.1 5.5 %all-to-all-start.3 = ((f32[32,2,2,128,128]{4,3,2,1,0:T(8,128)}), f32[32,2,2,128,128]{4,3,2,1,0:T(8,128)}, u32[]{:S(2)}, u32[]{:S(2)}) async-start(f32[32,2,2,128,128]{4,3,2,1,0:T(8,128)} %bitcast.143), calls=%async_computation.3 | async-start | bytes 16777216 | tf_op jit(solution)/shard_map/all_to_all | solution.py:383
  197.6 7.1 %shard_map.105 = f32[2,8,256,256]{3,2,1,0:T(8,128)} custom-call(s32[8,8]{1,0:T(8,128)} %live.7, s32[8]{0:T(128)} %policy.7, f32[8,2,4,256,256]{4,3,2,1,0:T(8,128)} %bitcast.133, bf16[8,256,256]{2,1,0:T(8,128)(2,1)} %get-tuple-element.25.rest_0_.rest_2_, bf16[8,256,256]{2,1,0:T(8,128)(2,1)} %get-tuple-element.26.rest_1_.rest_3_), custom_call_target="tpu_custom_call" | custom-call | flops 1610612736 | bytes 12582912 | tf_op jit(solution)/shard_map/pallas_call | solution.py:75
  204.6 3.0 collective-permute-start
  207.8 91.4 %collective-permute-done.t_ref = f32[2,8,256,256]{3,2,1,0:T(8,128)} collective-permute-done((f32[2,8,256,256]{3,2,1,0:T(8,128)}, f32[2,8,256,256]{3,2,1,0:T(8,128)}, u32[]{:S(2)}, u32[]{:S(2)}) %collective-permute-start) | collective-permute-done | bytes 4194336 | tf_op jit(solution)/shard_map/ppermute | solution.py:363
  299.2 7.6 %shard_map.106 = f32[8,2,2,1,2,128,128]{6,5,4,3,2,1,0:T(8,128)} custom-call(s32[208]{0:T(256)} %reshape.663.table, f32[2,8,256,256]{3,2,1,0:T(8,128)} %collective-permute-done.t_ref, f32[24,512,128]{2,1,0:T(8,128)} %pad_maximum_fusion.rest_0_.rest_1_.rest_2_.rest_3_, f32[24,512,128]{2,1,0:T(8,128)} %pad_maximum_fusion.rest_0_.rest_1_.rest_2_.rest_3_, ...), custom_call_target="tpu_custom_call" | custom-call | flops 1610612736 | bytes 12582912 | tf_op jit(solution)/shard_map/pallas_call | solution.py:152
  306.8 7.5 %all-to-all-start.2 = ((f32[32,1,2,128,128]{4,3,2,1,0:T(8,128)}), f32[32,1,2,128,128]{4,3,2,1,0:T(8,128)}, u32[]{:S(2)}, u32[]{:S(2)}) async-start(f32[32,1,2,128,128]{4,3,2,1,0:T(8,128)} %bitcast.154), calls=%async_computation.2 | async-start | bytes 8388608 | tf_op jit(solution)/shard_map/all_to_all | solution.py:383
  315.3 1.4 reduce_window_sum.13
  317.2 9.1 %fusion.8 = (s32[8,16]{1,0:T(8,128)S(1)}, s32[8,16]{1,0:T(8,128)S(1)}, s32[8,16]{1,0:T(8,128)S(1)}, s32[8,16]{1,0:T(8,128)S(1)}) fusion(s32[8,2]{1,0:T(8,128)S(1)} %multiply_add_fusion, s32[8,16,8,2]{3,2,1,0:T(8,128)S(1)} %copy.118, s32[8,16,8,9]{3,2,1,0:T(8,128)S(1)} %reshape.656, s32[]{:T(128)S(6)} %add.362), kind=kLoop, calls=%fused_computation.18 | loop fusion | flops 69120 | bytes 18500 | tf_op jit(solution)/shard_map/reduce_sum | solution.py:339
  331.9 8.4 %shard_map.112 = (f32[4,4,1024,128]{3,2,1,0:T(8,128)}, bf16[4,4,128,1024]{3,2,1,0:T(8,128)(2,1)}, bf16[4,4,128,1024]{3,2,1,0:T(8,128)(2,1)}, f32[4,128,256]{2,1,0:T(8,128)}, f32[128,256]{1,0:T(8,128)}) custom-call(s32[67]{0:T(128)} %add_add_fusion.4.table, f32[32,1,2,128,128]{4,3,2,1,0:T(8,128)} %all-to-all-done.4.got_ref, f32[1024,256]{1,0:T(8,128)} %bitcast.150), custom_call_target="tpu_custom_call" | custom-call | flops 805306368 | bytes 10485760 | tf_op jit(solution)/shard_map/pallas_call | solution.py:249
  340.4 8.4 %shard_map.113 = (f32[4,4,1024,128]{3,2,1,0:T(8,128)}, bf16[4,4,128,1024]{3,2,1,0:T(8,128)(2,1)}, bf16[4,4,128,1024]{3,2,1,0:T(8,128)(2,1)}, f32[4,128,256]{2,1,0:T(8,128)}, f32[128,256]{1,0:T(8,128)}) custom-call(s32[67]{0:T(128)} %add_add_fusion.3.table, ...), custom_call_target="tpu_custom_call", output_to_operand_aliasing={{0}: (3, {}), {1}: (4, {}), {2}: (5, {})} | custom-call | flops 805306368 | bytes 10485760 | tf_op jit(solution)/shard_map/pallas_call | solution.py:249
  348.7 8.6 %shard_map.114 = (f32[4,4,1024,128]{3,2,1,0:T(8,128)}, bf16[4,4,128,1024]{3,2,1,0:T(8,128)(2,1)}, bf16[4,4,128,1024]{3,2,1,0:T(8,128)(2,1)}, f32[4,128,256]{2,1,0:T(8,128)}, f32[128,256]{1,0:T(8,128)}) custom-call(s32[67]{0:T(128)} %add_add_fusion.2.table, ...), custom_call_target="tpu_custom_call", output_to_operand_aliasing={{0}: (3, {}), {1}: (4, {}), {2}: (5, {})} | custom-call | flops 805306368 | bytes 10485760 | tf_op jit(solution)/shard_map/pallas_call | solution.py:249
  357.3 2.7 collective-permute-start.8
  360.8 4.0 all-to-all-done.2.got_ref
  364.8 8.0 %shard_map.115 = (f32[4,4,1024,128]{3,2,1,0:T(8,128)}, bf16[4,4,128,1024]{3,2,1,0:T(8,128)(2,1)}, bf16[4,4,128,1024]{3,2,1,0:T(8,128)(2,1)}, f32[128,256]{1,0:T(...) custom-call(s32[67]{0:T(128)} %add_add_fusion.1.table, ...), custom_call_target="tpu_custom_call", output_to_operand_aliasing={{0}: (3, {}), {1}: (4, {}), {2}: (5, {})} | custom-call | flops 805306368 | bytes 10485760 | tf_op jit(solution)/shard_map/pallas_call | solution.py:249
  372.9 3.8 collective-permute-start.15
  377.8 3.6 collective-permute-start.13
  382.0 2.2 collective-permute-start.11
  387.9 2.2 collective-permute-done.13
  390.0 2.8 collective-permute-done.12
  392.8 2.2 collective-permute-done.9
  397.8 3.2 collective-permute-start.16
  402.8 5.2 %shard_map.116.rest_0_ = f32[2048,256]{1,0:T(8,128)} custom-call(s32[2]{0:T(128)} %pad_add_fusion.8.table, bf16[2048,1024]{1,0:T(8,128)(2,1)} %bitcast.134, bf16[2048,1024]{1,0:T(8,128)(2,1)} %bitcast.138, f32[128,256]{1,0:T(8,128)} %copy-done.3, f32[128,256]{1,0:T(8,128)} %copy-done.9), custom_call_target="tpu_custom_call" | custom-call | flops 805306368 | bytes 4194304 | tf_op jit(solution)/shard_map/pallas_call | solution.py:302
  408.0 2.2 collective-permute-start.17
  410.8 5.7 %shard_map.117.rest_0_ = f32[2048,256]{1,0:T(8,128)} custom-call(s32[2]{0:T(128)} %pad_add_fusion.7.table, bf16[2048,1024]{1,0:T(8,128)(2,1)} %bitcast.135, bf16[2048,1024]{1,0:T(8,128)(2,1)} %bitcast.139, f32[128,256]{1,0:T(8,128)} %copy-done.11, f32[128,256]{1,0:T(8,128)} %copy-done.12, f32[2048,256]{1,0:T(8,128)} %shard_map.116.rest_0_), custom_call_target="tpu_custom_call", output_to_operand_aliasing={{}: (5, {})} | custom-call | flops 805306368 | bytes 4194304 | tf_op jit(solution)/shard_map/pallas_call | solution.py:302
  417.8 5.7 %shard_map.118.rest_0_ = f32[2048,256]{1,0:T(8,128)} custom-call(s32[2]{0:T(128)} %pad_add_fusion.6.table, bf16[2048,1024]{1,0:T(8,128)(2,1)} %bitcast.136, bf16[2048,1024]{1,0:T(8,128)(2,1)} %bitcast.140, f32[128,256]{1,0:T(8,128)} %copy-done.13, f32[128,256]{1,0:T(8,128)} %copy-done.15, f32[2048,256]{1,0:T(8,128)} %shard_map.117.rest_0_), custom_call_target="tpu_custom_call", output_to_operand_aliasing={{}: (5, {})} | custom-call | flops 805306368 | bytes 4194304 | tf_op jit(solution)/shard_map/pallas_call | solution.py:302
  424.8 5.7 %shard_map.119 = f32[2048,256]{1,0:T(8,128)} custom-call(s32[2]{0:T(128)} %pad_add_fusion.5.table, bf16[2048,1024]{1,0:T(8,128)(2,1)} %bitcast.137, bf16[2048,1024]{1,0:T(8,128)(2,1)} %bitcast.141, f32[128,256]{1,0:T(8,128)} %copy-done.10, f32[128,256]{1,0:T(8,128)} %copy-done.14, f32[2048,256]{1,0:T(8,128)} %shard_map.118.rest_0_), custom_call_target="tpu_custom_call", output_to_operand_aliasing={{}: (5, {})} | custom-call | flops 805306368 | bytes 4194304 | tf_op jit(solution)/shard_map/pallas_call | solution.py:302
  430.5 33.1 %all_to_all.34 = f32[16,128,256]{2,1,0:T(8,128)S(1)} all-to-all(f32[16,128,256]{2,1,0:T(8,128)} %bitcast.144), channel_id=1, replica_groups=mesh['z'=4,'core'=2,'x'=4,'y'=4] {'x','y'}, dimensions={0} | all-to-all | bytes 4194304 | tf_op jit(solution)/shard_map/all_to_all | solution.py:383
  (160 shorter events, 30.3 us)
Async XLA Ops:
  2.8 35.6 %all-to-all-start = ((f32[16,1,72]{2,1,0:T(1,128)}), f32[16,1,72]{2,1,0:T(1,128)S(1)}, u32[]{:S(2)}, u32[]{:S(2)}) async-start(f32[16,1,72]{2,1,0:T(1,128)} %broadcast_in_dim.87), calls=%async_computation | async-start | bytes 16384 | tf_op jit(solution)/shard_map/all_to_all | solution.py:323
  10.0 48.6 %collective-permute-start.1 = (f32[8,512,128]{2,1,0:T(8,128)}, f32[8,512,128]{2,1,0:T(8,128)S(1)}, u32[]{:S(2)}, u32[]{:S(2)}) collective-permute-start(f32[8,512,128]{2,1,0:T(8,128)} %bitcast.145), channel_id=1, source_target_pairs={{0,4},{4,8},{8,12},{12,0},{1,5},{5,9},{9,13},{13,1},{2,6},{6,10},{... | collective-permute-start | bytes 6291464 | tf_op jit(solution)/shard_map/ppermute | solution.py:363
  19.6 10.7 %copy-start.16 = (f32[16,256]{1,0:T(8,128)S(1)}, f32[16,256]{1,0:T(8,128)}, u32[]{:S(2)}) copy-start(f32[16,256]{1,0:T(8,128)} %param.15) | copy-start | bytes 49156
  26.8 157.7 %collective-permute-start.5 = (f32[2,8,256,256]{3,2,1,0:T(8,128)}, f32[2,8,256,256]{3,2,1,0:T(8,128)}, u32[]{:S(2)}, u32[]{:S(2)}) collective-permute-start(f32[2,8,256,256]{3,2,1,0:T(8,128)} %shard_map.107), channel_id=1, source_target_pairs={{0,1},{1,2},{2,3},{3,0},{4,5},{5,6},{6,7},{7,4},{8,9},{9,10},{10,1... | collective-permute-start | bytes 12582920 | tf_op jit(solution)/shard_map/ppermute | solution.py:363
  28.4 148.6 %collective-permute-start.6 = (f32[2,8,256,256]{3,2,1,0:T(8,128)}, f32[2,8,256,256]{3,2,1,0:T(8,128)}, u32[]{:S(2)}, u32[]{:S(2)}) collective-permute-start(f32[2,8,256,256]{3,2,1,0:T(8,128)} %get-tuple-element.27), channel_id=1, source_target_pairs={{0,3},{1,0},{2,1},{3,2},{4,7},{5,4},{6,5},{7,6},{8,11},{9,8},{10,9... | collective-permute-start | bytes 12582920 | tf_op jit(solution)/shard_map/ppermute | solution.py:363
  31.1 8.6 %copy-start.7 = (f32[128,256]{1,0:T(8,128)S(1)}, f32[128,256]{1,0:T(8,128)}, u32[]{:S(2)}) copy-start(f32[128,256]{1,0:T(8,128)} %param.17) | copy-start | bytes 393220
  40.8 26.8 %all-to-all-start.1 = ((f32[8,136,256]{2,1,0:T(8,128)}), f32[8,136,256]{2,1,0:T(8,128)S(1)}, u32[]{:S(2)}, u32[]{:S(2)}) async-start(f32[8,136,256]{2,1,0:T(8,128)} %broadcast_in_dim.88), calls=%async_computation.1 | async-start | bytes 2228224 | tf_op jit(solution)/shard_map/all_to_all | solution.py:323
  58.6 1.4 copy-start.1
  67.6 7.2 %copy-start = (f32[8,256,2,128]{3,2,1,0:T(2,128)S(1)}, f32[8,256,2,128]{3,2,1,0:T(2,128)}, u32[]{:S(2)}) copy-start(f32[8,256,2,128]{3,2,1,0:T(2,128)} %param.11) | copy-start | bytes 6291460
  67.6 124.5 %all-to-all-start.4 = ((f32[32,1,2,128,128]{4,3,2,1,0:T(8,128)}), f32[32,1,2,128,128]{4,3,2,1,0:T(8,128)}, u32[]{:S(2)}, u32[]{:S(2)}) async-start(f32[32,1,2,128,128]{4,3,2,1,0:T(8,128)} %bitcast.155), calls=%async_computation.4 | async-start | bytes 8388608 | tf_op jit(solution)/shard_map/all_to_all | solution.py:383
  74.9 99.3 %copy-start.2 = (f32[8,512,128]{2,1,0:T(8,128)S(1)}, f32[8,512,128]{2,1,0:T(8,128)}, u32[]{:S(2)}) copy-start(f32[8,512,128]{2,1,0:T(8,128)} %copy-done.1) | copy-start | bytes 6291460
  74.9 71.5 %collective-permute-start.3 = (f32[4,512,128]{2,1,0:T(8,128)S(1)}, f32[4,512,128]{2,1,0:T(8,128)S(1)}, u32[]{:S(2)}, u32[]{:S(2)}) collective-permute-start(f32[4,512,128]{2,1,0:T(8,128)S(1)} %bitcast.157), channel_id=1, source_target_pairs={{0,12},{4,0},{8,4},{12,8},{1,13},{5,1},{9,5},{13,9},{2,14},{6,2},{... | collective-permute-start | bytes 3145736 | tf_op jit(solution)/shard_map/ppermute | solution.py:363
  146.5 24.6 %collective-permute-start.4 = (f32[4,512,128]{2,1,0:T(8,128)S(1)}, f32[4,512,128]{2,1,0:T(8,128)S(1)}, u32[]{:S(2)}, u32[]{:S(2)}) collective-permute-start(f32[4,512,128]{2,1,0:T(8,128)S(1)} %collective-permute-done.3), channel_id=1, source_target_pairs={{0,12},{4,0},{8,4},{12,8},{1,13},{5,1},{9,5},{13,9},{2,14},{6,2},{... | collective-permute-start | bytes 3145736 | tf_op jit(solution)/shard_map/ppermute | solution.py:363
  148.5 25.6 %collective-permute-start.2 = (f32[4,512,128]{2,1,0:T(8,128)S(1)}, f32[4,512,128]{2,1,0:T(8,128)S(1)}, u32[]{:S(2)}, u32[]{:S(2)}) collective-permute-start(f32[4,512,128]{2,1,0:T(8,128)S(1)} %slice.111), channel_id=1, source_target_pairs={{0,4},{4,8},{8,12},{12,0},{1,5},{5,9},{9,13},{13,1},{2,6},{6,10},{... | collective-permute-start | bytes 3145736 | tf_op jit(solution)/shard_map/ppermute | solution.py:363
  192.1 114.7 %all-to-all-start.3 = ((f32[32,2,2,128,128]{4,3,2,1,0:T(8,128)}), f32[32,2,2,128,128]{4,3,2,1,0:T(8,128)}, u32[]{:S(2)}, u32[]{:S(2)}) async-start(f32[32,2,2,128,128]{4,3,2,1,0:T(8,128)} %bitcast.143), calls=%async_computation.3 | async-start | bytes 16777216 | tf_op jit(solution)/shard_map/all_to_all | solution.py:383
  204.6 94.5 %collective-permute-start = (f32[2,8,256,256]{3,2,1,0:T(8,128)}, f32[2,8,256,256]{3,2,1,0:T(8,128)}, u32[]{:S(2)}, u32[]{:S(2)}) collective-permute-start(f32[2,8,256,256]{3,2,1,0:T(8,128)} %shard_map.105), channel_id=1, source_target_pairs={{0,2},{1,3},{2,0},{3,1},{4,6},{5,7},{6,4},{7,5},{8,10},{9,11},{10,... | collective-permute-start | bytes 12582920 | tf_op jit(solution)/shard_map/ppermute | solution.py:363
  306.8 58.0 %all-to-all-start.2 = ((f32[32,1,2,128,128]{4,3,2,1,0:T(8,128)}), f32[32,1,2,128,128]{4,3,2,1,0:T(8,128)}, u32[]{:S(2)}, u32[]{:S(2)}) async-start(f32[32,1,2,128,128]{4,3,2,1,0:T(8,128)} %bitcast.154), calls=%async_computation.2 | async-start | bytes 8388608 | tf_op jit(solution)/shard_map/all_to_all | solution.py:383
  357.3 24.1 %collective-permute-start.8 = (f32[4,128,256]{2,1,0:T(8,128)}, f32[4,128,256]{2,1,0:T(8,128)S(1)}, u32[]{:S(2)}, u32[]{:S(2)}) collective-permute-start(f32[4,128,256]{2,1,0:T(8,128)} %get-tuple-element.40), channel_id=1, source_target_pairs={{0,3},{1,0},{2,1},{3,2},{4,7},{5,4},{6,5},{7,6},{8,11},{9,8},{10,9... | collective-permute-start | bytes 1572872 | tf_op jit(solution)/shard_map/ppermute | solution.py:363
  360.0 21.8 %collective-permute-start.7 = (f32[4,128,256]{2,1,0:T(8,128)}, f32[4,128,256]{2,1,0:T(8,128)S(1)}, u32[]{:S(2)}, u32[]{:S(2)}) collective-permute-start(f32[4,128,256]{2,1,0:T(8,128)} %get-tuple-element.39), channel_id=1, source_target_pairs={{0,1},{1,2},{2,3},{3,0},{4,5},{5,6},{6,7},{7,4},{8,9},{9,10},{10,1... | collective-permute-start | bytes 1572872 | tf_op jit(solution)/shard_map/ppermute | solution.py:363
  364.8 17.0 %copy-start.8 = (f32[4,128,256]{2,1,0:T(8,128)S(1)}, f32[4,128,256]{2,1,0:T(8,128)}, u32[]{:S(2)}) copy-start(f32[4,128,256]{2,1,0:T(8,128)} %get-tuple-element.38) | copy-start | bytes 1572868
  364.8 30.2 %copy-start.5 = (f32[128,256]{1,0:T(8,128)S(1)}, f32[128,256]{1,0:T(8,128)}, u32[]{:S(2)}) copy-start(f32[128,256]{1,0:T(8,128)} %param.16) | copy-start | bytes 393220
  364.8 30.2 %copy-start.6 = (f32[128,256]{1,0:T(8,128)S(1)}, f32[128,256]{1,0:T(8,128)}, u32[]{:S(2)}) copy-start(f32[128,256]{1,0:T(8,128)} %get-tuple-element.45) | copy-start | bytes 393220
  372.9 11.3 %collective-permute-start.15 = (f32[128,256]{1,0:T(8,128)}, f32[128,256]{1,0:T(8,128)S(1)}, u32[]{:S(2)}, u32[]{:S(2)}) collective-permute-start(f32[128,256]{1,0:T(8,128)} %get-tuple-element.44), channel_id=1, source_target_pairs={{0,14},{1,15},{2,12},{3,13},{4,2},{5,3},{6,0},{7,1},{8,6},{9,7},{1... | collective-permute-start | bytes 393224 | tf_op jit(solution)/shard_map/ppermute | solution.py:372
  376.7 9.8 %collective-permute-start.14 = (f32[128,256]{1,0:T(8,128)}, f32[128,256]{1,0:T(8,128)S(1)}, u32[]{:S(2)}, u32[]{:S(2)}) collective-permute-start(f32[128,256]{1,0:T(8,128)} %get-tuple-element.43), channel_id=1, source_target_pairs={{0,10},{1,11},{2,8},{3,9},{4,14},{5,15},{6,12},{7,13},{8,2},{9,3},... | collective-permute-start | bytes 393224 | tf_op jit(solution)/shard_map/ppermute | solution.py:372
  377.8 12.3 %collective-permute-start.13 = (f32[128,256]{1,0:T(8,128)}, f32[128,256]{1,0:T(8,128)S(1)}, u32[]{:S(2)}, u32[]{:S(2)}) collective-permute-start(f32[128,256]{1,0:T(8,128)} %get-tuple-element.42), channel_id=1, source_target_pairs={{0,6},{1,7},{2,4},{3,5},{4,10},{5,11},{6,8},{7,9},{8,14},{9,15},{1... | collective-permute-start | bytes 393224 | tf_op jit(solution)/shard_map/ppermute | solution.py:372
  381.4 11.4 %collective-permute-start.12 = (f32[128,256]{1,0:T(8,128)}, f32[128,256]{1,0:T(8,128)S(1)}, u32[]{:S(2)}, u32[]{:S(2)}) collective-permute-start(f32[128,256]{1,0:T(8,128)} %get-tuple-element.41), channel_id=1, source_target_pairs={{0,2},{1,3},{2,0},{3,1},{4,6},{5,7},{6,4},{7,5},{8,10},{9,11},{10,... | collective-permute-start | bytes 393224 | tf_op jit(solution)/shard_map/ppermute | solution.py:372
  382.0 10.8 %collective-permute-start.11 = (f32[128,256]{1,0:T(8,128)S(1)}, f32[128,256]{1,0:T(8,128)S(1)}, u32[]{:S(2)}, u32[]{:S(2)}) collective-permute-start(f32[128,256]{1,0:T(8,128)S(1)} %get-tuple-element.84), channel_id=1, source_target_pairs={{0,12},{4,0},{8,4},{12,8},{1,13},{5,1},{9,5},{13,9},{2,14},{6,2},{... | collective-permute-start | bytes 393224 | tf_op jit(solution)/shard_map/ppermute | solution.py:363
  384.2 8.6 %collective-permute-start.10 = (f32[128,256]{1,0:T(8,128)S(1)}, f32[128,256]{1,0:T(8,128)S(1)}, u32[]{:S(2)}, u32[]{:S(2)}) collective-permute-start(f32[128,256]{1,0:T(8,128)S(1)} %get-tuple-element.85), channel_id=1, source_target_pairs={{0,8},{4,12},{8,0},{12,4},{1,9},{5,13},{9,1},{13,5},{2,10},{6,14},... | collective-permute-start | bytes 393224 | tf_op jit(solution)/shard_map/ppermute | solution.py:363
  386.5 8.5 %collective-permute-start.9 = (f32[128,256]{1,0:T(8,128)S(1)}, f32[128,256]{1,0:T(8,128)S(1)}, u32[]{:S(2)}, u32[]{:S(2)}) collective-permute-start(f32[128,256]{1,0:T(8,128)S(1)} %get-tuple-element.83), channel_id=1, source_target_pairs={{0,4},{4,8},{8,12},{12,0},{1,5},{5,9},{9,13},{13,1},{2,6},{6,10},{... | collective-permute-start | bytes 393224 | tf_op jit(solution)/shard_map/ppermute | solution.py:363
  395.1 7.0 %copy-start.3 = (f32[128,256]{1,0:T(8,128)}, f32[128,256]{1,0:T(8,128)S(1)}, u32[]{:S(2)}) copy-start(f32[128,256]{1,0:T(8,128)S(1)} %fusion.28.same_ref) | copy-start | bytes 393220
  395.1 7.0 %collective-permute-start.22 = (f32[128,256]{1,0:T(8,128)S(1)}, f32[128,256]{1,0:T(8,128)S(1)}, u32[]{:S(2)}, u32[]{:S(2)}) collective-permute-start(f32[128,256]{1,0:T(8,128)S(1)} %fusion.28.same_ref), channel_id=1, source_target_pairs={{0,16},{16,0},{32,48},{48,32},{64,80},{80,64},{96,112},{112,96},{1... | collective-permute-start | bytes 393224 | tf_op jit(solution)/shard_map/ppermute | solution.py:379
  395.9 12.1 %collective-permute-start.20 = (f32[128,256]{1,0:T(8,128)S(1)}, f32[128,256]{1,0:T(8,128)S(1)}, u32[]{:S(2)}, u32[]{:S(2)}) collective-permute-start(f32[128,256]{1,0:T(8,128)S(1)} %fusion.28.same_ref), channel_id=1, source_target_pairs={{0,32},{16,48},{32,64},{48,80},{64,96},{80,112},{96,0},{112,16},{1... | collective-permute-start | bytes 393224 | tf_op jit(solution)/shard_map/ppermute | solution.py:379
  397.1 13.1 %collective-permute-start.21 = (f32[128,256]{1,0:T(8,128)S(1)}, f32[128,256]{1,0:T(8,128)S(1)}, u32[]{:S(2)}, u32[]{:S(2)}) collective-permute-start(f32[128,256]{1,0:T(8,128)S(1)} %fusion.28.same_ref), channel_id=1, source_target_pairs={{0,48},{16,32},{32,80},{48,64},{64,112},{80,96},{96,16},{112,0},{1... | collective-permute-start | bytes 393224 | tf_op jit(solution)/shard_map/ppermute | solution.py:379
  397.8 25.7 %collective-permute-start.16 = (f32[128,256]{1,0:T(8,128)S(1)}, f32[128,256]{1,0:T(8,128)S(1)}, u32[]{:S(2)}, u32[]{:S(2)}) collective-permute-start(f32[128,256]{1,0:T(8,128)S(1)} %fusion.28.same_ref), channel_id=1, source_target_pairs={{0,64},{16,80},{32,96},{48,112},{64,0},{80,16},{96,32},{112,48},{1... | collective-permute-start | bytes 393224 | tf_op jit(solution)/shard_map/ppermute | solution.py:379
  401.0 15.5 %collective-permute-start.18 = (f32[128,256]{1,0:T(8,128)S(1)}, f32[128,256]{1,0:T(8,128)S(1)}, u32[]{:S(2)}, u32[]{:S(2)}) collective-permute-start(f32[128,256]{1,0:T(8,128)S(1)} %fusion.28.same_ref), channel_id=1, source_target_pairs={{0,96},{16,112},{32,0},{48,16},{64,32},{80,48},{96,64},{112,80},{1... | collective-permute-start | bytes 393224 | tf_op jit(solution)/shard_map/ppermute | solution.py:379
  402.1 0.7 copy-start.9
  402.1 14.4 %collective-permute-start.19 = (f32[128,256]{1,0:T(8,128)S(1)}, f32[128,256]{1,0:T(8,128)S(1)}, u32[]{:S(2)}, u32[]{:S(2)}) collective-permute-start(f32[128,256]{1,0:T(8,128)S(1)} %fusion.28.same_ref), channel_id=1, source_target_pairs={{0,112},{16,96},{32,16},{48,0},{64,48},{80,32},{96,80},{112,64},{1... | collective-permute-start | bytes 393224 | tf_op jit(solution)/shard_map/ppermute | solution.py:379
  408.0 2.2 copy-start.11
  408.0 15.5 %collective-permute-start.17 = (f32[128,256]{1,0:T(8,128)}, f32[128,256]{1,0:T(8,128)S(1)}, u32[]{:S(2)}, u32[]{:S(2)}) collective-permute-start(f32[128,256]{1,0:T(8,128)} %copy-done.3), channel_id=1, source_target_pairs={{0,80},{16,64},{32,112},{48,96},{64,16},{80,0},{96,48},{112,32},{1... | collective-permute-start | bytes 393224 | tf_op jit(solution)/shard_map/ppermute | solution.py:379
  410.2 0.6 copy-start.12
  416.5 0.7 copy-start.13
  417.2 0.6 copy-start.15
  423.5 0.7 copy-start.10
  424.2 0.6 copy-start.14
  430.5 33.2 %copy-start.4 = (f32[128,256]{1,0:T(8,128)S(1)}, f32[128,256]{1,0:T(8,128)}, u32[]{:S(2)}) copy-start(f32[128,256]{1,0:T(8,128)} %copy-done.3) | copy-start | bytes 393220

commit v9 on v8

--- a/solution.py
+++ b/solution.py
@@ -276,46 +276,33 @@
 TALL = 4 * CB
 
 
-def apply_kernel(table, high_ref, low_ref, same_ref, other_ref, *rest):
-    out_ref, x_high, x_low = rest[-3:]
+def apply_kernel(table, high_ref, low_ref, *rest):
+    blocks, (out_ref, x_high, x_low) = rest[:N_ROW], rest[N_ROW:]
 
     @pl.when(pl.program_id(0) == 0)
     def _():
-        core = table[1]
-        for place, ref in ((core, same_ref), (1 - core, other_ref)):
+        for i, ref in enumerate(blocks):
             high, low = split(ref[...])
-            x_high[place] = high
-            x_low[place] = low
-
-    right = (x_high[...].reshape(2 * CB, NCOL), x_low[...].reshape(2 * CB, NCOL))
-    result = dot3((high_ref[...], low_ref[...]), right)
-    if len(rest) > 3:
-        result = result + rest[0][...]
-    out_ref[...] = result
-
-
-def apply(table, high, low, same, other, prior):
-    wide = lambda shape: pl.BlockSpec(shape, lambda u, t: (u, 0))
-    fixed = pl.BlockSpec((CB, NCOL), lambda u, t: (0, 0))
-    columns = pl.BlockSpec((TALL, 2 * CB), lambda u, t: (u, t[0]))
-    before = [] if prior is None else [prior]
+            x_high[table[i]] = high
+            x_low[table[i]] = low
+
+    right = (x_high[...].reshape(N_ROW * CB, NCOL), x_low[...].reshape(N_ROW * CB, NCOL))
+    out_ref[...] = dot3((high_ref[...], low_ref[...]), right)
+
+
+def apply(table, high, low, blocks):
+    rows = pl.BlockSpec((TALL, N_ROW * CB), lambda u, t: (u, 0))
     return pl.pallas_call(
         apply_kernel,
         grid_spec=pltpu.PrefetchScalarGridSpec(
             num_scalar_prefetch=1,
             grid=(N_COL * CB // TALL,),
-            in_specs=[columns, columns, fixed, fixed] + [wide((TALL, NCOL))] * len(before),
-            out_specs=wide((TALL, NCOL)),
-            scratch_shapes=[pltpu.VMEM((2, CB, NCOL), bf16)] * 2,
+            in_specs=[rows, rows] + [pl.BlockSpec((CB, NCOL), lambda u, t: (0, 0))] * N_ROW,
+            out_specs=pl.BlockSpec((TALL, NCOL), lambda u, t: (u, 0)),
+            scratch_shapes=[pltpu.VMEM((N_ROW, CB, NCOL), bf16)] * 2,
         ),
         out_shape=jax.ShapeDtypeStruct((N_COL * CB, NCOL), f32),
-        input_output_aliases={5: 0} if before else {},
-        cost_estimate=pl.CostEstimate(
-            flops=3 * 2 * N_COL * CB * 2 * CB * NCOL,
-            bytes_accessed=4 * N_COL * CB * 4 * CB,
-            transcendentals=0,
-        ),
-    )(table, high, low, same, other, *before)
+    )(table, high, low, *blocks)
 
 
 def to_all(value, axes, count):
@@ -478,14 +465,12 @@
     coarse, *halves = made
     halves = [half.reshape(N_COL * CB, N_ROW * CB) for half in halves]
     z, core = lax.axis_index("z"), lax.axis_index("core")
-    blocks = {}
+    blocks, owners = [], []
     for dz in Z_ORDER:
         for dc in range(2):
-            blocks[dz, dc] = shifted_row(current, dz, dc) if dz or dc else current
-    part = None
-    for dz in Z_ORDER:
-        numbers = jnp.stack([(z - dz) % N_Z, core])
-        part = apply(numbers, *halves, blocks[dz, 0], blocks[dz, 1], part)
+            blocks.append(shifted_row(current, dz, dc) if dz or dc else current)
+            owners.append((z - dz) % N_Z * 2 + (core + dc) % 2)
+    part = apply(jnp.stack(owners), *halves, blocks)
     applied = jnp.sum(exchanged(part.reshape(N_COL, CB, NCOL), COL), axis=0)
     current = current + damping * (rhs - applied) / floor_diag
     return coarse.reshape(N_COL * CB, N_ROW, 1, CB), current

time: 466 us -> 459 us (0.985)
  Pallas kernels: 115 us -> 101 us
    pallas_call x4 -> x1, Pallas kernels: 22.4 us -> 8.32 us  [apply(): pl.pallas_call(apply_kernel, grid_spec=pltpu.PrefetchScalarGridSpec(num_s...]
    ppermute x7, waiting for transfers between devices: 0.02 us -> 5.1 us  [shifted_row(): return lax.ppermute(value, ROW, pairs)]
  transfers between devices with their start and end apart: 28 -> 28, of which waited for: 10 -> 13; matrix products, arithmetic and copies ran while one was open for 7% -> 6% of each run, Pallas kernels for 24% -> 20%
where the time goes in v9:
time: 459 us; the launch traced here: 458 us
  waiting for transfers between devices  211 us (46%)
  Pallas kernels  101 us (22%)
  starting transfers between devices  73.1 us (16%)
  blocking collectives  37 us (8%)
  other arithmetic  19.6 us (4%)
  local copies, waits for them, and re-layouts  14 us (3%)
    ppermute x12, waiting for transfers between devices, shifted(): lax.ppermute(value, axis, [(i, (i + steps) % count) for i in range(count)])  198 us
    all_to_all x1, blocking collectives, exchanged(): return lax.all_to_all(value, axes, split_axis=0, concat_axis=0, tiled=True)  37 us
    pallas_call x4, Pallas kernels, gather(): pl.pallas_call(functools.partial(gather_kernel, group), grid_spec=pltpu.P...  33.5 us
    pallas_call x4, Pallas kernels, products(): pl.pallas_call(functools.partial(product_kernel, base, lane), grid_spec=p...  30.3 us
    pallas_call x4, Pallas kernels, left_products(): pl.pallas_call(functools.partial(left_kernel, group, flips), grid_spec=pl...  29.2 us
    all_to_all x3, starting transfers between devices, exchanged(): return lax.all_to_all(value, axes, split_axis=0, concat_axis=0, tiled=True)  20.2 us
    ppermute x12, starting transfers between devices, shifted(): lax.ppermute(value, axis, [(i, (i + steps) % count) for i in range(count)])  19.5 us
    all_to_all x2, starting transfers between devices, to_all(): return lax.all_to_all(copies, axes, split_axis=0, concat_axis=0, tiled=True)  12.5 us
  transfers between devices with their start and end apart: 28, of which 13 were waited for; matrix products, arithmetic and copies ran while one was open for 6% of the time, Pallas kernels for 20%

profile of v9, /device:TPU:0, one launch (start us, length us, event | category | flops | bytes accessed | tf_op | source)
XLA Modules:
  0.0 457.6 jit_solution(489611346815604029)
XLA Ops:
  2.8 7.1 %all-to-all-start = ((f32[16,1,72]{2,1,0:T(1,128)}), f32[16,1,72]{2,1,0:T(1,128)S(1)}, u32[]{:S(2)}, u32[]{:S(2)}) async-start(f32[16,1,72]{2,1,0:T(1,128)} %broadcast_in_dim.87), calls=%async_computation | async-start | bytes 16384 | tf_op jit(solution)/shard_map/all_to_all | solution.py:310
  10.0 1.9 collective-permute-start.1
  11.9 7.7 %shard_map.104 = (f32[2,8,256,256]{3,2,1,0:T(8,128)}, bf16[8,256,256]{2,1,0:T(8,128)(2,1)}, bf16[8,256,256]{2,1,0:T(8,128)(2,1)}) custom-call(s32[8,8]{1,0:T(8,128)} %live.7, s32[8]{0:T(128)} %policy.7, f32[8,2,4,256,256]{4,3,2,1,0:T(8,128)} %bitcast.133, f32[8,512,128]{2,1,0:T(8,128)} %bitcast.142), custom_call_target="tpu_custom_call" | custom-call | flops 1610612736 | bytes 12582912 | tf_op jit(solution)/shard_map/pallas_call | solution.py:75
  19.6 7.2 %shard_map.107 = f32[2,8,256,256]{3,2,1,0:T(8,128)} custom-call(s32[8,8]{1,0:T(8,128)} %live.7, s32[8]{0:T(128)} %policy.7, f32[8,2,4,256,256]{4,3,2,1,0:T(8,128)} %bitcast.134, bf16[8,256,256]{2,1,0:T(8,128)(2,1)} %get-tuple-element.25.rest_0_.rest_2_, bf16[8,256,256]{2,1,0:T(8,128)(2,1)} %get-tuple-element.26.rest_1_.rest_3_), custom_call_target="tpu_custom_call" | custom-call | flops 1610612736 | bytes 12582912 | tf_op jit(solution)/shard_map/pallas_call | solution.py:75
  26.8 1.5 collective-permute-start.5
  28.4 1.7 collective-permute-start.6
  31.1 7.2 %shard_map.110.t_ref = f32[2,8,256,256]{3,2,1,0:T(8,128)} custom-call(s32[8,8]{1,0:T(8,128)} %live.7, s32[8]{0:T(128)} %policy.7, f32[8,2,4,256,256]{4,3,2,1,0:T(8,128)} %bitcast.135, f32[16,1,256]{2,1,0:T(1,128)} %reshape.672.rest_0_.rest_1_, f32[16,1,256]{2,1,0:T(1,128)} %reshape.672.rest_0_.rest_1_, ...), custom_call_target="tpu_custom_call" | custom-call | flops 1610612736 | bytes 12582912 | tf_op jit(solution)/shard_map/pallas_call | solution.py:75
  40.8 5.4 %all-to-all-start.1 = ((f32[8,136,256]{2,1,0:T(8,128)}), f32[8,136,256]{2,1,0:T(8,128)S(1)}, u32[]{:S(2)}, u32[]{:S(2)}) async-start(f32[8,136,256]{2,1,0:T(8,128)} %broadcast_in_dim.88), calls=%async_computation.1 | async-start | bytes 2228224 | tf_op jit(solution)/shard_map/all_to_all | solution.py:310
  48.2 10.4 %collective-permute-done.1.rest_1_.rest_3_ = f32[8,512,128]{2,1,0:T(8,128)S(1)} collective-permute-done((f32[8,512,128]{2,1,0:T(8,128)}, f32[8,512,128]{2,1,0:T(8,128)S(1)}, u32[]{:S(2)}, u32[]{:S(2)}) %collective-permute-start.1) | collective-permute-done | bytes 2097184 | tf_op jit(solution)/shard_map/ppermute | solution.py:350
  58.6 1.4 copy-done.1
  60.0 7.6 %shard_map.111 = f32[8,2,2,1,2,128,128]{6,5,4,3,2,1,0:T(8,128)} custom-call(s32[208]{0:T(256)} %reshape.663.table, f32[2,8,256,256]{3,2,1,0:T(8,128)} %shard_map.110.t_ref, f32[8,512,128]{2,1,0:T(8,128)} %bitcast.143, f32[8,512,128]{2,1,0:T(8,128)} %copy-done.1, f32[8,512,128]{2,1,0:T(8,128)} %bitcast.144, f32[8,512,128]{2,1,0:T(8,128)} %copy-done.1), custom_call_target="tpu_custom_call" | custom-call | flops 1610612736 | bytes 12582912 | tf_op jit(solution)/shard_map/pallas_call | solution.py:152
  67.6 7.2 %all-to-all-start.4 = ((f32[32,1,2,128,128]{4,3,2,1,0:T(8,128)}), f32[32,1,2,128,128]{4,3,2,1,0:T(8,128)}, u32[]{:S(2)}, u32[]{:S(2)}) async-start(f32[32,1,2,128,128]{4,3,2,1,0:T(8,128)} %bitcast.151), calls=%async_computation.4 | async-start | bytes 8388608 | tf_op jit(solution)/shard_map/all_to_all | solution.py:370
  74.9 3.0 collective-permute-start.3
  77.9 68.5 %collective-permute-done.3 = f32[4,512,128]{2,1,0:T(8,128)S(1)} collective-permute-done((f32[4,512,128]{2,1,0:T(8,128)S(1)}, f32[4,512,128]{2,1,0:T(8,128)S(1)}, u32[]{:S(2)}, u32[]{:S(2)}) %collective-permute-start.3) | collective-permute-done | bytes 1048608 | tf_op jit(solution)/shard_map/ppermute | solution.py:350
  148.5 1.3 collective-permute-start.2
  149.9 21.2 %collective-permute-done.4 = f32[4,512,128]{2,1,0:T(8,128)S(1)} collective-permute-done((f32[4,512,128]{2,1,0:T(8,128)S(1)}, f32[4,512,128]{2,1,0:T(8,128)S(1)}, u32[]{:S(2)}, u32[]{:S(2)}) %collective-permute-start.4) | collective-permute-done | bytes 1048608 | tf_op jit(solution)/shard_map/ppermute | solution.py:350
  171.1 3.0 collective-permute-done.2
  174.1 2.8 pad_maximum_fusion.rest_0_.rest_1_.rest_2_.rest_3_
  176.9 7.5 %shard_map.108.rest_4_ = f32[8,2,2,2,2,128,128]{6,5,4,3,2,1,0:T(8,128)} custom-call(s32[208]{0:T(256)} %reshape.663.table, f32[2,8,256,256]{3,2,1,0:T(8,128)} %collective-permute-done.6.t_ref, f32[24,512,128]{2,1,0:T(8,128)} %pad_maximum_fusion.rest_0_.rest_1_.rest_2_.rest_3_, f32[24,512,128]{2,1,0:T(8,128)} %pad_maximum_fusion.rest_0_.rest_1_.rest_2_.rest_3_, ...), custom_call_target="tpu_custom_call" | custom-call | flops 1610612736 | bytes 12582912 | tf_op jit(solution)/shard_map/pallas_call | solution.py:152
  184.5 7.6 %shard_map.109 = f32[8,2,2,2,2,128,128]{6,5,4,3,2,1,0:T(8,128)} custom-call(s32[208]{0:T(256)} %reshape.663.table, f32[2,8,256,256]{3,2,1,0:T(8,128)} %collective-permute-done.5.t_ref, f32[24,512,128]{2,1,0:T(8,128)} %pad_maximum_fusion.rest_0_.rest_1_.rest_2_.rest_3_, ...), custom_call_target="tpu_custom_call", output_to_operand_aliasing={{}: (6, {})} | custom-call | flops 1610612736 | bytes 12582912 | tf_op jit(solution)/shard_map/pallas_call | solution.py:152
  192.1 5.5 %all-to-all-start.3 = ((f32[32,2,2,128,128]{4,3,2,1,0:T(8,128)}), f32[32,2,2,128,128]{4,3,2,1,0:T(8,128)}, u32[]{:S(2)}, u32[]{:S(2)}) async-start(f32[32,2,2,128,128]{4,3,2,1,0:T(8,128)} %bitcast.138), calls=%async_computation.3 | async-start | bytes 16777216 | tf_op jit(solution)/shard_map/all_to_all | solution.py:370
  197.6 7.1 %shard_map.105 = f32[2,8,256,256]{3,2,1,0:T(8,128)} custom-call(s32[8,8]{1,0:T(8,128)} %live.7, s32[8]{0:T(128)} %policy.7, f32[8,2,4,256,256]{4,3,2,1,0:T(8,128)} %bitcast.136, bf16[8,256,256]{2,1,0:T(8,128)(2,1)} %get-tuple-element.25.rest_0_.rest_2_, bf16[8,256,256]{2,1,0:T(8,128)(2,1)} %get-tuple-element.26.rest_1_.rest_3_), custom_call_target="tpu_custom_call" | custom-call | flops 1610612736 | bytes 12582912 | tf_op jit(solution)/shard_map/pallas_call | solution.py:75
  204.6 3.0 collective-permute-start
  207.8 91.4 %collective-permute-done.t_ref = f32[2,8,256,256]{3,2,1,0:T(8,128)} collective-permute-done((f32[2,8,256,256]{3,2,1,0:T(8,128)}, f32[2,8,256,256]{3,2,1,0:T(8,128)}, u32[]{:S(2)}, u32[]{:S(2)}) %collective-permute-start) | collective-permute-done | bytes 4194336 | tf_op jit(solution)/shard_map/ppermute | solution.py:350
  299.2 7.6 %shard_map.106 = f32[8,2,2,1,2,128,128]{6,5,4,3,2,1,0:T(8,128)} custom-call(s32[208]{0:T(256)} %reshape.663.table, f32[2,8,256,256]{3,2,1,0:T(8,128)} %collective-permute-done.t_ref, f32[24,512,128]{2,1,0:T(8,128)} %pad_maximum_fusion.rest_0_.rest_1_.rest_2_.rest_3_, f32[24,512,128]{2,1,0:T(8,128)} %pad_maximum_fusion.rest_0_.rest_1_.rest_2_.rest_3_, ...), custom_call_target="tpu_custom_call" | custom-call | flops 1610612736 | bytes 12582912 | tf_op jit(solution)/shard_map/pallas_call | solution.py:152
  306.8 7.5 %all-to-all-start.2 = ((f32[32,1,2,128,128]{4,3,2,1,0:T(8,128)}), f32[32,1,2,128,128]{4,3,2,1,0:T(8,128)}, u32[]{:S(2)}, u32[]{:S(2)}) async-start(f32[32,1,2,128,128]{4,3,2,1,0:T(8,128)} %bitcast.150), calls=%async_computation.2 | async-start | bytes 8388608 | tf_op jit(solution)/shard_map/all_to_all | solution.py:370
  315.5 1.4 reduce_window_sum.13
  317.9 9.1 %fusion.8 = (s32[8,16]{1,0:T(8,128)S(1)}, s32[8,16]{1,0:T(8,128)S(1)}, s32[8,16]{1,0:T(8,128)S(1)}, s32[8,16]{1,0:T(8,128)S(1)}) fusion(s32[8,2]{1,0:T(8,128)S(1)} %multiply_add_fusion, s32[8,16,8,2]{3,2,1,0:T(8,128)S(1)} %copy.115, s32[8,16,8,9]{3,2,1,0:T(8,128)S(1)} %reshape.656, s32[]{:T(128)S(6)} %add.408), kind=kLoop, calls=%fused_computation.18 | loop fusion | flops 69120 | bytes 18500 | tf_op jit(solution)/shard_map/reduce_sum | solution.py:326
  331.8 8.4 %shard_map.112 = (f32[4,4,1024,128]{3,2,1,0:T(8,128)}, bf16[4,4,128,1024]{3,2,1,0:T(8,128)(2,1)}, bf16[4,4,128,1024]{3,2,1,0:T(8,128)(2,1)}, f32[4,128,256]{2,1,0:T(8,128)}, f32[128,256]{1,0:T(8,128)}) custom-call(s32[67]{0:T(128)} %add_add_fusion.4.table, f32[32,1,2,128,128]{4,3,2,1,0:T(8,128)} %all-to-all-done.4.got_ref, f32[1024,256]{1,0:T(8,128)} %bitcast.146), custom_call_target="tpu_custom_call" | custom-call | flops 805306368 | bytes 10485760 | tf_op jit(solution)/shard_map/pallas_call | solution.py:249
  340.2 8.4 %shard_map.113 = (f32[4,4,1024,128]{3,2,1,0:T(8,128)}, bf16[4,4,128,1024]{3,2,1,0:T(8,128)(2,1)}, bf16[4,4,128,1024]{3,2,1,0:T(8,128)(2,1)}, f32[4,128,256]{2,1,0:T(8,128)}, f32[128,256]{1,0:T(8,128)}) custom-call(s32[67]{0:T(128)} %add_add_fusion.3.table, ...), custom_call_target="tpu_custom_call", output_to_operand_aliasing={{0}: (3, {}), {1}: (4, {}), {2}: (5, {})} | custom-call | flops 805306368 | bytes 10485760 | tf_op jit(solution)/shard_map/pallas_call | solution.py:249
  348.6 8.7 %shard_map.114 = (f32[4,4,1024,128]{3,2,1,0:T(8,128)}, bf16[4,4,128,1024]{3,2,1,0:T(8,128)(2,1)}, bf16[4,4,128,1024]{3,2,1,0:T(8,128)(2,1)}, f32[4,128,256]{2,1,0:T(8,128)}, f32[128,256]{1,0:T(8,128)}) custom-call(s32[67]{0:T(128)} %add_add_fusion.2.table, ...), custom_call_target="tpu_custom_call", output_to_operand_aliasing={{0}: (3, {}), {1}: (4, {}), {2}: (5, {})} | custom-call | flops 805306368 | bytes 10485760 | tf_op jit(solution)/shard_map/pallas_call | solution.py:249
  357.3 2.8 collective-permute-start.8
  360.9 3.9 all-to-all-done.2.got_ref
  364.8 8.0 %shard_map.115 = (f32[4,4,1024,128]{3,2,1,0:T(8,128)}, bf16[4,4,128,1024]{3,2,1,0:T(8,128)(2,1)}, bf16[4,4,128,1024]{3,2,1,0:T(8,128)(2,1)}, f32[128,256]{1,0:T(...) custom-call(s32[67]{0:T(128)} %add_add_fusion.1.table, ...), custom_call_target="tpu_custom_call", output_to_operand_aliasing={{0}: (3, {}), {1}: (4, {}), {2}: (5, {})} | custom-call | flops 805306368 | bytes 10485760 | tf_op jit(solution)/shard_map/pallas_call | solution.py:249
  372.9 3.1 collective-permute-start.12
  376.3 4.9 %collective-permute-start.14 = (f32[128,256]{1,0:T(8,128)}, f32[128,256]{1,0:T(8,128)S(1)}, u32[]{:S(2)}, u32[]{:S(2)}) collective-permute-start(f32[128,256]{1,0:T(8,128)} %get-tuple-element.43), channel_id=1, source_target_pairs={{0,10},{1,11},{2,8},{3,9},{4,14},{5,15},{6,12},{7,13},{8,2},{9,3},... | collective-permute-start | bytes 393224 | tf_op jit(solution)/shard_map/ppermute | solution.py:359
  381.1 1.9 collective-permute-start.15
  383.3 3.2 collective-permute-start.11
  387.9 3.1 collective-permute-done.15
  392.0 2.2 collective-permute-done.10
  394.4 3.2 collective-permute-start.21
  397.6 3.0 collective-permute-start.20
  401.0 1.5 collective-permute-start.18
  402.4 2.5 collective-permute-start.17
  405.7 2.3 collective-permute-done.20.rest_5_
  408.6 2.2 collective-permute-done.17.rest_2_
  411.5 8.3 %shard_map.116 = f32[2048,256]{1,0:T(8,128)} custom-call(s32[8]{0:T(128)} %stack.82.table, bf16[2048,1024]{1,0:T(8,128)(2,1)} %bitcast.139, bf16[2048,1024]{1,0:T(8,128)(2,1)} %bitcast.140, f32[128,256]{1,0:T(8,128)} %copy-done.3, f32[128,256]{1,0:T(8,128)} %copy-done.15, f32[128,256]{1,0:T(8,128)} %copy-done.14, f32[128,256]{1,0:T(8,128)} %copy-done.13, ...), custom_call_target="tpu_custom_call" | custom-call | tf_op jit(solution)/shard_map/pallas_call | solution.py:295
  419.8 37.0 %all_to_all.34 = f32[16,128,256]{2,1,0:T(8,128)S(1)} all-to-all(f32[16,128,256]{2,1,0:T(8,128)} %bitcast.152), channel_id=1, replica_groups=mesh['z'=4,'core'=2,'x'=4,'y'=4] {'x','y'}, dimensions={0} | all-to-all | bytes 4194304 | tf_op jit(solution)/shard_map/all_to_all | solution.py:370
  (156 shorter events, 23.8 us)
Async XLA Ops:
  2.8 35.6 %all-to-all-start = ((f32[16,1,72]{2,1,0:T(1,128)}), f32[16,1,72]{2,1,0:T(1,128)S(1)}, u32[]{:S(2)}, u32[]{:S(2)}) async-start(f32[16,1,72]{2,1,0:T(1,128)} %broadcast_in_dim.87), calls=%async_computation | async-start | bytes 16384 | tf_op jit(solution)/shard_map/all_to_all | solution.py:310
  10.0 48.6 %collective-permute-start.1 = (f32[8,512,128]{2,1,0:T(8,128)}, f32[8,512,128]{2,1,0:T(8,128)S(1)}, u32[]{:S(2)}, u32[]{:S(2)}) collective-permute-start(f32[8,512,128]{2,1,0:T(8,128)} %bitcast.141), channel_id=1, source_target_pairs={{0,4},{4,8},{8,12},{12,0},{1,5},{5,9},{9,13},{13,1},{2,6},{6,10},{... | collective-permute-start | bytes 6291464 | tf_op jit(solution)/shard_map/ppermute | solution.py:350
  19.6 10.7 %copy-start.16 = (f32[16,256]{1,0:T(8,128)S(1)}, f32[16,256]{1,0:T(8,128)}, u32[]{:S(2)}) copy-start(f32[16,256]{1,0:T(8,128)} %param.15) | copy-start | bytes 49156
  26.8 157.7 %collective-permute-start.5 = (f32[2,8,256,256]{3,2,1,0:T(8,128)}, f32[2,8,256,256]{3,2,1,0:T(8,128)}, u32[]{:S(2)}, u32[]{:S(2)}) collective-permute-start(f32[2,8,256,256]{3,2,1,0:T(8,128)} %shard_map.107), channel_id=1, source_target_pairs={{0,1},{1,2},{2,3},{3,0},{4,5},{5,6},{6,7},{7,4},{8,9},{9,10},{10,1... | collective-permute-start | bytes 12582920 | tf_op jit(solution)/shard_map/ppermute | solution.py:350
  28.4 148.6 %collective-permute-start.6 = (f32[2,8,256,256]{3,2,1,0:T(8,128)}, f32[2,8,256,256]{3,2,1,0:T(8,128)}, u32[]{:S(2)}, u32[]{:S(2)}) collective-permute-start(f32[2,8,256,256]{3,2,1,0:T(8,128)} %get-tuple-element.27), channel_id=1, source_target_pairs={{0,3},{1,0},{2,1},{3,2},{4,7},{5,4},{6,5},{7,6},{8,11},{9,8},{10,9... | collective-permute-start | bytes 12582920 | tf_op jit(solution)/shard_map/ppermute | solution.py:350
  31.1 8.6 %copy-start.7 = (f32[128,256]{1,0:T(8,128)S(1)}, f32[128,256]{1,0:T(8,128)}, u32[]{:S(2)}) copy-start(f32[128,256]{1,0:T(8,128)} %param.17) | copy-start | bytes 393220
  40.8 26.8 %all-to-all-start.1 = ((f32[8,136,256]{2,1,0:T(8,128)}), f32[8,136,256]{2,1,0:T(8,128)S(1)}, u32[]{:S(2)}, u32[]{:S(2)}) async-start(f32[8,136,256]{2,1,0:T(8,128)} %broadcast_in_dim.88), calls=%async_computation.1 | async-start | bytes 2228224 | tf_op jit(solution)/shard_map/all_to_all | solution.py:310
  58.6 1.4 copy-start.1
  67.6 7.2 %copy-start = (f32[8,256,2,128]{3,2,1,0:T(2,128)S(1)}, f32[8,256,2,128]{3,2,1,0:T(2,128)}, u32[]{:S(2)}) copy-start(f32[8,256,2,128]{3,2,1,0:T(2,128)} %param.11) | copy-start | bytes 6291460
  67.6 124.5 %all-to-all-start.4 = ((f32[32,1,2,128,128]{4,3,2,1,0:T(8,128)}), f32[32,1,2,128,128]{4,3,2,1,0:T(8,128)}, u32[]{:S(2)}, u32[]{:S(2)}) async-start(f32[32,1,2,128,128]{4,3,2,1,0:T(8,128)} %bitcast.151), calls=%async_computation.4 | async-start | bytes 8388608 | tf_op jit(solution)/shard_map/all_to_all | solution.py:370
  74.9 99.3 %copy-start.2 = (f32[8,512,128]{2,1,0:T(8,128)S(1)}, f32[8,512,128]{2,1,0:T(8,128)}, u32[]{:S(2)}) copy-start(f32[8,512,128]{2,1,0:T(8,128)} %copy-done.1) | copy-start | bytes 6291460
  74.9 71.5 %collective-permute-start.3 = (f32[4,512,128]{2,1,0:T(8,128)S(1)}, f32[4,512,128]{2,1,0:T(8,128)S(1)}, u32[]{:S(2)}, u32[]{:S(2)}) collective-permute-start(f32[4,512,128]{2,1,0:T(8,128)S(1)} %bitcast.154), channel_id=1, source_target_pairs={{0,12},{4,0},{8,4},{12,8},{1,13},{5,1},{9,5},{13,9},{2,14},{6,2},{... | collective-permute-start | bytes 3145736 | tf_op jit(solution)/shard_map/ppermute | solution.py:350
  146.5 24.6 %collective-permute-start.4 = (f32[4,512,128]{2,1,0:T(8,128)S(1)}, f32[4,512,128]{2,1,0:T(8,128)S(1)}, u32[]{:S(2)}, u32[]{:S(2)}) collective-permute-start(f32[4,512,128]{2,1,0:T(8,128)S(1)} %collective-permute-done.3), channel_id=1, source_target_pairs={{0,12},{4,0},{8,4},{12,8},{1,13},{5,1},{9,5},{13,9},{2,14},{6,2},{... | collective-permute-start | bytes 3145736 | tf_op jit(solution)/shard_map/ppermute | solution.py:350
  148.5 25.6 %collective-permute-start.2 = (f32[4,512,128]{2,1,0:T(8,128)S(1)}, f32[4,512,128]{2,1,0:T(8,128)S(1)}, u32[]{:S(2)}, u32[]{:S(2)}) collective-permute-start(f32[4,512,128]{2,1,0:T(8,128)S(1)} %slice.111), channel_id=1, source_target_pairs={{0,4},{4,8},{8,12},{12,0},{1,5},{5,9},{9,13},{13,1},{2,6},{6,10},{... | collective-permute-start | bytes 3145736 | tf_op jit(solution)/shard_map/ppermute | solution.py:350
  192.1 114.7 %all-to-all-start.3 = ((f32[32,2,2,128,128]{4,3,2,1,0:T(8,128)}), f32[32,2,2,128,128]{4,3,2,1,0:T(8,128)}, u32[]{:S(2)}, u32[]{:S(2)}) async-start(f32[32,2,2,128,128]{4,3,2,1,0:T(8,128)} %bitcast.138), calls=%async_computation.3 | async-start | bytes 16777216 | tf_op jit(solution)/shard_map/all_to_all | solution.py:370
  204.6 94.5 %collective-permute-start = (f32[2,8,256,256]{3,2,1,0:T(8,128)}, f32[2,8,256,256]{3,2,1,0:T(8,128)}, u32[]{:S(2)}, u32[]{:S(2)}) collective-permute-start(f32[2,8,256,256]{3,2,1,0:T(8,128)} %shard_map.105), channel_id=1, source_target_pairs={{0,2},{1,3},{2,0},{3,1},{4,6},{5,7},{6,4},{7,5},{8,10},{9,11},{10,... | collective-permute-start | bytes 12582920 | tf_op jit(solution)/shard_map/ppermute | solution.py:350
  306.8 58.0 %all-to-all-start.2 = ((f32[32,1,2,128,128]{4,3,2,1,0:T(8,128)}), f32[32,1,2,128,128]{4,3,2,1,0:T(8,128)}, u32[]{:S(2)}, u32[]{:S(2)}) async-start(f32[32,1,2,128,128]{4,3,2,1,0:T(8,128)} %bitcast.150), calls=%async_computation.2 | async-start | bytes 8388608 | tf_op jit(solution)/shard_map/all_to_all | solution.py:370
  348.6 11.5 %copy-start.17 = (f32[4,128,256]{2,1,0:T(8,128)S(1)}, f32[4,128,256]{2,1,0:T(8,128)}, u32[]{:S(2)}) copy-start(f32[4,128,256]{2,1,0:T(8,128)} %get-tuple-element.39) | copy-start | bytes 1572868
  357.3 23.8 %collective-permute-start.8 = (f32[4,128,256]{2,1,0:T(8,128)}, f32[4,128,256]{2,1,0:T(8,128)S(1)}, u32[]{:S(2)}, u32[]{:S(2)}) collective-permute-start(f32[4,128,256]{2,1,0:T(8,128)} %get-tuple-element.40), channel_id=1, source_target_pairs={{0,3},{1,0},{2,1},{3,2},{4,7},{5,4},{6,5},{7,6},{8,11},{9,8},{10,9... | collective-permute-start | bytes 1572872 | tf_op jit(solution)/shard_map/ppermute | solution.py:350
  360.1 23.0 %collective-permute-start.7 = (f32[4,128,256]{2,1,0:T(8,128)S(1)}, f32[4,128,256]{2,1,0:T(8,128)S(1)}, u32[]{:S(2)}, u32[]{:S(2)}) collective-permute-start(f32[4,128,256]{2,1,0:T(8,128)S(1)} %copy-done.17), channel_id=1, source_target_pairs={{0,1},{1,2},{2,3},{3,0},{4,5},{5,6},{6,7},{7,4},{8,9},{9,10},{10,1... | collective-permute-start | bytes 1572872 | tf_op jit(solution)/shard_map/ppermute | solution.py:350
  364.8 18.2 %copy-start.8 = (f32[4,128,256]{2,1,0:T(8,128)S(1)}, f32[4,128,256]{2,1,0:T(8,128)}, u32[]{:S(2)}) copy-start(f32[4,128,256]{2,1,0:T(8,128)} %get-tuple-element.38) | copy-start | bytes 1572868
  364.8 29.3 %copy-start.5 = (f32[128,256]{1,0:T(8,128)S(1)}, f32[128,256]{1,0:T(8,128)}, u32[]{:S(2)}) copy-start(f32[128,256]{1,0:T(8,128)} %param.16) | copy-start | bytes 393220
  364.8 29.3 %copy-start.6 = (f32[128,256]{1,0:T(8,128)S(1)}, f32[128,256]{1,0:T(8,128)}, u32[]{:S(2)}) copy-start(f32[128,256]{1,0:T(8,128)} %get-tuple-element.45) | copy-start | bytes 393220
  372.9 10.4 %collective-permute-start.12 = (f32[128,256]{1,0:T(8,128)}, f32[128,256]{1,0:T(8,128)S(1)}, u32[]{:S(2)}, u32[]{:S(2)}) collective-permute-start(f32[128,256]{1,0:T(8,128)} %get-tuple-element.41), channel_id=1, source_target_pairs={{0,2},{1,3},{2,0},{3,1},{4,6},{5,7},{6,4},{7,5},{8,10},{9,11},{10,... | collective-permute-start | bytes 393224 | tf_op jit(solution)/shard_map/ppermute | solution.py:359
  375.9 10.6 %collective-permute-start.13 = (f32[128,256]{1,0:T(8,128)}, f32[128,256]{1,0:T(8,128)S(1)}, u32[]{:S(2)}, u32[]{:S(2)}) collective-permute-start(f32[128,256]{1,0:T(8,128)} %get-tuple-element.42), channel_id=1, source_target_pairs={{0,6},{1,7},{2,4},{3,5},{4,10},{5,11},{6,8},{7,9},{8,14},{9,15},{1... | collective-permute-start | bytes 393224 | tf_op jit(solution)/shard_map/ppermute | solution.py:359
  376.3 11.6 %collective-permute-start.14 = (f32[128,256]{1,0:T(8,128)}, f32[128,256]{1,0:T(8,128)S(1)}, u32[]{:S(2)}, u32[]{:S(2)}) collective-permute-start(f32[128,256]{1,0:T(8,128)} %get-tuple-element.43), channel_id=1, source_target_pairs={{0,10},{1,11},{2,8},{3,9},{4,14},{5,15},{6,12},{7,13},{8,2},{9,3},... | collective-permute-start | bytes 393224 | tf_op jit(solution)/shard_map/ppermute | solution.py:359
  381.1 9.8 %collective-permute-start.15 = (f32[128,256]{1,0:T(8,128)}, f32[128,256]{1,0:T(8,128)S(1)}, u32[]{:S(2)}, u32[]{:S(2)}) collective-permute-start(f32[128,256]{1,0:T(8,128)} %get-tuple-element.44), channel_id=1, source_target_pairs={{0,14},{1,15},{2,12},{3,13},{4,2},{5,3},{6,0},{7,1},{8,6},{9,7},{1... | collective-permute-start | bytes 393224 | tf_op jit(solution)/shard_map/ppermute | solution.py:359
  383.2 7.8 %collective-permute-start.9 = (f32[128,256]{1,0:T(8,128)S(1)}, f32[128,256]{1,0:T(8,128)S(1)}, u32[]{:S(2)}, u32[]{:S(2)}) collective-permute-start(f32[128,256]{1,0:T(8,128)S(1)} %get-tuple-element.83), channel_id=1, source_target_pairs={{0,4},{4,8},{8,12},{12,0},{1,5},{5,9},{9,13},{13,1},{2,6},{6,10},{... | collective-permute-start | bytes 393224 | tf_op jit(solution)/shard_map/ppermute | solution.py:350
  383.3 8.7 %collective-permute-start.11 = (f32[128,256]{1,0:T(8,128)S(1)}, f32[128,256]{1,0:T(8,128)S(1)}, u32[]{:S(2)}, u32[]{:S(2)}) collective-permute-start(f32[128,256]{1,0:T(8,128)S(1)} %get-tuple-element.84), channel_id=1, source_target_pairs={{0,12},{4,0},{8,4},{12,8},{1,13},{5,1},{9,5},{13,9},{2,14},{6,2},{... | collective-permute-start | bytes 393224 | tf_op jit(solution)/shard_map/ppermute | solution.py:350
  386.5 7.7 %collective-permute-start.10 = (f32[128,256]{1,0:T(8,128)S(1)}, f32[128,256]{1,0:T(8,128)S(1)}, u32[]{:S(2)}, u32[]{:S(2)}) collective-permute-start(f32[128,256]{1,0:T(8,128)S(1)} %get-tuple-element.85), channel_id=1, source_target_pairs={{0,8},{4,12},{8,0},{12,4},{1,9},{5,13},{9,1},{13,5},{2,10},{6,14},... | collective-permute-start | bytes 393224 | tf_op jit(solution)/shard_map/ppermute | solution.py:350
  394.3 16.5 %copy-start.3 = (f32[128,256]{1,0:T(8,128)}, f32[128,256]{1,0:T(8,128)S(1)}, u32[]{:S(2)}) copy-start(f32[128,256]{1,0:T(8,128)S(1)} %fusion.28.rest_0_) | copy-start | bytes 393220
  394.3 8.2 %collective-permute-start.22 = (f32[128,256]{1,0:T(8,128)S(1)}, f32[128,256]{1,0:T(8,128)S(1)}, u32[]{:S(2)}, u32[]{:S(2)}) collective-permute-start(f32[128,256]{1,0:T(8,128)S(1)} %fusion.28.rest_0_), channel_id=1, source_target_pairs={{0,80},{16,64},{32,112},{48,96},{64,16},{80,0},{96,48},{112,32},{1... | collective-permute-start | bytes 393224 | tf_op jit(solution)/shard_map/ppermute | solution.py:366
  394.4 10.6 %collective-permute-start.21 = (f32[128,256]{1,0:T(8,128)S(1)}, f32[128,256]{1,0:T(8,128)S(1)}, u32[]{:S(2)}, u32[]{:S(2)}) collective-permute-start(f32[128,256]{1,0:T(8,128)S(1)} %fusion.28.rest_0_), channel_id=1, source_target_pairs={{0,64},{16,80},{32,96},{48,112},{64,0},{80,16},{96,32},{112,48},{1... | collective-permute-start | bytes 393224 | tf_op jit(solution)/shard_map/ppermute | solution.py:366
  397.6 10.4 %collective-permute-start.20 = (f32[128,256]{1,0:T(8,128)S(1)}, f32[128,256]{1,0:T(8,128)S(1)}, u32[]{:S(2)}, u32[]{:S(2)}) collective-permute-start(f32[128,256]{1,0:T(8,128)S(1)} %fusion.28.rest_0_), channel_id=1, source_target_pairs={{0,112},{16,96},{32,16},{48,0},{64,48},{80,32},{96,80},{112,64},{1... | collective-permute-start | bytes 393224 | tf_op jit(solution)/shard_map/ppermute | solution.py:366
  400.6 8.0 %collective-permute-start.19 = (f32[128,256]{1,0:T(8,128)S(1)}, f32[128,256]{1,0:T(8,128)S(1)}, u32[]{:S(2)}, u32[]{:S(2)}) collective-permute-start(f32[128,256]{1,0:T(8,128)S(1)} %fusion.28.rest_0_), channel_id=1, source_target_pairs={{0,96},{16,112},{32,0},{48,16},{64,32},{80,48},{96,64},{112,80},{1... | collective-permute-start | bytes 393224 | tf_op jit(solution)/shard_map/ppermute | solution.py:366
  401.0 7.6 %collective-permute-start.18 = (f32[128,256]{1,0:T(8,128)S(1)}, f32[128,256]{1,0:T(8,128)S(1)}, u32[]{:S(2)}, u32[]{:S(2)}) collective-permute-start(f32[128,256]{1,0:T(8,128)S(1)} %fusion.28.rest_0_), channel_id=1, source_target_pairs={{0,48},{16,32},{32,80},{48,64},{64,112},{80,96},{96,16},{112,0},{1... | collective-permute-start | bytes 393224 | tf_op jit(solution)/shard_map/ppermute | solution.py:366
  402.4 8.4 %copy-start.9 = (f32[128,256]{1,0:T(8,128)}, f32[128,256]{1,0:T(8,128)S(1)}, u32[]{:S(2)}) copy-start(f32[128,256]{1,0:T(8,128)S(1)} %collective-permute-done.22.rest_7_) | copy-start | bytes 393220
  402.4 8.3 %collective-permute-start.17 = (f32[128,256]{1,0:T(8,128)S(1)}, f32[128,256]{1,0:T(8,128)S(1)}, u32[]{:S(2)}, u32[]{:S(2)}) collective-permute-start(f32[128,256]{1,0:T(8,128)S(1)} %fusion.28.rest_0_), channel_id=1, source_target_pairs={{0,32},{16,48},{32,64},{48,80},{64,96},{80,112},{96,0},{112,16},{1... | collective-permute-start | bytes 393224 | tf_op jit(solution)/shard_map/ppermute | solution.py:366
  404.9 5.9 %copy-start.10 = (f32[128,256]{1,0:T(8,128)}, f32[128,256]{1,0:T(8,128)S(1)}, u32[]{:S(2)}) copy-start(f32[128,256]{1,0:T(8,128)S(1)} %collective-permute-done.21.rest_6_) | copy-start | bytes 393220
  404.9 5.8 %collective-permute-start.16 = (f32[128,256]{1,0:T(8,128)S(1)}, f32[128,256]{1,0:T(8,128)S(1)}, u32[]{:S(2)}, u32[]{:S(2)}) collective-permute-start(f32[128,256]{1,0:T(8,128)S(1)} %fusion.28.rest_0_), channel_id=1, source_target_pairs={{0,16},{16,0},{32,48},{48,32},{64,80},{80,64},{96,112},{112,96},{1... | collective-permute-start | bytes 393224 | tf_op jit(solution)/shard_map/ppermute | solution.py:366
  408.0 2.8 copy-start.11
  408.6 2.3 copy-start.12
  408.6 2.3 copy-start.13
  410.8 0.7 copy-start.14
  410.8 0.7 copy-start.15
  419.8 37.1 %copy-start.4 = (f32[128,256]{1,0:T(8,128)S(1)}, f32[128,256]{1,0:T(8,128)}, u32[]{:S(2)}) copy-start(f32[128,256]{1,0:T(8,128)} %copy-done.3) | copy-start | bytes 393220
